TPU v7x, 32 devices: a whole 2x2x4 slice. The times are simulated.
32 devices in a mesh: grp: 2 (over x), seq: 16 (over z, y, core).
Axes of the slice: x: 2, y: 2, z: 4, core: 2. Of those that a mesh axis runs over, the one named last changes fastest.
Arguments:
- anchor_layers: float32 [2, 7077888], P(None, 'seq'), may hold values from -2 to 2
- anchor_other: float32 [2001408], P('seq'), may hold values from -4 to 4
- first_layers: float32 [2, 2, 7077888], P('grp', None, 'seq'), may hold values from -3.8146973e-06 to 3.8146973e-06
- first_other: float32 [2, 2001408], P('grp', 'seq'), may hold values from -3.8146973e-06 to 3.8146973e-06
- second_layers: float32 [2, 2, 7077888], P('grp', None, 'seq'), may hold values from 3.255518e-13 to 1.2997315e-12
- second_other: float32 [2, 2001408], P('grp', 'seq'), may hold values from 3.255518e-13 to 1.2997315e-12
- outer_layers: float32 [2, 7077888], P(None, 'seq'), may hold values from -0.15625 to 0.15625
- outer_other: float32 [2001408], P('seq'), may hold values from -0.15625 to 0.15625
- latents: float32 [8192, 20], P(('grp', 'seq')), may hold values from -6 to 6
- noise: float32 [8192, 20], P(('grp', 'seq')), may hold values from -6 to 6
- lengths: int32 [2, 12], P('grp'), may hold values from 1 to 512, 4096 in all within a row
- timesteps: int32 [2, 12], P('grp'), may hold values from 0 to 999
- null_flags: int32 [2, 12], P('grp'), may hold values 0 or 1
- captions: float32 [2, 12, 768], P('grp'), may hold values from -6 to 6
Outputs:
- weights_layers: float32 [2, 7077888], P(None, 'seq')
- weights_other: float32 [2001408], P('seq')
- moment_one_layers: float32 [2, 2, 7077888], P('grp', None, 'seq')
- moment_one_other: float32 [2, 2001408], P('grp', 'seq')
- moment_two_layers: float32 [2, 2, 7077888], P('grp', None, 'seq')
- moment_two_other: float32 [2, 2001408], P('grp', 'seq')
- average_layers: float32 [2, 7077888], P(None, 'seq')
- average_other: float32 [2001408], P('seq')
- momentum_layers: float32 [2, 7077888], P(None, 'seq')
- momentum_other: float32 [2001408], P('seq')
- loss_value: float32 [2], P('grp')
- clip_norm: float32 [2], P('grp')
Inputs may be any that keep to these rules, and one draw needn't show every extreme that they name: `lengths`: the 12 items of a group cover its 4096 frames in order; the longest has exactly 512 frames.
All inputs are finite; a program needn't handle non-finite values. No bound on the sum of `null_flags` on one device may be relied on, other than what follows from the above.
Results may differ from a plain program's by a relative error of at most 0.012.
Values may be sent and summed in bfloat16 or wider, within the bound.
A program may use at most 384 MiB of HBM per device.

v0:
```python
import math

import jax
import jax.numpy as jnp
from jax import lax
from jax.sharding import PartitionSpec as P

D = 768
HEADS = 12
HD = 64
FF = 3072
E = 512
L = 2
TSTEPS = 1000
STEP_COUNT = 10


HIGH = lax.Precision.HIGHEST
beta_one = 0.9
beta_two = 0.95
adam_eps = 1e-08
decay_rate = 0.01
inner_rate = 0.02
outer_rate = 0.7
outer_mu = 0.9
clip_at = 0.01
logit_scale = 30.0
contrast_weight = 0.05


def passed_along(value, axis, steps):
    count = lax.axis_size(axis)
    initial, last = (max(0, -steps), min(count, count - steps))
    return lax.ppermute(value, axis, [(source, source + steps) for source in range(initial, last)])


def dense(left, right):
    return jnp.dot(left, right, preferred_element_type=jnp.float32)


def exact(left, right):
    return jnp.dot(left, right, precision=HIGH, preferred_element_type=jnp.float32)


def contract_rows(left, right, precision=None):
    return lax.dot_general(
        left,
        right,
        (((0,), (0,)), ((), ())),
        precision=precision,
        preferred_element_type=jnp.float32,
    )


def against_rows(left, right, precision=None):
    return lax.dot_general(
        left,
        right,
        (((1,), (1,)), ((), ())),
        precision=precision,
        preferred_element_type=jnp.float32,
    )


def carve(flat, shapes):
    pieces = []
    start = 0
    for shape in shapes:
        count = math.prod(shape)
        pieces.append(flat[start : start + count].reshape(shape))
        start += count
    return pieces


def carve_layer(flat, shards):
    pieces = flat.reshape(shards, -1)
    cut = D // shards * (4 * D + FF)
    upper = pieces[:, :cut].reshape(D, 4 * D + FF)
    lower = pieces[:, cut:].reshape(FF, D)
    return [upper[:, : 3 * D], upper[:, 3 * D : 4 * D], upper[:, 4 * D :], lower]


def other_shapes(channels, width, text_width, joint_width, blocks):
    return [
        (channels, width),
        (width, channels),
        (width, width),
        (text_width, width),
        (width, joint_width),
        (text_width, joint_width),
        (2 * blocks + 1, width),
        (text_width,),
    ]


def norm_rows(hidden, gain):
    centred = hidden - jnp.mean(hidden, axis=-1, keepdims=True)
    return centred * lax.rsqrt(jnp.mean(centred * centred, axis=-1, keepdims=True) + 1e-05) * gain


def plan(steps):
    angle = (steps.astype(jnp.float32) / TSTEPS + 0.008) / 1.008 * (math.pi / 2)
    return jnp.cos(angle) ** 2


def time_features(steps):
    half = D // 2
    frequency = jnp.exp(-math.log(10000.0) * jnp.arange(half, dtype=jnp.float32) / half)
    angle = steps.astype(jnp.float32)[:, None] * frequency[None, :]
    return jnp.concatenate([jnp.cos(angle), jnp.sin(angle)], axis=1)


def contrast(audio_side, text_side):
    audio_unit = audio_side * lax.rsqrt(
        jnp.sum(audio_side * audio_side, axis=-1, keepdims=True) + 1e-06
    )
    text_unit = text_side * lax.rsqrt(
        jnp.sum(text_side * text_side, axis=-1, keepdims=True) + 1e-06
    )
    logits = logit_scale * jnp.dot(audio_unit, text_unit.T, precision=HIGH)
    diagonal = logit_scale * jnp.sum(audio_unit * text_unit, axis=-1)
    row_terms = jax.nn.logsumexp(logits, axis=1) - diagonal
    column_terms = jax.nn.logsumexp(logits, axis=0) - diagonal
    return 0.5 * (jnp.mean(row_terms) + jnp.mean(column_terms))


def split_heads(rows_in):
    return rows_in.reshape(rows_in.shape[0], HEADS, HD).transpose(1, 0, 2)


def join_heads(heads_in):
    return heads_in.transpose(1, 0, 2).reshape(heads_in.shape[1], HEADS * HD)


def gather_window(local_pairs):
    pieces = {}
    for step in (2, 1, -1, -2):
        pieces[step] = passed_along(local_pairs, "seq", step)
    return jnp.concatenate([pieces[2], pieces[1], local_pairs, pieces[-1], pieces[-2]], axis=0)


def return_window(grad_window, rows):
    total = grad_window[2 * rows : 3 * rows]
    for slot, step in ((0, 2), (1, 1), (3, -1), (4, -2)):
        total = total + passed_along(
            grad_window[slot * rows : (slot + 1) * rows].astype(jnp.bfloat16), "seq", -step
        ).astype(jnp.float32)
    return total


def attend_forward(queries, keys, values, keep):
    scale = HD ** (-0.5)

    def one_head(operands):
        query, key_rows, value_rows = operands
        scores = jnp.where(keep, against_rows(query, key_rows) * scale, -1e30)
        peak = jnp.max(scores, axis=-1, keepdims=True)
        weights = jnp.exp(scores - peak)
        total = jnp.sum(weights, axis=-1, keepdims=True)
        shares = (weights / total).astype(jnp.bfloat16)
        return (dense(shares, value_rows), peak[:, 0], total[:, 0])

    outputs, peaks, totals = lax.map(
        one_head, (split_heads(queries), split_heads(keys), split_heads(values))
    )
    return (join_heads(outputs), peaks, totals)


def attend_backward(queries, keys, values, keep, peaks, totals, grad_out):
    scale = HD ** (-0.5)

    def one_head(operands):
        query, key_rows, value_rows, peak, total, grad_head = operands
        scores = jnp.where(keep, against_rows(query, key_rows) * scale, -1e30)
        shares = jnp.exp(scores - peak[:, None]) / total[:, None]
        grad_value = contract_rows(shares.astype(jnp.bfloat16), grad_head)
        grad_shares = against_rows(grad_head, value_rows)
        inner = jnp.sum(grad_shares * shares, axis=-1, keepdims=True)
        grad_scores = (shares * (grad_shares - inner)).astype(jnp.bfloat16)
        grad_query = dense(grad_scores, key_rows) * scale
        grad_key = contract_rows(grad_scores, query) * scale
        return (grad_query, grad_key, grad_value)

    grad_query, grad_key, grad_value = lax.map(
        one_head,
        (
            split_heads(queries),
            split_heads(keys),
            split_heads(values),
            peaks,
            totals,
            split_heads(grad_out),
        ),
    )
    return (join_heads(grad_query), join_heads(grad_key), join_heads(grad_value))


def layer_forward(hidden, weights, gain_one, gain_two, keep):
    proj_qkv, proj_out, proj_up, proj_down = weights
    width = proj_out.shape[0]
    normed = norm_rows(hidden, gain_one).astype(jnp.bfloat16)
    projected = dense(normed, proj_qkv).astype(jnp.bfloat16)
    window = gather_window(projected[:, width:])
    attended, peaks, totals = attend_forward(
        projected[:, :width], window[:, :width], window[:, width:], keep
    )
    attended = attended.astype(jnp.bfloat16)
    middle = hidden + dense(attended, proj_out)
    second = norm_rows(middle, gain_two).astype(jnp.bfloat16)
    upper = dense(second, proj_up)
    activated = jax.nn.gelu(upper, approximate=True).astype(jnp.bfloat16)
    return (
        middle + dense(activated, proj_down),
        (
            hidden,
            normed,
            projected,
            window,
            peaks,
            totals,
            attended,
            middle,
            second,
            upper,
            activated,
        ),
    )


def layer_backward(grad_hidden, weights, gain_one, gain_two, keep, saved):
    hidden, normed, projected, window, peaks, totals, attended, middle, second, upper, activated = (
        saved
    )
    proj_qkv, proj_out, proj_up, proj_down = weights
    width = proj_out.shape[0]
    rows = hidden.shape[0]
    branch_top = grad_hidden.astype(jnp.bfloat16)
    grad_activated = against_rows(branch_top, proj_down)
    unused, pull_gelu = jax.vjp(lambda value: jax.nn.gelu(value, approximate=True), upper)
    grad_upper = pull_gelu(grad_activated)[0].astype(jnp.bfloat16)
    grad_second = against_rows(grad_upper, proj_up)
    unused, pull_two = jax.vjp(norm_rows, middle, gain_two)
    grad_middle, grad_gain_two = pull_two(grad_second)
    grad_middle = grad_middle + grad_hidden
    branch_mid = grad_middle.astype(jnp.bfloat16)
    grad_attended = against_rows(branch_mid, proj_out).astype(jnp.bfloat16)
    grad_query, grad_keys, grad_values = attend_backward(
        projected[:, :width],
        window[:, :width],
        window[:, width:],
        keep,
        peaks,
        totals,
        grad_attended,
    )
    grad_pairs = return_window(jnp.concatenate([grad_keys, grad_values], axis=1), rows)
    grad_projected = jnp.concatenate([grad_query, grad_pairs], axis=1).astype(jnp.bfloat16)
    grad_normed = against_rows(grad_projected, proj_qkv)
    unused, pull_one = jax.vjp(norm_rows, hidden, gain_one)
    grad_input, grad_gain_one = pull_one(grad_normed)
    operand_pairs = (
        normed,
        grad_projected,
        attended,
        branch_mid,
        second,
        grad_upper,
        activated,
        branch_top,
    )
    return (grad_middle + grad_input, operand_pairs, grad_gain_one, grad_gain_two)


def reduce_layer(operand_pairs, shards):
    normed, grad_projected, attended, branch_mid, second, grad_upper, activated, branch_top = (
        operand_pairs
    )
    upper_full = jnp.concatenate(
        [
            contract_rows(normed, grad_projected),
            contract_rows(attended, branch_mid),
            contract_rows(second, grad_upper),
        ],
        axis=1,
    )
    lower_full = contract_rows(activated, branch_top)
    flat_grad = jnp.concatenate(
        [upper_full.reshape(shards, -1), lower_full.reshape(shards, -1)], axis=1
    ).reshape(-1)
    return lax.psum_scatter(flat_grad, "seq", scatter_dimension=0, tiled=True)


def adam(grad, first, second, anchor):
    first = beta_one * first + (1.0 - beta_one) * grad
    second = beta_two * second + (1.0 - beta_two) * grad * grad
    stepped = first / (1.0 - beta_one**STEP_COUNT)
    scaled = second / (1.0 - beta_two**STEP_COUNT)
    delta = inner_rate * (stepped / (jnp.sqrt(scaled) + adam_eps) + decay_rate * anchor)
    return (first, second, delta)


def per_device(
    anchor_layers,
    anchor_other,
    first_layers,
    first_other,
    second_layers,
    second_other,
    outer_layers,
    outer_other,
    latents,
    noise,
    lengths,
    timesteps,
    null_flags,
    captions,
):
    seq_count = lax.axis_size("seq")
    group_count = lax.axis_size("grp")
    rank = lax.axis_index("seq")
    rows = latents.shape[0]
    channels = latents.shape[1]
    frames_group = rows * seq_count
    lengths = lengths[0]
    timesteps = timesteps[0]
    null_flags = null_flags[0]
    captions = captions[0]
    item_count = lengths.shape[0]
    text_width = captions.shape[1]
    other_low = lax.all_gather(anchor_other.astype(jnp.bfloat16), "seq", axis=0, tiled=True)
    w_in, w_out, w_time, w_text, w_audio, w_caption, gains, null_text = carve(
        other_low, other_shapes(channels, D, text_width, E, L)
    )
    w_time_f = w_time.astype(jnp.float32)
    w_text_f = w_text.astype(jnp.float32)
    w_audio_f = w_audio.astype(jnp.float32)
    w_caption_f = w_caption.astype(jnp.float32)
    gains_f = gains.astype(jnp.float32)
    null_f = null_text.astype(jnp.float32)
    places = rank * rows + jnp.arange(rows, dtype=jnp.int32)
    ends = jnp.cumsum(lengths)
    starts = ends - lengths
    item = jnp.sum((places[:, None] >= ends[None, :]).astype(jnp.int32), axis=1)
    onehot = (item[:, None] == jnp.arange(item_count, dtype=jnp.int32)[None, :]).astype(jnp.float32)
    key_places = rank * rows + jnp.arange(-2 * rows, 3 * rows, dtype=jnp.int32)
    key_item = jnp.sum((key_places[:, None] >= ends[None, :]).astype(jnp.int32), axis=1)
    key_item = jnp.where((key_places >= 0) & (key_places < frames_group), key_item, -1)
    keep = item[:, None] == key_item[None, :]
    lengths_f = lengths[:, None].astype(jnp.float32)
    alpha_bar = plan(timesteps)
    mixing = exact(onehot, jnp.stack([jnp.sqrt(alpha_bar), jnp.sqrt(1.0 - alpha_bar)], axis=1))
    noisy_low = (mixing[:, 0:1] * latents + mixing[:, 1:2] * noise).astype(jnp.bfloat16)
    features = time_features(timesteps)

    def condition_of(time_weight, text_weight, null_vector):
        text = jnp.where(null_flags[:, None] == 1, null_vector[None, :], captions)
        return jax.nn.silu(exact(features, time_weight) + exact(text, text_weight))

    condition, pull_condition = jax.vjp(condition_of, w_time_f, w_text_f, null_f)
    hidden = dense(noisy_low, w_in) + exact(onehot, condition)
    saved_all = []
    for depth in range(L):
        flat = lax.all_gather(anchor_layers[depth].astype(jnp.bfloat16), "seq", axis=0, tiled=True)
        weights = carve_layer(flat, seq_count)
        hidden, saved = layer_forward(
            hidden, weights, gains_f[2 * depth], gains_f[2 * depth + 1], keep
        )
        saved_all.append(saved)
    final = norm_rows(hidden, gains_f[2 * L])
    final_low = final.astype(jnp.bfloat16)
    predicted = dense(final_low, w_out)
    error = predicted - noise
    part_pool = contract_rows(onehot, final, HIGH)
    squared_sum, pool_sum = lax.psum((jnp.sum(error * error), part_pool), "seq")
    pooled = pool_sum / lengths_f
    audio_side = exact(pooled, w_audio_f)
    text_side = exact(captions, w_caption_f)
    clash, pull_clash = jax.vjp(contrast, audio_side, text_side)
    loss = squared_sum / (frames_group * channels) + contrast_weight * clash
    grad_audio_side, grad_text_side = pull_clash(jnp.float32(contrast_weight))
    grad_pred = (2.0 / (frames_group * channels) * error).astype(jnp.bfloat16)
    grad_w_out = contract_rows(final_low, grad_pred)
    grad_w_audio = contract_rows(part_pool / lengths_f, grad_audio_side, HIGH)
    first_here = ((starts >= rank * rows) & (starts < rank * rows + rows)).astype(jnp.float32)
    grad_w_caption = contract_rows(captions * first_here[:, None], grad_text_side, HIGH)
    grad_pooled = against_rows(grad_audio_side, w_audio_f, HIGH) / lengths_f
    grad_final = against_rows(grad_pred, w_out) + exact(onehot, grad_pooled)
    unused, pull_final = jax.vjp(norm_rows, hidden, gains_f[2 * L])
    grad_hidden, grad_gain_final = pull_final(grad_final)
    layer_grads = [None] * L
    gain_grads = [None] * (2 * L + 1)
    gain_grads[2 * L] = grad_gain_final
    for depth in reversed(range(L)):
        flat = lax.all_gather(anchor_layers[depth].astype(jnp.bfloat16), "seq", axis=0, tiled=True)
        weights = carve_layer(flat, seq_count)
        grad_hidden, operand_pairs, grad_gain_one, grad_gain_two = layer_backward(
            grad_hidden, weights, gains_f[2 * depth], gains_f[2 * depth + 1], keep, saved_all[depth]
        )
        gain_grads[2 * depth] = grad_gain_one
        gain_grads[2 * depth + 1] = grad_gain_two
        layer_grads[depth] = reduce_layer(operand_pairs, seq_count)
    stacked = jnp.stack(layer_grads)
    grad_w_in = contract_rows(noisy_low.astype(jnp.float32), grad_hidden, HIGH)
    grad_condition = contract_rows(onehot, grad_hidden, HIGH)
    grad_w_time, grad_w_text, grad_null = pull_condition(grad_condition)
    other_flat = jnp.concatenate(
        [
            grad_w_in.ravel(),
            grad_w_out.ravel(),
            grad_w_time.ravel(),
            grad_w_text.ravel(),
            grad_w_audio.ravel(),
            grad_w_caption.ravel(),
            jnp.stack(gain_grads).ravel(),
            grad_null,
        ]
    )
    other_grad = lax.psum_scatter(other_flat, "seq", scatter_dimension=0, tiled=True)
    square_part = jnp.sum(stacked * stacked) + jnp.sum(other_grad * other_grad)
    total_norm = jnp.sqrt(lax.psum(square_part, "seq"))
    factor = jnp.minimum(1.0, clip_at / (total_norm + 1e-06))
    first_l, second_l, delta_l = adam(
        stacked * factor, first_layers[0], second_layers[0], anchor_layers
    )
    first_o, second_o, delta_o = adam(
        other_grad * factor, first_other[0], second_other[0], anchor_other
    )
    share_l, share_o = (
        lax.psum_scatter(
            delta_l.astype(jnp.bfloat16), "grp", scatter_dimension=1, tiled=True
        ).astype(jnp.float32),
        lax.psum_scatter(
            delta_o.astype(jnp.bfloat16), "grp", scatter_dimension=0, tiled=True
        ).astype(jnp.float32),
    )
    summed_l, summed_o = (
        lax.all_gather(share_l.astype(jnp.bfloat16), "grp", axis=1, tiled=True).astype(
            share_l.dtype
        ),
        lax.all_gather(share_o.astype(jnp.bfloat16), "grp", axis=0, tiled=True).astype(
            share_o.dtype
        ),
    )
    mean_layers = summed_l / group_count
    mean_other = summed_o / group_count
    momentum_layers = outer_mu * outer_layers + mean_layers
    momentum_other = outer_mu * outer_other + mean_other
    new_layers = anchor_layers - outer_rate * (mean_layers + outer_mu * momentum_layers)
    new_other = anchor_other - outer_rate * (mean_other + outer_mu * momentum_other)
    return (
        new_layers,
        new_other,
        first_l[None],
        first_o[None],
        second_l[None],
        second_o[None],
        mean_layers,
        mean_other,
        momentum_layers,
        momentum_other,
        loss.reshape(1),
        total_norm.reshape(1),
    )


def solution(mesh):
    placed = (
        P(None, "seq"),
        P("seq"),
        P("grp", None, "seq"),
        P("grp", "seq"),
        P("grp", None, "seq"),
        P("grp", "seq"),
        P(None, "seq"),
        P("seq"),
        P(("grp", "seq"), None),
        P(("grp", "seq"), None),
        P("grp", None),
        P("grp", None),
        P("grp", None),
        P("grp", None, None),
    )
    return jax.shard_map(
        per_device,
        mesh=mesh,
        in_specs=placed,
        out_specs=(
            P(None, "seq"),
            P("seq"),
            P("grp", None, "seq"),
            P("grp", "seq"),
            P("grp", None, "seq"),
            P("grp", "seq"),
            P(None, "seq"),
            P("seq"),
            P(None, "seq"),
            P("seq"),
            P("grp"),
            P("grp"),
        ),
        check_vma=False,
    )
```

profile of v0, /device:TPU:0, one launch (start us, length us, event | category | flops | bytes accessed | tf_op | source)
XLA Modules:
  0.0 4312.9 jit_solution(3152955523248342755)
XLA Ops:
  13.1 5.0 dynamic-update-slice
  19.4 3.7 fusion.263
  26.6 104.0 %all-reduce.13.cloned.1.call-done = bf16[2001408]{0:T(1024)(128)(2,1)} async-done(((bf16[2001408]{0:T(1024)(128)(2,1)}), bf16[2001408]{0:T(1024)(128)(2,1)}) %all-reduce.13.cloned.1.call-update) | async-done | bytes 4002832
  142.5 132.7 %all-gather.8.cloned.1.call-done = bf16[1,7077888]{1,0:T(2,128)(2,1)} async-done(((bf16[1,442368]{1,0:T(2,128)(2,1)}), bf16[1,7077888]{1,0:T(2,128)(2,1)}) %all-gather.8.cloned.1.call-update) | async-done | bytes 14155792 | tf_op jit(solution)/shard_map/all_gather | solution.py:363
  275.2 299.7 %reduce = bf16[7077888]{0:T(1024)(128)(2,1)} reduce(bf16[1,7077888]{1,0:T(2,128)(2,1)} %all-gather.8.cloned.1.call-done, bf16[]{:T(256)} %constant.279), dimensions={0}, to_apply=%all-gather.reduce_sub_computation | reduce | bytes 28311554 | tf_op jit(solution)/shard_map/all_gather | solution.py:363
  574.9 18.2 reshape.602
  593.1 9.1 slice.290
  602.2 13.4 reshape.603
  618.9 4.0 collective-permute-start
  627.4 4.0 slice.299
  634.0 300.0 %reduce.1 = bf16[7077888]{0:T(1024)(128)(2,1)} reduce(bf16[1,7077888]{1,0:T(2,128)(2,1)} %all-gather.10.cloned.1.call-done, bf16[]{:T(256)} %constant.279), dimensions={0}, to_apply=%all-gather.1.reduce_sub_computation | reduce | bytes 28311554 | tf_op jit(solution)/shard_map/all_gather | solution.py:363
  933.9 17.7 reshape.608
  951.6 5.2 reshape.607
  957.4 9.1 slice.302
  966.6 13.4 reshape.609
  998.7 40.1 while.60
  1042.3 3.8 fusion.98
  1053.2 3.9 collective-permute-start.5
  1057.1 4.6 collective-permute-start.4
  1072.6 4.0 slice.311
  1076.6 5.3 reshape.613
  1090.4 13.3 collective-permute-done.7
  1107.2 4.0 copy.94
  1111.1 4.8 copy.97
  1115.9 4.0 copy.93
  1119.9 4.7 copy.96
  1124.6 39.8 while.61
  1167.9 3.8 fusion.94
  1179.2 69.1 %psum.21 = f32[12,768]{1,0:T(8,128)} all-reduce(f32[12,768]{1,0:T(8,128)} %fusion.145), channel_id=1, replica_groups=mesh['grp'=2,'seq'=16] {'seq'}, use_global_device_ids=true, to_apply=%region_22.23 | all-reduce | flops 9216 | bytes 73728 | tf_op jit(solution)/shard_map/psum | solution.py:374
  1263.4 7.4 fusion.119
  1270.8 5.9 fusion.243
  1278.8 4.4 multiply_reduce_fusion.4
  1294.2 112.7 %while.62 = (s32[]{:T(128)}, bf16[12,256,64]{1,2,0:T(8,128)(2,1)}, f32[12,1280,64]{1,2,0:T(8,128)}, f32[12,1280,64]{1,2,0:T(8,128)}, bf16[12,256,64]{2,1,0:T(8,1...) while((s32[]{:T(128)}, bf16[12,256,64]{1,2,0:T(8,128)(2,1)}, ...), condition=%wide.region_35.36_spmd.clone, body=%wide.region_33.35_spmd.clone.sunk | while | flops 213417728 | bytes 11753609 | solution.py:184
  1417.5 5.4 collective-permute-start.11
  1426.4 10.7 reshape.628
  1439.0 5.6 fusion.246
  1444.5 9.6 collective-permute-done.11
  1460.1 4.1 fusion.144
  1469.5 5.8 fusion.156
  1484.0 96.3 %while.63 = (s32[]{:T(128)}, bf16[12,256,64]{1,2,0:T(8,128)(2,1)S(1)}, f32[12,1280,64]{1,2,0:T(8,128)}, f32[12,1280,64]{1,2,0:T(8,128)}, bf16[12,256,64]{2,1,0:T...) while((s32[]{:T(128)}, ...), condition=%wide.region_42.43_spmd.clone, body=%wide.region_40.42_spmd.clone.sunk | while | flops 213417728 | bytes 11750537 | solution.py:184
  1580.3 3.7 fusion.90
  1586.8 14.2 collective-permute-start.15
  1604.5 10.7 reshape.625
  1615.2 14.6 pad_maximum_fusion.1
  1629.7 17.8 reshape.627
  1647.6 22.4 maximum_bitcast_fusion.1
  1670.0 25.8 copy.120
  1697.7 5.6 fusion.245
  1717.2 4.2 fusion.143
  1726.4 13.6 pad_maximum_fusion
  1740.0 18.1 reshape.624
  1758.1 22.4 maximum_bitcast_fusion
  1780.5 25.8 copy.119
  1817.9 3.6 multiply_reduce_fusion.19
  1821.6 1050.6 %all-reduce.19.cloned.1.call-done = (f32[7077888]{0:T(1024)}, f32[7077888]{0:T(1024)}, f32[2001408]{0:T(1024)}) async-done(((f32[7077888]{0:T(1024)}, f32[7077888]{0:T(1024)}, f32[2001408]{0:T(1024)}), (f32[7077888]{0:T(1024)}, f32[7077888]{0:T(1024)}, f32[2001408]{0:T(1024)})) %all-reduce.19.cloned.1.call-update) | async-done | bytes 64628752
  2878.3 4.3 multiply_reduce_fusion.2
  2883.9 32.6 all-reduce.6
  2920.3 16.1 multiply_convert_fusion.2
  2936.4 66.1 %copy.114 = bf16[2,442368]{0,1:T(8,128)(2,1)} copy(bf16[2,442368]{1,0:T(2,128)(2,1)} %multiply_convert_fusion.2) | data formatting | bytes 3538944
  3011.9 11.8 fusion.103
  3026.6 1196.6 %reduce-scatter.4.cloned.1.call-done = bf16[221184,2]{1,0:T(8,128)(2,1)} async-done(((bf16[442368,2]{1,0:T(8,128)(2,1)}), bf16[221184,2]{1,0:T(8,128)(2,1)}) %reduce-scatter.4.cloned.1.call-update) | async-done | bytes 884752
  4223.1 40.2 copy.115
  4265.9 27.2 all-gather.6.cloned.1.call-done
  4293.0 10.3 multiply_subtract_fusion
  (795 shorter events, 503.7 us)
Async XLA Ops:
  7.2 123.4 %all-reduce.13.cloned.1.call-start = ((), (), s32[]{:S(2)}) async-start(), calls=%async_computation.4 | async-start | bytes 8007680
  18.1 257.1 %all-gather.8.cloned.1.call-start = ((), (), s32[]{:S(2)}) async-start(), calls=%async_computation.2 | async-start | bytes 30081024 | tf_op jit(solution)/shard_map/all_gather | solution.py:363
  23.2 610.8 %all-gather.10.cloned.1.call-start = ((), (), s32[]{:S(2)}) async-start(), calls=%async_computation.3 | async-start | bytes 30081024 | tf_op jit(solution)/shard_map/all_gather | solution.py:363
  23.9 2848.2 %all-reduce.19.cloned.1.call-start = ((), (), s32[]{:S(2)}) async-start(), calls=%async_computation.8 | async-start | bytes 129261568
  24.2 110.2 %copy-start.110 = (s32[12,1]{0,1:T(1,128)}, s32[12,1]{0,1:T(1,128)S(1)}, u32[]{:S(2)}) copy-start(s32[12,1]{0,1:T(1,128)S(1)} %reduce-window.7) | copy-start | bytes 148
  24.9 115.1 %copy-start.65 = (s32[256]{0:T(256)}, s32[256]{0:T(256)S(1)}, u32[]{:S(2)}) copy-start(s32[256]{0:T(256)S(1)} %convert_reduce_fusion.1) | copy-start | bytes 3076
  26.6 114.0 %copy-start.52 = (bf16[256,20]{0,1:T(8,128)(2,1)}, bf16[256,20]{0,1:T(8,128)(2,1)S(1)}, u32[]{:S(2)}) copy-start(bf16[256,20]{0,1:T(8,128)(2,1)S(1)} %add_convert_fusion.1) | copy-start | bytes 30724
  141.0 898.5 %copy-start.10 = (f32[256,768]{1,0:T(8,128)}, f32[256,768]{1,0:T(8,128)S(1)}, u32[]{:S(2)}) copy-start(f32[256,768]{1,0:T(8,128)S(1)} %get-tuple-element.633) | copy-start | bytes 2359300
  141.0 474.6 %copy-start.72 = (f32[256]{0:T(256)}, f32[256]{0:T(256)S(1)}, u32[]{:S(2)}) copy-start(f32[256]{0:T(256)S(1)} %broadcast_multiply_fusion.4) | copy-start | bytes 3076
  141.8 473.8 %copy-start.84 = (f32[256]{0:T(256)}, f32[256]{0:T(256)S(1)}, u32[]{:S(2)}) copy-start(f32[256]{0:T(256)S(1)} %fusion.222) | copy-start | bytes 3076
  142.5 473.1 %copy-start.48 = (f32[768]{0:T(1024)}, f32[768]{0:T(1024)S(1)}, u32[]{:S(2)}) copy-start(f32[768]{0:T(1024)S(1)} %get-tuple-element.621) | copy-start | bytes 9220
  615.6 7.2 copy-start.120
  615.6 10.5 copy-start.60
  615.7 10.5 copy-start.111
  618.8 12.5 copy-start.27
  618.9 361.0 %collective-permute-start = (bf16[256,1536]{1,0:T(8,128)(2,1)S(1)}, bf16[256,1536]{1,0:T(8,128)(2,1)}, u32[]{:S(2)}, u32[]{:S(2)}) collective-permute-start(bf16[256,1536]{1,0:T(8,128)(2,1)S(1)} %slice.293), channel_id=1, source_target_pairs={{0,2},{1,3},{2,4},{3,5},{4,6},{5,7},{6,8},{7,9},{8,10},{9,11},{10,... | collective-permute-start | bytes 2359304 | tf_op jit(solution)/shard_map/ppermute | solution.py:34
  623.4 357.8 %collective-permute-start.1 = (bf16[256,1536]{1,0:T(8,128)(2,1)S(1)}, bf16[256,1536]{1,0:T(8,128)(2,1)}, u32[]{:S(2)}, u32[]{:S(2)}) collective-permute-start(bf16[256,1536]{1,0:T(8,128)(2,1)S(1)} %slice.293), channel_id=1, source_target_pairs={{0,1},{1,2},{2,3},{3,4},{4,5},{5,6},{6,7},{7,8},{8,9},{9,10},{10,1... | collective-permute-start | bytes 2359304 | tf_op jit(solution)/shard_map/ppermute | solution.py:34
  631.4 352.3 %collective-permute-start.3 = (bf16[256,1536]{1,0:T(8,128)(2,1)S(1)}, bf16[256,1536]{1,0:T(8,128)(2,1)}, u32[]{:S(2)}, u32[]{:S(2)}) collective-permute-start(bf16[256,1536]{1,0:T(8,128)(2,1)S(1)} %slice.293), channel_id=1, source_target_pairs={{2,0},{3,1},{4,2},{5,3},{6,4},{7,5},{8,6},{9,7},{10,8},{11,9},{12,... | collective-permute-start | bytes 2359304 | tf_op jit(solution)/shard_map/ppermute | solution.py:34
  632.7 349.8 %collective-permute-start.2 = (bf16[256,1536]{1,0:T(8,128)(2,1)S(1)}, bf16[256,1536]{1,0:T(8,128)(2,1)}, u32[]{:S(2)}, u32[]{:S(2)}) collective-permute-start(bf16[256,1536]{1,0:T(8,128)(2,1)S(1)} %slice.293), channel_id=1, source_target_pairs={{1,0},{2,1},{3,2},{4,3},{5,4},{6,5},{7,6},{8,7},{9,8},{10,9},{11,1... | collective-permute-start | bytes 2359304 | tf_op jit(solution)/shard_map/ppermute | solution.py:34
  1038.8 7.3 copy-start.33
  1039.4 6.7 slice-start.3
  1052.2 12.1 copy-start.51
  1053.2 34.8 collective-permute-start.5
  1057.1 29.6 collective-permute-start.4
  1081.9 21.9 collective-permute-start.7
  1083.2 6.1 collective-permute-start.6
  1165.1 6.7 slice-start.7
  1248.3 13.3 copy-start.29
  1248.3 13.3 copy-start.57
  1248.3 13.3 copy-start.68
  1248.3 13.3 copy-start.71
  1248.3 14.7 copy-start.107
  1263.3 7.4 copy-start.17
  1270.8 6.5 copy-start.36
  1270.8 7.4 copy-start.83
  1270.8 8.0 copy-start.80
  1270.8 8.0 copy-start.92
  1406.9 7.2 copy-start.4
  1416.2 28.3 collective-permute-start.8
  1417.5 36.7 collective-permute-start.11
  1422.9 31.3 collective-permute-start.10
  1425.1 29.1 collective-permute-start.9
  1439.0 15.2 copy-start.3
  1439.0 15.2 copy-start.5
  1444.5 12.0 copy-start.35
  1444.5 12.0 copy-start.78
  1444.5 12.0 copy-start.90
  1456.6 8.2 slice-start.5
  1466.1 9.8 slice-start
  1466.1 9.8 slice-start.1
  1585.5 117.8 %collective-permute-start.12 = (bf16[256,1536]{0,1:T(8,128)(2,1)}, bf16[256,1536]{0,1:T(8,128)(2,1)S(1)}, u32[]{:S(2)}, u32[]{:S(2)}) collective-permute-start(bf16[256,1536]{0,1:T(8,128)(2,1)} %get-tuple-element.601), channel_id=1, source_target_pairs={{2,0},{3,1},{4,2},{5,3},{6,4},{7,5},{8,6},{9,7},{10,8},{11,9},{12,... | collective-permute-start | bytes 2359304 | tf_op jit(solution)/shard_map/ppermute | solution.py:34
  1586.8 116.6 %collective-permute-start.15 = (bf16[256,1536]{0,1:T(8,128)(2,1)}, bf16[256,1536]{0,1:T(8,128)(2,1)}, u32[]{:S(2)}, u32[]{:S(2)}) collective-permute-start(bf16[256,1536]{0,1:T(8,128)(2,1)} %get-tuple-element.602), channel_id=1, source_target_pairs={{0,2},{1,3},{2,4},{3,5},{4,6},{5,7},{6,8},{7,9},{8,10},{9,11},{10,... | collective-permute-start | bytes 2359304 | tf_op jit(solution)/shard_map/ppermute | solution.py:34
  1601.0 102.4 %collective-permute-start.14 = (bf16[256,1536]{0,1:T(8,128)(2,1)}, bf16[256,1536]{0,1:T(8,128)(2,1)}, u32[]{:S(2)}, u32[]{:S(2)}) collective-permute-start(bf16[256,1536]{0,1:T(8,128)(2,1)} %get-tuple-element.603), channel_id=1, source_target_pairs={{0,1},{1,2},{2,3},{3,4},{4,5},{5,6},{6,7},{7,8},{8,9},{9,10},{10,1... | collective-permute-start | bytes 2359304 | tf_op jit(solution)/shard_map/ppermute | solution.py:34
  1603.2 100.2 %collective-permute-start.13 = (bf16[256,1536]{0,1:T(8,128)(2,1)S(1)}, bf16[256,1536]{0,1:T(8,128)(2,1)}, u32[]{:S(2)}, u32[]{:S(2)}) collective-permute-start(bf16[256,1536]{0,1:T(8,128)(2,1)S(1)} %get-tuple-element.604), channel_id=1, source_target_pairs={{1,0},{2,1},{3,2},{4,3},{5,4},{6,5},{7,6},{8,7},{9,8},{10,9},{11,1... | collective-permute-start | bytes 2359304 | tf_op jit(solution)/shard_map/ppermute | solution.py:34
  1670.0 25.8 copy-start.26
  1780.5 26.4 copy-start.45
  1780.5 27.0 copy-start.16
  1816.5 1189.9 %all-reduce.17.cloned.1.call-start = ((), (), s32[]{:S(2)}) async-start(), calls=%async_computation.7 | async-start | bytes 503808
  2878.3 42.0 copy-start.7
  2920.2 1302.9 %reduce-scatter.4.cloned.1.call-start = ((), (), s32[]{:S(2)}) async-start(), calls=%async_computation.6 | async-start | bytes 169869312
  3002.6 1260.8 %all-reduce.15.cloned.1.call-start = ((), (), s32[]{:S(2)}) async-start(), calls=%async_computation.5 | async-start | bytes 503808
  3011.8 1281.2 %all-gather.6.cloned.1.call-start = ((), (), s32[]{:S(2)}) async-start(), calls=%async_computation.1 | async-start | bytes 2654208 | tf_op jit(solution)/shard_map/all_gather | solution.py:437
  3011.9 11.8 copy-start.31
  3011.9 12.9 copy-start.30
  (97 other events, 280.6 us)
Sparse Core Ops, SparseCore 0:
  18.2 112.2 all-reduce.12
  132.7 142.4 all-gather.7
  277.4 143.3 all-gather.9
  1816.6 1055.5 all-reduce.18
  2920.4 20.2 all-reduce.16
  3002.7 1220.4 reduce-scatter.3
  4226.1 23.0 all-reduce.14
  4263.5 29.5 all-gather.5
where the time goes:
time: 4340 us; the launch traced here: 4310 us
  waiting for transfers between devices  2530 us (58%)
  other arithmetic  762 us (18%)
  local copies, waits for them, and re-layouts  464 us (11%)
  matrix products  372 us (9%)
  blocking collectives  102 us (2%)
  starting transfers between devices  49.9 us (1%)
    unnamed x13, waiting for transfers between devices  2350 us
    all_gather x2, other arithmetic, per_device(): lax.all_gather(anchor_layers[depth].astype(jnp.bfloat16), 'seq', axis=0,...  600 us
    unnamed x307, local copies, waits for them, and re-layouts  221 us
    dot_general x82, matrix products, against_rows(): lax.dot_general(left, right, (((1,), (1,)), ((), ())), precision=precisio...  134 us
    all_gather x2, waiting for transfers between devices, per_device(): lax.all_gather(anchor_layers[depth].astype(jnp.bfloat16), 'seq', axis=0,...  133 us
    dot_general x62, matrix products, contract_rows(): lax.dot_general(left, right, (((0,), (0,)), ((), ())), precision=precisio...  121 us
    dot_general x58, matrix products, dense(): return jnp.dot(left, right, preferred_element_type=jnp.float32)  97.4 us
  transfers between devices with their start and end apart: 24, of which 7 were waited for; matrix products, arithmetic and copies ran while one was open for 23% of the time, Pallas kernels for 0%

commit v1 on v0

--- a/solution.py
+++ b/solution.py
@@ -338,7 +338,8 @@
     gains_f = gains.astype(jnp.float32)
     null_f = null_text.astype(jnp.float32)
     places = rank * rows + jnp.arange(rows, dtype=jnp.int32)
-    ends = jnp.cumsum(lengths)
+    order = jnp.arange(item_count, dtype=jnp.int32)
+    ends = jnp.sum(jnp.where(order[None, :] <= order[:, None], lengths[None, :], 0), axis=1)
     starts = ends - lengths
     item = jnp.sum((places[:, None] >= ends[None, :]).astype(jnp.int32), axis=1)
     onehot = (item[:, None] == jnp.arange(item_count, dtype=jnp.int32)[None, :]).astype(jnp.float32)

time: 4340 us -> 4340 us (level)
  no operation moved by 1% of the time
where the time goes in v1:
time: 4340 us; the launch traced here: 4310 us
  waiting for transfers between devices  2530 us (58%)
  other arithmetic  762 us (18%)
  local copies, waits for them, and re-layouts  464 us (11%)
  matrix products  372 us (9%)
  blocking collectives  102 us (2%)
  starting transfers between devices  49.9 us (1%)
    unnamed x13, waiting for transfers between devices  2350 us
    all_gather x2, other arithmetic, per_device(): lax.all_gather(anchor_layers[depth].astype(jnp.bfloat16), 'seq', axis=0,...  600 us
    unnamed x307, local copies, waits for them, and re-layouts  221 us
    dot_general x82, matrix products, against_rows(): lax.dot_general(left, right, (((1,), (1,)), ((), ())), precision=precisio...  134 us
    all_gather x2, waiting for transfers between devices, per_device(): lax.all_gather(anchor_layers[depth].astype(jnp.bfloat16), 'seq', axis=0,...  133 us
    dot_general x62, matrix products, contract_rows(): lax.dot_general(left, right, (((0,), (0,)), ((), ())), precision=precisio...  121 us
    dot_general x58, matrix products, dense(): return jnp.dot(left, right, preferred_element_type=jnp.float32)  97.4 us
  transfers between devices with their start and end apart: 24, of which 7 were waited for; matrix products, arithmetic and copies ran while one was open for 23% of the time, Pallas kernels for 0%

profile of v1, /device:TPU:0, one launch (start us, length us, event | category | flops | bytes accessed | tf_op | source)
XLA Modules:
  0.0 4312.9 jit_solution(7886170958153634253)
XLA Ops:
  13.1 5.0 dynamic-update-slice
  19.5 3.7 fusion.263
  26.5 104.1 %all-reduce.13.cloned.1.call-done = bf16[2001408]{0:T(1024)(128)(2,1)} async-done(((bf16[2001408]{0:T(1024)(128)(2,1)}), bf16[2001408]{0:T(1024)(128)(2,1)}) %all-reduce.13.cloned.1.call-update) | async-done | bytes 4002832
  142.6 132.7 %all-gather.8.cloned.1.call-done = bf16[1,7077888]{1,0:T(2,128)(2,1)} async-done(((bf16[1,442368]{1,0:T(2,128)(2,1)}), bf16[1,7077888]{1,0:T(2,128)(2,1)}) %all-gather.8.cloned.1.call-update) | async-done | bytes 14155792 | tf_op jit(solution)/shard_map/all_gather | solution.py:364
  275.3 299.7 %reduce = bf16[7077888]{0:T(1024)(128)(2,1)} reduce(bf16[1,7077888]{1,0:T(2,128)(2,1)} %all-gather.8.cloned.1.call-done, bf16[]{:T(256)} %constant.276), dimensions={0}, to_apply=%all-gather.reduce_sub_computation | reduce | bytes 28311554 | tf_op jit(solution)/shard_map/all_gather | solution.py:364
  575.0 18.2 reshape.580
  593.2 9.1 slice.290
  602.3 13.4 reshape.581
  619.0 4.0 collective-permute-start
  627.4 4.0 slice.299
  634.0 300.0 %reduce.1 = bf16[7077888]{0:T(1024)(128)(2,1)} reduce(bf16[1,7077888]{1,0:T(2,128)(2,1)} %all-gather.10.cloned.1.call-done, bf16[]{:T(256)} %constant.276), dimensions={0}, to_apply=%all-gather.1.reduce_sub_computation | reduce | bytes 28311554 | tf_op jit(solution)/shard_map/all_gather | solution.py:364
  933.9 17.7 reshape.586
  951.6 5.2 reshape.585
  957.4 9.1 slice.302
  966.5 13.4 reshape.587
  998.7 40.1 while.60
  1042.3 3.8 fusion.98
  1053.2 3.9 collective-permute-start.5
  1057.1 4.6 collective-permute-start.4
  1072.7 4.0 slice.311
  1076.7 5.3 reshape.591
  1090.5 13.3 collective-permute-done.7
  1107.2 4.0 copy.94
  1111.2 4.8 copy.97
  1116.0 4.0 copy.93
  1119.9 4.7 copy.96
  1124.7 39.8 while.61
  1168.0 3.8 fusion.94
  1179.3 69.1 %psum.21 = f32[12,768]{1,0:T(8,128)} all-reduce(f32[12,768]{1,0:T(8,128)} %fusion.145), channel_id=1, replica_groups=mesh['grp'=2,'seq'=16] {'seq'}, use_global_device_ids=true, to_apply=%region_22.23 | all-reduce | flops 9216 | bytes 73728 | tf_op jit(solution)/shard_map/psum | solution.py:375
  1263.4 7.4 fusion.119
  1270.8 5.9 fusion.243
  1278.8 4.4 multiply_reduce_fusion.4
  1294.3 112.7 %while.62 = (s32[]{:T(128)}, bf16[12,256,64]{1,2,0:T(8,128)(2,1)}, f32[12,1280,64]{1,2,0:T(8,128)}, f32[12,1280,64]{1,2,0:T(8,128)}, bf16[12,256,64]{2,1,0:T(8,1...) while((s32[]{:T(128)}, bf16[12,256,64]{1,2,0:T(8,128)(2,1)}, ...), condition=%wide.region_35.36_spmd.clone, body=%wide.region_33.35_spmd.clone.sunk | while | flops 213417728 | bytes 11753609 | solution.py:184
  1417.5 5.4 collective-permute-start.11
  1426.4 10.7 reshape.605
  1439.0 5.6 fusion.246
  1444.6 9.6 collective-permute-done.11
  1460.1 4.1 fusion.144
  1469.5 5.8 fusion.156
  1484.0 96.3 %while.63 = (s32[]{:T(128)}, bf16[12,256,64]{1,2,0:T(8,128)(2,1)S(1)}, f32[12,1280,64]{1,2,0:T(8,128)}, f32[12,1280,64]{1,2,0:T(8,128)}, bf16[12,256,64]{2,1,0:T...) while((s32[]{:T(128)}, ...), condition=%wide.region_42.43_spmd.clone, body=%wide.region_40.42_spmd.clone.sunk | while | flops 213417728 | bytes 11750537 | solution.py:184
  1580.4 3.7 fusion.90
  1586.8 14.2 collective-permute-start.15
  1604.5 10.7 reshape.602
  1615.2 14.6 pad_maximum_fusion.1
  1629.8 17.8 reshape.604
  1647.6 22.4 maximum_bitcast_fusion.1
  1670.1 25.8 copy.120
  1697.8 5.6 fusion.245
  1717.2 4.2 fusion.143
  1726.5 13.6 pad_maximum_fusion
  1740.1 18.1 reshape.601
  1758.2 22.4 maximum_bitcast_fusion
  1780.6 25.8 copy.119
  1817.9 3.6 multiply_reduce_fusion.19
  1821.6 1050.6 %all-reduce.19.cloned.1.call-done = (f32[7077888]{0:T(1024)}, f32[7077888]{0:T(1024)}, f32[2001408]{0:T(1024)}) async-done(((f32[7077888]{0:T(1024)}, f32[7077888]{0:T(1024)}, f32[2001408]{0:T(1024)}), (f32[7077888]{0:T(1024)}, f32[7077888]{0:T(1024)}, f32[2001408]{0:T(1024)})) %all-reduce.19.cloned.1.call-update) | async-done | bytes 64628752
  2878.3 4.3 multiply_reduce_fusion.2
  2883.9 32.6 all-reduce.6
  2920.3 16.1 multiply_convert_fusion.2
  2936.4 66.1 %copy.114 = bf16[2,442368]{0,1:T(8,128)(2,1)} copy(bf16[2,442368]{1,0:T(2,128)(2,1)} %multiply_convert_fusion.2) | data formatting | bytes 3538944
  3012.0 11.7 fusion.103
  3026.6 1196.5 %reduce-scatter.4.cloned.1.call-done = bf16[221184,2]{1,0:T(8,128)(2,1)} async-done(((bf16[442368,2]{1,0:T(8,128)(2,1)}), bf16[221184,2]{1,0:T(8,128)(2,1)}) %reduce-scatter.4.cloned.1.call-update) | async-done | bytes 884752
  4223.1 40.2 copy.115
  4265.9 27.1 all-gather.6.cloned.1.call-done
  4293.0 10.3 multiply_subtract_fusion
  (795 shorter events, 503.6 us)
Async XLA Ops:
  7.2 123.4 %all-reduce.13.cloned.1.call-start = ((), (), s32[]{:S(2)}) async-start(), calls=%async_computation.4 | async-start | bytes 8007680
  18.1 257.2 %all-gather.8.cloned.1.call-start = ((), (), s32[]{:S(2)}) async-start(), calls=%async_computation.2 | async-start | bytes 30081024 | tf_op jit(solution)/shard_map/all_gather | solution.py:364
  23.2 610.8 %all-gather.10.cloned.1.call-start = ((), (), s32[]{:S(2)}) async-start(), calls=%async_computation.3 | async-start | bytes 30081024 | tf_op jit(solution)/shard_map/all_gather | solution.py:364
  24.0 2848.2 %all-reduce.19.cloned.1.call-start = ((), (), s32[]{:S(2)}) async-start(), calls=%async_computation.8 | async-start | bytes 129261568
  24.8 109.7 %copy-start.110 = (s32[12]{0:T(128)}, s32[12]{0:T(128)S(1)}, u32[]{:S(2)}) copy-start(s32[12]{0:T(128)S(1)} %select_reduce_fusion) | copy-start | bytes 148
  24.8 115.2 %copy-start.65 = (s32[256]{0:T(256)}, s32[256]{0:T(256)S(1)}, u32[]{:S(2)}) copy-start(s32[256]{0:T(256)S(1)} %convert_reduce_fusion.1) | copy-start | bytes 3076
  26.5 114.1 %copy-start.52 = (bf16[256,20]{0,1:T(8,128)(2,1)}, bf16[256,20]{0,1:T(8,128)(2,1)S(1)}, u32[]{:S(2)}) copy-start(bf16[256,20]{0,1:T(8,128)(2,1)S(1)} %add_convert_fusion.1) | copy-start | bytes 30724
  141.0 898.4 %copy-start.10 = (f32[256,768]{1,0:T(8,128)}, f32[256,768]{1,0:T(8,128)S(1)}, u32[]{:S(2)}) copy-start(f32[256,768]{1,0:T(8,128)S(1)} %get-tuple-element.633) | copy-start | bytes 2359300
  141.0 474.7 %copy-start.72 = (f32[256]{0:T(256)}, f32[256]{0:T(256)S(1)}, u32[]{:S(2)}) copy-start(f32[256]{0:T(256)S(1)} %broadcast_multiply_fusion.4) | copy-start | bytes 3076
  141.9 473.8 %copy-start.84 = (f32[256]{0:T(256)}, f32[256]{0:T(256)S(1)}, u32[]{:S(2)}) copy-start(f32[256]{0:T(256)S(1)} %fusion.222) | copy-start | bytes 3076
  142.6 473.1 %copy-start.48 = (f32[768]{0:T(1024)}, f32[768]{0:T(1024)S(1)}, u32[]{:S(2)}) copy-start(f32[768]{0:T(1024)S(1)} %get-tuple-element.621) | copy-start | bytes 9220
  615.7 7.2 copy-start.120
  615.7 10.5 copy-start.60
  615.7 10.5 copy-start.111
  618.9 12.5 copy-start.27
  619.0 361.0 %collective-permute-start = (bf16[256,1536]{1,0:T(8,128)(2,1)S(1)}, bf16[256,1536]{1,0:T(8,128)(2,1)}, u32[]{:S(2)}, u32[]{:S(2)}) collective-permute-start(bf16[256,1536]{1,0:T(8,128)(2,1)S(1)} %slice.293), channel_id=1, source_target_pairs={{0,2},{1,3},{2,4},{3,5},{4,6},{5,7},{6,8},{7,9},{8,10},{9,11},{10,... | collective-permute-start | bytes 2359304 | tf_op jit(solution)/shard_map/ppermute | solution.py:34
  623.4 357.8 %collective-permute-start.1 = (bf16[256,1536]{1,0:T(8,128)(2,1)S(1)}, bf16[256,1536]{1,0:T(8,128)(2,1)}, u32[]{:S(2)}, u32[]{:S(2)}) collective-permute-start(bf16[256,1536]{1,0:T(8,128)(2,1)S(1)} %slice.293), channel_id=1, source_target_pairs={{0,1},{1,2},{2,3},{3,4},{4,5},{5,6},{6,7},{7,8},{8,9},{9,10},{10,1... | collective-permute-start | bytes 2359304 | tf_op jit(solution)/shard_map/ppermute | solution.py:34
  631.4 352.3 %collective-permute-start.3 = (bf16[256,1536]{1,0:T(8,128)(2,1)S(1)}, bf16[256,1536]{1,0:T(8,128)(2,1)}, u32[]{:S(2)}, u32[]{:S(2)}) collective-permute-start(bf16[256,1536]{1,0:T(8,128)(2,1)S(1)} %slice.293), channel_id=1, source_target_pairs={{2,0},{3,1},{4,2},{5,3},{6,4},{7,5},{8,6},{9,7},{10,8},{11,9},{12,... | collective-permute-start | bytes 2359304 | tf_op jit(solution)/shard_map/ppermute | solution.py:34
  632.7 349.8 %collective-permute-start.2 = (bf16[256,1536]{1,0:T(8,128)(2,1)S(1)}, bf16[256,1536]{1,0:T(8,128)(2,1)}, u32[]{:S(2)}, u32[]{:S(2)}) collective-permute-start(bf16[256,1536]{1,0:T(8,128)(2,1)S(1)} %slice.293), channel_id=1, source_target_pairs={{1,0},{2,1},{3,2},{4,3},{5,4},{6,5},{7,6},{8,7},{9,8},{10,9},{11,1... | collective-permute-start | bytes 2359304 | tf_op jit(solution)/shard_map/ppermute | solution.py:34
  1038.8 7.3 copy-start.33
  1039.4 6.7 slice-start.3
  1052.2 12.1 copy-start.51
  1053.2 34.9 collective-permute-start.5
  1057.1 29.7 collective-permute-start.4
  1082.0 21.9 collective-permute-start.7
  1083.3 6.1 collective-permute-start.6
  1165.2 6.7 slice-start.7
  1248.4 13.2 copy-start.29
  1248.4 13.2 copy-start.57
  1248.4 13.2 copy-start.68
  1248.4 13.3 copy-start.71
  1248.4 14.6 copy-start.107
  1263.4 7.4 copy-start.17
  1270.8 6.5 copy-start.36
  1270.8 7.4 copy-start.83
  1270.8 8.0 copy-start.80
  1270.8 8.0 copy-start.92
  1407.0 7.2 copy-start.4
  1416.2 28.3 collective-permute-start.8
  1417.5 36.7 collective-permute-start.11
  1423.0 31.3 collective-permute-start.10
  1425.1 29.1 collective-permute-start.9
  1439.0 15.2 copy-start.3
  1439.0 15.2 copy-start.5
  1444.6 12.0 copy-start.35
  1444.6 12.0 copy-start.78
  1444.6 12.1 copy-start.90
  1456.6 8.2 slice-start.5
  1466.1 9.8 slice-start
  1466.1 9.8 slice-start.1
  1585.5 117.8 %collective-permute-start.12 = (bf16[256,1536]{0,1:T(8,128)(2,1)}, bf16[256,1536]{0,1:T(8,128)(2,1)S(1)}, u32[]{:S(2)}, u32[]{:S(2)}) collective-permute-start(bf16[256,1536]{0,1:T(8,128)(2,1)} %get-tuple-element.601), channel_id=1, source_target_pairs={{2,0},{3,1},{4,2},{5,3},{6,4},{7,5},{8,6},{9,7},{10,8},{11,9},{12,... | collective-permute-start | bytes 2359304 | tf_op jit(solution)/shard_map/ppermute | solution.py:34
  1586.8 116.6 %collective-permute-start.15 = (bf16[256,1536]{0,1:T(8,128)(2,1)}, bf16[256,1536]{0,1:T(8,128)(2,1)}, u32[]{:S(2)}, u32[]{:S(2)}) collective-permute-start(bf16[256,1536]{0,1:T(8,128)(2,1)} %get-tuple-element.602), channel_id=1, source_target_pairs={{0,2},{1,3},{2,4},{3,5},{4,6},{5,7},{6,8},{7,9},{8,10},{9,11},{10,... | collective-permute-start | bytes 2359304 | tf_op jit(solution)/shard_map/ppermute | solution.py:34
  1601.0 102.4 %collective-permute-start.14 = (bf16[256,1536]{0,1:T(8,128)(2,1)}, bf16[256,1536]{0,1:T(8,128)(2,1)}, u32[]{:S(2)}, u32[]{:S(2)}) collective-permute-start(bf16[256,1536]{0,1:T(8,128)(2,1)} %get-tuple-element.603), channel_id=1, source_target_pairs={{0,1},{1,2},{2,3},{3,4},{4,5},{5,6},{6,7},{7,8},{8,9},{9,10},{10,1... | collective-permute-start | bytes 2359304 | tf_op jit(solution)/shard_map/ppermute | solution.py:34
  1603.2 100.2 %collective-permute-start.13 = (bf16[256,1536]{0,1:T(8,128)(2,1)S(1)}, bf16[256,1536]{0,1:T(8,128)(2,1)}, u32[]{:S(2)}, u32[]{:S(2)}) collective-permute-start(bf16[256,1536]{0,1:T(8,128)(2,1)S(1)} %get-tuple-element.604), channel_id=1, source_target_pairs={{1,0},{2,1},{3,2},{4,3},{5,4},{6,5},{7,6},{8,7},{9,8},{10,9},{11,1... | collective-permute-start | bytes 2359304 | tf_op jit(solution)/shard_map/ppermute | solution.py:34
  1670.1 25.8 copy-start.26
  1780.6 26.4 copy-start.45
  1780.6 27.0 copy-start.16
  1816.5 1189.9 %all-reduce.17.cloned.1.call-start = ((), (), s32[]{:S(2)}) async-start(), calls=%async_computation.7 | async-start | bytes 503808
  2878.3 42.0 copy-start.7
  2920.2 1302.9 %reduce-scatter.4.cloned.1.call-start = ((), (), s32[]{:S(2)}) async-start(), calls=%async_computation.6 | async-start | bytes 169869312
  3002.6 1260.8 %all-reduce.15.cloned.1.call-start = ((), (), s32[]{:S(2)}) async-start(), calls=%async_computation.5 | async-start | bytes 503808
  3011.9 1281.1 %all-gather.6.cloned.1.call-start = ((), (), s32[]{:S(2)}) async-start(), calls=%async_computation.1 | async-start | bytes 2654208 | tf_op jit(solution)/shard_map/all_gather | solution.py:438
  3011.9 11.8 copy-start.31
  3011.9 12.9 copy-start.30
  (97 other events, 281.1 us)
Sparse Core Ops, SparseCore 0:
  18.2 112.3 all-reduce.12
  132.8 142.4 all-gather.7
  277.5 143.3 all-gather.9
  1816.7 1055.4 all-reduce.18
  2920.4 20.2 all-reduce.16
  3002.7 1220.4 reduce-scatter.3
  4226.1 23.0 all-reduce.14
  4263.5 29.4 all-gather.5

commit v2 on v1

--- a/solution.py
+++ b/solution.py
@@ -1,8 +1,11 @@
+import functools
 import math
 
 import jax
 import jax.numpy as jnp
 from jax import lax
+from jax.experimental import pallas as pl
+from jax.experimental.pallas import tpu as pltpu
 from jax.sharding import PartitionSpec as P
 
 D = 768
@@ -72,11 +75,15 @@
     return pieces
 
 
-def carve_layer(flat, shards):
-    pieces = flat.reshape(shards, -1)
+def layer_rows(piece, shards):
     cut = D // shards * (4 * D + FF)
-    upper = pieces[:, :cut].reshape(D, 4 * D + FF)
-    lower = pieces[:, cut:].reshape(FF, D)
+    return piece[:cut].reshape(D // shards, 4 * D + FF), piece[cut:].reshape(FF // shards, D)
+
+
+def gather_layer(anchor, shards):
+    upper, lower = layer_rows(anchor.astype(jnp.bfloat16), shards)
+    upper = lax.all_gather(upper, "seq", axis=0, tiled=True)
+    lower = lax.all_gather(lower, "seq", axis=0, tiled=True)
     return [upper[:, : 3 * D], upper[:, 3 * D : 4 * D], upper[:, 4 * D :], lower]
 
 
@@ -124,14 +131,6 @@
     return 0.5 * (jnp.mean(row_terms) + jnp.mean(column_terms))
 
 
-def split_heads(rows_in):
-    return rows_in.reshape(rows_in.shape[0], HEADS, HD).transpose(1, 0, 2)
-
-
-def join_heads(heads_in):
-    return heads_in.transpose(1, 0, 2).reshape(heads_in.shape[1], HEADS * HD)
-
-
 def gather_window(local_pairs):
     pieces = {}
     for step in (2, 1, -1, -2):
@@ -140,71 +139,138 @@
 
 
 def return_window(grad_window, rows):
-    total = grad_window[2 * rows : 3 * rows]
+    total = grad_window[2 * rows : 3 * rows].astype(jnp.float32)
     for slot, step in ((0, 2), (1, 1), (3, -1), (4, -2)):
         total = total + passed_along(
-            grad_window[slot * rows : (slot + 1) * rows].astype(jnp.bfloat16), "seq", -step
+            grad_window[slot * rows : (slot + 1) * rows], "seq", -step
         ).astype(jnp.float32)
     return total
 
 
-def attend_forward(queries, keys, values, keep):
-    scale = HD ** (-0.5)
-
-    def one_head(operands):
-        query, key_rows, value_rows = operands
-        scores = jnp.where(keep, against_rows(query, key_rows) * scale, -1e30)
-        peak = jnp.max(scores, axis=-1, keepdims=True)
-        weights = jnp.exp(scores - peak)
-        total = jnp.sum(weights, axis=-1, keepdims=True)
-        shares = (weights / total).astype(jnp.bfloat16)
-        return (dense(shares, value_rows), peak[:, 0], total[:, 0])
-
-    outputs, peaks, totals = lax.map(
-        one_head, (split_heads(queries), split_heads(keys), split_heads(values))
-    )
-    return (join_heads(outputs), peaks, totals)
-
-
-def attend_backward(queries, keys, values, keep, peaks, totals, grad_out):
-    scale = HD ** (-0.5)
-
-    def one_head(operands):
-        query, key_rows, value_rows, peak, total, grad_head = operands
-        scores = jnp.where(keep, against_rows(query, key_rows) * scale, -1e30)
-        shares = jnp.exp(scores - peak[:, None]) / total[:, None]
-        grad_value = contract_rows(shares.astype(jnp.bfloat16), grad_head)
-        grad_shares = against_rows(grad_head, value_rows)
-        inner = jnp.sum(grad_shares * shares, axis=-1, keepdims=True)
-        grad_scores = (shares * (grad_shares - inner)).astype(jnp.bfloat16)
-        grad_query = dense(grad_scores, key_rows) * scale
-        grad_key = contract_rows(grad_scores, query) * scale
-        return (grad_query, grad_key, grad_value)
-
-    grad_query, grad_key, grad_value = lax.map(
-        one_head,
-        (
-            split_heads(queries),
-            split_heads(keys),
-            split_heads(values),
-            peaks,
-            totals,
-            split_heads(grad_out),
+LANES = 128
+PAIRS = HEADS * HD // LANES
+VMEM_LIMIT = 50 * 1024 * 1024
+
+
+def lane_masks(dtype):
+    lane = lax.broadcasted_iota(jnp.int32, (1, LANES), 1)
+    return [(lane < HD).astype(dtype), (lane >= HD).astype(dtype)]
+
+
+def fill_bias(bias_ref, query_item_ref, key_item_ref):
+    keep = key_item_ref[...] == query_item_ref[...]
+    bias_ref[...] = jnp.where(keep, 0.0, -1e30).astype(jnp.float32)
+
+
+def attend_forward_kernel(q_ref, kv_ref, query_item_ref, key_item_ref, o_ref, lse_ref, bias_ref):
+    fill_bias(bias_ref, query_item_ref, key_item_ref)
+    width = HEADS * HD
+    masks = lane_masks(jnp.bfloat16)
+    lse_ref[...] = jnp.zeros_like(lse_ref)
+    for pair in range(PAIRS):
+        cols = slice(pair * LANES, (pair + 1) * LANES)
+        query = q_ref[:, cols] * jnp.bfloat16(HD ** (-0.5))
+        key_rows = kv_ref[:, cols]
+        value_rows = kv_ref[:, width + pair * LANES : width + (pair + 1) * LANES]
+        halves = []
+        for half in range(2):
+            scores = against_rows(key_rows, query * masks[half]) + bias_ref[...]
+            peak = jnp.max(scores, axis=0, keepdims=True)
+            weights = jnp.exp(scores - peak)
+            total = jnp.sum(weights, axis=0, keepdims=True)
+            shares = (weights * (1.0 / total)).astype(jnp.bfloat16)
+            mixed = contract_rows(value_rows, shares)
+            halves.append(mixed[half * HD : (half + 1) * HD])
+            lse_ref[2 * pair + half : 2 * pair + half + 1, :] = peak + jnp.log(total)
+        o_ref[:, cols] = jnp.concatenate(halves, axis=0).T.astype(o_ref.dtype)
+
+
+def attend_forward(queries, window, query_item, key_item):
+    rows, width = queries.shape
+    span = window.shape[0]
+    return pl.pallas_call(
+        attend_forward_kernel,
+        out_shape=(
+            jax.ShapeDtypeStruct((rows, width), jnp.bfloat16),
+            jax.ShapeDtypeStruct((16, rows), jnp.float32),
         ),
-    )
-    return (join_heads(grad_query), join_heads(grad_key), join_heads(grad_value))
-
-
-def layer_forward(hidden, weights, gain_one, gain_two, keep):
+        in_specs=[pl.BlockSpec(memory_space=pltpu.VMEM)] * 4,
+        out_specs=(pl.BlockSpec(memory_space=pltpu.VMEM),) * 2,
+        scratch_shapes=[pltpu.VMEM((span, rows), jnp.float32)],
+        compiler_params=pltpu.CompilerParams(vmem_limit_bytes=VMEM_LIMIT),
+        cost_estimate=pl.CostEstimate(
+            flops=4 * rows * span * width,
+            transcendentals=rows * span * HEADS,
+            bytes_accessed=4 * rows * width + 4 * span * width,
+        ),
+        name="attend_forward",
+    )(queries, window, query_item[None, :], key_item[:, None])
+
+
+def attend_backward_kernel(
+    q_ref, kv_ref, do_ref, lse_ref, query_item_ref, key_item_ref, dq_ref, dkv_ref, bias_ref
+):
+    fill_bias(bias_ref, query_item_ref, key_item_ref)
+    width = HEADS * HD
+    masks = lane_masks(jnp.bfloat16)
+    for pair in range(PAIRS):
+        cols = slice(pair * LANES, (pair + 1) * LANES)
+        value_cols = slice(width + pair * LANES, width + (pair + 1) * LANES)
+        query = q_ref[:, cols] * jnp.bfloat16(HD ** (-0.5))
+        key_rows = kv_ref[:, cols]
+        value_rows = kv_ref[:, value_cols]
+        grad_out = do_ref[:, cols]
+        halves = []
+        grad_key = grad_value = None
+        for half in range(2):
+            query_half = query * masks[half]
+            grad_half = grad_out * masks[half]
+            scores = against_rows(key_rows, query_half) + bias_ref[...]
+            shares = jnp.exp(scores - lse_ref[2 * pair + half : 2 * pair + half + 1, :])
+            grad_shares = against_rows(value_rows, grad_half)
+            inner = jnp.sum(grad_shares * shares, axis=0, keepdims=True)
+            grad_scores = (shares * (grad_shares - inner)).astype(jnp.bfloat16)
+            one_value = dense(shares.astype(jnp.bfloat16), grad_half)
+            one_key = dense(grad_scores, query_half)
+            grad_value = one_value if grad_value is None else grad_value + one_value
+            grad_key = one_key if grad_key is None else grad_key + one_key
+            one_query = contract_rows(key_rows, grad_scores)
+            halves.append(one_query[half * HD : (half + 1) * HD])
+        grad_query = jnp.concatenate(halves, axis=0).T * HD ** (-0.5)
+        dq_ref[:, cols] = grad_query.astype(dq_ref.dtype)
+        dkv_ref[:, cols] = grad_key.astype(dkv_ref.dtype)
+        dkv_ref[:, value_cols] = grad_value.astype(dkv_ref.dtype)
+
+
+def attend_backward(queries, window, grad_out, lse, query_item, key_item):
+    rows, width = queries.shape
+    span = window.shape[0]
+    return pl.pallas_call(
+        attend_backward_kernel,
+        out_shape=(
+            jax.ShapeDtypeStruct((rows, width), jnp.bfloat16),
+            jax.ShapeDtypeStruct((span, 2 * width), jnp.bfloat16),
+        ),
+        in_specs=[pl.BlockSpec(memory_space=pltpu.VMEM)] * 6,
+        out_specs=(pl.BlockSpec(memory_space=pltpu.VMEM),) * 2,
+        scratch_shapes=[pltpu.VMEM((span, rows), jnp.float32)],
+        compiler_params=pltpu.CompilerParams(vmem_limit_bytes=VMEM_LIMIT),
+        cost_estimate=pl.CostEstimate(
+            flops=10 * rows * span * width,
+            transcendentals=rows * span * HEADS,
+            bytes_accessed=8 * rows * width + 8 * span * width,
+        ),
+        name="attend_backward",
+    )(queries, window, grad_out, lse, query_item[None, :], key_item[:, None])
+
+
+def layer_forward(hidden, weights, gain_one, gain_two, items):
     proj_qkv, proj_out, proj_up, proj_down = weights
     width = proj_out.shape[0]
     normed = norm_rows(hidden, gain_one).astype(jnp.bfloat16)
     projected = dense(normed, proj_qkv).astype(jnp.bfloat16)
     window = gather_window(projected[:, width:])
-    attended, peaks, totals = attend_forward(
-        projected[:, :width], window[:, :width], window[:, width:], keep
-    )
-    attended = attended.astype(jnp.bfloat16)
+    attended, lse = attend_forward(projected[:, :width], window, *items)
     middle = hidden + dense(attended, proj_out)
     second = norm_rows(middle, gain_two).astype(jnp.bfloat16)
     upper = dense(second, proj_up)
@@ -216,8 +282,7 @@
             normed,
             projected,
             window,
-            peaks,
-            totals,
+            lse,
             attended,
             middle,
             second,
@@ -227,10 +292,8 @@
     )
 
 
-def layer_backward(grad_hidden, weights, gain_one, gain_two, keep, saved):
-    hidden, normed, projected, window, peaks, totals, attended, middle, second, upper, activated = (
-        saved
-    )
+def layer_backward(grad_hidden, weights, gain_one, gain_two, items, saved):
+    hidden, normed, projected, window, lse, attended, middle, second, upper, activated = saved
     proj_qkv, proj_out, proj_up, proj_down = weights
     width = proj_out.shape[0]
     rows = hidden.shape[0]
@@ -244,16 +307,11 @@
     grad_middle = grad_middle + grad_hidden
     branch_mid = grad_middle.astype(jnp.bfloat16)
     grad_attended = against_rows(branch_mid, proj_out).astype(jnp.bfloat16)
-    grad_query, grad_keys, grad_values = attend_backward(
-        projected[:, :width],
-        window[:, :width],
-        window[:, width:],
-        keep,
-        peaks,
-        totals,
-        grad_attended,
-    )
-    grad_pairs = return_window(jnp.concatenate([grad_keys, grad_values], axis=1), rows)
+    grad_query, grad_window = attend_backward(
+        projected[:, :width], window, grad_attended, lse, *items
+    )
+    grad_pairs = return_window(grad_window, rows)
+    grad_query = grad_query.astype(jnp.float32)
     grad_projected = jnp.concatenate([grad_query, grad_pairs], axis=1).astype(jnp.bfloat16)
     grad_normed = against_rows(grad_projected, proj_qkv)
     unused, pull_one = jax.vjp(norm_rows, hidden, gain_one)
@@ -277,17 +335,16 @@
     )
     upper_full = jnp.concatenate(
         [
-            contract_rows(normed, grad_projected),
-            contract_rows(attended, branch_mid),
-            contract_rows(second, grad_upper),
+            contract_rows(normed, grad_projected).astype(jnp.bfloat16),
+            contract_rows(attended, branch_mid).astype(jnp.bfloat16),
+            contract_rows(second, grad_upper).astype(jnp.bfloat16),
         ],
         axis=1,
     )
-    lower_full = contract_rows(activated, branch_top)
-    flat_grad = jnp.concatenate(
-        [upper_full.reshape(shards, -1), lower_full.reshape(shards, -1)], axis=1
-    ).reshape(-1)
-    return lax.psum_scatter(flat_grad, "seq", scatter_dimension=0, tiled=True)
+    lower_full = contract_rows(activated, branch_top).astype(jnp.bfloat16)
+    upper_own = lax.psum_scatter(upper_full, "seq", scatter_dimension=0, tiled=True)
+    lower_own = lax.psum_scatter(lower_full, "seq", scatter_dimension=0, tiled=True)
+    return jnp.concatenate([upper_own.reshape(-1), lower_own.reshape(-1)]).astype(jnp.float32)
 
 
 def adam(grad, first, second, anchor):
@@ -297,6 +354,165 @@
     scaled = second / (1.0 - beta_two**STEP_COUNT)
     delta = inner_rate * (stepped / (jnp.sqrt(scaled) + adam_eps) + decay_rate * anchor)
     return (first, second, delta)
+
+
+MESH = pl.DeviceIdType.MESH
+SUBLANES = 8
+CLOSE_RANKS = 16
+
+
+def greet_seq(me, count):
+    group = lax.axis_index("grp")
+    barrier = pltpu.get_barrier_semaphore()
+
+    def one(step, carry):
+        pl.semaphore_signal(
+            barrier, inc=1, device_id=(group, lax.rem(me + step, count)), device_id_type=MESH
+        )
+        return carry
+
+    lax.fori_loop(1, count, one, 0)
+    pl.semaphore_wait(barrier, count - 1)
+
+
+def sum_kernel(count, x_ref, out_ref, parts, own, totals, send_one, recv_one, send_two, recv_two):
+    me = lax.axis_index("seq")
+    group = lax.axis_index("grp")
+    greet_seq(me, count)
+
+    def slice_copy(step):
+        peer = lax.rem(me + step, count)
+        return pltpu.make_async_remote_copy(
+            src_ref=x_ref.at[peer],
+            dst_ref=parts.at[step],
+            send_sem=send_one.at[step],
+            recv_sem=recv_one.at[step],
+            device_id=(group, peer),
+            device_id_type=MESH,
+        )
+
+    def total_copy(step):
+        peer = lax.rem(me + step, count)
+        return pltpu.make_async_remote_copy(
+            src_ref=own,
+            dst_ref=totals.at[step],
+            send_sem=send_two.at[step],
+            recv_sem=recv_two.at[step],
+            device_id=(group, peer),
+            device_id_type=MESH,
+        )
+
+    def start_of(make):
+        def one(step, carry):
+            make(step).start()
+            return carry
+
+        return one
+
+    lax.fori_loop(1, count, start_of(slice_copy), 0)
+    own[...] = x_ref[me]
+
+    def gather_in(step, carry):
+        slice_copy(step).wait()
+        own[...] += parts[step]
+        return carry
+
+    lax.fori_loop(1, count, gather_in, 0)
+    lax.fori_loop(1, count, start_of(total_copy), 0)
+    out_ref[me] = own[...]
+
+    def spread(step, carry):
+        total_copy(step).wait()
+        out_ref[lax.rem(me + count - step, count)] = totals[step]
+        return carry
+
+    lax.fori_loop(1, count, spread, 0)
+
+
+def sum_over_seq(values, collective):
+    count = lax.axis_size("seq")
+    if count != CLOSE_RANKS:
+        return lax.psum(values, "seq")
+    sizes = [math.prod(value.shape) for value in values]
+    block = -(-sum(sizes) // (count * SUBLANES * LANES)) * SUBLANES
+    flat = jnp.concatenate([value.reshape(-1) for value in values])
+    flat = jnp.pad(flat, (0, count * block * LANES - flat.shape[0]))
+    shape = (count, block, LANES)
+    total = pl.pallas_call(
+        functools.partial(sum_kernel, count),
+        out_shape=jax.ShapeDtypeStruct(shape, jnp.float32),
+        in_specs=[pl.BlockSpec(memory_space=pltpu.VMEM)],
+        out_specs=pl.BlockSpec(memory_space=pltpu.VMEM),
+        scratch_shapes=[
+            pltpu.VMEM(shape, jnp.float32),
+            pltpu.VMEM(shape[1:], jnp.float32),
+            pltpu.VMEM(shape, jnp.float32),
+        ]
+        + [pltpu.SemaphoreType.DMA((count,))] * 4,
+        compiler_params=pltpu.CompilerParams(collective_id=collective, has_side_effects=True),
+        cost_estimate=pl.CostEstimate(
+            flops=math.prod(shape), transcendentals=0, bytes_accessed=16 * math.prod(shape)
+        ),
+        name="sum_over_seq",
+    )(flat.reshape(shape))
+    return carve(total.reshape(-1), [value.shape for value in values])
+
+
+def share_kernel(count, x_ref, out_ref, parts, send_sem, recv_sem):
+    me = lax.axis_index("seq")
+    group = lax.axis_index("grp")
+    greet_seq(me, count)
+
+    def copy_of(step):
+        return pltpu.make_async_remote_copy(
+            src_ref=x_ref,
+            dst_ref=parts.at[step],
+            send_sem=send_sem.at[step],
+            recv_sem=recv_sem.at[step],
+            device_id=(group, lax.rem(me + step, count)),
+            device_id_type=MESH,
+        )
+
+    def start(step, carry):
+        copy_of(step).start()
+        return carry
+
+    lax.fori_loop(1, count, start, 0)
+    out_ref[me] = x_ref[...]
+
+    def finish(step, carry):
+        copy_of(step).wait()
+        out_ref[lax.rem(me + count - step, count)] = parts[step]
+        return carry
+
+    lax.fori_loop(1, count, finish, 0)
+
+
+def sum_scalar_over_seq(value, collective):
+    count = lax.axis_size("seq")
+    if count != CLOSE_RANKS:
+        return lax.psum(value, "seq")
+    shape = (count, SUBLANES, LANES)
+    shared = pl.pallas_call(
+        functools.partial(share_kernel, count),
+        out_shape=jax.ShapeDtypeStruct(shape, jnp.float32),
+        in_specs=[pl.BlockSpec(memory_space=pltpu.VMEM)],
+        out_specs=pl.BlockSpec(memory_space=pltpu.VMEM),
+        scratch_shapes=[pltpu.VMEM(shape, jnp.float32)]
+        + [pltpu.SemaphoreType.DMA((count,))] * 2,
+        compiler_params=pltpu.CompilerParams(collective_id=collective, has_side_effects=True),
+        name="share_over_seq",
+    )(jnp.full(shape[1:], value, jnp.float32))
+    return jnp.sum(shared[:, 0, 0])
+
+
+def group_mean(delta, count):
+    low = lax.reduce_precision(delta, 8, 7)
+    total = low
+    for step in range(1, count):
+        moves = [(source, (source + step) % count) for source in range(count)]
+        total = total + lax.ppermute(low.astype(jnp.bfloat16), "grp", moves).astype(jnp.float32)
+    return total / count
 
 
 def per_device(
@@ -327,7 +543,11 @@
     captions = captions[0]
     item_count = lengths.shape[0]
     text_width = captions.shape[1]
-    other_low = lax.all_gather(anchor_other.astype(jnp.bfloat16), "seq", axis=0, tiled=True)
+    other_size = anchor_other.shape[0]
+    padded = -(-other_size // 2048) * 2048
+    other_rows = jnp.pad(anchor_other.astype(jnp.bfloat16), (0, padded - other_size))
+    other_rows = lax.all_gather(other_rows.reshape(-1, LANES), "seq", axis=0, tiled=True)
+    other_low = other_rows.reshape(seq_count, padded)[:, :other_size].reshape(-1)
     w_in, w_out, w_time, w_text, w_audio, w_caption, gains, null_text = carve(
         other_low, other_shapes(channels, D, text_width, E, L)
     )
@@ -340,13 +560,12 @@
     places = rank * rows + jnp.arange(rows, dtype=jnp.int32)
     order = jnp.arange(item_count, dtype=jnp.int32)
     ends = jnp.sum(jnp.where(order[None, :] <= order[:, None], lengths[None, :], 0), axis=1)
-    starts = ends - lengths
     item = jnp.sum((places[:, None] >= ends[None, :]).astype(jnp.int32), axis=1)
     onehot = (item[:, None] == jnp.arange(item_count, dtype=jnp.int32)[None, :]).astype(jnp.float32)
     key_places = rank * rows + jnp.arange(-2 * rows, 3 * rows, dtype=jnp.int32)
     key_item = jnp.sum((key_places[:, None] >= ends[None, :]).astype(jnp.int32), axis=1)
     key_item = jnp.where((key_places >= 0) & (key_places < frames_group), key_item, -1)
-    keep = item[:, None] == key_item[None, :]
+    items = (item, key_item)
     lengths_f = lengths[:, None].astype(jnp.float32)
     alpha_bar = plan(timesteps)
     mixing = exact(onehot, jnp.stack([jnp.sqrt(alpha_bar), jnp.sqrt(1.0 - alpha_bar)], axis=1))
@@ -360,11 +579,11 @@
     condition, pull_condition = jax.vjp(condition_of, w_time_f, w_text_f, null_f)
     hidden = dense(noisy_low, w_in) + exact(onehot, condition)
     saved_all = []
+    gathered = [gather_layer(anchor_layers[depth], seq_count) for depth in range(L)]
     for depth in range(L):
-        flat = lax.all_gather(anchor_layers[depth].astype(jnp.bfloat16), "seq", axis=0, tiled=True)
-        weights = carve_layer(flat, seq_count)
+        weights = gathered[depth]
         hidden, saved = layer_forward(
-            hidden, weights, gains_f[2 * depth], gains_f[2 * depth + 1], keep
+            hidden, weights, gains_f[2 * depth], gains_f[2 * depth + 1], items
         )
         saved_all.append(saved)
     final = norm_rows(hidden, gains_f[2 * L])
@@ -372,7 +591,7 @@
     predicted = dense(final_low, w_out)
     error = predicted - noise
     part_pool = contract_rows(onehot, final, HIGH)
-    squared_sum, pool_sum = lax.psum((jnp.sum(error * error), part_pool), "seq")
+    squared_sum, pool_sum = sum_over_seq((jnp.sum(error * error), part_pool), 1)
     pooled = pool_sum / lengths_f
     audio_side = exact(pooled, w_audio_f)
     text_side = exact(captions, w_caption_f)
@@ -380,10 +599,9 @@
     loss = squared_sum / (frames_group * channels) + contrast_weight * clash
     grad_audio_side, grad_text_side = pull_clash(jnp.float32(contrast_weight))
     grad_pred = (2.0 / (frames_group * channels) * error).astype(jnp.bfloat16)
-    grad_w_out = contract_rows(final_low, grad_pred)
-    grad_w_audio = contract_rows(part_pool / lengths_f, grad_audio_side, HIGH)
-    first_here = ((starts >= rank * rows) & (starts < rank * rows + rows)).astype(jnp.float32)
-    grad_w_caption = contract_rows(captions * first_here[:, None], grad_text_side, HIGH)
+    grad_w_out = contract_rows(grad_pred, final_low)
+    grad_w_audio = contract_rows(pooled, grad_audio_side, HIGH)
+    grad_w_caption = contract_rows(captions, grad_text_side, HIGH)
     grad_pooled = against_rows(grad_audio_side, w_audio_f, HIGH) / lengths_f
     grad_final = against_rows(grad_pred, w_out) + exact(onehot, grad_pooled)
     unused, pull_final = jax.vjp(norm_rows, hidden, gains_f[2 * L])
@@ -392,10 +610,9 @@
     gain_grads = [None] * (2 * L + 1)
     gain_grads[2 * L] = grad_gain_final
     for depth in reversed(range(L)):
-        flat = lax.all_gather(anchor_layers[depth].astype(jnp.bfloat16), "seq", axis=0, tiled=True)
-        weights = carve_layer(flat, seq_count)
+        weights = gathered[depth]
         grad_hidden, operand_pairs, grad_gain_one, grad_gain_two = layer_backward(
-            grad_hidden, weights, gains_f[2 * depth], gains_f[2 * depth + 1], keep, saved_all[depth]
+            grad_hidden, weights, gains_f[2 * depth], gains_f[2 * depth + 1], items, saved_all[depth]
         )
         gain_grads[2 * depth] = grad_gain_one
         gain_grads[2 * depth + 1] = grad_gain_two
@@ -403,6 +620,10 @@
     stacked = jnp.stack(layer_grads)
     grad_w_in = contract_rows(noisy_low.astype(jnp.float32), grad_hidden, HIGH)
     grad_condition = contract_rows(onehot, grad_hidden, HIGH)
+    grad_w_in, grad_w_out, grad_condition, gain_rows = sum_over_seq(
+        (grad_w_in, grad_w_out, grad_condition, jnp.stack(gain_grads)), 2
+    )
+    grad_w_out = grad_w_out.T
     grad_w_time, grad_w_text, grad_null = pull_condition(grad_condition)
     other_flat = jnp.concatenate(
         [
@@ -412,13 +633,13 @@
             grad_w_text.ravel(),
             grad_w_audio.ravel(),
             grad_w_caption.ravel(),
-            jnp.stack(gain_grads).ravel(),
+            gain_rows.ravel(),
             grad_null,
         ]
     )
-    other_grad = lax.psum_scatter(other_flat, "seq", scatter_dimension=0, tiled=True)
+    other_grad = lax.dynamic_slice_in_dim(other_flat, rank * other_size, other_size)
     square_part = jnp.sum(stacked * stacked) + jnp.sum(other_grad * other_grad)
-    total_norm = jnp.sqrt(lax.psum(square_part, "seq"))
+    total_norm = jnp.sqrt(sum_scalar_over_seq(square_part, 3))
     factor = jnp.minimum(1.0, clip_at / (total_norm + 1e-06))
     first_l, second_l, delta_l = adam(
         stacked * factor, first_layers[0], second_layers[0], anchor_layers
@@ -426,24 +647,8 @@
     first_o, second_o, delta_o = adam(
         other_grad * factor, first_other[0], second_other[0], anchor_other
     )
-    share_l, share_o = (
-        lax.psum_scatter(
-            delta_l.astype(jnp.bfloat16), "grp", scatter_dimension=1, tiled=True
-        ).astype(jnp.float32),
-        lax.psum_scatter(
-            delta_o.astype(jnp.bfloat16), "grp", scatter_dimension=0, tiled=True
-        ).astype(jnp.float32),
-    )
-    summed_l, summed_o = (
-        lax.all_gather(share_l.astype(jnp.bfloat16), "grp", axis=1, tiled=True).astype(
-            share_l.dtype
-        ),
-        lax.all_gather(share_o.astype(jnp.bfloat16), "grp", axis=0, tiled=True).astype(
-            share_o.dtype
-        ),
-    )
-    mean_layers = summed_l / group_count
-    mean_other = summed_o / group_count
+    mean_layers = group_mean(delta_l, group_count)
+    mean_other = group_mean(delta_o, group_count)
     momentum_layers = outer_mu * outer_layers + mean_layers
     momentum_other = outer_mu * outer_other + mean_other
     new_layers = anchor_layers - outer_rate * (mean_layers + outer_mu * momentum_layers)

time: 4340 us -> 1030 us (0.24)
  waiting for transfers between devices: 2530 us -> 398 us
  other arithmetic: 762 us -> 126 us
  local copies, waits for them, and re-layouts: 464 us -> 158 us
  matrix products: 372 us -> 123 us
  Pallas kernels: 0 us -> 139 us
  blocking collectives: 102 us -> 0 us
    unnamed x13 -> x9, waiting for transfers between devices: 2350 us -> 0.15 us
    all_gather x2 -> x0, other arithmetic: 600 us -> none  [per_device(): lax.all_gather(anchor_layers[depth].astype(jnp.bfloat16), 'seq', axis=0,...]
    unnamed x307 -> x311, local copies, waits for them, and re-layouts: 221 us -> 38.9 us
    pallas_call x0 -> x7, Pallas kernels: none -> 139 us  [the longest x2 68.3 us: sum_over_seq(): pl.pallas_call(functools.partial(sum_kernel, count), out_shape=jax.ShapeD...]
    reshape x12 -> x8, local copies, waits for them, and re-layouts: 131 us -> 17.1 us  [the longest x2 14.2 us: per_device(): other_rows.reshape(seq_count, padded)[:, :other_size].reshape(-1)]
    psum x2 -> x0, blocking collectives: 102 us -> none  [the longest x1 69.1 us: per_device(): squared_sum, pool_sum = lax.psum((jnp.sum(error * error), part_pool), 'seq')]
    ppermute x16, waiting for transfers between devices: 23 us -> 120 us  [passed_along(): lax.ppermute(value, axis, [(source, source + steps) for source in range(i...]
    dot_general x82 -> x10, matrix products: 134 us -> 38.1 us  [against_rows(): lax.dot_general(left, right, (((1,), (1,)), ((), ())), precision=precisio...]
  transfers between devices with their start and end apart: 24 -> 27, of which waited for: 7 -> 14; matrix products, arithmetic and copies ran while one was open for 23% -> 31% of each run, Pallas kernels for 0% -> 10%
where the time goes in v2:
time: 1030 us; the launch traced here: 1020 us
  waiting for transfers between devices  398 us (39%)
  local copies, waits for them, and re-layouts  158 us (15%)
  Pallas kernels  139 us (13%)
  other arithmetic  126 us (12%)
  matrix products  123 us (12%)
  starting transfers between devices  49.2 us (5%)
  between operations  22.5 us (2%)
    all_gather x2, waiting for transfers between devices, gather_layer(): upper = lax.all_gather(upper, 'seq', axis=0, tiled=True)  128 us
    ppermute x16, waiting for transfers between devices, passed_along(): lax.ppermute(value, axis, [(source, source + steps) for source in range(i...  120 us
    reduce_scatter x2, waiting for transfers between devices, reduce_layer(): lax.psum_scatter(upper_full, 'seq', scatter_dimension=0, tiled=True)  81.4 us
    pallas_call x2, Pallas kernels, sum_over_seq(): pl.pallas_call(functools.partial(sum_kernel, count), out_shape=jax.ShapeD...  68.3 us
    ppermute x16, starting transfers between devices, passed_along(): lax.ppermute(value, axis, [(source, source + steps) for source in range(i...  46.3 us
    unnamed x311, local copies, waits for them, and re-layouts  38.9 us
    ppermute x2, waiting for transfers between devices, group_mean(): lax.ppermute(low.astype(jnp.bfloat16), 'grp', moves).astype(jnp.float32)  38.8 us
    dot_general x10, matrix products, against_rows(): lax.dot_general(left, right, (((1,), (1,)), ((), ())), precision=precisio...  38.1 us
  transfers between devices with their start and end apart: 27, of which 14 were waited for; matrix products, arithmetic and copies ran while one was open for 31% of the time, Pallas kernels for 10%

profile of v2, /device:TPU:0, one launch (start us, length us, event | category | flops | bytes accessed | tf_op | source)
XLA Modules:
  0.0 1016.8 jit_solution(10294996976092428281)
XLA Ops:
  9.1 6.0 fusion.161
  15.0 10.7 %slice_reduce_fusion.1 = bf16[294912]{0:T(1024)(128)(2,1)} fusion(bf16[1,442368]{1,0:T(2,128)(2,1)S(1)} %get-tuple-element.85), kind=kLoop, calls=%fused_computation.85 | loop fusion | bytes 1179648 | tf_op jit(solution)/shard_map/slice | solution.py:80
  27.9 5.6 slice_reduce_fusion.3
  35.6 9.9 slice_reduce_fusion
  47.9 15.5 %all-gather.6.cloned.1.call-done = bf16[15872,128]{1,0:T(8,128)(2,1)} async-done(((bf16[992,128]{1,0:T(8,128)(2,1)}), bf16[15872,128]{1,0:T(8,128)(2,1)}) %all-gather.6.cloned.1.call-update) | async-done | bytes 4063248 | tf_op jit(solution)/shard_map/all_gather | solution.py:549
  63.4 4.6 reshape.585
  68.0 4.4 slice.243
  72.4 9.6 reshape.586
  82.1 7.8 slice.188
  97.1 49.1 %all-gather.8.cloned.1.call-done = bf16[768,6144]{1,0:T(8,128)(2,1)} async-done(((bf16[48,6144]{1,0:T(8,128)(2,1)}), bf16[768,6144]{1,0:T(8,128)(2,1)}) %all-gather.8.cloned.1.call-update) | async-done | bytes 9437200 | tf_op jit(solution)/shard_map/all_gather | solution.py:85
  151.4 3.4 collective-permute-start
  157.6 5.6 slice_reduce_fusion.2
  169.5 26.3 %collective-permute-done = bf16[256,1536]{1,0:T(8,128)(2,1)} collective-permute-done((bf16[256,1536]{1,0:T(8,128)(2,1)}, bf16[256,1536]{1,0:T(8,128)(2,1)}, u32[]{:S(2)}, u32[]{:S(2)}) %collective-permute-start) | collective-permute-done | bytes 786464 | tf_op jit(solution)/shard_map/ppermute | solution.py:37
  200.4 14.8 %attend_forward.2 = (bf16[256,768]{1,0:T(8,128)(2,1)S(1)}, f32[16,256]{1,0:T(8,128)S(1)}) custom-call(bf16[256,768]{1,0:T(8,128)(2,1)S(1)} %slice.252.q_ref, bf16[1280,1536]{1,0:T(8,128)(2,1)} %copy-done.57, s32[1,256]{1,0:T(1,128)S(1)} %bitcast.96, s32[1280,1]{1,0:T(8,128)S(1)} %reshape_select_fusion.key_item_ref), custom_call_target="tpu_custom_call" | custom-call | flops 1006632960 | bytes 4718592 | tf_op jit(solution)/shard_map/attend_forward/pallas_call | solution.py:191
  216.1 3.6 fusion.6
  219.7 8.7 all-gather.10.cloned.1.call-done
  228.4 5.5 fusion.166
  234.1 78.5 %all-gather.12.cloned.1.call-done = bf16[768,6144]{1,0:T(8,128)(2,1)} async-done(((bf16[48,6144]{1,0:T(8,128)(2,1)}), bf16[768,6144]{1,0:T(8,128)(2,1)}) %all-gather.12.cloned.1.call-update) | async-done | bytes 9437200 | tf_op jit(solution)/shard_map/all_gather | solution.py:85
  316.8 3.4 collective-permute-start.4
  323.5 7.4 slice.220
  338.7 11.7 %collective-permute-done.4 = bf16[256,1536]{1,0:T(8,128)(2,1)} collective-permute-done((bf16[256,1536]{1,0:T(8,128)(2,1)}, bf16[256,1536]{1,0:T(8,128)(2,1)}, u32[]{:S(2)}, u32[]{:S(2)}) %collective-permute-start.4) | collective-permute-done | bytes 786464 | tf_op jit(solution)/shard_map/ppermute | solution.py:37
  356.4 10.1 collective-permute-done.7
  367.4 14.2 %attend_forward.3 = (bf16[256,768]{1,0:T(8,128)(2,1)S(1)}, f32[16,256]{1,0:T(8,128)S(1)}) custom-call(bf16[256,768]{1,0:T(8,128)(2,1)S(1)} %slice.261.q_ref, bf16[1280,1536]{1,0:T(8,128)(2,1)} %constant_dynamic-update-slice_fusion.5.kv_ref, s32[1,256]{1,0:T(1,128)S(1)} %bitcast.97, s32[1280,1]{1,0:T(8,128)S(1)} %reshape_select_fusion.key_item_ref), custom_call_target="tpu_custom_call" | custom-call | flops 1006632960 | bytes 4718592 | tf_op jit(solution)/shard_map/attend_forward/pallas_call | solution.py:191
  384.4 3.3 fusion.2
  387.8 5.9 all-gather.14.cloned.1.call-done
  393.7 5.5 fusion.168
  407.9 33.8 %sum_over_seq.2 = f32[16,8,128]{2,1,0:T(8,128)} custom-call(f32[16,8,128]{2,1,0:T(8,128)} %fusion.75.x_ref), custom_call_target="tpu_custom_call" | custom-call | flops 16384 | bytes 262144 | tf_op jit(solution)/shard_map/sum_over_seq/pallas_call | solution.py:441
  456.9 4.4 convolution_convert_fusion
  461.7 6.3 fusion.27
  468.0 5.4 multiply_reduce_fusion.2
  476.1 17.1 %attend_backward.2 = (bf16[256,768]{1,0:T(8,128)(2,1)S(1)}, bf16[1280,1536]{1,0:T(8,128)(2,1)}) custom-call(bf16[256,768]{1,0:T(8,128)(2,1)S(1)} %slice.261.q_ref, bf16[1280,1536]{1,0:T(8,128)(2,1)} %constant_dynamic-update-slice_fusion.5.kv_ref, bf16[256,768]{1,0:T(8,128)(2,1)S(1)} %convolution_convert_fusion.11.do_ref, ...), custom_call_target="tpu_custom_call" | custom-call | flops 2516582400 | bytes 9437184 | tf_op jit(solution)/shard_map/attend_backward/pallas_call | solution.py:248
  496.7 4.6 collective-permute-start.11
  504.1 17.7 %collective-permute-done.8 = bf16[256,1536]{1,0:T(8,128)(2,1)S(1)} collective-permute-done((bf16[256,1536]{1,0:T(8,128)(2,1)S(1)}, bf16[256,1536]{1,0:T(8,128)(2,1)S(1)}, u32[]{:S(2)}, u32[]{:S(2)}) %collective-permute-start.8) | collective-permute-done | bytes 786464 | tf_op jit(solution)/shard_map/ppermute | solution.py:37
  521.8 23.3 %collective-permute-done.11 = bf16[256,1536]{1,0:T(8,128)(2,1)S(1)} collective-permute-done((bf16[256,1536]{1,0:T(8,128)(2,1)S(1)}, bf16[256,1536]{1,0:T(8,128)(2,1)S(1)}, u32[]{:S(2)}, u32[]{:S(2)}) %collective-permute-start.11) | collective-permute-done | bytes 786464 | tf_op jit(solution)/shard_map/ppermute | solution.py:37
  546.8 4.1 multiply_reduce_fusion.3
  553.3 4.4 convolution_convert_fusion.3
  563.0 3.3 convolution_convert_fusion.1
  567.7 4.1 pad_maximum_fusion.1
  572.8 4.9 multiply_reduce_fusion.17
  592.6 7.0 fusion.20
  599.7 4.8 multiply_reduce_fusion.4
  606.9 16.8 %attend_backward.3 = (bf16[256,768]{1,0:T(8,128)(2,1)S(1)}, bf16[1280,1536]{1,0:T(8,128)(2,1)}) custom-call(bf16[256,768]{1,0:T(8,128)(2,1)S(1)} %slice.252.q_ref, bf16[1280,1536]{1,0:T(8,128)(2,1)} %copy-done.57, bf16[256,768]{1,0:T(8,128)(2,1)S(1)} %convolution_convert_fusion.10.do_ref, f32[16,256]{1,0:T(8,128)S(1)} %get-tuple-element.25.lse_ref, ...), custom_call_target="tpu_custom_call" | custom-call | flops 2516582400 | bytes 9437184 | tf_op jit(solution)/shard_map/attend_backward/pallas_call | solution.py:248
  623.8 3.6 fusion.159
  628.8 14.9 %collective-permute-start.15 = (bf16[256,1536]{1,0:T(8,128)(2,1)}, bf16[256,1536]{1,0:T(8,128)(2,1)}, u32[]{:S(2)}, u32[]{:S(2)}) collective-permute-start(bf16[256,1536]{1,0:T(8,128)(2,1)} %get-tuple-element.75), channel_id=1, source_target_pairs={{0,2},{1,3},{2,4},{3,5},{4,6},{5,7},{6,8},{7,9},{8,10},{9,11},{10,... | collective-permute-start | bytes 2359304 | tf_op jit(solution)/shard_map/ppermute | solution.py:37
  653.2 5.2 convolution_convert_fusion.4
  658.5 31.1 %collective-permute-done.15 = bf16[256,1536]{1,0:T(8,128)(2,1)} collective-permute-done((bf16[256,1536]{1,0:T(8,128)(2,1)}, bf16[256,1536]{1,0:T(8,128)(2,1)}, u32[]{:S(2)}, u32[]{:S(2)}) %collective-permute-start.15) | collective-permute-done | bytes 786464 | tf_op jit(solution)/shard_map/ppermute | solution.py:37
  692.2 4.4 multiply_reduce_fusion.6
  700.0 34.5 %sum_over_seq.3 = f32[16,24,128]{2,1,0:T(8,128)} custom-call(f32[16,24,128]{2,1,0:T(8,128)} %bitcast.114), custom_call_target="tpu_custom_call" | custom-call | flops 49152 | bytes 786432 | tf_op jit(solution)/shard_map/sum_over_seq/pallas_call | solution.py:441
  737.3 3.5 fusion.89
  740.7 3.2 reshape.606
  744.0 3.5 fusion.87
  747.5 3.3 reshape.607
  755.3 4.3 pad_maximum_fusion
  777.1 11.2 %maximum_convert_fusion.1 = f32[1,442368]{1,0:T(1,128)} fusion(bf16[1,147456]{1,0:T(2,128)(2,1)S(1)} %bitcast.111, bf16[1,294912]{1,0:T(2,128)(2,1)S(1)} %bitcast.102), kind=kLoop, calls=%fused_computation.62 | loop fusion | flops 1769472 | bytes 2654208 | tf_op jit(solution)/shard_map/convert_element_type | solution.py:347
  788.2 11.1 %fusion.189 = f32[1,1,442368]{2,1,0:T(1,128)} fusion(bf16[1,147456]{1,0:T(2,128)(2,1)S(1)} %bitcast.112, bf16[1,294912]{1,0:T(2,128)(2,1)S(1)} %bitcast.103), kind=kLoop, calls=%fused_computation.360 | loop fusion | flops 1769472 | bytes 2654208 | tf_op jit(solution)/shard_map/stack | solution.py:620
  799.3 81.4 %reduce-scatter.5.cloned.1.call-done = bf16[48,6144]{1,0:T(8,128)(2,1)} async-done(((bf16[768,6144]{1,0:T(8,128)(2,1)}), bf16[48,6144]{1,0:T(8,128)(2,1)}) %reduce-scatter.5.cloned.1.call-update) | async-done | bytes 589840 | tf_op jit(solution)/shard_map/reduce_scatter | solution.py:345
  882.7 10.8 %maximum_convert_fusion = f32[1,442368]{1,0:T(1,128)S(1)} fusion(bf16[1,147456]{1,0:T(2,128)(2,1)S(1)} %bitcast.109, bf16[1,294912]{1,0:T(2,128)(2,1)S(1)} %bitcast.104), kind=kLoop, calls=%fused_computation.61 | loop fusion | flops 1769472 | bytes 2654208 | tf_op jit(solution)/shard_map/convert_element_type | solution.py:347
  893.5 11.2 %fusion.188 = f32[1,1,442368]{2,1,0:T(1,128)} fusion(bf16[1,147456]{1,0:T(2,128)(2,1)S(1)} %bitcast.110, bf16[1,294912]{1,0:T(2,128)(2,1)S(1)} %bitcast.105), kind=kLoop, calls=%fused_computation.359 | loop fusion | flops 1769472 | bytes 2654208 | tf_op jit(solution)/shard_map/stack | solution.py:620
  904.7 4.3 multiply_reduce_fusion
  910.9 8.2 share_over_seq.1
  925.0 16.0 %fusion.153 = (bf16[2,442368]{1,0:T(2,128)(2,1)S(1)}, f32[2,442368]{1,0:T(2,128)S(1)}) fusion(f32[2,442368]{1,0:T(2,128)S(1)} %copy-done, f32[1,2,442368]{2,1,0:T(2,128)} %param.18, f32[]{:T(128)S(6)} %min.3, f32[1,442368]{1,0:T(1,128)S(1)} %copy-done.4, f32[1,442368]{1,0:T(1,128)S(1)} %copy-done.6, f32[1,2,442368]{2,1,0:T(2,128)} %param.16), kind=kLoop, calls=%fused_computation.343 | loop fusion | flops 15925248 | bytes 19464196 | tf_op jit(solution)/shard_map/convert_element_type | solution.py:514
  941.1 9.5 fusion.11
  954.4 38.7 %collective-permute-done.16 = bf16[2,442368]{1,0:T(2,128)(2,1)S(1)} collective-permute-done((bf16[2,442368]{1,0:T(2,128)(2,1)S(1)}, bf16[2,442368]{1,0:T(2,128)(2,1)S(1)}, u32[]{:S(2)}, u32[]{:S(2)}) %collective-permute-start.16) | collective-permute-done | bytes 1769504 | tf_op jit(solution)/shard_map/ppermute | solution.py:514
  993.1 14.7 %multiply_subtract_fusion = (f32[2,442368]{1,0:T(2,128)}, f32[2,442368]{1,0:T(2,128)}, f32[2,442368]{1,0:T(2,128)}) fusion(f32[2,442368]{1,0:T(2,128)S(1)} %copy-done, f32[2,442368]{1,0:T(2,128)S(1)} %copy-done.30, f32[2,442368]{1,0:T(2,128)S(1)} %get-tuple-element.63, bf16[2,442368]{1,0:T(2,128)(2,1)S(1)} %collective-permute-done.16), kind=kLoop, calls=%fused_computation.34 | loop fusion | flops 7962624 | bytes 23003136 | tf_op jit(solution)/shard_map/sub | solution.py:654
  (501 shorter events, 172.5 us)
Async XLA Ops:
  7.2 56.3 %all-gather.6.cloned.1.call-start = ((), (), s32[]{:S(2)}) async-start(), calls=%async_computation.4 | async-start | bytes 4317184 | tf_op jit(solution)/shard_map/all_gather | solution.py:549
  9.0 137.2 %all-gather.8.cloned.1.call-start = ((), (), s32[]{:S(2)}) async-start(), calls=%async_computation.5 | async-start | bytes 10027008 | tf_op jit(solution)/shard_map/all_gather | solution.py:85
  27.9 200.5 %all-gather.10.cloned.1.call-start = ((), (), s32[]{:S(2)}) async-start(), calls=%async_computation.6 | async-start | bytes 5013504 | tf_op jit(solution)/shard_map/all_gather | solution.py:86
  35.6 277.0 %all-gather.12.cloned.1.call-start = ((), (), s32[]{:S(2)}) async-start(), calls=%async_computation.7 | async-start | bytes 10027008 | tf_op jit(solution)/shard_map/all_gather | solution.py:85
  46.6 347.2 %all-gather.14.cloned.1.call-start = ((), (), s32[]{:S(2)}) async-start(), calls=%async_computation.8 | async-start | bytes 5013504 | tf_op jit(solution)/shard_map/all_gather | solution.py:86
  47.3 44.1 %copy-start.124 = (pred[12]{0:T(512)(128)(4,1)}, pred[12]{0:T(512)(128)(4,1)S(1)}, u32[]{:S(2)}) copy-start(pred[12]{0:T(512)(128)(4,1)S(1)} %compare_bitcast_fusion) | copy-start | bytes 40
  47.9 45.5 %copy-start.52 = (f32[12,384]{1,0:T(8,128)}, f32[12,384]{1,0:T(8,128)S(1)}, u32[]{:S(2)}) copy-start(f32[12,384]{1,0:T(8,128)S(1)} %get-tuple-element.88) | copy-start | bytes 55300
  47.9 45.4 %copy-start.54 = (f32[12,384]{1,0:T(8,128)}, f32[12,384]{1,0:T(8,128)S(1)}, u32[]{:S(2)}) copy-start(f32[12,384]{1,0:T(8,128)S(1)} %get-tuple-element.89) | copy-start | bytes 55300
  47.9 47.8 %copy-start.67 = (bf16[256,20]{0,1:T(8,128)(2,1)}, bf16[256,20]{0,1:T(8,128)(2,1)S(1)}, u32[]{:S(2)}) copy-start(bf16[256,20]{0,1:T(8,128)(2,1)S(1)} %add_convert_fusion.3) | copy-start | bytes 30724
  90.7 58.8 %copy-start.58 = (f32[768]{0:T(1024)}, f32[768]{0:T(1024)S(1)}, u32[]{:S(2)}) copy-start(f32[768]{0:T(1024)S(1)} %get-tuple-element.45) | copy-start | bytes 9220
  90.7 125.4 %copy-start.60 = (f32[768]{0:T(1024)}, f32[768]{0:T(1024)S(1)}, u32[]{:S(2)}) copy-start(f32[768]{0:T(1024)S(1)} %get-tuple-element.44) | copy-start | bytes 9220
  90.7 221.9 %copy-start.62 = (f32[768]{0:T(1024)}, f32[768]{0:T(1024)S(1)}, u32[]{:S(2)}) copy-start(f32[768]{0:T(1024)S(1)} %get-tuple-element.43) | copy-start | bytes 9220
  90.7 293.1 %copy-start.64 = (f32[768]{0:T(1024)}, f32[768]{0:T(1024)S(1)}, u32[]{:S(2)}) copy-start(f32[768]{0:T(1024)S(1)} %get-tuple-element.42) | copy-start | bytes 9220
  90.7 310.5 %copy-start.69 = (f32[768]{0:T(1024)}, f32[768]{0:T(1024)S(1)}, u32[]{:S(2)}) copy-start(f32[768]{0:T(1024)S(1)} %get-tuple-element.41) | copy-start | bytes 9220
  91.4 58.0 %copy-start.74 = (f32[768]{0:T(1024)}, f32[768]{0:T(1024)S(1)}, u32[]{:S(2)}) copy-start(f32[768]{0:T(1024)S(1)} %slice_convert_fusion.3) | copy-start | bytes 9220
  96.9 52.6 %copy-start.82 = (f32[256]{0:T(256)}, f32[256]{0:T(256)S(1)}, u32[]{:S(2)}) copy-start(f32[256]{0:T(256)S(1)} %broadcast_multiply_fusion.4) | copy-start | bytes 3076
  97.1 52.4 %copy-start.104 = (f32[256]{0:T(256)}, f32[256]{0:T(256)S(1)}, u32[]{:S(2)}) copy-start(f32[256]{0:T(256)S(1)} %multiply_reduce_fusion.15) | copy-start | bytes 3076
  97.1 52.3 %copy-start.94 = (f32[256]{0:T(256)}, f32[256]{0:T(256)S(1)}, u32[]{:S(2)}) copy-start(f32[256]{0:T(256)S(1)} %fusion.125) | copy-start | bytes 3076
  151.4 44.4 %collective-permute-start = (bf16[256,1536]{1,0:T(8,128)(2,1)}, bf16[256,1536]{1,0:T(8,128)(2,1)}, u32[]{:S(2)}, u32[]{:S(2)}) collective-permute-start(bf16[256,1536]{1,0:T(8,128)(2,1)} %slice.253), channel_id=1, source_target_pairs={{0,2},{1,3},{2,4},{3,5},{4,6},{5,7},{6,8},{7,9},{8,10},{9,11},{10,... | collective-permute-start | bytes 2359304 | tf_op jit(solution)/shard_map/ppermute | solution.py:37
  154.8 42.2 %collective-permute-start.1 = (bf16[256,1536]{1,0:T(8,128)(2,1)}, bf16[256,1536]{1,0:T(8,128)(2,1)}, u32[]{:S(2)}, u32[]{:S(2)}) collective-permute-start(bf16[256,1536]{1,0:T(8,128)(2,1)} %slice.253), channel_id=1, source_target_pairs={{0,1},{1,2},{2,3},{3,4},{4,5},{5,6},{6,7},{7,8},{8,9},{9,10},{10,1... | collective-permute-start | bytes 2359304 | tf_op jit(solution)/shard_map/ppermute | solution.py:37
  163.2 35.0 %copy-start.32 = (bf16[256,2304]{1,0:T(8,128)(2,1)S(1)}, bf16[256,2304]{1,0:T(8,128)(2,1)}, u32[]{:S(2)}) copy-start(bf16[256,2304]{1,0:T(8,128)(2,1)} %copy-done.31) | copy-start | bytes 3538948
  165.3 606.9 %reduce-scatter.11.cloned.1.call-start = ((), (), s32[]{:S(2)}) async-start(), calls=%async_computation.12 | async-start | bytes 5013504 | tf_op jit(solution)/shard_map/reduce_scatter | solution.py:346
  166.7 31.6 %collective-permute-start.3 = (bf16[256,1536]{1,0:T(8,128)(2,1)}, bf16[256,1536]{1,0:T(8,128)(2,1)S(1)}, u32[]{:S(2)}, u32[]{:S(2)}) collective-permute-start(bf16[256,1536]{1,0:T(8,128)(2,1)} %slice.253), channel_id=1, source_target_pairs={{2,0},{3,1},{4,2},{5,3},{6,4},{7,5},{8,6},{9,7},{10,8},{11,9},{12,... | collective-permute-start | bytes 2359304 | tf_op jit(solution)/shard_map/ppermute | solution.py:37
  168.0 30.3 %collective-permute-start.2 = (bf16[256,1536]{1,0:T(8,128)(2,1)}, bf16[256,1536]{1,0:T(8,128)(2,1)S(1)}, u32[]{:S(2)}, u32[]{:S(2)}) collective-permute-start(bf16[256,1536]{1,0:T(8,128)(2,1)} %slice.253), channel_id=1, source_target_pairs={{1,0},{2,1},{3,2},{4,3},{5,4},{6,5},{7,6},{8,7},{9,8},{10,9},{11,1... | collective-permute-start | bytes 2359304 | tf_op jit(solution)/shard_map/ppermute | solution.py:37
  233.8 81.9 %copy-start.7 = (f32[256,768]{1,0:T(8,128)}, f32[256,768]{1,0:T(8,128)S(1)}, u32[]{:S(2)}) copy-start(f32[256,768]{1,0:T(8,128)S(1)} %get-tuple-element.99) | copy-start | bytes 2359300
  233.9 81.9 %copy-start.84 = (f32[256]{0:T(256)}, f32[256]{0:T(256)S(1)}, u32[]{:S(2)}) copy-start(f32[256]{0:T(256)S(1)} %broadcast_multiply_fusion.2) | copy-start | bytes 3076
  234.1 81.7 %copy-start.108 = (f32[256]{0:T(256)}, f32[256]{0:T(256)S(1)}, u32[]{:S(2)}) copy-start(f32[256]{0:T(256)S(1)} %multiply_reduce_fusion.13) | copy-start | bytes 3076
  234.1 81.7 %copy-start.96 = (f32[256]{0:T(256)}, f32[256]{0:T(256)S(1)}, u32[]{:S(2)}) copy-start(f32[256]{0:T(256)S(1)} %fusion.127) | copy-start | bytes 3076
  316.8 33.5 %collective-permute-start.4 = (bf16[256,1536]{1,0:T(8,128)(2,1)}, bf16[256,1536]{1,0:T(8,128)(2,1)}, u32[]{:S(2)}, u32[]{:S(2)}) collective-permute-start(bf16[256,1536]{1,0:T(8,128)(2,1)} %slice.262), channel_id=1, source_target_pairs={{0,2},{1,3},{2,4},{3,5},{4,6},{5,7},{6,8},{7,9},{8,10},{9,11},{10,... | collective-permute-start | bytes 2359304 | tf_op jit(solution)/shard_map/ppermute | solution.py:37
  320.2 32.2 %collective-permute-start.5 = (bf16[256,1536]{1,0:T(8,128)(2,1)}, bf16[256,1536]{1,0:T(8,128)(2,1)}, u32[]{:S(2)}, u32[]{:S(2)}) collective-permute-start(bf16[256,1536]{1,0:T(8,128)(2,1)} %slice.262), channel_id=1, source_target_pairs={{0,1},{1,2},{2,3},{3,4},{4,5},{5,6},{6,7},{7,8},{8,9},{9,10},{10,1... | collective-permute-start | bytes 2359304 | tf_op jit(solution)/shard_map/ppermute | solution.py:37
  332.0 52.4 %slice-start.3 = ((s8[9437184]{0:T(1024)(128)(4,1)}), s8[4194304]{0:T(1024)(128)(4,1)S(1)}, s32[]{:S(2)}) async-start(s8[9437184]{0:T(1024)(128)(4,1)} %bitcast.118), calls=%async_computation.16 | async-start | bytes 8388608
  336.1 30.4 %collective-permute-start.7 = (bf16[256,1536]{1,0:T(8,128)(2,1)}, bf16[256,1536]{1,0:T(8,128)(2,1)S(1)}, u32[]{:S(2)}, u32[]{:S(2)}) collective-permute-start(bf16[256,1536]{1,0:T(8,128)(2,1)} %slice.262), channel_id=1, source_target_pairs={{2,0},{3,1},{4,2},{5,3},{6,4},{7,5},{8,6},{9,7},{10,8},{11,9},{12,... | collective-permute-start | bytes 2359304 | tf_op jit(solution)/shard_map/ppermute | solution.py:37
  337.4 18.1 %collective-permute-start.6 = (bf16[256,1536]{1,0:T(8,128)(2,1)}, bf16[256,1536]{1,0:T(8,128)(2,1)S(1)}, u32[]{:S(2)}, u32[]{:S(2)}) collective-permute-start(bf16[256,1536]{1,0:T(8,128)(2,1)} %slice.262), channel_id=1, source_target_pairs={{1,0},{2,1},{3,2},{4,3},{5,4},{6,5},{7,6},{8,7},{9,8},{10,9},{11,1... | collective-permute-start | bytes 2359304 | tf_op jit(solution)/shard_map/ppermute | solution.py:37
  354.5 30.0 %slice-start.4 = ((s8[9437184]{0:T(1024)(128)(4,1)}), s8[4194304]{0:T(1024)(128)(4,1)S(1)}, s32[]{:S(2)}) async-start(s8[9437184]{0:T(1024)(128)(4,1)} %bitcast.118), calls=%async_computation.17 | async-start | bytes 8388608
  401.4 52.5 %copy-start.28 = (bf16[256,768]{1,0:T(8,128)(2,1)}, bf16[256,768]{1,0:T(8,128)(2,1)S(1)}, u32[]{:S(2)}) copy-start(bf16[256,768]{1,0:T(8,128)(2,1)S(1)} %multiply_convert_fusion.6) | copy-start | bytes 1179652
  461.4 312.2 %reduce-scatter.7.cloned.1.call-start = ((), (), s32[]{:S(2)}) async-start(), calls=%async_computation.10 | async-start | bytes 5013504 | tf_op jit(solution)/shard_map/reduce_scatter | solution.py:346
  473.9 77.5 %copy-start.18 = (f32[256,768]{1,0:T(8,128)}, f32[256,768]{1,0:T(8,128)S(1)}, u32[]{:S(2)}) copy-start(f32[256,768]{1,0:T(8,128)S(1)} %add_add_fusion.8) | copy-start | bytes 2359300
  495.3 51.5 %copy-start.9 = (f32[256,768]{1,0:T(8,128)S(1)}, f32[256,768]{1,0:T(8,128)}, u32[]{:S(2)}) copy-start(f32[256,768]{1,0:T(8,128)} %copy-done.7) | copy-start | bytes 2359300
  495.3 51.5 %copy-start.63 = (f32[768]{0:T(1024)S(1)}, f32[768]{0:T(1024)}, u32[]{:S(2)}) copy-start(f32[768]{0:T(1024)} %copy-done.62) | copy-start | bytes 9220
  495.3 51.5 %copy-start.85 = (f32[256]{0:T(256)S(1)}, f32[256]{0:T(256)}, u32[]{:S(2)}) copy-start(f32[256]{0:T(256)} %copy-done.84) | copy-start | bytes 3076
  495.3 51.5 %copy-start.97 = (f32[256]{0:T(256)S(1)}, f32[256]{0:T(256)}, u32[]{:S(2)}) copy-start(f32[256]{0:T(256)} %copy-done.96) | copy-start | bytes 3076
  495.3 26.5 %collective-permute-start.8 = (bf16[256,1536]{1,0:T(8,128)(2,1)S(1)}, bf16[256,1536]{1,0:T(8,128)(2,1)S(1)}, u32[]{:S(2)}, u32[]{:S(2)}) collective-permute-start(bf16[256,1536]{1,0:T(8,128)(2,1)S(1)} %get-tuple-element.78), channel_id=1, source_target_pairs={{2,0},{3,1},{4,2},{5,3},{6,4},{7,5},{8,6},{9,7},{10,8},{11,9},{12,... | collective-permute-start | bytes 2359304 | tf_op jit(solution)/shard_map/ppermute | solution.py:37
  496.7 48.4 %collective-permute-start.11 = (bf16[256,1536]{1,0:T(8,128)(2,1)S(1)}, bf16[256,1536]{1,0:T(8,128)(2,1)S(1)}, u32[]{:S(2)}, u32[]{:S(2)}) collective-permute-start(bf16[256,1536]{1,0:T(8,128)(2,1)S(1)} %get-tuple-element.79), channel_id=1, source_target_pairs={{0,2},{1,3},{2,4},{3,5},{4,6},{5,7},{6,8},{7,9},{8,10},{9,11},{10,... | collective-permute-start | bytes 2359304 | tf_op jit(solution)/shard_map/ppermute | solution.py:37
  501.3 43.8 %collective-permute-start.10 = (bf16[256,1536]{1,0:T(8,128)(2,1)S(1)}, bf16[256,1536]{1,0:T(8,128)(2,1)S(1)}, u32[]{:S(2)}, u32[]{:S(2)}) collective-permute-start(bf16[256,1536]{1,0:T(8,128)(2,1)S(1)} %get-tuple-element.80), channel_id=1, source_target_pairs={{0,1},{1,2},{2,3},{3,4},{4,5},{5,6},{6,7},{7,8},{8,9},{9,10},{10,1... | collective-permute-start | bytes 2359304 | tf_op jit(solution)/shard_map/ppermute | solution.py:37
  502.8 42.3 %collective-permute-start.9 = (bf16[256,1536]{1,0:T(8,128)(2,1)S(1)}, bf16[256,1536]{1,0:T(8,128)(2,1)S(1)}, u32[]{:S(2)}, u32[]{:S(2)}) collective-permute-start(bf16[256,1536]{1,0:T(8,128)(2,1)S(1)} %get-tuple-element.81), channel_id=1, source_target_pairs={{1,0},{2,1},{3,2},{4,3},{5,4},{6,5},{7,6},{8,7},{9,8},{10,9},{11,1... | collective-permute-start | bytes 2359304 | tf_op jit(solution)/shard_map/ppermute | solution.py:37
  557.7 217.4 %reduce-scatter.9.cloned.1.call-start = ((), (), s32[]{:S(2)}) async-start(), calls=%async_computation.11 | async-start | bytes 10027008 | tf_op jit(solution)/shard_map/reduce_scatter | solution.py:345
  571.9 308.8 %reduce-scatter.5.cloned.1.call-start = ((), (), s32[]{:S(2)}) async-start(), calls=%async_computation.9 | async-start | bytes 10027008 | tf_op jit(solution)/shard_map/reduce_scatter | solution.py:345
  623.7 23.5 %copy-start.121 = (f32[12]{0:T(128)S(1)}, f32[12]{0:T(128)}, u32[]{:S(2)}) copy-start(f32[12]{0:T(128)} %copy-done.120) | copy-start | bytes 148
  623.7 23.5 %copy-start.123 = (f32[12]{0:T(128)S(1)}, f32[12]{0:T(128)}, u32[]{:S(2)}) copy-start(f32[12]{0:T(128)} %copy-done.122) | copy-start | bytes 148
  623.7 23.5 %copy-start.132 = (f32[12]{0:T(128)S(1)}, f32[12]{0:T(128)}, u32[]{:S(2)}) copy-start(f32[12]{0:T(128)} %get-tuple-element.38) | copy-start | bytes 148
  623.7 25.4 %copy-start.114 = (f32[768]{0:T(1024)S(1)}, f32[768]{0:T(1024)}, u32[]{:S(2)}) copy-start(f32[768]{0:T(1024)} %get-tuple-element.34) | copy-start | bytes 9220
  627.4 25.8 %copy-start.13 = (f32[256,768]{1,0:T(8,128)S(1)}, f32[256,768]{1,0:T(8,128)}, u32[]{:S(2)}) copy-start(f32[256,768]{1,0:T(8,128)} %copy-done.11) | copy-start | bytes 2359300
  627.4 31.1 %collective-permute-start.12 = (bf16[256,1536]{1,0:T(8,128)(2,1)}, bf16[256,1536]{1,0:T(8,128)(2,1)}, u32[]{:S(2)}, u32[]{:S(2)}) collective-permute-start(bf16[256,1536]{1,0:T(8,128)(2,1)} %get-tuple-element.74), channel_id=1, source_target_pairs={{2,0},{3,1},{4,2},{5,3},{6,4},{7,5},{8,6},{9,7},{10,8},{11,9},{12,... | collective-permute-start | bytes 2359304 | tf_op jit(solution)/shard_map/ppermute | solution.py:37
  628.8 60.8 %collective-permute-start.15 = (bf16[256,1536]{1,0:T(8,128)(2,1)}, bf16[256,1536]{1,0:T(8,128)(2,1)}, u32[]{:S(2)}, u32[]{:S(2)}) collective-permute-start(bf16[256,1536]{1,0:T(8,128)(2,1)} %get-tuple-element.75), channel_id=1, source_target_pairs={{0,2},{1,3},{2,4},{3,5},{4,6},{5,7},{6,8},{7,9},{8,10},{9,11},{10,... | collective-permute-start | bytes 2359304 | tf_op jit(solution)/shard_map/ppermute | solution.py:37
  643.7 45.9 %collective-permute-start.14 = (bf16[256,1536]{1,0:T(8,128)(2,1)}, bf16[256,1536]{1,0:T(8,128)(2,1)}, u32[]{:S(2)}, u32[]{:S(2)}) collective-permute-start(bf16[256,1536]{1,0:T(8,128)(2,1)} %get-tuple-element.76), channel_id=1, source_target_pairs={{0,1},{1,2},{2,3},{3,4},{4,5},{5,6},{6,7},{7,8},{8,9},{9,10},{10,1... | collective-permute-start | bytes 2359304 | tf_op jit(solution)/shard_map/ppermute | solution.py:37
  645.9 43.7 %collective-permute-start.13 = (bf16[256,1536]{1,0:T(8,128)(2,1)}, bf16[256,1536]{1,0:T(8,128)(2,1)}, u32[]{:S(2)}, u32[]{:S(2)}) collective-permute-start(bf16[256,1536]{1,0:T(8,128)(2,1)} %get-tuple-element.77), channel_id=1, source_target_pairs={{1,0},{2,1},{3,2},{4,3},{5,4},{6,5},{7,6},{8,7},{9,8},{10,9},{11,1... | collective-permute-start | bytes 2359304 | tf_op jit(solution)/shard_map/ppermute | solution.py:37
  658.4 33.8 %copy-start.59 = (f32[768]{0:T(1024)S(1)}, f32[768]{0:T(1024)}, u32[]{:S(2)}) copy-start(f32[768]{0:T(1024)} %copy-done.58) | copy-start | bytes 9220
  658.4 33.9 %copy-start.83 = (f32[256]{0:T(256)S(1)}, f32[256]{0:T(256)}, u32[]{:S(2)}) copy-start(f32[256]{0:T(256)} %copy-done.82) | copy-start | bytes 3076
  658.4 33.9 %copy-start.95 = (f32[256]{0:T(256)S(1)}, f32[256]{0:T(256)}, u32[]{:S(2)}) copy-start(f32[256]{0:T(256)} %copy-done.94) | copy-start | bytes 3076
  698.2 39.1 %copy-start.53 = (f32[12,384]{1,0:T(8,128)S(1)}, f32[12,384]{1,0:T(8,128)}, u32[]{:S(2)}) copy-start(f32[12,384]{1,0:T(8,128)} %copy-done.52) | copy-start | bytes 55300
  698.2 39.1 %copy-start.55 = (f32[12,384]{1,0:T(8,128)S(1)}, f32[12,384]{1,0:T(8,128)}, u32[]{:S(2)}) copy-start(f32[12,384]{1,0:T(8,128)} %copy-done.54) | copy-start | bytes 55300
  923.5 29.6 %collective-permute-start.17 = (bf16[125088]{0:T(1024)(128)(2,1)S(1)}, bf16[125088]{0:T(1024)(128)(2,1)S(1)}, u32[]{:S(2)}, u32[]{:S(2)}) collective-permute-start(bf16[125088]{0:T(1024)(128)(2,1)S(1)} %get-tuple-element.55), channel_id=1, source_target_pairs={{0,16},{16,0},{1,17},{17,1},{2,18},{18,2},{3,19},{19,3},{4,20},{20... | collective-permute-start | bytes 750536 | tf_op jit(solution)/shard_map/ppermute | solution.py:514
  950.6 42.5 %copy-start.30 = (f32[2,442368]{1,0:T(2,128)S(1)}, f32[2,442368]{1,0:T(2,128)}, u32[]{:S(2)}) copy-start(f32[2,442368]{1,0:T(2,128)} %param.20) | copy-start | bytes 10616836
  952.9 40.2 %collective-permute-start.16 = (bf16[2,442368]{1,0:T(2,128)(2,1)S(1)}, bf16[2,442368]{1,0:T(2,128)(2,1)S(1)}, u32[]{:S(2)}, u32[]{:S(2)}) collective-permute-start(bf16[2,442368]{1,0:T(2,128)(2,1)S(1)} %get-tuple-element.62), channel_id=1, source_target_pairs={{0,16},{16,0},{1,17},{17,1},{2,18},{18,2},{3,19},{19,3},{4,20},{20... | collective-permute-start | bytes 5308424 | tf_op jit(solution)/shard_map/ppermute | solution.py:514
  (109 other events, 798.1 us)
Sparse Core Ops, SparseCore 0:
  10.9 52.5 all-gather.5
  66.3 79.9 all-gather.7
  149.1 79.1 all-gather.9
  231.1 81.4 all-gather.11
  315.3 78.4 all-gather.13
  461.5 106.7 reduce-scatter.10
  572.7 74.4 reduce-scatter.6
  651.2 113.6 reduce-scatter.8
  769.6 111.1 reduce-scatter.4

commit v3 on v2

--- a/solution.py
+++ b/solution.py
@@ -80,10 +80,7 @@
     return piece[:cut].reshape(D // shards, 4 * D + FF), piece[cut:].reshape(FF // shards, D)
 
 
-def gather_layer(anchor, shards):
-    upper, lower = layer_rows(anchor.astype(jnp.bfloat16), shards)
-    upper = lax.all_gather(upper, "seq", axis=0, tiled=True)
-    lower = lax.all_gather(lower, "seq", axis=0, tiled=True)
+def split_upper(upper, lower):
     return [upper[:, : 3 * D], upper[:, 3 * D : 4 * D], upper[:, 4 * D :], lower]
 
 
@@ -329,7 +326,7 @@
     return (grad_middle + grad_input, operand_pairs, grad_gain_one, grad_gain_two)
 
 
-def reduce_layer(operand_pairs, shards):
+def layer_gradients(operand_pairs):
     normed, grad_projected, attended, branch_mid, second, grad_upper, activated, branch_top = (
         operand_pairs
     )
@@ -342,9 +339,7 @@
         axis=1,
     )
     lower_full = contract_rows(activated, branch_top).astype(jnp.bfloat16)
-    upper_own = lax.psum_scatter(upper_full, "seq", scatter_dimension=0, tiled=True)
-    lower_own = lax.psum_scatter(lower_full, "seq", scatter_dimension=0, tiled=True)
-    return jnp.concatenate([upper_own.reshape(-1), lower_own.reshape(-1)]).astype(jnp.float32)
+    return upper_full, lower_full
 
 
 def adam(grad, first, second, anchor):
@@ -459,9 +454,21 @@
 
 
 def share_kernel(count, x_ref, out_ref, parts, send_sem, recv_sem):
-    me = lax.axis_index("seq")
-    group = lax.axis_index("grp")
-    greet_seq(me, count)
+    seq = lax.axis_size("seq")
+    me = lax.axis_index("grp") * seq + lax.axis_index("seq")
+
+    def place(step):
+        peer = lax.rem(me + step, count)
+        return peer // seq, lax.rem(peer, seq)
+
+    barrier = pltpu.get_barrier_semaphore()
+
+    def greet(step, carry):
+        pl.semaphore_signal(barrier, inc=1, device_id=place(step), device_id_type=MESH)
+        return carry
+
+    lax.fori_loop(1, count, greet, 0)
+    pl.semaphore_wait(barrier, count - 1)
 
     def copy_of(step):
         return pltpu.make_async_remote_copy(
@@ -469,7 +476,7 @@
             dst_ref=parts.at[step],
             send_sem=send_sem.at[step],
             recv_sem=recv_sem.at[step],
-            device_id=(group, lax.rem(me + step, count)),
+            device_id=place(step),
             device_id_type=MESH,
         )
 
@@ -488,22 +495,570 @@
     lax.fori_loop(1, count, finish, 0)
 
 
-def sum_scalar_over_seq(value, collective):
-    count = lax.axis_size("seq")
-    if count != CLOSE_RANKS:
-        return lax.psum(value, "seq")
-    shape = (count, SUBLANES, LANES)
+def sums_by_group(value, collective):
+    groups, count = lax.axis_size("grp"), lax.axis_size("seq")
+    shape = (groups * count, SUBLANES, LANES)
     shared = pl.pallas_call(
-        functools.partial(share_kernel, count),
+        functools.partial(share_kernel, groups * count),
         out_shape=jax.ShapeDtypeStruct(shape, jnp.float32),
         in_specs=[pl.BlockSpec(memory_space=pltpu.VMEM)],
         out_specs=pl.BlockSpec(memory_space=pltpu.VMEM),
         scratch_shapes=[pltpu.VMEM(shape, jnp.float32)]
-        + [pltpu.SemaphoreType.DMA((count,))] * 2,
+        + [pltpu.SemaphoreType.DMA((groups * count,))] * 2,
         compiler_params=pltpu.CompilerParams(collective_id=collective, has_side_effects=True),
-        name="share_over_seq",
+        name="share_over_all",
     )(jnp.full(shape[1:], value, jnp.float32))
-    return jnp.sum(shared[:, 0, 0])
+    return jnp.sum(shared[:, 0, 0].reshape(groups, count), axis=1)
+
+
+GRID = (4, 2, 2)
+GATHER_Y_LAG = 2
+GATHER_X_LAG = 5
+GATHER_AHEAD = 1
+GATHER_LANES = 256
+
+
+def place_of(me):
+    return me // 4, lax.rem(me // 2, 2), lax.rem(me, 2)
+
+
+def rank_of(along, across, core):
+    return (along * 2 + across) * 2 + core
+
+
+def gather_kernel(shared, *refs):
+    pieces = len(shared)
+    own_refs, out_refs = refs[:pieces], refs[pieces : 2 * pieces]
+    local_sem, z_send, z_recv, y_send, y_recv, x_send, x_recv, c_send, c_recv = refs[2 * pieces :]
+    group, me = lax.axis_index("grp"), lax.axis_index("seq")
+    z, y, core = place_of(me)
+    z_size = GRID[0]
+    across, sibling, twin = (
+        (group, rank_of(z, 1 - y, core)),
+        (group, rank_of(z, y, 1 - core)),
+        (1 - group, me),
+    )
+    barrier = pltpu.get_barrier_semaphore()
+    for there in (across, sibling, twin):
+        pl.semaphore_signal(barrier, inc=1, device_id=there, device_id_type=MESH)
+
+    @pl.when(z > 0)
+    def _():
+        pl.semaphore_signal(
+            barrier, inc=1, device_id=(group, rank_of(z - 1, y, core)), device_id_type=MESH
+        )
+
+    @pl.when(z < z_size - 1)
+    def _():
+        pl.semaphore_signal(
+            barrier, inc=1, device_id=(group, rank_of(z + 1, y, core)), device_id_type=MESH
+        )
+
+    neighbours = (z > 0).astype(jnp.int32) + (z < z_size - 1).astype(jnp.int32)
+    pl.semaphore_wait(barrier, 3 + neighbours)
+
+    def half_of(ref, piece, half):
+        if half is None:
+            return ref
+        span = ref.shape[-1] // 2
+        return ref.at[:, pl.ds(pl.multiple_of(half * span, LANES), span)]
+
+    def move(piece, half, there, along, over, send, recv, own=False):
+        dst = half_of(out_refs[piece].at[rank_of(along, over, core)], piece, half)
+        src = half_of(own_refs[piece], piece, half) if own else dst
+        return pltpu.make_async_remote_copy(
+            src_ref=src, dst_ref=dst, send_sem=send, recv_sem=recv, device_id=there, device_id_type=MESH
+        )
+
+    def z_move(piece, along, forward, own=False):
+        there = (group, rank_of(z + (1 if forward else -1), y, core))
+        half = group if shared[piece] else None
+        return move(
+            piece, half, there, along, y, z_send.at[piece, along, int(forward)], z_recv.at[piece, along], own
+        )
+
+    def y_move(piece, along, own=False, over=None):
+        half = group if shared[piece] else None
+        over = y if over is None else over
+        return move(piece, half, across, along, over, y_send.at[piece, along], y_recv.at[piece, along], own)
+
+    def x_move(piece, along, over, arriving=False):
+        half = 1 - group if arriving else group
+        slot = along * 2 + over
+        return move(piece, half, twin, along, over, x_send.at[piece, slot], x_recv.at[piece, slot])
+
+    def c_move(piece, along, over, half, slot, own=False):
+        return move(
+            piece,
+            half,
+            sibling,
+            along,
+            over,
+            c_send.at[piece, along * 2 + over, slot],
+            c_recv.at[piece, along * 2 + over, slot],
+            own,
+        )
+
+    def each_along(distance, action):
+        if distance == 0:
+            action(z, True, True)
+            return
+
+        @pl.when(z - distance >= 0)
+        def _():
+            action(z - distance, True, False)
+
+        @pl.when(z + distance < z_size)
+        def _():
+            action(z + distance, False, True)
+
+    def own_sends(piece):
+        pltpu.make_async_copy(own_refs[piece], out_refs[piece].at[me], local_sem.at[piece]).start()
+
+        @pl.when(z + 1 < z_size)
+        def _():
+            z_move(piece, z, True, own=True).start()
+
+        @pl.when(z > 0)
+        def _():
+            z_move(piece, z, False, own=True).start()
+
+        y_move(piece, z, own=True).start()
+        c_move(piece, z, y, None, 0, own=True).start()
+
+    def z_arrivals(piece, distance):
+        if distance == 0:
+            return
+
+        def one(along, onward, backward):
+            z_move(piece, along, onward).wait_recv()
+
+            @pl.when((z + 1 < z_size) if onward else (z > 0))
+            def _():
+                z_move(piece, along, onward).start()
+
+            y_move(piece, along).start()
+            if shared[piece]:
+                x_move(piece, along, y).start()
+            c_move(piece, along, y, group if shared[piece] else None, 0).start()
+
+        each_along(distance, one)
+
+    def y_arrivals(piece, distance):
+        def one(along, *_):
+            y_move(piece, along, over=1 - y).wait_recv()
+            if shared[piece]:
+                x_move(piece, along, 1 - y).start()
+            c_move(piece, along, 1 - y, group if shared[piece] else None, 0).start()
+
+        each_along(distance, one)
+
+    def x_arrivals(piece, distance):
+        if not shared[piece]:
+            return
+
+        def one(along, *_):
+            for turn in range(2):
+                over = y if turn == 0 else 1 - y
+                if distance == 0 and turn == 0:
+                    continue
+                x_move(piece, along, over, arriving=True).wait_recv()
+                c_move(piece, along, over, 1 - group, 1).start()
+
+        each_along(distance, one)
+
+    def drain(piece, distance):
+        def one(along, onward, backward):
+            own = distance == 0
+            half = group if shared[piece] else None
+            for turn in range(2):
+                over = y if turn == 0 else 1 - y
+                mine = own and turn == 0
+                whole = None if mine else half
+                c_move(piece, along, over, whole, 0).wait()
+                if shared[piece] and not mine:
+                    c_move(piece, along, over, 1 - group, 1).wait()
+                    x_move(piece, along, over).wait_send()
+            y_move(piece, along).wait_send()
+            if onward:
+
+                @pl.when(z + 1 < z_size)
+                def _():
+                    z_move(piece, along, True).wait_send()
+
+            if backward:
+
+                @pl.when(z > 0)
+                def _():
+                    z_move(piece, along, False).wait_send()
+
+        each_along(distance, one)
+        if distance == 0:
+            pltpu.make_async_copy(own_refs[piece], out_refs[piece].at[me], local_sem.at[piece]).wait()
+
+    slots = [(piece, distance) for piece in range(pieces) for distance in range(z_size)]
+    own_sends(0)
+    for turn in range(len(slots) + GATHER_X_LAG):
+        if turn < len(slots):
+            piece, distance = slots[turn]
+            if distance == GATHER_AHEAD and piece + 1 < pieces:
+                own_sends(piece + 1)
+            z_arrivals(piece, distance)
+        if 0 <= turn - GATHER_Y_LAG < len(slots):
+            y_arrivals(*slots[turn - GATHER_Y_LAG])
+        if 0 <= turn - GATHER_X_LAG < len(slots):
+            x_arrivals(*slots[turn - GATHER_X_LAG])
+    for slot in slots:
+        drain(*slot)
+
+
+def gather_pieces(pieces, shared, collective):
+    count = lax.axis_size("seq")
+    if count != math.prod(GRID) or lax.axis_size("grp") != 2:
+        return [lax.all_gather(piece, "seq", axis=0) for piece in pieces]
+    amount = len(pieces)
+    sems = [
+        (amount,),
+        (amount, 4, 2),
+        (amount, 4),
+        (amount, 4),
+        (amount, 4),
+        (amount, 8),
+        (amount, 8),
+        (amount, 8, 2),
+        (amount, 8, 2),
+    ]
+    return pl.pallas_call(
+        functools.partial(gather_kernel, tuple(shared)),
+        out_shape=[jax.ShapeDtypeStruct((count,) + piece.shape, piece.dtype) for piece in pieces],
+        in_specs=[pl.BlockSpec(memory_space=pl.ANY)] * amount,
+        out_specs=[pl.BlockSpec(memory_space=pl.ANY)] * amount,
+        scratch_shapes=[pltpu.SemaphoreType.DMA(shape) for shape in sems],
+        compiler_params=pltpu.CompilerParams(collective_id=collective, has_side_effects=True),
+        name="gather_pieces",
+    )(*pieces)
+
+
+ROW_GROUP = 16
+UPPER_CUTS = 3
+LOWER_CUTS = 1
+SCATTER_LAG = 2
+
+
+def scatter_kernel(pieces, amount, *refs):
+    grads, outs, twins = (refs[k * amount : (k + 1) * amount] for k in range(3))
+    squares = refs[3 * amount]
+    rest = refs[3 * amount + 1 :]
+    count = len(pieces)
+    own, beside, facing, from_left, from_right, ready = (
+        rest[k * count : (k + 1) * count] for k in range(6)
+    )
+    load_sem, c_send, c_recv, y_send, y_recv, z_send, z_recv, x_send, x_recv = rest[6 * count :]
+    group, me = lax.axis_index("grp"), lax.axis_index("seq")
+    z, y, core = place_of(me)
+    z_size = GRID[0]
+    across, sibling = (group, rank_of(z, 1 - y, core)), (group, rank_of(z, y, 1 - core))
+    twin = (1 - group, me)
+    left, right = (group, rank_of(z - 1, y, core)), (group, rank_of(z + 1, y, core))
+    has_left, has_right = z > 0, z < z_size - 1
+    barrier = pltpu.get_barrier_semaphore()
+    for there in (across, sibling, twin):
+        pl.semaphore_signal(barrier, inc=1, device_id=there, device_id_type=MESH)
+
+    @pl.when(has_left)
+    def _():
+        pl.semaphore_signal(barrier, inc=1, device_id=left, device_id_type=MESH)
+
+    @pl.when(has_right)
+    def _():
+        pl.semaphore_signal(barrier, inc=1, device_id=right, device_id_type=MESH)
+
+    neighbours = has_left.astype(jnp.int32) + has_right.astype(jnp.int32)
+    pl.semaphore_wait(barrier, 3 + neighbours)
+    squares[...] = jnp.zeros_like(squares)
+
+    def part(piece, along, over, owner):
+        which, row, rows, column, columns = pieces[piece]
+        return grads[which].at[rank_of(along, over, owner), pl.ds(row, rows), pl.ds(column, columns)]
+
+    def load(piece, along, over):
+        slot = along * 2 + over
+        return pltpu.make_async_copy(
+            part(piece, along, over, core), own[piece].at[slot], load_sem.at[piece, slot]
+        )
+
+    def remote(src, dst, send, recv, there):
+        return pltpu.make_async_remote_copy(
+            src_ref=src, dst_ref=dst, send_sem=send, recv_sem=recv, device_id=there, device_id_type=MESH
+        )
+
+    def c_move(piece, along, over):
+        slot = along * 2 + over
+        return remote(
+            part(piece, along, over, 1 - core),
+            beside[piece].at[slot],
+            c_send.at[piece, slot],
+            c_recv.at[piece, slot],
+            sibling,
+        )
+
+    def y_move(piece, along):
+        return remote(
+            own[piece].at[along * 2 + 1 - y],
+            facing[piece].at[along],
+            y_send.at[piece, along],
+            y_recv.at[piece, along],
+            across,
+        )
+
+    def z_move(piece, along, forward):
+        side = 0 if forward else 1
+        return remote(
+            facing[piece].at[along],
+            (from_left if forward else from_right)[piece].at[along],
+            z_send.at[piece, along],
+            z_recv.at[piece, along, side],
+            right if forward else left,
+        )
+
+    def x_move(piece):
+        which, row, height, column, columns = pieces[piece]
+        return remote(
+            ready[piece],
+            twins[which].at[pl.ds(row, height), pl.ds(column, columns)],
+            x_send.at[piece],
+            x_recv.at[piece],
+            twin,
+        )
+
+    def each_along(distance, action):
+        if distance == 0:
+            action(z, None)
+            return
+
+        @pl.when(z - distance >= 0)
+        def _():
+            action(z - distance, False)
+
+        @pl.when(z + distance < z_size)
+        def _():
+            action(z + distance, True)
+
+    def by_rows(piece, body):
+        def one(step, carry):
+            body(pl.ds(pl.multiple_of(step * ROW_GROUP, ROW_GROUP), ROW_GROUP))
+            return carry
+
+        lax.fori_loop(0, pieces[piece][2] // ROW_GROUP, one, 0)
+
+    def wide(ref, slot, rows):
+        return ref[slot, rows, :].astype(jnp.float32)
+
+    def begin(piece):
+        for distance in reversed(range(z_size)):
+
+            def one(along, _):
+                for over in range(2):
+                    load(piece, along, over).start()
+                    c_move(piece, along, over).start()
+
+            each_along(distance, one)
+
+    def c_stage(piece, distance):
+        def one(along, _):
+            for turn in range(2):
+                over = 1 - y if turn == 0 else y
+                slot = along * 2 + over
+                load(piece, along, over).wait()
+                c_move(piece, along, over).wait_recv()
+
+                def add(rows):
+                    total = wide(own[piece], slot, rows) + wide(beside[piece], slot, rows)
+                    own[piece][slot, rows, :] = total.astype(jnp.bfloat16)
+
+                by_rows(piece, add)
+                if turn == 0:
+                    y_move(piece, along).start()
+
+        each_along(distance, one)
+
+    def y_stage(piece, distance):
+        which, row, height, column, columns = pieces[piece]
+
+        def one(along, forward):
+            y_move(piece, along).wait_recv()
+            slot = along * 2 + y
+            if forward is None:
+
+                def add(rows):
+                    total = wide(own[piece], slot, rows) + wide(facing[piece], along, rows)
+                    there = pl.ds(pl.multiple_of(row + rows.start, ROW_GROUP), ROW_GROUP)
+                    outs[which][there, pl.ds(column, columns)] = total
+
+                by_rows(piece, add)
+                for side, present, source in ((True, has_left, from_left), (False, has_right, from_right)):
+
+                    @pl.when(present)
+                    def _():
+                        z_move(piece, along, side).wait_recv()
+
+                        def more(rows):
+                            there = pl.ds(pl.multiple_of(row + rows.start, ROW_GROUP), ROW_GROUP)
+                            outs[which][there, pl.ds(column, columns)] += wide(source[piece], along, rows)
+
+                        by_rows(piece, more)
+
+                def finish(rows):
+                    there = pl.ds(pl.multiple_of(row + rows.start, ROW_GROUP), ROW_GROUP)
+                    total = outs[which][there, pl.ds(column, columns)]
+                    ready[piece][rows, :] = total.astype(jnp.bfloat16)
+                    square = total[:SUBLANES] * total[:SUBLANES] + total[SUBLANES:] * total[SUBLANES:]
+                    for k in range(columns // LANES):
+                        squares[...] += square[:, k * LANES : (k + 1) * LANES]
+
+                by_rows(piece, finish)
+                x_move(piece).start()
+                return
+            source, present = (from_left, has_left) if forward else (from_right, has_right)
+
+            @pl.when(present)
+            def _():
+                z_move(piece, along, forward).wait_recv()
+
+                def add(rows):
+                    total = wide(own[piece], slot, rows) + wide(facing[piece], along, rows)
+                    total = total + wide(source[piece], along, rows)
+                    facing[piece][along, rows, :] = total.astype(jnp.bfloat16)
+
+                by_rows(piece, add)
+
+            @pl.when(jnp.logical_not(present))
+            def _():
+                def add(rows):
+                    total = wide(own[piece], slot, rows) + wide(facing[piece], along, rows)
+                    facing[piece][along, rows, :] = total.astype(jnp.bfloat16)
+
+                by_rows(piece, add)
+
+            z_move(piece, along, forward).start()
+
+        each_along(distance, one)
+
+    def drain(piece, distance):
+        def one(along, forward):
+            for over in range(2):
+                c_move(piece, along, over).wait_send()
+            y_move(piece, along).wait_send()
+            if forward is not None:
+                z_move(piece, along, forward).wait_send()
+
+        each_along(distance, one)
+
+    slots = [(piece, distance) for piece in range(count) for distance in reversed(range(z_size))]
+    for piece in range(min(2, count)):
+        begin(piece)
+    for turn in range(len(slots) + SCATTER_LAG):
+        if turn < len(slots):
+            c_stage(*slots[turn])
+            piece, distance = slots[turn]
+            if distance == 0 and piece + 2 < count:
+                begin(piece + 2)
+        if turn >= SCATTER_LAG:
+            y_stage(*slots[turn - SCATTER_LAG])
+    for slot in slots:
+        drain(*slot)
+    for piece in range(count):
+        x_move(piece).wait()
+
+
+def scatter_layer(upper, lower, collective):
+    count = math.prod(GRID)
+    grads = [grad.reshape(count, grad.shape[0] // count, grad.shape[1]) for grad in (upper, lower)]
+    pieces = []
+    for which, cuts in ((0, UPPER_CUTS), (1, LOWER_CUTS)):
+        rows, columns = grads[which].shape[1:]
+        if which == 0:
+            pieces += [(0, 0, rows, k * (columns // cuts), columns // cuts) for k in range(cuts)]
+        else:
+            pieces += [(1, k * (rows // cuts), rows // cuts, 0, columns) for k in range(cuts)]
+    amount = len(pieces)
+    places = math.prod(GRID[:2])
+
+    def room(slots):
+        return [pltpu.VMEM((slots, piece[2], piece[4]), jnp.bfloat16) for piece in pieces]
+
+    sems = [
+        (amount, places),
+        (amount, places),
+        (amount, places),
+        (amount, GRID[0]),
+        (amount, GRID[0]),
+        (amount, GRID[0]),
+        (amount, GRID[0], 2),
+        (amount,),
+        (amount,),
+    ]
+    own_upper, own_lower, twin_upper, twin_lower, squares = pl.pallas_call(
+        functools.partial(scatter_kernel, tuple(pieces), 2),
+        out_shape=[jax.ShapeDtypeStruct(grad.shape[1:], jnp.float32) for grad in grads]
+        + [jax.ShapeDtypeStruct(grad.shape[1:], jnp.bfloat16) for grad in grads]
+        + [jax.ShapeDtypeStruct((SUBLANES, LANES), jnp.float32)],
+        in_specs=[pl.BlockSpec(memory_space=pl.ANY)] * 2,
+        out_specs=[pl.BlockSpec(memory_space=pltpu.VMEM)] * 2
+        + [pl.BlockSpec(memory_space=pl.ANY)] * 2
+        + [pl.BlockSpec(memory_space=pltpu.VMEM)],
+        scratch_shapes=room(places)
+        + room(places)
+        + room(GRID[0])
+        + room(GRID[0])
+        + room(GRID[0])
+        + [pltpu.VMEM((piece[2], piece[4]), jnp.bfloat16) for piece in pieces]
+        + [pltpu.SemaphoreType.DMA(shape) for shape in sems],
+        compiler_params=pltpu.CompilerParams(
+            collective_id=collective, has_side_effects=True, vmem_limit_bytes=VMEM_LIMIT
+        ),
+        name="scatter_layer",
+    )(*grads)
+    return (own_upper, own_lower), (twin_upper, twin_lower), jnp.sum(squares)
+
+
+def lay_out_kernel(shards, view_ref, *outs):
+    cut = D // shards * (4 * D + FF) // LANES
+    for layer in range(L):
+        upper, lower = outs[2 * layer : 2 * layer + 2]
+        for ref, base in ((upper, 0), (lower, cut)):
+            across = ref.shape[1] // LANES
+            for row in range(0, ref.shape[0], ROW_GROUP):
+                for column in range(across):
+                    start = L * (base + row * across + column) + layer
+                    rows = view_ref[pl.ds(start, ROW_GROUP, stride=L * across), :]
+                    ref[row : row + ROW_GROUP, column * LANES : (column + 1) * LANES] = rows.astype(
+                        jnp.bfloat16
+                    )
+
+
+def flat_view(array):
+    layers, size = array.shape
+    return array.reshape(layers, size // LANES, LANES).transpose(1, 0, 2).reshape(-1, LANES)
+
+
+def lay_out(anchor, shards):
+    if shards != math.prod(GRID):
+        return [layer_rows(anchor[depth].astype(jnp.bfloat16), shards) for depth in range(L)]
+    shapes = [(D // shards, 4 * D + FF), (FF // shards, D)] * L
+    outs = pl.pallas_call(
+        functools.partial(lay_out_kernel, shards),
+        out_shape=[jax.ShapeDtypeStruct(shape, jnp.bfloat16) for shape in shapes],
+        in_specs=[pl.BlockSpec(memory_space=pltpu.VMEM)],
+        out_specs=[pl.BlockSpec(memory_space=pltpu.VMEM)] * len(shapes),
+        compiler_params=pltpu.CompilerParams(vmem_limit_bytes=VMEM_LIMIT),
+        name="lay_out",
+    )(flat_view(anchor))
+    return [(outs[2 * depth], outs[2 * depth + 1]) for depth in range(L)]
+
+
+def flatten(parts):
+    return jnp.concatenate([part.reshape(-1) for part in parts])
 
 
 def group_mean(delta, count):
@@ -513,6 +1068,84 @@
         moves = [(source, (source + step) % count) for source in range(count)]
         total = total + lax.ppermute(low.astype(jnp.bfloat16), "grp", moves).astype(jnp.float32)
     return total / count
+
+
+STEP_BLOCKS = 8
+
+
+def delta_of(grad, first, second, anchor):
+    return adam(grad, first, second, anchor)[2]
+
+
+def step_kernel(cut, factors, *refs):
+    own, twin = refs[: 2 * L], refs[2 * L : 4 * L]
+    anchor, first, second, outer, twin_first, twin_second = refs[4 * L : 4 * L + 6]
+    new, one, two, mean_out, momentum_out, own_flat, twin_flat = refs[4 * L + 6 :]
+    step = pl.program_id(0)
+    block = anchor.shape[0]
+
+    @pl.when(step == 0)
+    def _():
+        for grads, flat in ((own, own_flat), (twin, twin_flat)):
+            for layer in range(L):
+                for ref, base in zip(grads[2 * layer : 2 * layer + 2], (0, cut)):
+                    across = ref.shape[1] // LANES
+                    for row in range(0, ref.shape[0], ROW_GROUP):
+                        for column in range(across):
+                            start = L * (base + row * across + column) + layer
+                            flat[pl.ds(start, ROW_GROUP, stride=L * across), :] = ref[
+                                row : row + ROW_GROUP, column * LANES : (column + 1) * LANES
+                            ].astype(jnp.float32)
+
+    def low(value):
+        return value.astype(jnp.bfloat16).astype(jnp.float32)
+
+    rows = pl.ds(pl.multiple_of(step * block, SUBLANES), block)
+    grad, weight = own_flat[rows, :], anchor[...]
+    first_own, second_own = first[...], second[...]
+    clipped = grad * factors[0]
+    one[...] = beta_one * first_own + (1.0 - beta_one) * clipped
+    two[...] = beta_two * second_own + (1.0 - beta_two) * clipped * clipped
+    delta_own = delta_of(low(grad) * factors[0], low(first_own), low(second_own), weight)
+    delta_twin = delta_of(
+        twin_flat[rows, :] * factors[1],
+        twin_first[...].astype(jnp.float32),
+        twin_second[...].astype(jnp.float32),
+        weight,
+    )
+    mean = (delta_own + delta_twin) / 2
+    momentum = outer_mu * outer[...] + mean
+    mean_out[...] = mean
+    momentum_out[...] = momentum
+    new[...] = weight - outer_rate * (mean + outer_mu * momentum)
+
+
+def step_layers(factors, own, twin, views, shards):
+    rows = views[0].shape[0]
+    block = rows // STEP_BLOCKS
+    whole = pl.BlockSpec(memory_space=pltpu.VMEM)
+    part = pl.BlockSpec((block, LANES), lambda k: (k, 0))
+    return pl.pallas_call(
+        functools.partial(step_kernel, D // shards * (4 * D + FF) // LANES),
+        grid=(STEP_BLOCKS,),
+        out_shape=[jax.ShapeDtypeStruct((rows, LANES), jnp.float32)] * 5,
+        in_specs=[pl.BlockSpec(memory_space=pltpu.SMEM)] + [whole] * (4 * L) + [part] * 6,
+        out_specs=[part] * 5,
+        scratch_shapes=[pltpu.VMEM((rows, LANES), jnp.float32)] * 2,
+        compiler_params=pltpu.CompilerParams(
+            vmem_limit_bytes=VMEM_LIMIT, dimension_semantics=("arbitrary",)
+        ),
+        name="step_layers",
+    )(factors, *own, *twin, *views)
+
+
+def from_view(view):
+    rows, lanes = view.shape
+    return view.reshape(rows // L, L, lanes).transpose(1, 0, 2).reshape(L, rows // L * lanes)
+
+
+def swapped(value):
+    return lax.ppermute(value, "grp", [(0, 1), (1, 0)])
 
 
 def per_device(
@@ -534,6 +1167,8 @@
     seq_count = lax.axis_size("seq")
     group_count = lax.axis_size("grp")
     rank = lax.axis_index("seq")
+    group = lax.axis_index("grp")
+    close = seq_count == math.prod(GRID) and group_count == 2
     rows = latents.shape[0]
     channels = latents.shape[1]
     frames_group = rows * seq_count
@@ -544,9 +1179,22 @@
     item_count = lengths.shape[0]
     text_width = captions.shape[1]
     other_size = anchor_other.shape[0]
-    padded = -(-other_size // 2048) * 2048
+    padded = -(-other_size // 4096) * 4096
     other_rows = jnp.pad(anchor_other.astype(jnp.bfloat16), (0, padded - other_size))
-    other_rows = lax.all_gather(other_rows.reshape(-1, LANES), "seq", axis=0, tiled=True)
+    own_rows = lay_out(anchor_layers, seq_count)
+    early = 1
+    pieces = [other_rows.reshape(-1, GATHER_LANES)] + [rows for pair in own_rows[:early] for rows in pair]
+    other_rows, *early_rows = gather_pieces(pieces, [True] + [True, False] * early, 4)
+    if close:
+        first_view, second_view = flat_view(first_layers[0]), flat_view(second_layers[0])
+        sources, other_rows = lax.optimization_barrier(
+            ((first_view, second_view, first_other[0], second_other[0]), other_rows)
+        )
+        twin_views = [swapped(value.astype(jnp.bfloat16)) for value in sources[:2]]
+        twin_moments = [swapped(value.astype(jnp.bfloat16)).astype(jnp.float32) for value in sources[2:]]
+    late_rows = [lax.all_gather(rows, "seq", axis=0) for pair in own_rows[early:] for rows in pair]
+    layer_parts = [rows.reshape(-1, rows.shape[-1]) for rows in early_rows + late_rows]
+    gathered = [split_upper(*layer_parts[2 * depth : 2 * depth + 2]) for depth in range(L)]
     other_low = other_rows.reshape(seq_count, padded)[:, :other_size].reshape(-1)
     w_in, w_out, w_time, w_text, w_audio, w_caption, gains, null_text = carve(
         other_low, other_shapes(channels, D, text_width, E, L)
@@ -579,7 +1227,6 @@
     condition, pull_condition = jax.vjp(condition_of, w_time_f, w_text_f, null_f)
     hidden = dense(noisy_low, w_in) + exact(onehot, condition)
     saved_all = []
-    gathered = [gather_layer(anchor_layers[depth], seq_count) for depth in range(L)]
     for depth in range(L):
         weights = gathered[depth]
         hidden, saved = layer_forward(
@@ -607,6 +1254,8 @@
     unused, pull_final = jax.vjp(norm_rows, hidden, gains_f[2 * L])
     grad_hidden, grad_gain_final = pull_final(grad_final)
     layer_grads = [None] * L
+    own_grads = [None] * L
+    twin_grads = [None] * L
     gain_grads = [None] * (2 * L + 1)
     gain_grads[2 * L] = grad_gain_final
     for depth in reversed(range(L)):
@@ -616,8 +1265,12 @@
         )
         gain_grads[2 * depth] = grad_gain_one
         gain_grads[2 * depth + 1] = grad_gain_two
-        layer_grads[depth] = reduce_layer(operand_pairs, seq_count)
-    stacked = jnp.stack(layer_grads)
+        layer_grads[depth] = layer_gradients(operand_pairs)
+        if depth > 0 and close:
+            own_grads[depth] = [
+                lax.psum_scatter(grad, "seq", scatter_dimension=0, tiled=True)
+                for grad in layer_grads[depth]
+            ]
     grad_w_in = contract_rows(noisy_low.astype(jnp.float32), grad_hidden, HIGH)
     grad_condition = contract_rows(onehot, grad_hidden, HIGH)
     grad_w_in, grad_w_out, grad_condition, gain_rows = sum_over_seq(
@@ -638,20 +1291,62 @@
         ]
     )
     other_grad = lax.dynamic_slice_in_dim(other_flat, rank * other_size, other_size)
-    square_part = jnp.sum(stacked * stacked) + jnp.sum(other_grad * other_grad)
-    total_norm = jnp.sqrt(sum_scalar_over_seq(square_part, 3))
-    factor = jnp.minimum(1.0, clip_at / (total_norm + 1e-06))
-    first_l, second_l, delta_l = adam(
-        stacked * factor, first_layers[0], second_layers[0], anchor_layers
-    )
-    first_o, second_o, delta_o = adam(
-        other_grad * factor, first_other[0], second_other[0], anchor_other
-    )
-    mean_layers = group_mean(delta_l, group_count)
-    mean_other = group_mean(delta_o, group_count)
-    momentum_layers = outer_mu * outer_layers + mean_layers
+    other_grad_square = jnp.sum(other_grad * other_grad)
+    if close:
+        other_grad_low = other_grad.astype(jnp.bfloat16)
+        twin_other = swapped(other_grad_low).astype(jnp.float32)
+        own_grads[0], twin_grads[0], square_part = scatter_layer(*layer_grads[0], 5)
+        square_part = square_part + other_grad_square
+        for depth in range(1, L):
+            twin_grads[depth] = [swapped(grad) for grad in own_grads[depth]]
+            for grad in own_grads[depth]:
+                wide = grad.astype(jnp.float32)
+                square_part = square_part + jnp.sum(wide * wide)
+        norms = jnp.sqrt(sums_by_group(square_part, 3))
+        total_norm = lax.dynamic_index_in_dim(norms, group, keepdims=False)
+        twin_norm = lax.dynamic_index_in_dim(norms, 1 - group, keepdims=False)
+        factor = jnp.minimum(1.0, clip_at / (total_norm + 1e-06))
+        twin_factor = jnp.minimum(1.0, clip_at / (twin_norm + 1e-06))
+        views = [flat_view(anchor_layers), first_view, second_view, flat_view(outer_layers)]
+        stepped = step_layers(
+            jnp.stack([factor, twin_factor]),
+            [part for grads in own_grads for part in grads],
+            [part for grads in twin_grads for part in grads],
+            views + twin_views,
+            seq_count,
+        )
+        new_layers, first_l, second_l, mean_layers, momentum_layers = map(from_view, stepped)
+        first_o, second_o, _ = adam(other_grad * factor, first_other[0], second_other[0], anchor_other)
+
+        def low(value):
+            return lax.reduce_precision(value, 8, 7)
+
+        delta_o = delta_of(low(other_grad) * factor, low(first_other[0]), low(second_other[0]), anchor_other)
+        delta_twin = delta_of(twin_other * twin_factor, *twin_moments, anchor_other)
+        mean_other = (delta_o + delta_twin) / 2
+    else:
+        stacked = jnp.stack(
+            [
+                flatten(
+                    lax.psum_scatter(grad, "seq", scatter_dimension=0, tiled=True).astype(jnp.float32)
+                    for grad in grads
+                )
+                for grads in layer_grads
+            ]
+        )
+        total_norm = jnp.sqrt(lax.psum(jnp.sum(stacked * stacked) + other_grad_square, "seq"))
+        factor = jnp.minimum(1.0, clip_at / (total_norm + 1e-06))
+        first_l, second_l, delta_l = adam(
+            stacked * factor, first_layers[0], second_layers[0], anchor_layers
+        )
+        first_o, second_o, delta_o = adam(
+            other_grad * factor, first_other[0], second_other[0], anchor_other
+        )
+        mean_layers = group_mean(delta_l, group_count)
+        mean_other = group_mean(delta_o, group_count)
+        momentum_layers = outer_mu * outer_layers + mean_layers
+        new_layers = anchor_layers - outer_rate * (mean_layers + outer_mu * momentum_layers)
     momentum_other = outer_mu * outer_other + mean_other
-    new_layers = anchor_layers - outer_rate * (mean_layers + outer_mu * momentum_layers)
     new_other = anchor_other - outer_rate * (mean_other + outer_mu * momentum_other)
     return (
         new_layers,

time: 1030 us -> 857 us (0.83)
  waiting for transfers between devices: 398 us -> 91.7 us
  Pallas kernels: 139 us -> 384 us
  other arithmetic: 126 us -> 49.2 us
  local copies, waits for them, and re-layouts: 158 us -> 110 us
  starting transfers between devices: 49.2 us -> 73.2 us
    pallas_call x1 -> x5, Pallas kernels: 8.16 us -> 269 us  [the longest x1 128 us: gather_pieces(): pl.pallas_call(functools.partial(gather_kernel, tuple(shared)), out_shape...]
    all_gather x5 -> x2, waiting for transfers between devices: 158 us -> 0.04 us  [per_device(): lax.all_gather(rows, 'seq', axis=0)]
    reduce_scatter x4 -> x2, waiting for transfers between devices: 81.4 us -> 0.02 us  [per_device(): lax.psum_scatter(grad, 'seq', scatter_dimension=0, tiled=True)]
    slice x9 -> x1, local copies, waits for them, and re-layouts: 45 us -> 1.23 us  [sums_by_group(): return jnp.sum(shared[:, 0, 0].reshape(groups, count), axis=1)]
    ppermute x16, waiting for transfers between devices: 120 us -> 77.9 us  [passed_along(): lax.ppermute(value, axis, [(source, source + steps) for source in range(i...]
    convert_element_type x4, other arithmetic: 40.1 us -> 6.63 us  [the longest x2 5.19 us: per_device(): twin_views = [swapped(value.astype(jnp.bfloat16)) for value in sources[:2]]]
    ppermute x2 -> x7, waiting for transfers between devices: 38.8 us -> 13.7 us  [swapped(): return lax.ppermute(value, 'grp', [(0, 1), (1, 0)])]
    another operation x4 -> x3, other arithmetic: 26.6 us -> 5.66 us  [the longest x2 22.3 us: per_device(): stacked = jnp.stack(layer_grads)]
  transfers between devices with their start and end apart: 27 -> 27, of which waited for: 14 -> 6; matrix products, arithmetic and copies ran while one was open for 31% -> 31% of each run, Pallas kernels for 10% -> 42%
where the time goes in v3:
time: 857 us; the launch traced here: 849 us
  Pallas kernels  384 us (45%)
  matrix products  117 us (14%)
  local copies, waits for them, and re-layouts  110 us (13%)
  waiting for transfers between devices  91.7 us (11%)
  starting transfers between devices  73.2 us (9%)
  other arithmetic  49.2 us (6%)
  between operations  23.2 us (3%)
    pallas_call x1, Pallas kernels, gather_pieces(): pl.pallas_call(functools.partial(gather_kernel, tuple(shared)), out_shape...  128 us
    pallas_call x1, Pallas kernels, scatter_layer(): pl.pallas_call(functools.partial(scatter_kernel, tuple(pieces), 2), out_s...  105 us
    ppermute x16, waiting for transfers between devices, passed_along(): lax.ppermute(value, axis, [(source, source + steps) for source in range(i...  77.9 us
    ppermute x16, starting transfers between devices, passed_along(): lax.ppermute(value, axis, [(source, source + steps) for source in range(i...  64.4 us
    pallas_call x2, Pallas kernels, sum_over_seq(): pl.pallas_call(functools.partial(sum_kernel, count), out_shape=jax.ShapeD...  52.8 us
    unnamed x295, local copies, waits for them, and re-layouts  51.7 us
    dot_general x14, matrix products, contract_rows(): lax.dot_general(left, right, (((0,), (0,)), ((), ())), precision=precisio...  35.4 us
    pallas_call x2, Pallas kernels, attend_backward(): pl.pallas_call(attend_backward_kernel, out_shape=(jax.ShapeDtypeStruct((r...  33.9 us
  transfers between devices with their start and end apart: 27, of which 6 were waited for; matrix products, arithmetic and copies ran while one was open for 31% of the time, Pallas kernels for 42%

profile of v3, /device:TPU:0, one launch (start us, length us, event | category | flops | bytes accessed | tf_op | source)
XLA Modules:
  0.0 848.9 jit_solution(10803077516566154195)
XLA Ops:
  7.3 4.3 lay_out.1
  18.2 127.7 %gather_pieces.1 = (bf16[16,496,256]{2,1,0:T(8,128)(2,1)}, bf16[16,48,6144]{2,1,0:T(8,128)(2,1)}, bf16[16,192,768]{2,1,0:T(8,128)(2,1)}) custom-call(bf16[496,256]{1,0:T(8,128)(2,1)} %reshape.484.refs_0_, bf16[48,6144]{1,0:T(8,128)(2,1)} %copy-done.3, bf16[192,768]{1,0:T(8,128)(2,1)} %copy-done.4), custom_call_target="tpu_custom_call" | custom-call | tf_op jit(solution)/shard_map/gather_pieces/pallas_call | solution.py:731
  145.9 3.6 copy.67
  151.7 9.2 %reshape.548 = bf16[2001408]{0:T(1024)(128)(2,1)} reshape(bf16[16,125088]{1,0:T(8,128)(2,1)} %slice.199) | data formatting | bytes 8005632
  160.9 7.9 slice.154
  177.5 3.1 convolution_convert_fusion.7
  183.8 3.2 collective-permute-start.1
  190.2 39.4 %collective-permute-done = bf16[256,1536]{1,0:T(8,128)(2,1)} collective-permute-done((bf16[256,1536]{1,0:T(8,128)(2,1)}, bf16[256,1536]{1,0:T(8,128)(2,1)}, u32[]{:S(2)}, u32[]{:S(2)}) %collective-permute-start) | collective-permute-done | bytes 786464 | tf_op jit(solution)/shard_map/ppermute | solution.py:37
  236.5 14.1 %attend_forward.2 = (bf16[256,768]{1,0:T(8,128)(2,1)S(1)}, f32[16,256]{1,0:T(8,128)S(1)}) custom-call(bf16[256,768]{1,0:T(8,128)(2,1)S(1)} %slice.207.q_ref, bf16[1280,1536]{1,0:T(8,128)(2,1)} %copy-done.53, s32[1,256]{1,0:T(1,128)S(1)} %bitcast.114, s32[1280,1]{1,0:T(8,128)S(1)} %reshape_select_fusion.key_item_ref), custom_call_target="tpu_custom_call" | custom-call | flops 1006632960 | bytes 4718592 | tf_op jit(solution)/shard_map/attend_forward/pallas_call | solution.py:188
  252.8 4.6 fusion.6
  259.9 3.2 convolution_convert_fusion.6
  264.2 21.7 %collective-permute-start.4 = (bf16[256,1536]{1,0:T(8,128)(2,1)}, bf16[256,1536]{1,0:T(8,128)(2,1)}, u32[]{:S(2)}, u32[]{:S(2)}) collective-permute-start(bf16[256,1536]{1,0:T(8,128)(2,1)} %slice.215), channel_id=1, source_target_pairs={{0,2},{1,3},{2,4},{3,5},{4,6},{5,7},{6,8},{7,9},{8,10},{9,11},{10,... | collective-permute-start | bytes 2359304 | tf_op jit(solution)/shard_map/ppermute | solution.py:37
  290.1 7.4 slice.176
  299.4 3.8 convert_element_type.249
  304.6 2.5 multiply_reduce_fusion.22
  315.6 2.2 constant_dynamic-update-slice_fusion.7
  318.8 18.3 %collective-permute-done.7 = bf16[256,1536]{1,0:T(8,128)(2,1)S(1)} collective-permute-done((bf16[256,1536]{1,0:T(8,128)(2,1)}, bf16[256,1536]{1,0:T(8,128)(2,1)S(1)}, u32[]{:S(2)}, u32[]{:S(2)}) %collective-permute-start.7) | collective-permute-done | bytes 786464 | tf_op jit(solution)/shard_map/ppermute | solution.py:37
  338.1 14.2 %attend_forward.3 = (bf16[256,768]{1,0:T(8,128)(2,1)S(1)}, f32[16,256]{1,0:T(8,128)S(1)}) custom-call(bf16[256,768]{1,0:T(8,128)(2,1)S(1)} %slice.214.q_ref, bf16[1280,1536]{1,0:T(8,128)(2,1)} %constant_dynamic-update-slice_fusion.5.kv_ref, s32[1,256]{1,0:T(1,128)S(1)} %bitcast.115, s32[1280,1]{1,0:T(8,128)S(1)} %reshape_select_fusion.key_item_ref), custom_call_target="tpu_custom_call" | custom-call | flops 1006632960 | bytes 4718592 | tf_op jit(solution)/shard_map/attend_forward/pallas_call | solution.py:188
  355.0 3.3 fusion.2
  358.4 5.5 fusion.174
  371.4 14.6 %sum_over_seq.2 = f32[16,8,128]{2,1,0:T(8,128)} custom-call(f32[16,8,128]{2,1,0:T(8,128)} %fusion.83.x_ref), custom_call_target="tpu_custom_call" | custom-call | flops 16384 | bytes 262144 | tf_op jit(solution)/shard_map/sum_over_seq/pallas_call | solution.py:436
  398.0 2.4 multiply_reduce_fusion.18
  402.3 2.7 convolution_bitcast_fusion.1
  407.1 4.4 convolution_convert_fusion
  411.8 6.3 fusion.21
  418.2 4.8 multiply_reduce_fusion.2
  425.7 17.1 %attend_backward.2 = (bf16[256,768]{1,0:T(8,128)(2,1)S(1)}, bf16[1280,1536]{1,0:T(8,128)(2,1)}) custom-call(bf16[256,768]{1,0:T(8,128)(2,1)S(1)} %slice.214.q_ref, bf16[1280,1536]{1,0:T(8,128)(2,1)} %constant_dynamic-update-slice_fusion.5.kv_ref, bf16[256,768]{1,0:T(8,128)(2,1)S(1)} %convolution_convert_fusion.11.do_ref, ...), custom_call_target="tpu_custom_call" | custom-call | flops 2516582400 | bytes 9437184 | tf_op jit(solution)/shard_map/attend_backward/pallas_call | solution.py:245
  442.9 3.6 fusion.166
  446.4 2.9 collective-permute-start.10
  449.4 2.6 collective-permute-start.11
  455.3 2.7 convolution_bitcast_fusion
  457.9 3.1 copy.57
  461.0 3.1 copy.69
  468.3 2.8 convolution_convert_fusion.8
  471.1 5.0 convolution_convert_fusion.1
  476.1 19.9 %collective-permute-done.11 = bf16[256,1536]{1,0:T(8,128)(2,1)} collective-permute-done((bf16[256,1536]{1,0:T(8,128)(2,1)}, bf16[256,1536]{1,0:T(8,128)(2,1)}, u32[]{:S(2)}, u32[]{:S(2)}) %collective-permute-start.11) | collective-permute-done | bytes 786464 | tf_op jit(solution)/shard_map/ppermute | solution.py:37
  496.0 2.6 add_convert_fusion.1
  498.7 3.6 multiply_reduce_fusion.3
  504.3 3.2 fusion.14
  510.3 16.8 %attend_backward.3 = (bf16[256,768]{1,0:T(8,128)(2,1)S(1)}, bf16[1280,1536]{1,0:T(8,128)(2,1)}) custom-call(bf16[256,768]{1,0:T(8,128)(2,1)S(1)} %slice.207.q_ref, bf16[1280,1536]{1,0:T(8,128)(2,1)} %copy-done.53, bf16[256,768]{1,0:T(8,128)(2,1)S(1)} %convolution_convert_fusion.10.do_ref, f32[16,256]{1,0:T(8,128)S(1)} %get-tuple-element.55.lse_ref, ...), custom_call_target="tpu_custom_call" | custom-call | flops 2516582400 | bytes 9437184 | tf_op jit(solution)/shard_map/attend_backward/pallas_call | solution.py:245
  527.1 3.5 fusion.165
  533.3 14.3 %collective-permute-start.14 = (bf16[256,1536]{1,0:T(8,128)(2,1)}, bf16[256,1536]{1,0:T(8,128)(2,1)}, u32[]{:S(2)}, u32[]{:S(2)}) collective-permute-start(bf16[256,1536]{1,0:T(8,128)(2,1)} %get-tuple-element.113), channel_id=1, source_target_pairs={{0,1},{1,2},{2,3},{3,4},{4,5},{5,6},{6,7},{7,8},{8,9},{9,10},{10,1... | collective-permute-start | bytes 2359304 | tf_op jit(solution)/shard_map/ppermute | solution.py:37
  547.6 5.0 collective-permute-start.15
  554.2 2.4 copy.55
  556.6 2.5 convolution_convert_fusion.2
  559.1 8.2 pad_maximum_fusion.1
  568.4 5.2 convolution_convert_fusion.4
  573.6 4.5 convolution_convert_fusion.3
  581.9 3.0 add_convert_fusion
  585.0 3.7 multiply_reduce_fusion.6
  591.0 38.2 %sum_over_seq.3 = f32[16,24,128]{2,1,0:T(8,128)} custom-call(f32[16,24,128]{2,1,0:T(8,128)} %bitcast.135), custom_call_target="tpu_custom_call" | custom-call | flops 49152 | bytes 786432 | tf_op jit(solution)/shard_map/sum_over_seq/pallas_call | solution.py:436
  630.1 3.5 fusion.95
  633.6 3.5 fusion.97
  637.1 3.3 reshape.515
  640.4 3.3 reshape.514
  645.4 3.3 constant_dynamic-update-slice_fusion.15
  648.7 3.4 constant_dynamic-update-slice_fusion.14
  652.1 2.5 fusion.33
  664.5 4.0 pad_maximum_fusion
  668.5 105.2 %scatter_layer.1 = (f32[48,6144]{1,0:T(8,128)S(1)}, f32[192,768]{1,0:T(8,128)S(1)}, bf16[48,6144]{1,0:T(8,128)(2,1)S(1)}, bf16[192,768]{1,0:T(8,128)(2,1)S(1)}, f32[8,128]{1,0:T(8,128)S(1)}) custom-call(bf16[16,48,6144]{2,1,0:T(8,128)(2,1)} %bitcast.118, bf16[16,192,768]{2,1,0:T(8,128)(2,1)} %bitcast.131), custom_call_target="tpu_custom_call" | custom-call | tf_op jit(solution)/shard_map/scatter_layer/pallas_call | solution.py:1001
  784.2 9.6 %share_over_all.1 = f32[32,8,128]{2,1,0:T(8,128)} custom-call(f32[8,128]{1,0:T(8,128)} %broadcast_in_dim.166.x_ref), custom_call_target="tpu_custom_call" | custom-call | tf_op jit(solution)/shard_map/share_over_all/pallas_call | solution.py:501
  799.4 3.8 multiply_subtract_fusion
  807.4 11.8 %collective-permute-done.16.refs_6_ = bf16[48,6144]{1,0:T(8,128)(2,1)S(1)} collective-permute-done((bf16[48,6144]{1,0:T(8,128)(2,1)}, bf16[48,6144]{1,0:T(8,128)(2,1)S(1)}, u32[]{:S(2)}, u32[]{:S(2)}) %collective-permute-start.16) | collective-permute-done | bytes 589856 | tf_op jit(solution)/shard_map/ppermute | solution.py:1148
  819.2 21.9 %step_layers.1 = (f32[6912,128]{1,0:T(8,128)}, f32[6912,128]{1,0:T(8,128)}, f32[6912,128]{1,0:T(8,128)}, f32[6912,128]{1,0:T(8,128)}, f32[6912,128]{1,0:T(8,128)}) custom-call(f32[2]{0:T(128)S(1)} %pad_maximum_fusion.11.factors, f32[48,6144]{1,0:T(8,128)} %copy-done.1, f32[192,768]{1,0:T(8,128)S(1)} %get-tuple-element.60.refs_1_, ...), custom_call_target="tpu_custom_call" | custom-call | tf_op jit(solution)/shard_map/step_layers/pallas_call | solution.py:1128
  (481 shorter events, 133.0 us)
Async XLA Ops:
  7.2 252.7 %all-gather.5.cloned.1.call-start = ((), (), s32[]{:S(2)}) async-start(), calls=%async_computation.4 | async-start | bytes 10027008 | tf_op jit(solution)/shard_map/all_gather | solution.py:1195
  13.1 345.3 %all-gather.7.cloned.1.call-start = ((), (), s32[]{:S(2)}) async-start(), calls=%async_computation.5 | async-start | bytes 5013504 | tf_op jit(solution)/shard_map/all_gather | solution.py:1195
  169.8 82.9 %copy-start.56 = (f32[768]{0:T(1024)}, f32[768]{0:T(1024)S(1)}, u32[]{:S(2)}) copy-start(f32[768]{0:T(1024)S(1)} %get-tuple-element.88) | copy-start | bytes 9220
  169.9 90.0 %copy-start.58 = (f32[768]{0:T(1024)}, f32[768]{0:T(1024)S(1)}, u32[]{:S(2)}) copy-start(f32[768]{0:T(1024)S(1)} %get-tuple-element.87) | copy-start | bytes 9220
  169.9 184.5 %copy-start.60 = (f32[768]{0:T(1024)}, f32[768]{0:T(1024)S(1)}, u32[]{:S(2)}) copy-start(f32[768]{0:T(1024)S(1)} %get-tuple-element.86) | copy-start | bytes 9220
  169.9 196.0 %copy-start.64 = (f32[768]{0:T(1024)}, f32[768]{0:T(1024)S(1)}, u32[]{:S(2)}) copy-start(f32[768]{0:T(1024)S(1)} %get-tuple-element.85) | copy-start | bytes 9220
  181.6 48.0 %collective-permute-start = (bf16[256,1536]{1,0:T(8,128)(2,1)}, bf16[256,1536]{1,0:T(8,128)(2,1)}, u32[]{:S(2)}, u32[]{:S(2)}) collective-permute-start(bf16[256,1536]{1,0:T(8,128)(2,1)} %slice.208), channel_id=1, source_target_pairs={{0,2},{1,3},{2,4},{3,5},{4,6},{5,7},{6,8},{7,9},{8,10},{9,11},{10,... | collective-permute-start | bytes 2359304 | tf_op jit(solution)/shard_map/ppermute | solution.py:37
  183.8 46.9 %collective-permute-start.1 = (bf16[256,1536]{1,0:T(8,128)(2,1)}, bf16[256,1536]{1,0:T(8,128)(2,1)}, u32[]{:S(2)}, u32[]{:S(2)}) collective-permute-start(bf16[256,1536]{1,0:T(8,128)(2,1)} %slice.208), channel_id=1, source_target_pairs={{0,1},{1,2},{2,3},{3,4},{4,5},{5,6},{6,7},{7,8},{8,9},{9,10},{10,1... | collective-permute-start | bytes 2359304 | tf_op jit(solution)/shard_map/ppermute | solution.py:37
  187.0 45.0 %collective-permute-start.2 = (bf16[256,1536]{1,0:T(8,128)(2,1)}, bf16[256,1536]{1,0:T(8,128)(2,1)}, u32[]{:S(2)}, u32[]{:S(2)}) collective-permute-start(bf16[256,1536]{1,0:T(8,128)(2,1)} %slice.208), channel_id=1, source_target_pairs={{1,0},{2,1},{3,2},{4,3},{5,4},{6,5},{7,6},{8,7},{9,8},{10,9},{11,1... | collective-permute-start | bytes 2359304 | tf_op jit(solution)/shard_map/ppermute | solution.py:37
  188.3 45.2 %collective-permute-start.3 = (bf16[256,1536]{1,0:T(8,128)(2,1)}, bf16[256,1536]{1,0:T(8,128)(2,1)}, u32[]{:S(2)}, u32[]{:S(2)}) collective-permute-start(bf16[256,1536]{1,0:T(8,128)(2,1)} %slice.208), channel_id=1, source_target_pairs={{2,0},{3,1},{4,2},{5,3},{6,4},{7,5},{8,6},{9,7},{10,8},{11,9},{12,... | collective-permute-start | bytes 2359304 | tf_op jit(solution)/shard_map/ppermute | solution.py:37
  189.6 589.0 %reduce-scatter.5.cloned.1.call-start = ((), (), s32[]{:S(2)}) async-start(), calls=%async_computation.3 | async-start | bytes 5013504 | tf_op jit(solution)/shard_map/reduce_scatter | solution.py:1271
  259.9 26.0 %copy-start.26 = (f32[125088]{0:T(1024)S(1)}, f32[125088]{0:T(1024)}, u32[]{:S(2)}) copy-start(f32[125088]{0:T(1024)} %reduce) | copy-start | bytes 1501060
  263.1 26.9 %copy-start.30 = (bf16[256,2304]{1,0:T(8,128)(2,1)}, bf16[256,2304]{1,0:T(8,128)(2,1)S(1)}, u32[]{:S(2)}) copy-start(bf16[256,2304]{1,0:T(8,128)(2,1)S(1)} %convolution_convert_fusion.6) | copy-start | bytes 3538948
  264.2 47.3 %collective-permute-start.4 = (bf16[256,1536]{1,0:T(8,128)(2,1)}, bf16[256,1536]{1,0:T(8,128)(2,1)}, u32[]{:S(2)}, u32[]{:S(2)}) collective-permute-start(bf16[256,1536]{1,0:T(8,128)(2,1)} %slice.215), channel_id=1, source_target_pairs={{0,2},{1,3},{2,4},{3,5},{4,6},{5,7},{6,8},{7,9},{8,10},{9,11},{10,... | collective-permute-start | bytes 2359304 | tf_op jit(solution)/shard_map/ppermute | solution.py:37
  286.6 510.6 %collective-permute-start.20 = (bf16[125088]{0:T(1024)(128)(2,1)}, bf16[125088]{0:T(1024)(128)(2,1)}, u32[]{:S(2)}, u32[]{:S(2)}) collective-permute-start(bf16[125088]{0:T(1024)(128)(2,1)} %convert_element_type.251), channel_id=1, source_target_pairs={{0,16},{16,0},{1,17},{17,1},{2,18},{18,2},{3,19},{19,3},{4,20},{20... | collective-permute-start | bytes 750536 | tf_op jit(solution)/shard_map/ppermute | solution.py:1148
  287.4 26.2 %collective-permute-start.5 = (bf16[256,1536]{1,0:T(8,128)(2,1)}, bf16[256,1536]{1,0:T(8,128)(2,1)}, u32[]{:S(2)}, u32[]{:S(2)}) collective-permute-start(bf16[256,1536]{1,0:T(8,128)(2,1)} %slice.215), channel_id=1, source_target_pairs={{0,1},{1,2},{2,3},{3,4},{4,5},{5,6},{6,7},{7,8},{8,9},{9,10},{10,1... | collective-permute-start | bytes 2359304 | tf_op jit(solution)/shard_map/ppermute | solution.py:37
  304.6 50.5 %slice-start.6 = ((s8[9437184]{0:T(1024)(128)(4,1)}), s8[4194304]{0:T(1024)(128)(4,1)S(1)}, s32[]{:S(2)}) async-start(s8[9437184]{0:T(1024)(128)(4,1)} %bitcast.145), calls=%async_computation.12 | async-start | bytes 8388608
  307.6 10.3 %collective-permute-start.6 = (bf16[256,1536]{1,0:T(8,128)(2,1)}, bf16[256,1536]{1,0:T(8,128)(2,1)S(1)}, u32[]{:S(2)}, u32[]{:S(2)}) collective-permute-start(bf16[256,1536]{1,0:T(8,128)(2,1)} %slice.215), channel_id=1, source_target_pairs={{1,0},{2,1},{3,2},{4,3},{5,4},{6,5},{7,6},{8,7},{9,8},{10,9},{11,1... | collective-permute-start | bytes 2359304 | tf_op jit(solution)/shard_map/ppermute | solution.py:37
  308.9 28.2 %collective-permute-start.7 = (bf16[256,1536]{1,0:T(8,128)(2,1)}, bf16[256,1536]{1,0:T(8,128)(2,1)S(1)}, u32[]{:S(2)}, u32[]{:S(2)}) collective-permute-start(bf16[256,1536]{1,0:T(8,128)(2,1)} %slice.215), channel_id=1, source_target_pairs={{2,0},{3,1},{4,2},{5,3},{6,4},{7,5},{8,6},{9,7},{10,8},{11,9},{12,... | collective-permute-start | bytes 2359304 | tf_op jit(solution)/shard_map/ppermute | solution.py:37
  315.6 39.4 %slice-start.7 = ((s8[9437184]{0:T(1024)(128)(4,1)}), s8[4194304]{0:T(1024)(128)(4,1)S(1)}, s32[]{:S(2)}) async-start(s8[9437184]{0:T(1024)(128)(4,1)} %bitcast.145), calls=%async_computation.13 | async-start | bytes 8388608
  338.1 14.2 %copy-start.10 = (f32[256,768]{1,0:T(8,128)S(1)}, f32[256,768]{1,0:T(8,128)}, u32[]{:S(2)}) copy-start(f32[256,768]{1,0:T(8,128)} %copy-done.9) | copy-start | bytes 2359300
  338.1 17.0 %slice-start.8 = ((s8[9437184]{0:T(1024)(128)(4,1)}), s8[1048576]{0:T(1024)(128)(4,1)S(1)}, s32[]{:S(2)}) async-start(s8[9437184]{0:T(1024)(128)(4,1)} %bitcast.145), calls=%async_computation.14 | async-start | bytes 2097152
  392.4 12.5 %copy-start.6 = (f32[256,768]{1,0:T(8,128)S(1)}, f32[256,768]{1,0:T(8,128)}, u32[]{:S(2)}) copy-start(f32[256,768]{1,0:T(8,128)} %copy-done.5) | copy-start | bytes 2359300
  392.5 12.5 %copy-start.34 = (f32[256,768]{1,0:T(8,128)S(1)}, f32[256,768]{1,0:T(8,128)}, u32[]{:S(2)}) copy-start(f32[256,768]{1,0:T(8,128)} %fusion.119) | copy-start | bytes 2359300
  392.5 12.5 %copy-start.65 = (f32[768]{0:T(1024)S(1)}, f32[768]{0:T(1024)}, u32[]{:S(2)}) copy-start(f32[768]{0:T(1024)} %copy-done.64) | copy-start | bytes 9220
  392.5 12.5 %copy-start.68 = (f32[256]{0:T(256)S(1)}, f32[256]{0:T(256)}, u32[]{:S(2)}) copy-start(f32[256]{0:T(256)} %copy-done.67) | copy-start | bytes 3076
  392.5 12.5 %copy-start.78 = (f32[256]{0:T(256)S(1)}, f32[256]{0:T(256)}, u32[]{:S(2)}) copy-start(f32[256]{0:T(256)} %copy-done.77) | copy-start | bytes 3076
  411.5 368.7 %reduce-scatter.3.cloned.1.call-start = ((), (), s32[]{:S(2)}) async-start(), calls=%async_computation.2 | async-start | bytes 10027008 | tf_op jit(solution)/shard_map/reduce_scatter | solution.py:1271
  423.5 19.3 %copy-start.19 = (f32[256,768]{1,0:T(8,128)}, f32[256,768]{1,0:T(8,128)S(1)}, u32[]{:S(2)}) copy-start(f32[256,768]{1,0:T(8,128)S(1)} %add_add_fusion.8) | copy-start | bytes 2359300
  442.8 12.4 %copy-start.121 = (f32[12]{0:T(128)S(1)}, f32[12]{0:T(128)}, u32[]{:S(2)}) copy-start(f32[12]{0:T(128)} %get-tuple-element.83) | copy-start | bytes 148
  442.8 12.4 %copy-start.71 = (f32[12,512]{1,0:T(8,128)S(1)}, f32[12,512]{1,0:T(8,128)}, u32[]{:S(2)}) copy-start(f32[12,512]{1,0:T(8,128)} %get-tuple-element.142) | copy-start | bytes 73732
  442.8 12.4 %copy-start.72 = (f32[12,512]{1,0:T(8,128)S(1)}, f32[12,512]{1,0:T(8,128)}, u32[]{:S(2)}) copy-start(f32[12,512]{1,0:T(8,128)} %get-tuple-element.146) | copy-start | bytes 73732
  442.8 12.4 %copy-start.113 = (f32[12]{0:T(128)S(1)}, f32[12]{0:T(128)}, u32[]{:S(2)}) copy-start(f32[12]{0:T(128)} %add_rsqrt_fusion.1) | copy-start | bytes 148
  446.4 29.6 %collective-permute-start.10 = (bf16[256,1536]{1,0:T(8,128)(2,1)}, bf16[256,1536]{1,0:T(8,128)(2,1)}, u32[]{:S(2)}, u32[]{:S(2)}) collective-permute-start(bf16[256,1536]{1,0:T(8,128)(2,1)} %get-tuple-element.117), channel_id=1, source_target_pairs={{0,1},{1,2},{2,3},{3,4},{4,5},{5,6},{6,7},{7,8},{8,9},{9,10},{10,1... | collective-permute-start | bytes 2359304 | tf_op jit(solution)/shard_map/ppermute | solution.py:37
  449.4 46.7 %collective-permute-start.11 = (bf16[256,1536]{1,0:T(8,128)(2,1)}, bf16[256,1536]{1,0:T(8,128)(2,1)}, u32[]{:S(2)}, u32[]{:S(2)}) collective-permute-start(bf16[256,1536]{1,0:T(8,128)(2,1)} %get-tuple-element.116), channel_id=1, source_target_pairs={{0,2},{1,3},{2,4},{3,5},{4,6},{5,7},{6,8},{7,9},{8,10},{9,11},{10,... | collective-permute-start | bytes 2359304 | tf_op jit(solution)/shard_map/ppermute | solution.py:37
  452.0 44.1 %collective-permute-start.8 = (bf16[256,1536]{1,0:T(8,128)(2,1)}, bf16[256,1536]{1,0:T(8,128)(2,1)}, u32[]{:S(2)}, u32[]{:S(2)}) collective-permute-start(bf16[256,1536]{1,0:T(8,128)(2,1)} %get-tuple-element.115), channel_id=1, source_target_pairs={{2,0},{3,1},{4,2},{5,3},{6,4},{7,5},{8,6},{9,7},{10,8},{11,9},{12,... | collective-permute-start | bytes 2359304 | tf_op jit(solution)/shard_map/ppermute | solution.py:37
  453.2 42.8 %collective-permute-start.9 = (bf16[256,1536]{1,0:T(8,128)(2,1)}, bf16[256,1536]{1,0:T(8,128)(2,1)}, u32[]{:S(2)}, u32[]{:S(2)}) collective-permute-start(bf16[256,1536]{1,0:T(8,128)(2,1)} %get-tuple-element.118), channel_id=1, source_target_pairs={{1,0},{2,1},{3,2},{4,3},{5,4},{6,5},{7,6},{8,7},{9,8},{10,9},{11,1... | collective-permute-start | bytes 2359304 | tf_op jit(solution)/shard_map/ppermute | solution.py:37
  476.1 22.6 %copy-start.11 = (f32[256,768]{1,0:T(8,128)S(1)}, f32[256,768]{1,0:T(8,128)}, u32[]{:S(2)}) copy-start(f32[256,768]{1,0:T(8,128)} %copy-done.9) | copy-start | bytes 2359300
  476.1 22.6 %copy-start.59 = (f32[768]{0:T(1024)S(1)}, f32[768]{0:T(1024)}, u32[]{:S(2)}) copy-start(f32[768]{0:T(1024)} %copy-done.58) | copy-start | bytes 9220
  476.1 22.6 %copy-start.76 = (f32[256]{0:T(256)S(1)}, f32[256]{0:T(256)}, u32[]{:S(2)}) copy-start(f32[256]{0:T(256)} %copy-done.75) | copy-start | bytes 3076
  476.1 22.6 %copy-start.87 = (f32[256]{0:T(256)S(1)}, f32[256]{0:T(256)}, u32[]{:S(2)}) copy-start(f32[256]{0:T(256)} %copy-done.86) | copy-start | bytes 3076
  509.8 42.9 %copy-start.7 = (f32[256,768]{1,0:T(8,128)}, f32[256,768]{1,0:T(8,128)S(1)}, u32[]{:S(2)}) copy-start(f32[256,768]{1,0:T(8,128)S(1)} %add_add_fusion.6) | copy-start | bytes 2359300
  530.6 26.0 %copy-start.12 = (f32[256,768]{1,0:T(8,128)S(1)}, f32[256,768]{1,0:T(8,128)}, u32[]{:S(2)}) copy-start(f32[256,768]{1,0:T(8,128)} %copy-done.9) | copy-start | bytes 2359300
  530.6 47.5 %collective-permute-start.12 = (bf16[256,1536]{1,0:T(8,128)(2,1)}, bf16[256,1536]{1,0:T(8,128)(2,1)}, u32[]{:S(2)}, u32[]{:S(2)}) collective-permute-start(bf16[256,1536]{1,0:T(8,128)(2,1)} %get-tuple-element.111), channel_id=1, source_target_pairs={{2,0},{3,1},{4,2},{5,3},{6,4},{7,5},{8,6},{9,7},{10,8},{11,9},{12,... | collective-permute-start | bytes 2359304 | tf_op jit(solution)/shard_map/ppermute | solution.py:37
  532.0 47.9 %collective-permute-start.13 = (bf16[256,1536]{1,0:T(8,128)(2,1)}, bf16[256,1536]{1,0:T(8,128)(2,1)}, u32[]{:S(2)}, u32[]{:S(2)}) collective-permute-start(bf16[256,1536]{1,0:T(8,128)(2,1)} %get-tuple-element.114), channel_id=1, source_target_pairs={{1,0},{2,1},{3,2},{4,3},{5,4},{6,5},{7,6},{8,7},{9,8},{10,9},{11,1... | collective-permute-start | bytes 2359304 | tf_op jit(solution)/shard_map/ppermute | solution.py:37
  533.3 46.9 %collective-permute-start.14 = (bf16[256,1536]{1,0:T(8,128)(2,1)}, bf16[256,1536]{1,0:T(8,128)(2,1)}, u32[]{:S(2)}, u32[]{:S(2)}) collective-permute-start(bf16[256,1536]{1,0:T(8,128)(2,1)} %get-tuple-element.113), channel_id=1, source_target_pairs={{0,1},{1,2},{2,3},{3,4},{4,5},{5,6},{6,7},{7,8},{8,9},{9,10},{10,1... | collective-permute-start | bytes 2359304 | tf_op jit(solution)/shard_map/ppermute | solution.py:37
  547.6 34.3 %collective-permute-start.15 = (bf16[256,1536]{1,0:T(8,128)(2,1)}, bf16[256,1536]{1,0:T(8,128)(2,1)}, u32[]{:S(2)}, u32[]{:S(2)}) collective-permute-start(bf16[256,1536]{1,0:T(8,128)(2,1)} %get-tuple-element.112), channel_id=1, source_target_pairs={{0,2},{1,3},{2,4},{3,5},{4,6},{5,7},{6,8},{7,9},{8,10},{9,11},{10,... | collective-permute-start | bytes 2359304 | tf_op jit(solution)/shard_map/ppermute | solution.py:37
  578.1 220.6 %collective-permute-start.22 = (bf16[125088]{0:T(1024)(128)(2,1)}, bf16[125088]{0:T(1024)(128)(2,1)}, u32[]{:S(2)}, u32[]{:S(2)}) collective-permute-start(bf16[125088]{0:T(1024)(128)(2,1)} %convert_element_type.255), channel_id=1, source_target_pairs={{0,16},{16,0},{1,17},{17,1},{2,18},{18,2},{3,19},{19,3},{4,20},{20... | collective-permute-start | bytes 750536 | tf_op jit(solution)/shard_map/ppermute | solution.py:1148
  579.9 225.6 %collective-permute-start.18 = (bf16[6912,128]{1,0:T(8,128)(2,1)}, bf16[6912,128]{1,0:T(8,128)(2,1)}, u32[]{:S(2)}, u32[]{:S(2)}) collective-permute-start(bf16[6912,128]{1,0:T(8,128)(2,1)} %convert_element_type.249), channel_id=1, source_target_pairs={{0,16},{16,0},{1,17},{17,1},{2,18},{18,2},{3,19},{19,3},{4,20},{20... | collective-permute-start | bytes 5308424 | tf_op jit(solution)/shard_map/ppermute | solution.py:1148
  580.2 225.2 %collective-permute-start.19 = (bf16[6912,128]{1,0:T(8,128)(2,1)}, bf16[6912,128]{1,0:T(8,128)(2,1)}, u32[]{:S(2)}, u32[]{:S(2)}) collective-permute-start(bf16[6912,128]{1,0:T(8,128)(2,1)} %convert_element_type.250), channel_id=1, source_target_pairs={{0,16},{16,0},{1,17},{17,1},{2,18},{18,2},{3,19},{19,3},{4,20},{20... | collective-permute-start | bytes 5308424 | tf_op jit(solution)/shard_map/ppermute | solution.py:1148
  588.8 41.3 %copy-start.70 = (f32[768]{0:T(1024)S(1)}, f32[768]{0:T(1024)}, u32[]{:S(2)}) copy-start(f32[768]{0:T(1024)} %copy-done.69) | copy-start | bytes 9220
  588.8 41.3 %copy-start.111 = (pred[12]{0:T(512)(128)(4,1)S(1)}, pred[12]{0:T(512)(128)(4,1)}, u32[]{:S(2)}) copy-start(pred[12]{0:T(512)(128)(4,1)} %copy-done.110) | copy-start | bytes 40
  589.2 44.5 %copy-start.50 = (f32[12,384]{1,0:T(8,128)S(1)}, f32[12,384]{1,0:T(8,128)}, u32[]{:S(2)}) copy-start(f32[12,384]{1,0:T(8,128)} %copy-done.49) | copy-start | bytes 55300
  589.2 44.5 %copy-start.52 = (f32[12,384]{1,0:T(8,128)S(1)}, f32[12,384]{1,0:T(8,128)}, u32[]{:S(2)}) copy-start(f32[12,384]{1,0:T(8,128)} %copy-done.51) | copy-start | bytes 55300
  652.1 12.4 %slice-start.1 = ((s8[4718592]{0:T(1024)(128)(4,1)}), s8[4194304]{0:T(1024)(128)(4,1)S(1)}, s32[]{:S(2)}) async-start(s8[4718592]{0:T(1024)(128)(4,1)} %bitcast.119), calls=%async_computation.7 | async-start | bytes 8388608
  661.7 137.6 %collective-permute-start.21 = (bf16[125088]{0:T(1024)(128)(2,1)}, bf16[125088]{0:T(1024)(128)(2,1)}, u32[]{:S(2)}, u32[]{:S(2)}) collective-permute-start(bf16[125088]{0:T(1024)(128)(2,1)} %dynamic_slice.18), channel_id=1, source_target_pairs={{0,16},{16,0},{1,17},{17,1},{2,18},{18,2},{3,19},{19,3},{4,20},{20... | collective-permute-start | bytes 750536 | tf_op jit(solution)/shard_map/ppermute | solution.py:1148
  668.5 130.8 %copy-start.27 = (f32[125088]{0:T(1024)S(1)}, f32[125088]{0:T(1024)}, u32[]{:S(2)}) copy-start(f32[125088]{0:T(1024)} %reduce) | copy-start | bytes 1501060
  668.5 130.8 %copy-start.29 = (f32[125088]{0:T(1024)S(1)}, f32[125088]{0:T(1024)}, u32[]{:S(2)}) copy-start(f32[125088]{0:T(1024)} %reduce.1) | copy-start | bytes 1501060
  668.5 130.8 %copy-start.38 = (f32[125088]{0:T(1024)S(1)}, f32[125088]{0:T(1024)}, u32[]{:S(2)}) copy-start(f32[125088]{0:T(1024)} %param.15) | copy-start | bytes 1501060
  668.5 130.8 %copy-start.44 = (f32[125088]{0:T(1024)S(1)}, f32[125088]{0:T(1024)}, u32[]{:S(2)}) copy-start(f32[125088]{0:T(1024)} %param.21) | copy-start | bytes 1501060
  797.2 10.1 %collective-permute-start.17 = (bf16[192,768]{1,0:T(8,128)(2,1)}, bf16[192,768]{1,0:T(8,128)(2,1)S(1)}, u32[]{:S(2)}, u32[]{:S(2)}) collective-permute-start(bf16[192,768]{1,0:T(8,128)(2,1)} %reduce-scatter.5.cloned.1.call-done.refs_3_), channel_id=1, source_target_pairs={{0,16},{16,0},{1,17},{17,1},{2,18},{18,2},{3,19},{19,3},{4,20},{20... | collective-permute-start | bytes 884744 | tf_op jit(solution)/shard_map/ppermute | solution.py:1148
  798.7 20.4 %collective-permute-start.16 = (bf16[48,6144]{1,0:T(8,128)(2,1)}, bf16[48,6144]{1,0:T(8,128)(2,1)S(1)}, u32[]{:S(2)}, u32[]{:S(2)}) collective-permute-start(bf16[48,6144]{1,0:T(8,128)(2,1)} %reduce-scatter.3.cloned.1.call-done.refs_2_), channel_id=1, source_target_pairs={{0,16},{16,0},{1,17},{17,1},{2,18},{18,2},{3,19},{19,3},{4,20},{20... | collective-permute-start | bytes 1769480 | tf_op jit(solution)/shard_map/ppermute | solution.py:1148
  799.3 19.8 %copy-start = (bf16[48,6144]{1,0:T(8,128)(2,1)S(1)}, bf16[48,6144]{1,0:T(8,128)(2,1)}, u32[]{:S(2)}) copy-start(bf16[48,6144]{1,0:T(8,128)(2,1)} %reduce-scatter.3.cloned.1.call-done.refs_2_) | copy-start | bytes 1769476
  799.4 19.8 %copy-start.2 = (bf16[192,768]{1,0:T(8,128)(2,1)S(1)}, bf16[192,768]{1,0:T(8,128)(2,1)}, u32[]{:S(2)}) copy-start(bf16[192,768]{1,0:T(8,128)(2,1)} %reduce-scatter.5.cloned.1.call-done.refs_3_) | copy-start | bytes 884740
  (102 other events, 478.6 us)
Sparse Core Ops, SparseCore 0:
  13.2 119.4 all-gather.4
  189.7 69.7 all-gather.6
  411.6 103.6 reduce-scatter.4
  567.4 126.3 reduce-scatter.2

commit v4 on v3

--- a/solution.py
+++ b/solution.py
@@ -31,10 +31,20 @@
 contrast_weight = 0.05
 
 
-def passed_along(value, axis, steps):
+def block_of(rank, close):
+    if not close:
+        return rank
+    turn = (rank // 4) % 2
+    return rank + 2 * turn * (1 - 2 * ((rank // 2) % 2))
+
+
+def passed_along(value, axis, steps, close):
     count = lax.axis_size(axis)
+    holder = {block_of(rank, close): rank for rank in range(count)}
     initial, last = (max(0, -steps), min(count, count - steps))
-    return lax.ppermute(value, axis, [(source, source + steps) for source in range(initial, last)])
+    return lax.ppermute(
+        value, axis, [(holder[source], holder[source + steps]) for source in range(initial, last)]
+    )
 
 
 def dense(left, right):
@@ -128,18 +138,18 @@
     return 0.5 * (jnp.mean(row_terms) + jnp.mean(column_terms))
 
 
-def gather_window(local_pairs):
+def gather_window(local_pairs, close):
     pieces = {}
     for step in (2, 1, -1, -2):
-        pieces[step] = passed_along(local_pairs, "seq", step)
+        pieces[step] = passed_along(local_pairs, "seq", step, close)
     return jnp.concatenate([pieces[2], pieces[1], local_pairs, pieces[-1], pieces[-2]], axis=0)
 
 
-def return_window(grad_window, rows):
+def return_window(grad_window, rows, close):
     total = grad_window[2 * rows : 3 * rows].astype(jnp.float32)
     for slot, step in ((0, 2), (1, 1), (3, -1), (4, -2)):
         total = total + passed_along(
-            grad_window[slot * rows : (slot + 1) * rows], "seq", -step
+            grad_window[slot * rows : (slot + 1) * rows], "seq", -step, close
         ).astype(jnp.float32)
     return total
 
@@ -261,39 +271,22 @@
     )(queries, window, grad_out, lse, query_item[None, :], key_item[:, None])
 
 
-def layer_forward(hidden, weights, gain_one, gain_two, items):
+def layer_forward(hidden, normed, queries, window, weights, gain_two, items):
     proj_qkv, proj_out, proj_up, proj_down = weights
-    width = proj_out.shape[0]
-    normed = norm_rows(hidden, gain_one).astype(jnp.bfloat16)
-    projected = dense(normed, proj_qkv).astype(jnp.bfloat16)
-    window = gather_window(projected[:, width:])
-    attended, lse = attend_forward(projected[:, :width], window, *items)
+    attended, lse = attend_forward(queries, window, *items)
     middle = hidden + dense(attended, proj_out)
     second = norm_rows(middle, gain_two).astype(jnp.bfloat16)
     upper = dense(second, proj_up)
     activated = jax.nn.gelu(upper, approximate=True).astype(jnp.bfloat16)
     return (
         middle + dense(activated, proj_down),
-        (
-            hidden,
-            normed,
-            projected,
-            window,
-            lse,
-            attended,
-            middle,
-            second,
-            upper,
-            activated,
-        ),
-    )
-
-
-def layer_backward(grad_hidden, weights, gain_one, gain_two, items, saved):
-    hidden, normed, projected, window, lse, attended, middle, second, upper, activated = saved
+        (normed, queries, window, lse, attended, middle, second, upper, activated),
+    )
+
+
+def layer_backward(grad_hidden, weights, gain_two, items, saved):
+    normed, queries, window, lse, attended, middle, second, upper, activated = saved
     proj_qkv, proj_out, proj_up, proj_down = weights
-    width = proj_out.shape[0]
-    rows = hidden.shape[0]
     branch_top = grad_hidden.astype(jnp.bfloat16)
     grad_activated = against_rows(branch_top, proj_down)
     unused, pull_gelu = jax.vjp(lambda value: jax.nn.gelu(value, approximate=True), upper)
@@ -304,42 +297,58 @@
     grad_middle = grad_middle + grad_hidden
     branch_mid = grad_middle.astype(jnp.bfloat16)
     grad_attended = against_rows(branch_mid, proj_out).astype(jnp.bfloat16)
-    grad_query, grad_window = attend_backward(
-        projected[:, :width], window, grad_attended, lse, *items
-    )
-    grad_pairs = return_window(grad_window, rows)
-    grad_query = grad_query.astype(jnp.float32)
-    grad_projected = jnp.concatenate([grad_query, grad_pairs], axis=1).astype(jnp.bfloat16)
-    grad_normed = against_rows(grad_projected, proj_qkv)
-    unused, pull_one = jax.vjp(norm_rows, hidden, gain_one)
-    grad_input, grad_gain_one = pull_one(grad_normed)
-    operand_pairs = (
-        normed,
-        grad_projected,
-        attended,
-        branch_mid,
-        second,
-        grad_upper,
-        activated,
-        branch_top,
-    )
-    return (grad_middle + grad_input, operand_pairs, grad_gain_one, grad_gain_two)
-
-
-def layer_gradients(operand_pairs):
-    normed, grad_projected, attended, branch_mid, second, grad_upper, activated, branch_top = (
-        operand_pairs
-    )
+    grad_query, grad_window = attend_backward(queries, window, grad_attended, lse, *items)
+    operand_pairs = (attended, branch_mid, second, grad_upper, activated, branch_top)
+    return grad_middle, grad_query, grad_window, operand_pairs, grad_gain_two
+
+
+def layer_gradients(qkv_parts, operand_pairs):
+    attended, branch_mid, second, grad_upper, activated, branch_top = operand_pairs
+    pairs = qkv_parts + [(attended, branch_mid), (second, grad_upper)]
     upper_full = jnp.concatenate(
-        [
-            contract_rows(normed, grad_projected).astype(jnp.bfloat16),
-            contract_rows(attended, branch_mid).astype(jnp.bfloat16),
-            contract_rows(second, grad_upper).astype(jnp.bfloat16),
-        ],
-        axis=1,
+        [contract_rows(left, right).astype(jnp.bfloat16) for left, right in pairs], axis=1
     )
     lower_full = contract_rows(activated, branch_top).astype(jnp.bfloat16)
     return upper_full, lower_full
+
+
+def frame_window(frames, gathered_frames, own_block, close):
+    if close:
+        count = gathered_frames.shape[0]
+        parts = [
+            lax.dynamic_index_in_dim(
+                gathered_frames, jnp.clip(own_block + step, 0, count - 1), keepdims=False
+            )
+            for step in range(-2, 3)
+        ]
+    else:
+        parts = [passed_along(frames, "seq", -step, close) for step in range(-2, 0)] + [frames]
+        parts += [passed_along(frames, "seq", -step, close) for step in range(1, 3)]
+    return jnp.concatenate(parts, axis=1)
+
+
+def thirds_left(value):
+    items = value.shape[0]
+    thirds = value.reshape(items, -1, 3)
+    zero = jnp.zeros_like(thirds[:, :, 0])
+    even = jnp.concatenate([thirds[:, :, 0], thirds[:, :, 1], zero, zero], axis=0)
+    odd = jnp.concatenate([zero, zero, thirds[:, :, 1], thirds[:, :, 2]], axis=0)
+    return jnp.stack([even, odd], axis=2).reshape(4 * items, -1)
+
+
+def thirds_right(value):
+    half = value.shape[1] // 2
+    wide = jnp.zeros_like(value)
+    narrow = wide[:, :half]
+    return jnp.concatenate(
+        [
+            jnp.concatenate([value, narrow], axis=1),
+            jnp.concatenate([wide, value[:, :half]], axis=1),
+            jnp.concatenate([value[:, half:], wide], axis=1),
+            jnp.concatenate([narrow, value], axis=1),
+        ],
+        axis=0,
+    )
 
 
 def adam(grad, first, second, anchor):
@@ -1182,9 +1191,14 @@
     padded = -(-other_size // 4096) * 4096
     other_rows = jnp.pad(anchor_other.astype(jnp.bfloat16), (0, padded - other_size))
     own_rows = lay_out(anchor_layers, seq_count)
-    early = 1
-    pieces = [other_rows.reshape(-1, GATHER_LANES)] + [rows for pair in own_rows[:early] for rows in pair]
-    other_rows, *early_rows = gather_pieces(pieces, [True] + [True, False] * early, 4)
+    early = L
+    own_block = block_of(rank, close)
+    frames = jnp.concatenate([latents, noise], axis=1).T
+    pieces = [frames, other_rows.reshape(-1, GATHER_LANES)]
+    pieces += [part for pair in own_rows[:early] for part in pair]
+    gathered_frames, other_rows, *early_rows = gather_pieces(
+        pieces, [False, True] + [True, False] * early, 4
+    )
     if close:
         first_view, second_view = flat_view(first_layers[0]), flat_view(second_layers[0])
         sources, other_rows = lax.optimization_barrier(
@@ -1192,8 +1206,8 @@
         )
         twin_views = [swapped(value.astype(jnp.bfloat16)) for value in sources[:2]]
         twin_moments = [swapped(value.astype(jnp.bfloat16)).astype(jnp.float32) for value in sources[2:]]
-    late_rows = [lax.all_gather(rows, "seq", axis=0) for pair in own_rows[early:] for rows in pair]
-    layer_parts = [rows.reshape(-1, rows.shape[-1]) for rows in early_rows + late_rows]
+    late_rows = [lax.all_gather(part, "seq", axis=0) for pair in own_rows[early:] for part in pair]
+    layer_parts = [part.reshape(-1, part.shape[-1]) for part in early_rows + late_rows]
     gathered = [split_upper(*layer_parts[2 * depth : 2 * depth + 2]) for depth in range(L)]
     other_low = other_rows.reshape(seq_count, padded)[:, :other_size].reshape(-1)
     w_in, w_out, w_time, w_text, w_audio, w_caption, gains, null_text = carve(
@@ -1205,32 +1219,50 @@
     w_caption_f = w_caption.astype(jnp.float32)
     gains_f = gains.astype(jnp.float32)
     null_f = null_text.astype(jnp.float32)
-    places = rank * rows + jnp.arange(rows, dtype=jnp.int32)
+    places = own_block * rows + jnp.arange(rows, dtype=jnp.int32)
     order = jnp.arange(item_count, dtype=jnp.int32)
     ends = jnp.sum(jnp.where(order[None, :] <= order[:, None], lengths[None, :], 0), axis=1)
     item = jnp.sum((places[:, None] >= ends[None, :]).astype(jnp.int32), axis=1)
-    onehot = (item[:, None] == jnp.arange(item_count, dtype=jnp.int32)[None, :]).astype(jnp.float32)
-    key_places = rank * rows + jnp.arange(-2 * rows, 3 * rows, dtype=jnp.int32)
+    key_places = own_block * rows + jnp.arange(-2 * rows, 3 * rows, dtype=jnp.int32)
     key_item = jnp.sum((key_places[:, None] >= ends[None, :]).astype(jnp.int32), axis=1)
     key_item = jnp.where((key_places >= 0) & (key_places < frames_group), key_item, -1)
     items = (item, key_item)
+    window_hot = (key_item[:, None] == jnp.arange(item_count, dtype=jnp.int32)[None, :]).astype(
+        jnp.float32
+    )
+    inner = slice(2 * rows, 3 * rows)
+    onehot = window_hot[inner]
     lengths_f = lengths[:, None].astype(jnp.float32)
     alpha_bar = plan(timesteps)
-    mixing = exact(onehot, jnp.stack([jnp.sqrt(alpha_bar), jnp.sqrt(1.0 - alpha_bar)], axis=1))
-    noisy_low = (mixing[:, 0:1] * latents + mixing[:, 1:2] * noise).astype(jnp.bfloat16)
+    mixing = exact(window_hot, jnp.stack([jnp.sqrt(alpha_bar), jnp.sqrt(1.0 - alpha_bar)], axis=1))
+    near = frame_window(frames, gathered_frames, own_block, close).T
+    noise = near[inner, channels:]
+    noisy_low = (mixing[:, 0:1] * near[:, :channels] + mixing[:, 1:2] * near[:, channels:]).astype(
+        jnp.bfloat16
+    )
     features = time_features(timesteps)
 
-    def condition_of(time_weight, text_weight, null_vector):
-        text = jnp.where(null_flags[:, None] == 1, null_vector[None, :], captions)
-        return jax.nn.silu(exact(features, time_weight) + exact(text, text_weight))
-
-    condition, pull_condition = jax.vjp(condition_of, w_time_f, w_text_f, null_f)
-    hidden = dense(noisy_low, w_in) + exact(onehot, condition)
+    text = jnp.where(null_flags[:, None] == 1, null_f[None, :], captions)
+    before_silu = exact(features, w_time_f) + exact(text, w_text_f)
+    condition, pull_silu = jax.vjp(jax.nn.silu, before_silu)
+    hidden_window = dense(noisy_low, w_in) + exact(window_hot, condition)
     saved_all = []
+    entering = []
     for depth in range(L):
         weights = gathered[depth]
+        proj_qkv = weights[0]
+        if depth == 0:
+            normed_window = norm_rows(hidden_window, gains_f[0]).astype(jnp.bfloat16)
+            hidden, normed = hidden_window[inner], normed_window[inner]
+            queries = dense(normed, proj_qkv[:, :D]).astype(jnp.bfloat16)
+            window = dense(normed_window, proj_qkv[:, D:]).astype(jnp.bfloat16)
+        else:
+            normed = norm_rows(hidden, gains_f[2 * depth]).astype(jnp.bfloat16)
+            window = gather_window(dense(normed, proj_qkv[:, D:]).astype(jnp.bfloat16), close)
+            queries = dense(normed, proj_qkv[:, :D]).astype(jnp.bfloat16)
+        entering.append(hidden)
         hidden, saved = layer_forward(
-            hidden, weights, gains_f[2 * depth], gains_f[2 * depth + 1], items
+            hidden, normed, queries, window, weights, gains_f[2 * depth + 1], items
         )
         saved_all.append(saved)
     final = norm_rows(hidden, gains_f[2 * L])
@@ -1247,8 +1279,6 @@
     grad_audio_side, grad_text_side = pull_clash(jnp.float32(contrast_weight))
     grad_pred = (2.0 / (frames_group * channels) * error).astype(jnp.bfloat16)
     grad_w_out = contract_rows(grad_pred, final_low)
-    grad_w_audio = contract_rows(pooled, grad_audio_side, HIGH)
-    grad_w_caption = contract_rows(captions, grad_text_side, HIGH)
     grad_pooled = against_rows(grad_audio_side, w_audio_f, HIGH) / lengths_f
     grad_final = against_rows(grad_pred, w_out) + exact(onehot, grad_pooled)
     unused, pull_final = jax.vjp(norm_rows, hidden, gains_f[2 * L])
@@ -1260,37 +1290,89 @@
     gain_grads[2 * L] = grad_gain_final
     for depth in reversed(range(L)):
         weights = gathered[depth]
-        grad_hidden, operand_pairs, grad_gain_one, grad_gain_two = layer_backward(
-            grad_hidden, weights, gains_f[2 * depth], gains_f[2 * depth + 1], items, saved_all[depth]
-        )
-        gain_grads[2 * depth] = grad_gain_one
-        gain_grads[2 * depth + 1] = grad_gain_two
-        layer_grads[depth] = layer_gradients(operand_pairs)
+        proj_qkv = weights[0]
+        grad_middle, grad_query, grad_pairs, operand_pairs, gain_grads[2 * depth + 1] = layer_backward(
+            grad_hidden, weights, gains_f[2 * depth + 1], items, saved_all[depth]
+        )
+        normed = saved_all[depth][0]
+        if depth == 0:
+            qkv_parts = [(normed, grad_query), (normed_window, grad_pairs)]
+            grad_normed = against_rows(grad_pairs, proj_qkv[:, D:])
+            grad_own = grad_normed[inner] + against_rows(grad_query, proj_qkv[:, :D])
+            grad_normed = jnp.concatenate(
+                [grad_normed[: 2 * rows], grad_own, grad_normed[3 * rows :]], axis=0
+            )
+            unused, pull_one = jax.vjp(norm_rows, hidden_window, gains_f[0])
+        else:
+            grad_pairs = return_window(grad_pairs, rows, close).astype(jnp.bfloat16)
+            grad_projected = jnp.concatenate([grad_query, grad_pairs], axis=1)
+            qkv_parts = [(normed, grad_projected)]
+            grad_normed = against_rows(grad_projected, proj_qkv)
+            unused, pull_one = jax.vjp(norm_rows, entering[depth], gains_f[2 * depth])
+        grad_input, gain_grads[2 * depth] = pull_one(grad_normed)
+        layer_grads[depth] = layer_gradients(qkv_parts, operand_pairs)
+        if depth > 0:
+            grad_hidden = grad_middle + grad_input
+            if close:
+                grad_hidden, layer_grads[depth] = lax.optimization_barrier(
+                    (grad_hidden, layer_grads[depth])
+                )
+        else:
+            grad_hidden = jnp.concatenate(
+                [grad_input[: 2 * rows], grad_input[inner] + grad_middle, grad_input[3 * rows :]], axis=0
+            )
         if depth > 0 and close:
             own_grads[depth] = [
                 lax.psum_scatter(grad, "seq", scatter_dimension=0, tiled=True)
                 for grad in layer_grads[depth]
             ]
     grad_w_in = contract_rows(noisy_low.astype(jnp.float32), grad_hidden, HIGH)
-    grad_condition = contract_rows(onehot, grad_hidden, HIGH)
+    grad_condition = contract_rows(window_hot, grad_hidden, HIGH)
     grad_w_in, grad_w_out, grad_condition, gain_rows = sum_over_seq(
         (grad_w_in, grad_w_out, grad_condition, jnp.stack(gain_grads)), 2
     )
-    grad_w_out = grad_w_out.T
-    grad_w_time, grad_w_text, grad_null = pull_condition(grad_condition)
-    other_flat = jnp.concatenate(
+    grad_before = pull_silu(grad_condition)[0]
+    grad_null = jnp.sum(
+        jnp.where(null_flags[:, None] == 1, against_rows(grad_before, w_text_f, HIGH), 0.0), axis=0
+    )
+    straight = jnp.concatenate([grad_w_in, grad_w_out.T.reshape(channels, D), gain_rows, grad_null[None]])
+    lead = 2 * channels
+    identity = jnp.eye(straight.shape[0], dtype=jnp.float32)
+    features_at, text_at = lead, lead + D
+    audio_at = text_at + text_width
+    caption_at = audio_at + D * E // D
+    gains_at = caption_at + text_width * E // D
+    view_rows = gains_at + gain_rows.shape[0] + 1
+
+    def placed_left(value, start):
+        return jnp.pad(value, ((0, 0), (start, view_rows - start - value.shape[1])))
+
+    left = jnp.concatenate(
         [
-            grad_w_in.ravel(),
-            grad_w_out.ravel(),
-            grad_w_time.ravel(),
-            grad_w_text.ravel(),
-            grad_w_audio.ravel(),
-            grad_w_caption.ravel(),
-            gain_rows.ravel(),
-            grad_null,
-        ]
-    )
-    other_grad = lax.dynamic_slice_in_dim(other_flat, rank * other_size, other_size)
+            placed_left(identity[:, :lead], 0) + placed_left(identity[:, lead:], gains_at),
+            placed_left(features, features_at),
+            placed_left(text, text_at),
+            placed_left(thirds_left(pooled), audio_at),
+            placed_left(thirds_left(captions), caption_at),
+        ],
+        axis=0,
+    )
+    right = jnp.concatenate(
+        [
+            straight,
+            grad_before,
+            grad_before,
+            thirds_right(grad_audio_side),
+            thirds_right(grad_text_side),
+        ],
+        axis=0,
+    )
+    own_rows_count = -(-other_size // D) + 1
+    left = jnp.pad(left, ((0, 0), (0, own_rows_count)))
+    own_start = rank * other_size
+    own_left = lax.dynamic_slice_in_dim(left, own_start // D, own_rows_count, axis=1)
+    own_view = contract_rows(own_left, right, HIGH)
+    other_grad = lax.dynamic_slice_in_dim(own_view.reshape(-1), own_start % D, other_size)
     other_grad_square = jnp.sum(other_grad * other_grad)
     if close:
         other_grad_low = other_grad.astype(jnp.bfloat16)

time: 857 us -> 762 us (0.89)
  waiting for transfers between devices: 91.7 us -> 39.7 us
  starting transfers between devices: 73.2 us -> 25.1 us
    ppermute x16 -> x8, waiting for transfers between devices: 77.9 us -> 25.8 us  [passed_along(): lax.ppermute(value, axis, [(holder[source], holder[source + steps]) for s...]
    ppermute x16 -> x8, starting transfers between devices: 64.4 us -> 18.5 us  [passed_along(): lax.ppermute(value, axis, [(holder[source], holder[source + steps]) for s...]
    pallas_call x2, Pallas kernels: 52.8 us -> 27.5 us  [sum_over_seq(): pl.pallas_call(functools.partial(sum_kernel, count), out_shape=jax.ShapeD...]
    unnamed x295 -> x348, local copies, waits for them, and re-layouts: 51.7 us -> 35.4 us
    pallas_call x1, Pallas kernels: 105 us -> 117 us  [scatter_layer(): pl.pallas_call(functools.partial(scatter_kernel, tuple(pieces), 2), out_s...]
    concatenate x1 -> x9, local copies, waits for them, and re-layouts: 1.3 us -> 12.1 us  [the longest x1 6.51 us: per_device(): jnp.concatenate([placed_left(identity[:, :lead], 0) + placed_left(identit...]
    dot_general x10 -> x7, matrix products: 19.2 us -> 10.2 us  [exact(): jnp.dot(left, right, precision=HIGH, preferred_element_type=jnp.float32)]
    dot_general x10 -> x12, matrix products: 28.5 us -> 35 us  [dense(): return jnp.dot(left, right, preferred_element_type=jnp.float32)]
  transfers between devices with their start and end apart: 27 -> 17, of which waited for: 6 -> 5; matrix products, arithmetic and copies ran while one was open for 31% -> 20% of each run, Pallas kernels for 42% -> 22%
where the time goes in v4:
time: 762 us; the launch traced here: 752 us
  Pallas kernels  381 us (50%)
  matrix products  122 us (16%)
  local copies, waits for them, and re-layouts  104 us (14%)
  other arithmetic  57.1 us (7%)
  waiting for transfers between devices  39.7 us (5%)
  starting transfers between devices  25.1 us (3%)
  between operations  24.2 us (3%)
    pallas_call x1, Pallas kernels, gather_pieces(): pl.pallas_call(functools.partial(gather_kernel, tuple(shared)), out_shape...  136 us
    pallas_call x1, Pallas kernels, scatter_layer(): pl.pallas_call(functools.partial(scatter_kernel, tuple(pieces), 2), out_s...  117 us
    dot_general x12, matrix products, against_rows(): lax.dot_general(left, right, (((1,), (1,)), ((), ())), precision=precisio...  36.2 us
    dot_general x14, matrix products, contract_rows(): lax.dot_general(left, right, (((0,), (0,)), ((), ())), precision=precisio...  35.7 us
    unnamed x348, local copies, waits for them, and re-layouts  35.4 us
    dot_general x12, matrix products, dense(): return jnp.dot(left, right, preferred_element_type=jnp.float32)  35 us
    pallas_call x2, Pallas kernels, attend_backward(): pl.pallas_call(attend_backward_kernel, out_shape=(jax.ShapeDtypeStruct((r...  33.5 us
    pallas_call x2, Pallas kernels, attend_forward(): pl.pallas_call(attend_forward_kernel, out_shape=(jax.ShapeDtypeStruct((ro...  28.3 us
  transfers between devices with their start and end apart: 17, of which 5 were waited for; matrix products, arithmetic and copies ran while one was open for 20% of the time, Pallas kernels for 22%

profile of v4, /device:TPU:0, one launch (start us, length us, event | category | flops | bytes accessed | tf_op | source)
XLA Modules:
  0.0 752.0 jit_solution(6006579052116201523)
XLA Ops:
  9.3 3.5 lay_out.1
  20.6 136.0 %gather_pieces.1 = (f32[16,40,256]{2,1,0:T(8,128)}, bf16[16,496,256]{2,1,0:T(8,128)(2,1)}, bf16[16,48,6144]{2,1,0:T(8,128)(2,1)}, bf16[16,192,768]{2,1,0:T(8,128...) custom-call(f32[40,256]{1,0:T(8,128)} %maximum_bitcast_fusion.refs_0_, ...), custom_call_target="tpu_custom_call" | custom-call | tf_op jit(solution)/shard_map/gather_pieces/pallas_call | solution.py:740
  156.6 3.6 copy.189
  160.2 2.2 slice.281
  162.4 9.3 %reshape.558 = bf16[2001408]{0:T(1024)(128)(2,1)} reshape(bf16[16,125088]{1,0:T(8,128)(2,1)} %slice.281) | data formatting | bytes 8005632
  171.6 8.3 %slice.218 = bf16[2606,768]{1,0:T(8,128)(2,1)} reshape(bf16[2001408]{0:T(1024)(128)(2,1)} %reshape.558) | data formatting | bytes 8005632 | tf_op jit(solution)/shard_map/slice | solution.py:83
  190.4 2.1 fusion.176
  194.4 2.5 convolution_convert_fusion.14.q_ref
  196.9 6.6 convolution_convert_fusion.kv_ref
  203.9 14.1 %attend_forward.2 = (bf16[256,768]{1,0:T(8,128)(2,1)S(1)}, f32[16,256]{1,0:T(8,128)S(1)}) custom-call(bf16[256,768]{1,0:T(8,128)(2,1)S(1)} %convolution_convert_fusion.14.q_ref, bf16[1280,1536]{1,0:T(8,128)(2,1)} %convolution_convert_fusion.kv_ref, s32[1,256]{1,0:T(1,128)S(1)} %bitcast.146, s32[1280,1]{1,0:T(8,128)S(1)} %reshape_select_fusion.key_item_ref), custom_call_target="tpu_custom_call" | custom-call | flops 1006632960 | bytes 4718592 | tf_op jit(solution)/shard_map/attend_forward/pallas_call | solution.py:198
  220.2 4.4 fusion.6
  224.7 2.5 fusion.178
  227.6 3.5 convolution_convert_fusion.7
  231.1 3.6 collective-permute-start
  234.6 2.9 collective-permute-start.1
  240.1 7.3 slice.242
  248.4 2.4 multiply_reduce_fusion.22
  259.0 8.3 %collective-permute-done.3 = bf16[256,1536]{1,0:T(8,128)(2,1)} collective-permute-done((bf16[256,1536]{1,0:T(8,128)(2,1)}, bf16[256,1536]{1,0:T(8,128)(2,1)}, u32[]{:S(2)}, u32[]{:S(2)}) %collective-permute-start.3) | collective-permute-done | bytes 786464 | tf_op jit(solution)/shard_map/ppermute | solution.py:45
  270.4 14.2 %attend_forward.3 = (bf16[256,768]{1,0:T(8,128)(2,1)S(1)}, f32[16,256]{1,0:T(8,128)S(1)}) custom-call(bf16[256,768]{1,0:T(8,128)(2,1)S(1)} %convolution_convert_fusion.13.q_ref, bf16[1280,1536]{1,0:T(8,128)(2,1)} %copy-done.72, s32[1,256]{1,0:T(1,128)S(1)} %bitcast.147, s32[1280,1]{1,0:T(8,128)S(1)} %reshape_select_fusion.key_item_ref), custom_call_target="tpu_custom_call" | custom-call | flops 1006632960 | bytes 4718592 | tf_op jit(solution)/shard_map/attend_forward/pallas_call | solution.py:198
  286.8 4.0 fusion.2
  290.9 2.5 fusion.180
  298.2 2.1 fusion.95.x_ref
  302.4 11.8 %sum_over_seq.2 = f32[16,8,128]{2,1,0:T(8,128)} custom-call(f32[16,8,128]{2,1,0:T(8,128)} %fusion.95.x_ref), custom_call_target="tpu_custom_call" | custom-call | flops 16384 | bytes 262144 | tf_op jit(solution)/shard_map/sum_over_seq/pallas_call | solution.py:445
  320.7 2.4 multiply_reduce_fusion.18
  327.8 5.6 fusion.23
  333.5 2.1 multiply_reduce_fusion.5
  336.7 16.7 %attend_backward.2 = (bf16[256,768]{1,0:T(8,128)(2,1)S(1)}, bf16[1280,1536]{1,0:T(8,128)(2,1)}) custom-call(bf16[256,768]{1,0:T(8,128)(2,1)S(1)} %convolution_convert_fusion.13.q_ref, bf16[1280,1536]{1,0:T(8,128)(2,1)} %copy-done.72, bf16[256,768]{1,0:T(8,128)(2,1)S(1)} %convolution_convert_fusion.12.do_ref, f32[16,256]{1,0:T(8,128)S(1)} %get-tuple-element.61.lse_ref, ...), custom_call_target="tpu_custom_call" | custom-call | flops 2516582400 | bytes 9437184 | tf_op jit(solution)/shard_map/attend_backward/pallas_call | solution.py:255
  353.4 3.6 fusion.168
  357.0 3.9 collective-permute-start.7
  360.8 2.6 collective-permute-start.6
  366.4 3.6 convolution_convert_fusion.4
  371.5 4.4 convolution_convert_fusion.3
  375.9 2.2 collective-permute-done.7
  378.2 15.4 %collective-permute-done.4 = bf16[256,1536]{1,0:T(8,128)(2,1)} collective-permute-done((bf16[256,1536]{1,0:T(8,128)(2,1)}, bf16[256,1536]{1,0:T(8,128)(2,1)}, u32[]{:S(2)}, u32[]{:S(2)}) %collective-permute-start.4) | collective-permute-done | bytes 786464 | tf_op jit(solution)/shard_map/ppermute | solution.py:45
  393.5 2.6 add_convert_fusion
  396.1 3.3 multiply_reduce_fusion.9
  402.0 4.1 pad_maximum_fusion
  406.4 3.5 convert_element_type.261
  410.0 2.2 collective-permute-start.10
  425.3 2.6 reshape.510
  436.2 2.1 slice_reduce_fusion.2
  443.7 6.5 concatenate.87
  450.9 7.3 fusion.16
  458.2 4.6 multiply_reduce_fusion.7
  464.0 16.9 %attend_backward.3 = (bf16[256,768]{1,0:T(8,128)(2,1)S(1)}, bf16[1280,1536]{1,0:T(8,128)(2,1)}) custom-call(bf16[256,768]{1,0:T(8,128)(2,1)S(1)} %convolution_convert_fusion.14.q_ref, bf16[1280,1536]{1,0:T(8,128)(2,1)} %convolution_convert_fusion.kv_ref, bf16[256,768]{1,0:T(8,128)(2,1)S(1)} %convolution_convert_fusion.11.do_ref, ...), custom_call_target="tpu_custom_call" | custom-call | flops 2516582400 | bytes 9437184 | tf_op jit(solution)/shard_map/attend_backward/pallas_call | solution.py:255
  480.9 5.4 fusion.27
  487.3 2.2 copy-done.8
  492.6 4.0 broadcast_add_fusion
  498.4 2.1 fusion.24
  500.6 3.8 fusion.25
  505.1 15.7 %sum_over_seq.3 = f32[16,24,128]{2,1,0:T(8,128)} custom-call(f32[16,24,128]{2,1,0:T(8,128)} %bitcast.175), custom_call_target="tpu_custom_call" | custom-call | flops 49152 | bytes 786432 | tf_op jit(solution)/shard_map/sum_over_seq/pallas_call | solution.py:445
  525.1 2.6 convolution_convert_fusion.9
  527.7 2.4 copy.151
  530.1 3.0 convolution_convert_fusion.2
  533.2 4.4 convolution_convert_fusion.1
  537.6 3.4 convolution_convert_fusion.6
  541.0 7.0 pad_maximum_fusion.1
  548.1 117.4 %scatter_layer.1 = (f32[48,6144]{1,0:T(8,128)S(1)}, f32[192,768]{1,0:T(8,128)S(1)}, bf16[48,6144]{1,0:T(8,128)(2,1)S(1)}, bf16[192,768]{1,0:T(8,128)(2,1)S(1)}, f32[8,128]{1,0:T(8,128)S(1)}) custom-call(bf16[16,48,6144]{2,1,0:T(8,128)(2,1)} %bitcast.150, bf16[16,192,768]{2,1,0:T(8,128)(2,1)} %bitcast.160), custom_call_target="tpu_custom_call" | custom-call | tf_op jit(solution)/shard_map/scatter_layer/pallas_call | solution.py:1010
  667.8 2.3 fusion.36
  671.8 2.4 fusion.90
  683.9 12.6 %share_over_all.1 = f32[32,8,128]{2,1,0:T(8,128)} custom-call(f32[8,128]{1,0:T(8,128)} %broadcast_in_dim.177.x_ref), custom_call_target="tpu_custom_call" | custom-call | tf_op jit(solution)/shard_map/share_over_all/pallas_call | solution.py:510
  702.1 3.7 multiply_subtract_fusion
  710.1 11.8 %collective-permute-done.8.refs_6_ = bf16[48,6144]{1,0:T(8,128)(2,1)S(1)} collective-permute-done((bf16[48,6144]{1,0:T(8,128)(2,1)}, bf16[48,6144]{1,0:T(8,128)(2,1)S(1)}, u32[]{:S(2)}, u32[]{:S(2)}) %collective-permute-start.8) | collective-permute-done | bytes 589856 | tf_op jit(solution)/shard_map/ppermute | solution.py:1157
  721.9 21.9 %step_layers.1 = (f32[6912,128]{1,0:T(8,128)}, f32[6912,128]{1,0:T(8,128)}, f32[6912,128]{1,0:T(8,128)}, f32[6912,128]{1,0:T(8,128)}, f32[6912,128]{1,0:T(8,128)}) custom-call(f32[2]{0:T(128)S(1)} %pad_maximum_fusion.16.factors, f32[48,6144]{1,0:T(8,128)} %copy-done.1, f32[192,768]{1,0:T(8,128)S(1)} %get-tuple-element.72.refs_1_, ...), custom_call_target="tpu_custom_call" | custom-call | tf_op jit(solution)/shard_map/step_layers/pallas_call | solution.py:1137
  (559 shorter events, 124.3 us)
Async XLA Ops:
  7.2 671.1 %reduce-scatter.5.cloned.1.call-start = ((), (), s32[]{:S(2)}) async-start(), calls=%async_computation.3 | async-start | bytes 5013504 | tf_op jit(solution)/shard_map/reduce_scatter | solution.py:1326
  8.5 11.6 %copy-start.103 = (f32[256,20]{0,1:T(8,128)S(1)}, f32[256,20]{0,1:T(8,128)}, u32[]{:S(2)}) copy-start(f32[256,20]{0,1:T(8,128)} %param.23) | copy-start | bytes 61444
  8.5 11.5 %copy-start.104 = (f32[256,20]{0,1:T(8,128)S(1)}, f32[256,20]{0,1:T(8,128)}, u32[]{:S(2)}) copy-start(f32[256,20]{0,1:T(8,128)} %param.22) | copy-start | bytes 61444
  181.0 66.5 %copy-start.84 = (s32[1280]{0:T(1024)}, s32[1280]{0:T(1024)S(1)}, u32[]{:S(2)}) copy-start(s32[1280]{0:T(1024)S(1)} %and_select_fusion) | copy-start | bytes 15364
  188.9 38.5 %copy-start.86 = (f32[768]{0:T(1024)}, f32[768]{0:T(1024)S(1)}, u32[]{:S(2)}) copy-start(f32[768]{0:T(1024)S(1)} %get-tuple-element.102) | copy-start | bytes 9220
  188.9 97.9 %copy-start.73 = (f32[768]{0:T(1024)}, f32[768]{0:T(1024)S(1)}, u32[]{:S(2)}) copy-start(f32[768]{0:T(1024)S(1)} %get-tuple-element.101) | copy-start | bytes 9220
  188.9 104.9 %copy-start.79 = (f32[768]{0:T(1024)}, f32[768]{0:T(1024)S(1)}, u32[]{:S(2)}) copy-start(f32[768]{0:T(1024)S(1)} %get-tuple-element.100) | copy-start | bytes 9220
  192.5 25.4 %copy-start.7 = (f32[1280,768]{0,1:T(8,128)}, f32[1280,768]{0,1:T(8,128)S(1)}, u32[]{:S(2)}) copy-start(f32[1280,768]{0,1:T(8,128)S(1)} %get-tuple-element.158) | copy-start | bytes 11796484
  227.2 20.3 %copy-start.96 = (f32[256]{0:T(256)}, f32[256]{0:T(256)S(1)}, u32[]{:S(2)}) copy-start(f32[256]{0:T(256)S(1)} %broadcast_multiply_fusion.3) | copy-start | bytes 3076
  227.4 20.1 %copy-start.124 = (f32[256]{0:T(256)}, f32[256]{0:T(256)S(1)}, u32[]{:S(2)}) copy-start(f32[256]{0:T(256)S(1)} %multiply_reduce_fusion.14) | copy-start | bytes 3076
  227.4 20.1 %copy-start.105 = (f32[256]{0:T(256)}, f32[256]{0:T(256)S(1)}, u32[]{:S(2)}) copy-start(f32[256]{0:T(256)S(1)} %fusion.141) | copy-start | bytes 3076
  227.6 23.7 %copy-start.34 = (bf16[256,768]{0,1:T(8,128)(2,1)}, bf16[256,768]{0,1:T(8,128)(2,1)S(1)}, u32[]{:S(2)}) copy-start(bf16[256,768]{0,1:T(8,128)(2,1)S(1)} %multiply_convert_fusion.4) | copy-start | bytes 1179652
  231.1 23.2 %collective-permute-start = (bf16[256,1536]{1,0:T(8,128)(2,1)}, bf16[256,1536]{1,0:T(8,128)(2,1)}, u32[]{:S(2)}, u32[]{:S(2)}) collective-permute-start(bf16[256,1536]{1,0:T(8,128)(2,1)} %convolution_convert_fusion.7), channel_id=1, source_target_pairs={{0,2},{1,3},{2,6},{3,7},{6,4},{7,5},{4,8},{5,9},{8,10},{9,11},{10,... | collective-permute-start | bytes 2359304 | tf_op jit(solution)/shard_map/ppermute | solution.py:45
  234.6 20.8 %collective-permute-start.1 = (bf16[256,1536]{1,0:T(8,128)(2,1)}, bf16[256,1536]{1,0:T(8,128)(2,1)}, u32[]{:S(2)}, u32[]{:S(2)}) collective-permute-start(bf16[256,1536]{1,0:T(8,128)(2,1)} %convolution_convert_fusion.7), channel_id=1, source_target_pairs={{0,1},{1,2},{2,3},{3,6},{6,7},{7,4},{4,5},{5,8},{8,9},{9,10},{10,1... | collective-permute-start | bytes 2359304 | tf_op jit(solution)/shard_map/ppermute | solution.py:45
  237.5 20.3 %collective-permute-start.2 = (bf16[256,1536]{1,0:T(8,128)(2,1)}, bf16[256,1536]{1,0:T(8,128)(2,1)}, u32[]{:S(2)}, u32[]{:S(2)}) collective-permute-start(bf16[256,1536]{1,0:T(8,128)(2,1)} %convolution_convert_fusion.7), channel_id=1, source_target_pairs={{1,0},{2,1},{3,2},{6,3},{7,6},{4,7},{5,4},{8,5},{9,8},{10,9},{11,1... | collective-permute-start | bytes 2359304 | tf_op jit(solution)/shard_map/ppermute | solution.py:45
  238.8 28.5 %collective-permute-start.3 = (bf16[256,1536]{1,0:T(8,128)(2,1)}, bf16[256,1536]{1,0:T(8,128)(2,1)}, u32[]{:S(2)}, u32[]{:S(2)}) collective-permute-start(bf16[256,1536]{1,0:T(8,128)(2,1)} %convolution_convert_fusion.7), channel_id=1, source_target_pairs={{2,0},{3,1},{6,2},{7,3},{4,6},{5,7},{8,4},{9,5},{10,8},{11,9},{14,... | collective-permute-start | bytes 2359304 | tf_op jit(solution)/shard_map/ppermute | solution.py:45
  253.1 67.7 %copy-start.137 = (f32[12]{0:T(128)}, f32[12]{0:T(128)S(1)}, u32[]{:S(2)}) copy-start(f32[12]{0:T(128)S(1)} %add_rsqrt_fusion.1) | copy-start | bytes 148
  293.4 24.2 %copy-start.88 = (f32[256]{0:T(256)}, f32[256]{0:T(256)S(1)}, u32[]{:S(2)}) copy-start(f32[256]{0:T(256)S(1)} %broadcast_multiply_fusion.1) | copy-start | bytes 3076
  293.6 24.1 %copy-start.128 = (f32[256]{0:T(256)}, f32[256]{0:T(256)S(1)}, u32[]{:S(2)}) copy-start(f32[256]{0:T(256)S(1)} %multiply_reduce_fusion.12) | copy-start | bytes 3076
  293.6 24.0 %copy-start.94 = (f32[256]{0:T(256)}, f32[256]{0:T(256)S(1)}, u32[]{:S(2)}) copy-start(f32[256]{0:T(256)S(1)} %fusion.143) | copy-start | bytes 3076
  294.3 31.0 %copy-start.36 = (bf16[256,768]{0,1:T(8,128)(2,1)}, bf16[256,768]{0,1:T(8,128)(2,1)S(1)}, u32[]{:S(2)}) copy-start(bf16[256,768]{0,1:T(8,128)(2,1)S(1)} %multiply_convert_fusion.6) | copy-start | bytes 1179652
  327.7 43.8 %copy-start.22 = (f32[256,768]{0,1:T(8,128)}, f32[256,768]{0,1:T(8,128)S(1)}, u32[]{:S(2)}) copy-start(f32[256,768]{0,1:T(8,128)S(1)} %get-tuple-element.121) | copy-start | bytes 2359300
  327.7 43.8 %copy-start.118 = (f32[256]{0:T(256)}, f32[256]{0:T(256)S(1)}, u32[]{:S(2)}) copy-start(f32[256]{0:T(256)S(1)} %negate_multiply_fusion.4) | copy-start | bytes 3076
  335.9 17.5 %copy-start.24 = (f32[256,768]{0,1:T(8,128)}, f32[256,768]{0,1:T(8,128)S(1)}, u32[]{:S(2)}) copy-start(f32[256,768]{0,1:T(8,128)S(1)} %get-tuple-element.119) | copy-start | bytes 2359300
  357.0 21.2 %collective-permute-start.7 = (bf16[256,1536]{1,0:T(8,128)(2,1)}, bf16[256,1536]{1,0:T(8,128)(2,1)}, u32[]{:S(2)}, u32[]{:S(2)}) collective-permute-start(bf16[256,1536]{1,0:T(8,128)(2,1)} %get-tuple-element.127), channel_id=1, source_target_pairs={{0,2},{1,3},{2,6},{3,7},{6,4},{7,5},{4,8},{5,9},{8,10},{9,11},{10,... | collective-permute-start | bytes 2359304 | tf_op jit(solution)/shard_map/ppermute | solution.py:45
  360.8 17.3 %collective-permute-start.6 = (bf16[256,1536]{1,0:T(8,128)(2,1)}, bf16[256,1536]{1,0:T(8,128)(2,1)}, u32[]{:S(2)}, u32[]{:S(2)}) collective-permute-start(bf16[256,1536]{1,0:T(8,128)(2,1)} %get-tuple-element.128), channel_id=1, source_target_pairs={{0,1},{1,2},{2,3},{3,6},{6,7},{7,4},{4,5},{5,8},{8,9},{9,10},{10,1... | collective-permute-start | bytes 2359304 | tf_op jit(solution)/shard_map/ppermute | solution.py:45
  363.4 14.7 %collective-permute-start.5 = (bf16[256,1536]{1,0:T(8,128)(2,1)}, bf16[256,1536]{1,0:T(8,128)(2,1)}, u32[]{:S(2)}, u32[]{:S(2)}) collective-permute-start(bf16[256,1536]{1,0:T(8,128)(2,1)} %get-tuple-element.129), channel_id=1, source_target_pairs={{1,0},{2,1},{3,2},{6,3},{7,6},{4,7},{5,4},{8,5},{9,8},{10,9},{11,1... | collective-permute-start | bytes 2359304 | tf_op jit(solution)/shard_map/ppermute | solution.py:45
  364.7 28.8 %collective-permute-start.4 = (bf16[256,1536]{1,0:T(8,128)(2,1)}, bf16[256,1536]{1,0:T(8,128)(2,1)}, u32[]{:S(2)}, u32[]{:S(2)}) collective-permute-start(bf16[256,1536]{1,0:T(8,128)(2,1)} %get-tuple-element.126), channel_id=1, source_target_pairs={{2,0},{3,1},{6,2},{7,3},{4,6},{5,7},{8,4},{9,5},{10,8},{11,9},{14,... | collective-permute-start | bytes 2359304 | tf_op jit(solution)/shard_map/ppermute | solution.py:45
  375.9 20.2 %copy-start.87 = (f32[768]{0:T(1024)S(1)}, f32[768]{0:T(1024)}, u32[]{:S(2)}) copy-start(f32[768]{0:T(1024)} %copy-done.86) | copy-start | bytes 9220
  375.9 20.2 %copy-start.97 = (f32[256]{0:T(256)S(1)}, f32[256]{0:T(256)}, u32[]{:S(2)}) copy-start(f32[256]{0:T(256)} %copy-done.96) | copy-start | bytes 3076
  402.0 61.1 %copy-start.19 = (f32[256,768]{0,1:T(8,128)}, f32[256,768]{0,1:T(8,128)S(1)}, u32[]{:S(2)}) copy-start(f32[256,768]{0,1:T(8,128)S(1)} %add_add_fusion.6) | copy-start | bytes 2359300
  406.2 273.8 %reduce-scatter.3.cloned.1.call-start = ((), (), s32[]{:S(2)}) async-start(), calls=%async_computation.2 | async-start | bytes 10027008 | tf_op jit(solution)/shard_map/reduce_scatter | solution.py:1326
  410.0 298.1 %collective-permute-start.10 = (bf16[6912,128]{1,0:T(8,128)(2,1)}, bf16[6912,128]{1,0:T(8,128)(2,1)}, u32[]{:S(2)}, u32[]{:S(2)}) collective-permute-start(bf16[6912,128]{1,0:T(8,128)(2,1)} %convert_element_type.261), channel_id=1, source_target_pairs={{0,16},{16,0},{1,17},{17,1},{2,18},{18,2},{3,19},{19,3},{4,20},{20... | collective-permute-start | bytes 5308424 | tf_op jit(solution)/shard_map/ppermute | solution.py:1157
  413.5 294.6 %collective-permute-start.11 = (bf16[6912,128]{1,0:T(8,128)(2,1)}, bf16[6912,128]{1,0:T(8,128)(2,1)}, u32[]{:S(2)}, u32[]{:S(2)}) collective-permute-start(bf16[6912,128]{1,0:T(8,128)(2,1)} %convert_element_type.262), channel_id=1, source_target_pairs={{0,16},{16,0},{1,17},{17,1},{2,18},{18,2},{3,19},{19,3},{4,20},{20... | collective-permute-start | bytes 5308424 | tf_op jit(solution)/shard_map/ppermute | solution.py:1157
  414.3 285.7 %collective-permute-start.14 = (bf16[125088]{0:T(1024)(128)(2,1)}, bf16[125088]{0:T(1024)(128)(2,1)}, u32[]{:S(2)}, u32[]{:S(2)}) collective-permute-start(bf16[125088]{0:T(1024)(128)(2,1)} %convert_element_type.267), channel_id=1, source_target_pairs={{0,16},{16,0},{1,17},{17,1},{2,18},{18,2},{3,19},{19,3},{4,20},{20... | collective-permute-start | bytes 750536 | tf_op jit(solution)/shard_map/ppermute | solution.py:1157
  417.0 283.6 %collective-permute-start.12 = (bf16[125088]{0:T(1024)(128)(2,1)}, bf16[125088]{0:T(1024)(128)(2,1)}, u32[]{:S(2)}, u32[]{:S(2)}) collective-permute-start(bf16[125088]{0:T(1024)(128)(2,1)} %convert_element_type.263), channel_id=1, source_target_pairs={{0,16},{16,0},{1,17},{17,1},{2,18},{18,2},{3,19},{19,3},{4,20},{20... | collective-permute-start | bytes 750536 | tf_op jit(solution)/shard_map/ppermute | solution.py:1157
  419.6 10.7 %copy-start.108 = (f32[768]{0:T(1024)S(1)}, f32[768]{0:T(1024)}, u32[]{:S(2)}) copy-start(f32[768]{0:T(1024)} %get-tuple-element.88) | copy-start | bytes 9220
  419.6 11.3 %copy-start.37 = (bf16[256,768]{0,1:T(8,128)(2,1)S(1)}, bf16[256,768]{0,1:T(8,128)(2,1)}, u32[]{:S(2)}) copy-start(bf16[256,768]{0,1:T(8,128)(2,1)} %copy-done.36) | copy-start | bytes 1179652
  419.6 11.3 %copy-start.59 = (f32[256,20]{0,1:T(8,128)S(1)}, f32[256,20]{0,1:T(8,128)}, u32[]{:S(2)}) copy-start(f32[256,20]{0,1:T(8,128)} %copy-done.58) | copy-start | bytes 61444
  450.9 12.4 %slice-start.7 = ((s8[9437184]{0:T(1024)(128)(4,1)}), s8[4194304]{0:T(1024)(128)(4,1)S(1)}, s32[]{:S(2)}) async-start(s8[9437184]{0:T(1024)(128)(4,1)} %bitcast.181), calls=%async_computation.11 | async-start | bytes 8388608
  450.9 12.4 %slice-start.8 = ((s8[9437184]{0:T(1024)(128)(4,1)}), s8[4194304]{0:T(1024)(128)(4,1)S(1)}, s32[]{:S(2)}) async-start(s8[9437184]{0:T(1024)(128)(4,1)} %bitcast.181), calls=%async_computation.12 | async-start | bytes 8388608
  463.1 17.7 %copy-start.116 = (f32[256]{0:T(256)}, f32[256]{0:T(256)S(1)}, u32[]{:S(2)}) copy-start(f32[256]{0:T(256)S(1)} %negate_multiply_fusion.1) | copy-start | bytes 3076
  463.3 17.6 %copy-start.43 = (bf16[256,768]{0,1:T(8,128)(2,1)}, bf16[256,768]{0,1:T(8,128)(2,1)S(1)}, u32[]{:S(2)}) copy-start(bf16[256,768]{0,1:T(8,128)(2,1)S(1)} %fusion.83) | copy-start | bytes 1179652
  500.5 21.2 %copy-start.44 = (bf16[256,768]{0,1:T(8,128)(2,1)S(1)}, bf16[256,768]{0,1:T(8,128)(2,1)}, u32[]{:S(2)}) copy-start(bf16[256,768]{0,1:T(8,128)(2,1)} %copy-done.43) | copy-start | bytes 1179652
  548.0 119.2 %copy-start.46 = (f32[16,24,128]{2,1,0:T(8,128)S(1)}, f32[16,24,128]{2,1,0:T(8,128)}, u32[]{:S(2)}) copy-start(f32[16,24,128]{2,1,0:T(8,128)} %sum_over_seq.3) | copy-start | bytes 589828
  548.0 119.7 %slice-start.3 = ((f32[16,24,128]{2,1,0:T(8,128)}), f32[3,24,128]{2,1,0:T(8,128)S(1)}, s32[]{:S(2)}) async-start(f32[16,24,128]{2,1,0:T(8,128)} %sum_over_seq.3), calls=%async_computation.7 | async-start | bytes 73728 | tf_op jit(solution)/shard_map/slice | solution.py:83
  548.0 119.7 %copy-start.52 = (f32[12,768]{1,0:T(8,128)S(1)}, f32[12,768]{1,0:T(8,128)}, u32[]{:S(2)}) copy-start(f32[12,768]{1,0:T(8,128)} %copy-done.51) | copy-start | bytes 110596
  548.0 119.8 %copy-start.132 = (pred[12]{0:T(512)(128)(4,1)S(1)}, pred[12]{0:T(512)(128)(4,1)}, u32[]{:S(2)}) copy-start(pred[12]{0:T(512)(128)(4,1)} %copy-done.130) | copy-start | bytes 40
  548.0 122.1 %copy-start.64 = (f32[12,768]{1,0:T(8,128)S(1)}, f32[12,768]{1,0:T(8,128)}, u32[]{:S(2)}) copy-start(f32[12,768]{1,0:T(8,128)} %get-tuple-element.141) | copy-start | bytes 110596
  548.1 122.1 %copy-start.65 = (f32[12,768]{1,0:T(8,128)S(1)}, f32[12,768]{1,0:T(8,128)}, u32[]{:S(2)}) copy-start(f32[12,768]{1,0:T(8,128)} %get-tuple-element.142) | copy-start | bytes 110596
  548.1 122.1 %copy-start.66 = (f32[12,768]{1,0:T(8,128)S(1)}, f32[12,768]{1,0:T(8,128)}, u32[]{:S(2)}) copy-start(f32[12,768]{1,0:T(8,128)} %get-tuple-element.180) | copy-start | bytes 110596
  548.1 122.1 %copy-start.67 = (f32[12,768]{1,0:T(8,128)S(1)}, f32[12,768]{1,0:T(8,128)}, u32[]{:S(2)}) copy-start(f32[12,768]{1,0:T(8,128)} %get-tuple-element.181) | copy-start | bytes 110596
  548.1 122.1 %copy-start.68 = (f32[12,768]{1,0:T(8,128)S(1)}, f32[12,768]{1,0:T(8,128)}, u32[]{:S(2)}) copy-start(f32[12,768]{1,0:T(8,128)} %concatenate.92) | copy-start | bytes 110596
  548.1 122.1 %copy-start.69 = (f32[12,768]{1,0:T(8,128)S(1)}, f32[12,768]{1,0:T(8,128)}, u32[]{:S(2)}) copy-start(f32[12,768]{1,0:T(8,128)} %concatenate.93) | copy-start | bytes 110596
  548.1 122.1 %copy-start.70 = (f32[12,768]{1,0:T(8,128)S(1)}, f32[12,768]{1,0:T(8,128)}, u32[]{:S(2)}) copy-start(f32[12,768]{1,0:T(8,128)} %concatenate.96) | copy-start | bytes 110596
  548.1 122.1 %copy-start.71 = (f32[12,768]{1,0:T(8,128)S(1)}, f32[12,768]{1,0:T(8,128)}, u32[]{:S(2)}) copy-start(f32[12,768]{1,0:T(8,128)} %concatenate.97) | copy-start | bytes 110596
  671.7 30.3 %copy-start.31 = (f32[125088]{0:T(1024)S(1)}, f32[125088]{0:T(1024)}, u32[]{:S(2)}) copy-start(f32[125088]{0:T(1024)} %reduce.2) | copy-start | bytes 1501060
  671.7 30.3 %copy-start.33 = (f32[125088]{0:T(1024)S(1)}, f32[125088]{0:T(1024)}, u32[]{:S(2)}) copy-start(f32[125088]{0:T(1024)} %reduce.3) | copy-start | bytes 1501060
  674.2 27.9 %copy-start.41 = (f32[125088]{0:T(1024)S(1)}, f32[125088]{0:T(1024)}, u32[]{:S(2)}) copy-start(f32[125088]{0:T(1024)} %param.15) | copy-start | bytes 1501060
  676.2 25.9 %collective-permute-start.13 = (bf16[125088]{0:T(1024)(128)(2,1)}, bf16[125088]{0:T(1024)(128)(2,1)}, u32[]{:S(2)}, u32[]{:S(2)}) collective-permute-start(bf16[125088]{0:T(1024)(128)(2,1)} %dynamic_slice.50), channel_id=1, source_target_pairs={{0,16},{16,0},{1,17},{17,1},{2,18},{18,2},{3,19},{19,3},{4,20},{20... | collective-permute-start | bytes 750536 | tf_op jit(solution)/shard_map/ppermute | solution.py:1157
  699.9 10.2 %collective-permute-start.9 = (bf16[192,768]{1,0:T(8,128)(2,1)}, bf16[192,768]{1,0:T(8,128)(2,1)S(1)}, u32[]{:S(2)}, u32[]{:S(2)}) collective-permute-start(bf16[192,768]{1,0:T(8,128)(2,1)} %reduce-scatter.5.cloned.1.call-done.refs_3_), channel_id=1, source_target_pairs={{0,16},{16,0},{1,17},{17,1},{2,18},{18,2},{3,19},{19,3},{4,20},{20... | collective-permute-start | bytes 884744 | tf_op jit(solution)/shard_map/ppermute | solution.py:1157
  700.6 21.3 %collective-permute-start.8 = (bf16[48,6144]{1,0:T(8,128)(2,1)}, bf16[48,6144]{1,0:T(8,128)(2,1)S(1)}, u32[]{:S(2)}, u32[]{:S(2)}) collective-permute-start(bf16[48,6144]{1,0:T(8,128)(2,1)} %reduce-scatter.3.cloned.1.call-done.refs_2_), channel_id=1, source_target_pairs={{0,16},{16,0},{1,17},{17,1},{2,18},{18,2},{3,19},{19,3},{4,20},{20... | collective-permute-start | bytes 1769480 | tf_op jit(solution)/shard_map/ppermute | solution.py:1157
  702.1 19.8 %copy-start = (bf16[48,6144]{1,0:T(8,128)(2,1)S(1)}, bf16[48,6144]{1,0:T(8,128)(2,1)}, u32[]{:S(2)}) copy-start(bf16[48,6144]{1,0:T(8,128)(2,1)} %reduce-scatter.3.cloned.1.call-done.refs_2_) | copy-start | bytes 1769476
  702.1 19.8 %copy-start.2 = (bf16[192,768]{1,0:T(8,128)(2,1)S(1)}, bf16[192,768]{1,0:T(8,128)(2,1)}, u32[]{:S(2)}) copy-start(bf16[192,768]{1,0:T(8,128)(2,1)} %reduce-scatter.5.cloned.1.call-done.refs_3_) | copy-start | bytes 884740
  (125 other events, 522.1 us)
Sparse Core Ops, SparseCore 0:
  406.3 75.3 reduce-scatter.4
  486.4 131.7 reduce-scatter.2

commit v5 on v4

--- a/solution.py
+++ b/solution.py
@@ -155,6 +155,7 @@
 
 
 LANES = 128
+LOG2E = math.log2(math.e)
 PAIRS = HEADS * HD // LANES
 VMEM_LIMIT = 50 * 1024 * 1024
 
@@ -181,14 +182,13 @@
         value_rows = kv_ref[:, width + pair * LANES : width + (pair + 1) * LANES]
         halves = []
         for half in range(2):
-            scores = against_rows(key_rows, query * masks[half]) + bias_ref[...]
+            scores = against_rows(key_rows, query * masks[half]) * LOG2E + bias_ref[...]
             peak = jnp.max(scores, axis=0, keepdims=True)
-            weights = jnp.exp(scores - peak)
+            weights = jnp.exp2(scores - peak)
             total = jnp.sum(weights, axis=0, keepdims=True)
-            shares = (weights * (1.0 / total)).astype(jnp.bfloat16)
-            mixed = contract_rows(value_rows, shares)
+            mixed = contract_rows(value_rows, weights.astype(jnp.bfloat16)) * (1.0 / total)
             halves.append(mixed[half * HD : (half + 1) * HD])
-            lse_ref[2 * pair + half : 2 * pair + half + 1, :] = peak + jnp.log(total)
+            lse_ref[2 * pair + half : 2 * pair + half + 1, :] = peak + jnp.log2(total)
         o_ref[:, cols] = jnp.concatenate(halves, axis=0).T.astype(o_ref.dtype)
 
 
@@ -232,8 +232,8 @@
         for half in range(2):
             query_half = query * masks[half]
             grad_half = grad_out * masks[half]
-            scores = against_rows(key_rows, query_half) + bias_ref[...]
-            shares = jnp.exp(scores - lse_ref[2 * pair + half : 2 * pair + half + 1, :])
+            scores = against_rows(key_rows, query_half) * LOG2E + bias_ref[...]
+            shares = jnp.exp2(scores - lse_ref[2 * pair + half : 2 * pair + half + 1, :])
             grad_shares = against_rows(value_rows, grad_half)
             inner = jnp.sum(grad_shares * shares, axis=0, keepdims=True)
             grad_scores = (shares * (grad_shares - inner)).astype(jnp.bfloat16)
@@ -284,7 +284,7 @@
     )
 
 
-def layer_backward(grad_hidden, weights, gain_two, items, saved):
+def layer_backward(grad_hidden, weights, gain_two, items, saved, early):
     normed, queries, window, lse, attended, middle, second, upper, activated = saved
     proj_qkv, proj_out, proj_up, proj_down = weights
     branch_top = grad_hidden.astype(jnp.bfloat16)
@@ -297,19 +297,18 @@
     grad_middle = grad_middle + grad_hidden
     branch_mid = grad_middle.astype(jnp.bfloat16)
     grad_attended = against_rows(branch_mid, proj_out).astype(jnp.bfloat16)
+    lower_full = contract_rows(activated, branch_top).astype(jnp.bfloat16)
+    pairs = [(attended, branch_mid), (second, grad_upper)]
+    if early:
+        grad_attended, rest_full = lax.optimization_barrier((grad_attended, side_by_side(pairs)))
     grad_query, grad_window = attend_backward(queries, window, grad_attended, lse, *items)
-    operand_pairs = (attended, branch_mid, second, grad_upper, activated, branch_top)
-    return grad_middle, grad_query, grad_window, operand_pairs, grad_gain_two
-
-
-def layer_gradients(qkv_parts, operand_pairs):
-    attended, branch_mid, second, grad_upper, activated, branch_top = operand_pairs
-    pairs = qkv_parts + [(attended, branch_mid), (second, grad_upper)]
-    upper_full = jnp.concatenate(
+    return grad_middle, grad_query, grad_window, (rest_full if early else pairs), lower_full, grad_gain_two
+
+
+def side_by_side(pairs):
+    return jnp.concatenate(
         [contract_rows(left, right).astype(jnp.bfloat16) for left, right in pairs], axis=1
     )
-    lower_full = contract_rows(activated, branch_top).astype(jnp.bfloat16)
-    return upper_full, lower_full
 
 
 def frame_window(frames, gathered_frames, own_block, close):
@@ -327,35 +326,36 @@
     return jnp.concatenate(parts, axis=1)
 
 
-def thirds_left(value):
-    items = value.shape[0]
-    thirds = value.reshape(items, -1, 3)
-    zero = jnp.zeros_like(thirds[:, :, 0])
-    even = jnp.concatenate([thirds[:, :, 0], thirds[:, :, 1], zero, zero], axis=0)
-    odd = jnp.concatenate([zero, zero, thirds[:, :, 1], thirds[:, :, 2]], axis=0)
-    return jnp.stack([even, odd], axis=2).reshape(4 * items, -1)
-
-
-def thirds_right(value):
-    half = value.shape[1] // 2
-    wide = jnp.zeros_like(value)
-    narrow = wide[:, :half]
-    return jnp.concatenate(
+def thirds(value, right, at):
+    joint = right.shape[1]
+    half = joint // 2
+    inside = (at >= 0) & (at < value.shape[1] * joint // D)
+    matrix_row, odd = at // 2 * 3, at % 2
+    wanted = jnp.stack(
         [
-            jnp.concatenate([value, narrow], axis=1),
-            jnp.concatenate([wide, value[:, :half]], axis=1),
-            jnp.concatenate([value[:, half:], wide], axis=1),
-            jnp.concatenate([narrow, value], axis=1),
-        ],
-        axis=0,
-    )
+            jnp.where(inside & (odd == parity), matrix_row + offset, -1)
+            for parity, offset in ((0, 0), (0, 1), (1, 1), (1, 2))
+        ]
+    )
+    width = jnp.arange(value.shape[1], dtype=jnp.int32)
+    choice = (width[:, None, None] == wanted[None]).astype(jnp.float32)
+    left = jnp.einsum("iw,wkv->kiv", value, choice, precision=HIGH)
+    rights = jnp.stack(
+        [
+            jnp.pad(right, ((0, 0), (0, half))),
+            jnp.pad(right[:, :half], ((0, 0), (joint, 0))),
+            jnp.pad(right[:, half:], ((0, 0), (0, joint))),
+            jnp.pad(right, ((0, 0), (half, 0))),
+        ]
+    )
+    return jnp.einsum("kiv,kid->vd", left, rights, precision=HIGH)
 
 
 def adam(grad, first, second, anchor):
     first = beta_one * first + (1.0 - beta_one) * grad
     second = beta_two * second + (1.0 - beta_two) * grad * grad
-    stepped = first / (1.0 - beta_one**STEP_COUNT)
-    scaled = second / (1.0 - beta_two**STEP_COUNT)
+    stepped = first * (1.0 / (1.0 - beta_one**STEP_COUNT))
+    scaled = second * (1.0 / (1.0 - beta_two**STEP_COUNT))
     delta = inner_rate * (stepped / (jnp.sqrt(scaled) + adam_eps) + decay_rate * anchor)
     return (first, second, delta)
 
@@ -433,15 +433,19 @@
     lax.fori_loop(1, count, spread, 0)
 
 
+def in_slices(values, count):
+    size = sum(math.prod(value.shape) for value in values)
+    block = -(-size // (count * SUBLANES * LANES)) * SUBLANES
+    flat = jnp.concatenate([value.reshape(-1) for value in values])
+    return jnp.pad(flat, (0, count * block * LANES - size)).reshape(count, block, LANES)
+
+
 def sum_over_seq(values, collective):
     count = lax.axis_size("seq")
     if count != CLOSE_RANKS:
         return lax.psum(values, "seq")
-    sizes = [math.prod(value.shape) for value in values]
-    block = -(-sum(sizes) // (count * SUBLANES * LANES)) * SUBLANES
-    flat = jnp.concatenate([value.reshape(-1) for value in values])
-    flat = jnp.pad(flat, (0, count * block * LANES - flat.shape[0]))
-    shape = (count, block, LANES)
+    small = in_slices(values, count)
+    shape = small.shape
     total = pl.pallas_call(
         functools.partial(sum_kernel, count),
         out_shape=jax.ShapeDtypeStruct(shape, jnp.float32),
@@ -458,7 +462,7 @@
             flops=math.prod(shape), transcendentals=0, bytes_accessed=16 * math.prod(shape)
         ),
         name="sum_over_seq",
-    )(flat.reshape(shape))
+    )(small)
     return carve(total.reshape(-1), [value.shape for value in values])
 
 
@@ -524,7 +528,6 @@
 GATHER_Y_LAG = 2
 GATHER_X_LAG = 5
 GATHER_AHEAD = 1
-GATHER_LANES = 256
 
 
 def place_of(me):
@@ -569,6 +572,9 @@
     def half_of(ref, piece, half):
         if half is None:
             return ref
+        if ref.shape[-1] == LANES:
+            span = ref.shape[-2] // 2
+            return ref.at[pl.ds(pl.multiple_of(half * span, ROW_GROUP), span), :]
         span = ref.shape[-1] // 2
         return ref.at[:, pl.ds(pl.multiple_of(half * span, LANES), span)]
 
@@ -750,19 +756,28 @@
 
 ROW_GROUP = 16
 UPPER_CUTS = 3
-LOWER_CUTS = 1
 SCATTER_LAG = 2
 
 
-def scatter_kernel(pieces, amount, *refs):
-    grads, outs, twins = (refs[k * amount : (k + 1) * amount] for k in range(3))
-    squares = refs[3 * amount]
-    rest = refs[3 * amount + 1 :]
+def scatter_kernel(pieces, amount, carried, *refs):
+    grads, passing = refs[:amount], refs[amount : amount + carried]
+    small = refs[amount + carried]
+    refs = refs[amount + carried + 1 :]
+    outs, twins = refs[:amount], refs[amount : 2 * amount]
+    passed = refs[2 * amount : 2 * amount + carried]
+    squares, small_out = refs[2 * amount + carried : 2 * amount + carried + 2]
+    rest = refs[2 * amount + carried + 2 :]
     count = len(pieces)
+    ranks = lax.axis_size("seq")
     own, beside, facing, from_left, from_right, ready = (
         rest[k * count : (k + 1) * count] for k in range(6)
     )
-    load_sem, c_send, c_recv, y_send, y_recv, z_send, z_recv, x_send, x_recv = rest[6 * count :]
+    load_sem, c_send, c_recv, y_send, y_recv, z_send, z_recv, x_send, x_recv = rest[
+        6 * count : 6 * count + 9
+    ]
+    pass_send, pass_recv, parts, own_sum, totals, send_one, recv_one, send_two, recv_two = rest[
+        6 * count + 9 :
+    ]
     group, me = lax.axis_index("grp"), lax.axis_index("seq")
     z, y, core = place_of(me)
     z_size = GRID[0]
@@ -771,19 +786,15 @@
     left, right = (group, rank_of(z - 1, y, core)), (group, rank_of(z + 1, y, core))
     has_left, has_right = z > 0, z < z_size - 1
     barrier = pltpu.get_barrier_semaphore()
-    for there in (across, sibling, twin):
+    pl.semaphore_signal(barrier, inc=1, device_id=twin, device_id_type=MESH)
+
+    def greet(step, carry):
+        there = (group, lax.rem(me + step, ranks))
         pl.semaphore_signal(barrier, inc=1, device_id=there, device_id_type=MESH)
-
-    @pl.when(has_left)
-    def _():
-        pl.semaphore_signal(barrier, inc=1, device_id=left, device_id_type=MESH)
-
-    @pl.when(has_right)
-    def _():
-        pl.semaphore_signal(barrier, inc=1, device_id=right, device_id_type=MESH)
-
-    neighbours = has_left.astype(jnp.int32) + has_right.astype(jnp.int32)
-    pl.semaphore_wait(barrier, 3 + neighbours)
+        return carry
+
+    lax.fori_loop(1, ranks, greet, 0)
+    pl.semaphore_wait(barrier, ranks)
     squares[...] = jnp.zeros_like(squares)
 
     def part(piece, along, over, owner):
@@ -840,6 +851,50 @@
             twin,
         )
 
+    def pass_move(k):
+        return remote(passing[k], passed[k], pass_send.at[k], pass_recv.at[k], twin)
+
+    def slice_move(step):
+        peer = lax.rem(me + step, ranks)
+        return remote(
+            small.at[peer], parts.at[step], send_one.at[step], recv_one.at[step], (group, peer)
+        )
+
+    def total_move(step):
+        peer = lax.rem(me + step, ranks)
+        return remote(own_sum, totals.at[step], send_two.at[step], recv_two.at[step], (group, peer))
+
+    def small_begin():
+        def one(step, carry):
+            slice_move(step).start()
+            return carry
+
+        lax.fori_loop(1, ranks, one, 0)
+        own_sum[...] = small[me]
+
+    def small_middle():
+        def gather_in(step, carry):
+            slice_move(step).wait()
+            own_sum[...] += parts[step]
+            return carry
+
+        lax.fori_loop(1, ranks, gather_in, 0)
+
+        def one(step, carry):
+            total_move(step).start()
+            return carry
+
+        lax.fori_loop(1, ranks, one, 0)
+        small_out[me] = own_sum[...]
+
+    def small_end():
+        def spread(step, carry):
+            total_move(step).wait()
+            small_out[lax.rem(me + ranks - step, ranks)] = totals[step]
+            return carry
+
+        lax.fori_loop(1, ranks, spread, 0)
+
     def each_along(distance, action):
         if distance == 0:
             action(z, None)
@@ -964,11 +1019,17 @@
         each_along(distance, one)
 
     slots = [(piece, distance) for piece in range(count) for distance in reversed(range(z_size))]
-    for piece in range(min(2, count)):
+    begin(0)
+    small_begin()
+    for piece in range(1, min(2, count)):
         begin(piece)
+    for k in range(carried):
+        pass_move(k).start()
     for turn in range(len(slots) + SCATTER_LAG):
         if turn < len(slots):
             c_stage(*slots[turn])
+            if turn == z_size:
+                small_middle()
             piece, distance = slots[turn]
             if distance == 0 and piece + 2 < count:
                 begin(piece + 2)
@@ -978,18 +1039,18 @@
         drain(*slot)
     for piece in range(count):
         x_move(piece).wait()
-
-
-def scatter_layer(upper, lower, collective):
+    for k in range(carried):
+        pass_move(k).wait()
+    small_end()
+
+
+def scatter_grads(grads, cuts, passing, values, collective):
     count = math.prod(GRID)
-    grads = [grad.reshape(count, grad.shape[0] // count, grad.shape[1]) for grad in (upper, lower)]
+    grads = [grad.reshape(count, grad.shape[0] // count, grad.shape[1]) for grad in grads]
     pieces = []
-    for which, cuts in ((0, UPPER_CUTS), (1, LOWER_CUTS)):
+    for which, cut in enumerate(cuts):
         rows, columns = grads[which].shape[1:]
-        if which == 0:
-            pieces += [(0, 0, rows, k * (columns // cuts), columns // cuts) for k in range(cuts)]
-        else:
-            pieces += [(1, k * (rows // cuts), rows // cuts, 0, columns) for k in range(cuts)]
+        pieces += [(which, 0, rows, k * (columns // cut), columns // cut) for k in range(cut)]
     amount = len(pieces)
     places = math.prod(GRID[:2])
 
@@ -1007,28 +1068,48 @@
         (amount,),
         (amount,),
     ]
-    own_upper, own_lower, twin_upper, twin_lower, squares = pl.pallas_call(
-        functools.partial(scatter_kernel, tuple(pieces), 2),
+    small = in_slices(values, count)
+    slot = small.shape[1:]
+    carried = len(passing)
+    sems += [(carried,)] * 2
+    kinds = len(grads)
+    *arrays, squares, total = pl.pallas_call(
+        functools.partial(scatter_kernel, tuple(pieces), kinds, carried),
         out_shape=[jax.ShapeDtypeStruct(grad.shape[1:], jnp.float32) for grad in grads]
         + [jax.ShapeDtypeStruct(grad.shape[1:], jnp.bfloat16) for grad in grads]
-        + [jax.ShapeDtypeStruct((SUBLANES, LANES), jnp.float32)],
-        in_specs=[pl.BlockSpec(memory_space=pl.ANY)] * 2,
-        out_specs=[pl.BlockSpec(memory_space=pltpu.VMEM)] * 2
-        + [pl.BlockSpec(memory_space=pl.ANY)] * 2
+        + [jax.ShapeDtypeStruct(part.shape, part.dtype) for part in passing]
+        + [jax.ShapeDtypeStruct((SUBLANES, LANES), jnp.float32)]
+        + [jax.ShapeDtypeStruct(small.shape, jnp.float32)],
+        in_specs=[pl.BlockSpec(memory_space=pl.ANY)] * (kinds + carried)
         + [pl.BlockSpec(memory_space=pltpu.VMEM)],
+        out_specs=[pl.BlockSpec(memory_space=pltpu.VMEM)] * kinds
+        + [pl.BlockSpec(memory_space=pl.ANY)] * (kinds + carried)
+        + [pl.BlockSpec(memory_space=pltpu.VMEM)] * 2,
         scratch_shapes=room(places)
         + room(places)
         + room(GRID[0])
         + room(GRID[0])
         + room(GRID[0])
         + [pltpu.VMEM((piece[2], piece[4]), jnp.bfloat16) for piece in pieces]
-        + [pltpu.SemaphoreType.DMA(shape) for shape in sems],
+        + [pltpu.SemaphoreType.DMA(shape) for shape in sems]
+        + [
+            pltpu.VMEM(small.shape, jnp.float32),
+            pltpu.VMEM(slot, jnp.float32),
+            pltpu.VMEM(small.shape, jnp.float32),
+        ]
+        + [pltpu.SemaphoreType.DMA((count,))] * 4,
         compiler_params=pltpu.CompilerParams(
             collective_id=collective, has_side_effects=True, vmem_limit_bytes=VMEM_LIMIT
         ),
-        name="scatter_layer",
-    )(*grads)
-    return (own_upper, own_lower), (twin_upper, twin_lower), jnp.sum(squares)
+        name="scatter_grads",
+    )(*grads, *passing, small)
+    return (
+        arrays[:kinds],
+        arrays[kinds : 2 * kinds],
+        arrays[2 * kinds :],
+        jnp.sum(squares),
+        carve(total.reshape(-1), [value.shape for value in values]),
+    )
 
 
 def lay_out_kernel(shards, view_ref, *outs):
@@ -1051,6 +1132,59 @@
     return array.reshape(layers, size // LANES, LANES).transpose(1, 0, 2).reshape(-1, LANES)
 
 
+def unpack_kernel(size, x_ref, lead_ref, time_ref, text_ref, audio_ref, caption_ref, tail_ref, flat):
+    count, rows = x_ref.shape[:2]
+    lane = lax.broadcasted_iota(jnp.int32, (rows, LANES), 1)
+    for rank in range(count):
+        base, phase = divmod(rank * size, LANES)
+        shard = x_ref[rank].astype(jnp.float32)
+        if phase == 0:
+            flat[base : base + rows, :] = shard
+            continue
+        turned = pltpu.roll(shard, phase, axis=1)
+        pltpu.store(flat.at[pl.ds(base, rows), :], turned, mask=lane >= phase)
+        pltpu.store(flat.at[pl.ds(base + 1, rows), :], turned, mask=lane < phase)
+    start = lead_ref.shape[0]
+    lead_ref[...] = flat[:start, :]
+    for ref in (time_ref, text_ref, audio_ref, caption_ref):
+        across = ref.shape[1] // LANES
+        for row in range(0, ref.shape[0], ROW_GROUP):
+            for column in range(across):
+                ref[row : row + ROW_GROUP, column * LANES : (column + 1) * LANES] = flat[
+                    pl.ds(start + row * across + column, ROW_GROUP, stride=across), :
+                ].astype(jnp.bfloat16)
+        start += ref.shape[0] * across
+    tail_ref[...] = flat[start : start + tail_ref.shape[0], :]
+
+
+def unpack_others(gathered, size, channels, text_width):
+    count, rows, lanes = gathered.shape
+    lead = 2 * channels * D // LANES
+    shapes = [(D, D), (text_width, D), (D, E), (text_width, E)]
+    tail = (2 * L + 1 + 1) * D // LANES
+    whole = -(-count * size // LANES)
+    outs = pl.pallas_call(
+        functools.partial(unpack_kernel, size),
+        out_shape=[jax.ShapeDtypeStruct((lead, LANES), jnp.float32)]
+        + [jax.ShapeDtypeStruct(shape, jnp.bfloat16) for shape in shapes]
+        + [jax.ShapeDtypeStruct((tail, LANES), jnp.float32)],
+        in_specs=[pl.BlockSpec(memory_space=pltpu.VMEM)],
+        out_specs=[pl.BlockSpec(memory_space=pltpu.VMEM)] * 6,
+        scratch_shapes=[pltpu.VMEM((whole + 2 * rows, LANES), jnp.float32)],
+        compiler_params=pltpu.CompilerParams(vmem_limit_bytes=VMEM_LIMIT),
+        name="unpack_others",
+    )(gathered)
+    w_in, w_out = outs[0].reshape(2, channels * D)
+    tail_rows = outs[5].reshape(-1, D)
+    return (
+        w_in.reshape(channels, D).astype(jnp.bfloat16),
+        w_out.reshape(D, channels).astype(jnp.bfloat16),
+        *outs[1:5],
+        tail_rows[:-1],
+        tail_rows[-1],
+    )
+
+
 def lay_out(anchor, shards):
     if shards != math.prod(GRID):
         return [layer_rows(anchor[depth].astype(jnp.bfloat16), shards) for depth in range(L)]
@@ -1086,28 +1220,26 @@
     return adam(grad, first, second, anchor)[2]
 
 
-def step_kernel(cut, factors, *refs):
-    own, twin = refs[: 2 * L], refs[2 * L : 4 * L]
-    anchor, first, second, outer, twin_first, twin_second = refs[4 * L : 4 * L + 6]
-    new, one, two, mean_out, momentum_out, own_flat, twin_flat = refs[4 * L + 6 :]
+def step_kernel(cut, places, factors, *refs):
+    amount = len(places)
+    own, twin = refs[:amount], refs[amount : 2 * amount]
+    anchor, first, second, outer, twin_first, twin_second = refs[2 * amount : 2 * amount + 6]
+    new, one, two, mean_out, momentum_out, own_flat, twin_flat = refs[2 * amount + 6 :]
     step = pl.program_id(0)
     block = anchor.shape[0]
 
     @pl.when(step == 0)
     def _():
         for grads, flat in ((own, own_flat), (twin, twin_flat)):
-            for layer in range(L):
-                for ref, base in zip(grads[2 * layer : 2 * layer + 2], (0, cut)):
-                    across = ref.shape[1] // LANES
-                    for row in range(0, ref.shape[0], ROW_GROUP):
-                        for column in range(across):
-                            start = L * (base + row * across + column) + layer
-                            flat[pl.ds(start, ROW_GROUP, stride=L * across), :] = ref[
-                                row : row + ROW_GROUP, column * LANES : (column + 1) * LANES
-                            ].astype(jnp.float32)
-
-    def low(value):
-        return value.astype(jnp.bfloat16).astype(jnp.float32)
+            for ref, (layer, first_column) in zip(grads, places):
+                base, width = (cut, ref.shape[1]) if first_column is None else (0, 4 * D + FF)
+                across, skip = width // LANES, (first_column or 0) // LANES
+                for row in range(0, ref.shape[0], ROW_GROUP):
+                    for column in range(ref.shape[1] // LANES):
+                        start = L * (base + row * across + skip + column) + layer
+                        flat[pl.ds(start, ROW_GROUP, stride=L * across), :] = ref[
+                            row : row + ROW_GROUP, column * LANES : (column + 1) * LANES
+                        ].astype(jnp.float32)
 
     rows = pl.ds(pl.multiple_of(step * block, SUBLANES), block)
     grad, weight = own_flat[rows, :], anchor[...]
@@ -1115,14 +1247,10 @@
     clipped = grad * factors[0]
     one[...] = beta_one * first_own + (1.0 - beta_one) * clipped
     two[...] = beta_two * second_own + (1.0 - beta_two) * clipped * clipped
-    delta_own = delta_of(low(grad) * factors[0], low(first_own), low(second_own), weight)
-    delta_twin = delta_of(
-        twin_flat[rows, :] * factors[1],
-        twin_first[...].astype(jnp.float32),
-        twin_second[...].astype(jnp.float32),
-        weight,
-    )
-    mean = (delta_own + delta_twin) / 2
+    rounded = grad.astype(jnp.bfloat16).astype(jnp.float32)
+    delta_own = delta_of(rounded * factors[0], first_own, second_own, weight)
+    delta_twin = delta_of(twin_flat[rows, :] * factors[1], twin_first[...], twin_second[...], weight)
+    mean = (delta_own + delta_twin) * 0.5
     momentum = outer_mu * outer[...] + mean
     mean_out[...] = mean
     momentum_out[...] = momentum
@@ -1131,14 +1259,16 @@
 
 def step_layers(factors, own, twin, views, shards):
     rows = views[0].shape[0]
+    places = tuple((layer, column) for _, layer, column in own)
+    own = [grad for grad, _, _ in own]
     block = rows // STEP_BLOCKS
     whole = pl.BlockSpec(memory_space=pltpu.VMEM)
     part = pl.BlockSpec((block, LANES), lambda k: (k, 0))
     return pl.pallas_call(
-        functools.partial(step_kernel, D // shards * (4 * D + FF) // LANES),
+        functools.partial(step_kernel, D // shards * (4 * D + FF) // LANES, places),
         grid=(STEP_BLOCKS,),
         out_shape=[jax.ShapeDtypeStruct((rows, LANES), jnp.float32)] * 5,
-        in_specs=[pl.BlockSpec(memory_space=pltpu.SMEM)] + [whole] * (4 * L) + [part] * 6,
+        in_specs=[pl.BlockSpec(memory_space=pltpu.SMEM)] + [whole] * (2 * len(own)) + [part] * 6,
         out_specs=[part] * 5,
         scratch_shapes=[pltpu.VMEM((rows, LANES), jnp.float32)] * 2,
         compiler_params=pltpu.CompilerParams(
@@ -1194,7 +1324,7 @@
     early = L
     own_block = block_of(rank, close)
     frames = jnp.concatenate([latents, noise], axis=1).T
-    pieces = [frames, other_rows.reshape(-1, GATHER_LANES)]
+    pieces = [frames, other_rows.reshape(-1, LANES)]
     pieces += [part for pair in own_rows[:early] for part in pair]
     gathered_frames, other_rows, *early_rows = gather_pieces(
         pieces, [False, True] + [True, False] * early, 4
@@ -1204,15 +1334,17 @@
         sources, other_rows = lax.optimization_barrier(
             ((first_view, second_view, first_other[0], second_other[0]), other_rows)
         )
-        twin_views = [swapped(value.astype(jnp.bfloat16)) for value in sources[:2]]
-        twin_moments = [swapped(value.astype(jnp.bfloat16)).astype(jnp.float32) for value in sources[2:]]
+        twin_views = [swapped(value) for value in sources[:2]]
+        twin_moments = [swapped(value) for value in sources[2:]]
     late_rows = [lax.all_gather(part, "seq", axis=0) for pair in own_rows[early:] for part in pair]
     layer_parts = [part.reshape(-1, part.shape[-1]) for part in early_rows + late_rows]
     gathered = [split_upper(*layer_parts[2 * depth : 2 * depth + 2]) for depth in range(L)]
-    other_low = other_rows.reshape(seq_count, padded)[:, :other_size].reshape(-1)
-    w_in, w_out, w_time, w_text, w_audio, w_caption, gains, null_text = carve(
-        other_low, other_shapes(channels, D, text_width, E, L)
-    )
+    if close:
+        other_parts = unpack_others(other_rows, other_size, channels, text_width)
+    else:
+        other_low = other_rows.reshape(seq_count, padded)[:, :other_size].reshape(-1)
+        other_parts = carve(other_low, other_shapes(channels, D, text_width, E, L))
+    w_in, w_out, w_time, w_text, w_audio, w_caption, gains, null_text = other_parts
     w_time_f = w_time.astype(jnp.float32)
     w_text_f = w_text.astype(jnp.float32)
     w_audio_f = w_audio.astype(jnp.float32)
@@ -1284,16 +1416,21 @@
     unused, pull_final = jax.vjp(norm_rows, hidden, gains_f[2 * L])
     grad_hidden, grad_gain_final = pull_final(grad_final)
     layer_grads = [None] * L
-    own_grads = [None] * L
-    twin_grads = [None] * L
+    sent_early = [None] * L
     gain_grads = [None] * (2 * L + 1)
     gain_grads[2 * L] = grad_gain_final
     for depth in reversed(range(L)):
         weights = gathered[depth]
         proj_qkv = weights[0]
-        grad_middle, grad_query, grad_pairs, operand_pairs, gain_grads[2 * depth + 1] = layer_backward(
-            grad_hidden, weights, gains_f[2 * depth + 1], items, saved_all[depth]
-        )
+        early = depth > 0 and close
+        grad_middle, grad_query, grad_pairs, rest, lower_full, gain_grads[2 * depth + 1] = layer_backward(
+            grad_hidden, weights, gains_f[2 * depth + 1], items, saved_all[depth], early
+        )
+        if early:
+            sent_early[depth] = [
+                lax.psum_scatter(grad, "seq", scatter_dimension=0, tiled=True)
+                for grad in (lower_full, rest)
+            ]
         normed = saved_all[depth][0]
         if depth == 0:
             qkv_parts = [(normed, grad_query), (normed_window, grad_pairs)]
@@ -1310,78 +1447,83 @@
             grad_normed = against_rows(grad_projected, proj_qkv)
             unused, pull_one = jax.vjp(norm_rows, entering[depth], gains_f[2 * depth])
         grad_input, gain_grads[2 * depth] = pull_one(grad_normed)
-        layer_grads[depth] = layer_gradients(qkv_parts, operand_pairs)
+        if early:
+            layer_grads[depth] = [side_by_side(qkv_parts)]
+        else:
+            layer_grads[depth] = [side_by_side(qkv_parts + rest), lower_full]
         if depth > 0:
             grad_hidden = grad_middle + grad_input
-            if close:
-                grad_hidden, layer_grads[depth] = lax.optimization_barrier(
-                    (grad_hidden, layer_grads[depth])
-                )
         else:
             grad_hidden = jnp.concatenate(
                 [grad_input[: 2 * rows], grad_input[inner] + grad_middle, grad_input[3 * rows :]], axis=0
             )
-        if depth > 0 and close:
-            own_grads[depth] = [
-                lax.psum_scatter(grad, "seq", scatter_dimension=0, tiled=True)
-                for grad in layer_grads[depth]
-            ]
     grad_w_in = contract_rows(noisy_low.astype(jnp.float32), grad_hidden, HIGH)
     grad_condition = contract_rows(window_hot, grad_hidden, HIGH)
-    grad_w_in, grad_w_out, grad_condition, gain_rows = sum_over_seq(
-        (grad_w_in, grad_w_out, grad_condition, jnp.stack(gain_grads)), 2
-    )
-    grad_before = pull_silu(grad_condition)[0]
-    grad_null = jnp.sum(
-        jnp.where(null_flags[:, None] == 1, against_rows(grad_before, w_text_f, HIGH), 0.0), axis=0
-    )
-    straight = jnp.concatenate([grad_w_in, grad_w_out.T.reshape(channels, D), gain_rows, grad_null[None]])
     lead = 2 * channels
-    identity = jnp.eye(straight.shape[0], dtype=jnp.float32)
     features_at, text_at = lead, lead + D
     audio_at = text_at + text_width
     caption_at = audio_at + D * E // D
     gains_at = caption_at + text_width * E // D
-    view_rows = gains_at + gain_rows.shape[0] + 1
-
-    def placed_left(value, start):
-        return jnp.pad(value, ((0, 0), (start, view_rows - start - value.shape[1])))
-
-    left = jnp.concatenate(
-        [
-            placed_left(identity[:, :lead], 0) + placed_left(identity[:, lead:], gains_at),
-            placed_left(features, features_at),
-            placed_left(text, text_at),
-            placed_left(thirds_left(pooled), audio_at),
-            placed_left(thirds_left(captions), caption_at),
-        ],
-        axis=0,
-    )
-    right = jnp.concatenate(
-        [
-            straight,
-            grad_before,
-            grad_before,
-            thirds_right(grad_audio_side),
-            thirds_right(grad_text_side),
-        ],
-        axis=0,
-    )
     own_rows_count = -(-other_size // D) + 1
-    left = jnp.pad(left, ((0, 0), (0, own_rows_count)))
     own_start = rank * other_size
-    own_left = lax.dynamic_slice_in_dim(left, own_start // D, own_rows_count, axis=1)
-    own_view = contract_rows(own_left, right, HIGH)
+    own_row = own_start // D
+    own_at = own_row + jnp.arange(own_rows_count, dtype=jnp.int32)
+
+    def own_part(value, start):
+        reach = gains_at + 2 * own_rows_count
+        value = jnp.pad(value, ((0, 0), (start, reach - start - value.shape[1])))
+        return lax.dynamic_slice_in_dim(value, own_row, own_rows_count, axis=1)
+
+    def own_rows_at(start, amount):
+        there = start + jnp.arange(amount, dtype=jnp.int32)
+        return (there[:, None] == own_at[None, :]).astype(jnp.float32)
+
+    left_condition = own_part(features, features_at) + own_part(text, text_at)
+    early_view = thirds(pooled, grad_audio_side, own_at - audio_at)
+    early_view = early_view + thirds(captions, grad_text_side, own_at - caption_at)
+    early_view, left_condition, layer_grads[0] = lax.optimization_barrier(
+        (early_view, left_condition, layer_grads[0])
+    )
+    small_grads = (grad_w_in, grad_w_out, grad_condition, jnp.stack(gain_grads))
+    if close:
+        sent = sent_early[1:]
+        late = [layer_grads[depth][0] for depth in range(1, L)] + list(layer_grads[0])
+        own_late, twin_late, passed, square_part, small_grads = scatter_grads(
+            late,
+            [1] * (L - 1) + [UPPER_CUTS, 1],
+            [part for parts in sent for part in parts],
+            small_grads,
+            5,
+        )
+        own_parts = [(own_late[L - 1], 0, 0), (own_late[L], 0, None)]
+        twin_parts = [twin_late[L - 1], twin_late[L]]
+        for depth in range(1, L):
+            lower, rest = sent[depth - 1]
+            own_parts += [(own_late[depth - 1], depth, 0), (rest, depth, 3 * D), (lower, depth, None)]
+            twin_parts += [twin_late[depth - 1], passed[2 * depth - 1], passed[2 * depth - 2]]
+    else:
+        small_grads = lax.psum(small_grads, "seq")
+    grad_w_in, grad_w_out, grad_condition, gain_rows = small_grads
+    grad_before = pull_silu(grad_condition)[0]
+    grad_null = jnp.sum(
+        jnp.where(null_flags[:, None] == 1, against_rows(grad_before, w_text_f, HIGH), 0.0), axis=0
+    )
+    own_view = early_view + contract_rows(left_condition, grad_before, HIGH)
+    for value, start in (
+        (grad_w_in, 0),
+        (grad_w_out.T.reshape(channels, D), channels),
+        (gain_rows, gains_at),
+        (grad_null[None], gains_at + gain_rows.shape[0]),
+    ):
+        own_view = own_view + contract_rows(own_rows_at(start, value.shape[0]), value, HIGH)
     other_grad = lax.dynamic_slice_in_dim(own_view.reshape(-1), own_start % D, other_size)
     other_grad_square = jnp.sum(other_grad * other_grad)
     if close:
         other_grad_low = other_grad.astype(jnp.bfloat16)
         twin_other = swapped(other_grad_low).astype(jnp.float32)
-        own_grads[0], twin_grads[0], square_part = scatter_layer(*layer_grads[0], 5)
         square_part = square_part + other_grad_square
-        for depth in range(1, L):
-            twin_grads[depth] = [swapped(grad) for grad in own_grads[depth]]
-            for grad in own_grads[depth]:
+        for parts in sent:
+            for grad in parts:
                 wide = grad.astype(jnp.float32)
                 square_part = square_part + jnp.sum(wide * wide)
         norms = jnp.sqrt(sums_by_group(square_part, 3))
@@ -1392,18 +1534,15 @@
         views = [flat_view(anchor_layers), first_view, second_view, flat_view(outer_layers)]
         stepped = step_layers(
             jnp.stack([factor, twin_factor]),
-            [part for grads in own_grads for part in grads],
-            [part for grads in twin_grads for part in grads],
+            own_parts,
+            twin_parts,
             views + twin_views,
             seq_count,
         )
         new_layers, first_l, second_l, mean_layers, momentum_layers = map(from_view, stepped)
         first_o, second_o, _ = adam(other_grad * factor, first_other[0], second_other[0], anchor_other)
-
-        def low(value):
-            return lax.reduce_precision(value, 8, 7)
-
-        delta_o = delta_of(low(other_grad) * factor, low(first_other[0]), low(second_other[0]), anchor_other)
+        rounded = lax.reduce_precision(other_grad, 8, 7)
+        delta_o = delta_of(rounded * factor, first_other[0], second_other[0], anchor_other)
         delta_twin = delta_of(twin_other * twin_factor, *twin_moments, anchor_other)
         mean_other = (delta_o + delta_twin) / 2
     else:

time: 762 us -> 697 us (0.915)
  local copies, waits for them, and re-layouts: 104 us -> 62.1 us
  waiting for transfers between devices: 39.7 us -> 24.5 us
  Pallas kernels: 381 us -> 370 us
  matrix products: 122 us -> 131 us
    pallas_call x2 -> x1, Pallas kernels: 27.5 us -> 11.8 us  [sum_over_seq(): pl.pallas_call(functools.partial(sum_kernel, count), out_shape=jax.ShapeD...]
    slice x11 -> x5, local copies, waits for them, and re-layouts: 18.6 us -> 3.39 us  [carve(): pieces.append(flat[start:start + count].reshape(shape))]
    ppermute x7 -> x5, waiting for transfers between devices: 13.8 us -> 0.01 us  [swapped(): return lax.ppermute(value, 'grp', [(0, 1), (1, 0)])]
    pallas_call x1 -> x2, Pallas kernels: 117 us -> 129 us  [the longest x1 125 us: scatter_grads(): pl.pallas_call(functools.partial(scatter_kernel, tuple(pieces), kinds, ca...]
    concatenate x8 -> x0, local copies, waits for them, and re-layouts: 11.3 us -> none  [the longest x1 6.51 us: per_device(): jnp.concatenate([placed_left(identity[:, :lead], 0) + placed_left(identit...]
    ppermute x8, waiting for transfers between devices: 25.8 us -> 15.1 us  [passed_along(): lax.ppermute(value, axis, [(holder[source], holder[source + steps]) for s...]
    unnamed x348 -> x328, local copies, waits for them, and re-layouts: 35.4 us -> 26.1 us
    reduce_scatter x2, waiting for transfers between devices: 0.02 us -> 9.3 us  [per_device(): lax.psum_scatter(grad, 'seq', scatter_dimension=0, tiled=True)]
  transfers between devices with their start and end apart: 17 -> 15, of which waited for: 5 -> 4; matrix products, arithmetic and copies ran while one was open for 20% -> 26% of each run, Pallas kernels for 22% -> 31%
where the time goes in v5:
time: 697 us; the launch traced here: 688 us
  Pallas kernels  370 us (53%)
  matrix products  131 us (19%)
  local copies, waits for them, and re-layouts  62.1 us (9%)
  other arithmetic  49.8 us (7%)
  starting transfers between devices  26.9 us (4%)
  waiting for transfers between devices  24.5 us (4%)
  between operations  23.9 us (3%)
    pallas_call x1, Pallas kernels, gather_pieces(): pl.pallas_call(functools.partial(gather_kernel, tuple(shared)), out_shape...  136 us
    pallas_call x1, Pallas kernels, scatter_grads(): pl.pallas_call(functools.partial(scatter_kernel, tuple(pieces), kinds, ca...  125 us
    dot_general x17, matrix products, contract_rows(): lax.dot_general(left, right, (((0,), (0,)), ((), ())), precision=precisio...  40 us
    dot_general x12, matrix products, dense(): return jnp.dot(left, right, preferred_element_type=jnp.float32)  36.6 us
    dot_general x12, matrix products, against_rows(): lax.dot_general(left, right, (((1,), (1,)), ((), ())), precision=precisio...  35.2 us
    pallas_call x2, Pallas kernels, attend_backward(): pl.pallas_call(attend_backward_kernel, out_shape=(jax.ShapeDtypeStruct((r...  33.2 us
    unnamed x328, local copies, waits for them, and re-layouts  26.1 us
    pallas_call x2, Pallas kernels, attend_forward(): pl.pallas_call(attend_forward_kernel, out_shape=(jax.ShapeDtypeStruct((ro...  24.2 us
  transfers between devices with their start and end apart: 15, of which 4 were waited for; matrix products, arithmetic and copies ran while one was open for 26% of the time, Pallas kernels for 31%

profile of v5, /device:TPU:0, one launch (start us, length us, event | category | flops | bytes accessed | tf_op | source)
XLA Modules:
  0.0 688.3 jit_solution(13129507559380952778)
XLA Ops:
  8.8 3.5 lay_out.1
  15.9 2.1 reduce.2
  18.0 2.1 reduce.3
  20.7 136.0 %gather_pieces.1 = (f32[16,40,256]{2,1,0:T(8,128)}, bf16[16,992,128]{2,1,0:T(8,128)(2,1)}, bf16[16,48,6144]{2,1,0:T(8,128)(2,1)}, bf16[16,192,768]{2,1,0:T(8,128...) custom-call(f32[40,256]{1,0:T(8,128)} %maximum_bitcast_fusion.refs_0_, ...), custom_call_target="tpu_custom_call" | custom-call | tf_op jit(solution)/shard_map/gather_pieces/pallas_call | solution.py:746
  156.7 4.0 unpack_others.1
  169.1 2.0 fusion.190
  172.0 8.0 %convolution_convert_fusion.kv_ref = bf16[1280,1536]{1,0:T(8,128)(2,1)} fusion(bf16[1280,768]{0,1:T(8,128)(2,1)S(1)} %multiply_convert_fusion, bf16[768,6144]{1,0:T(8,128)(2,1)} %bitcast.204), kind=kOutput, calls=%fused_computation.1 | convolution fusion | flops 3021864960 | bytes 8257536 | tf_op jit(solution)/shard_map/dot_general | solution.py:51
  182.2 12.1 %attend_forward.2 = (bf16[256,768]{1,0:T(8,128)(2,1)S(1)}, f32[16,256]{1,0:T(8,128)S(1)}) custom-call(bf16[256,768]{1,0:T(8,128)(2,1)S(1)} %convolution_convert_fusion.14.q_ref, bf16[1280,1536]{1,0:T(8,128)(2,1)} %convolution_convert_fusion.kv_ref, s32[1,256]{1,0:T(1,128)S(1)} %bitcast.186, s32[1280,1]{1,0:T(8,128)S(1)} %reshape_select_fusion.key_item_ref), custom_call_target="tpu_custom_call" | custom-call | flops 1006632960 | bytes 4718592 | tf_op jit(solution)/shard_map/attend_forward/pallas_call | solution.py:198
  196.4 4.3 fusion.6
  200.8 2.7 fusion.192
  204.3 3.4 convolution_convert_fusion.7
  207.7 3.6 collective-permute-start
  211.3 2.9 collective-permute-start.1
  216.7 2.1 collective-permute-start.10
  218.8 2.5 convolution_convert_fusion.13.q_ref
  235.0 8.9 %collective-permute-done.3 = bf16[256,1536]{1,0:T(8,128)(2,1)} collective-permute-done((bf16[256,1536]{1,0:T(8,128)(2,1)}, bf16[256,1536]{1,0:T(8,128)(2,1)}, u32[]{:S(2)}, u32[]{:S(2)}) %collective-permute-start.3) | collective-permute-done | bytes 786464 | tf_op jit(solution)/shard_map/ppermute | solution.py:45
  247.0 12.1 %attend_forward.3 = (bf16[256,768]{1,0:T(8,128)(2,1)S(1)}, f32[16,256]{1,0:T(8,128)S(1)}) custom-call(bf16[256,768]{1,0:T(8,128)(2,1)S(1)} %copy-done.18, bf16[1280,1536]{1,0:T(8,128)(2,1)} %copy-done.75, s32[1,256]{1,0:T(1,128)S(1)} %bitcast.187, s32[1280,1]{1,0:T(8,128)S(1)} %copy-done.7), custom_call_target="tpu_custom_call" | custom-call | flops 1006632960 | bytes 4718592 | tf_op jit(solution)/shard_map/attend_forward/pallas_call | solution.py:198
  259.1 2.0 fusion.193
  261.3 4.4 fusion.2
  265.8 2.5 fusion.194
  270.1 2.0 fusion.48
  273.5 2.5 multiply_reduce_fusion.23
  276.0 2.1 fusion.104.x_ref
  278.2 11.8 %sum_over_seq.1 = f32[16,8,128]{2,1,0:T(8,128)} custom-call(f32[16,8,128]{2,1,0:T(8,128)} %fusion.104.x_ref), custom_call_target="tpu_custom_call" | custom-call | flops 16384 | bytes 262144 | tf_op jit(solution)/shard_map/sum_over_seq/pallas_call | solution.py:449
  297.7 2.3 multiply_reduce_fusion.18
  302.8 2.1 multiply_reduce_fusion.3
  306.4 4.4 convolution_convert_fusion.1
  310.9 2.5 fusion.36
  313.4 2.3 iota_compare_fusion.2
  315.7 7.2 %fusion.23 = bf16[256,3072]{1,0:T(8,128)(2,1)S(1)} fusion(f32[256,3072]{1,0:T(8,128)} %copy-done.148, bf16[3072,768]{1,0:T(8,128)(2,1)} %bitcast.224, f32[256,768]{0,1:T(8,128)S(1)} %get-tuple-element.139, f32[256]{0:T(256)} %copy-done.124), kind=kOutput, calls=%fused_computation.44 | convolution fusion | flops 1224081408 | bytes 10224640 | tf_op jit(solution)/shard_map/dot_general | solution.py:69
  322.9 4.1 multiply_reduce_fusion.9
  332.3 2.9 pad_maximum_fusion.1
  335.2 16.6 %attend_backward.2 = (bf16[256,768]{1,0:T(8,128)(2,1)S(1)}, bf16[1280,1536]{1,0:T(8,128)(2,1)}) custom-call(bf16[256,768]{1,0:T(8,128)(2,1)S(1)} %copy-done.19, bf16[1280,1536]{1,0:T(8,128)(2,1)} %copy-done.75, bf16[256,768]{1,0:T(8,128)(2,1)S(1)} %convolution_convert_fusion.12.do_ref, f32[16,256]{1,0:T(8,128)S(1)} %get-tuple-element.82.lse_ref, ...), custom_call_target="tpu_custom_call" | custom-call | flops 2516582400 | bytes 9437184 | tf_op jit(solution)/shard_map/attend_backward/pallas_call | solution.py:255
  351.9 3.7 fusion.184
  358.2 4.0 collective-permute-start.6
  362.2 4.5 collective-permute-start.7
  373.6 2.0 fusion.37
  377.4 2.0 collective-permute-start.12
  379.4 2.0 collective-permute-start.9
  381.4 5.9 collective-permute-done.7
  387.3 2.6 add_convert_fusion
  390.0 3.6 multiply_reduce_fusion.5
  395.6 3.5 fusion.16
  402.1 16.6 %attend_backward.3 = (bf16[256,768]{1,0:T(8,128)(2,1)S(1)}, bf16[1280,1536]{1,0:T(8,128)(2,1)}) custom-call(bf16[256,768]{1,0:T(8,128)(2,1)S(1)} %copy-done.21, bf16[1280,1536]{1,0:T(8,128)(2,1)} %convolution_convert_fusion.kv_ref, bf16[256,768]{1,0:T(8,128)(2,1)S(1)} %convolution_convert_fusion.11.do_ref, f32[16,256]{1,0:T(8,128)S(1)} %get-tuple-element.85.lse_ref, ...), custom_call_target="tpu_custom_call" | custom-call | flops 2516582400 | bytes 9437184 | tf_op jit(solution)/shard_map/attend_backward/pallas_call | solution.py:255
  418.8 6.5 fusion.27
  430.1 1.9 fusion.177
  437.6 2.5 convolution_convert_fusion.9
  440.2 2.4 copy.132
  442.6 2.6 convolution_convert_fusion.8
  445.2 2.4 copy.133
  447.6 3.0 convolution_convert_fusion.3
  450.8 3.6 convolution_convert_fusion.6
  454.5 6.9 %pad_maximum_fusion = bf16[768,6144]{1,0:T(8,128)(2,1)} fusion(bf16[768,3072]{1,0:T(8,128)(2,1)S(1)} %convolution_convert_fusion.3, bf16[768,768]{1,0:T(8,128)(2,1)S(1)} %copy-done.39, bf16[768,1536]{1,0:T(8,128)(2,1)S(1)} %convolution_convert_fusion.6, bf16[768,768]{1,0:T(8,128)(2,1)S(1)} %copy-done.38), kind=kLoop, calls=%fused_computation | loop fusion | flops 37748736 | bytes 18874368 | tf_op jit(solution)/shard_map/concatenate | solution.py:309
  461.4 2.1 fusion.24
  463.7 6.4 convolution_convert_fusion.2
  470.1 2.9 convolution_convert_fusion.4
  474.8 9.3 %reduce-scatter.5.cloned.1.call-done.refs_4_.refs_3_ = bf16[48,3840]{1,0:T(8,128)(2,1)} async-done(((bf16[768,3840]{1,0:T(8,128)(2,1)}), bf16[48,3840]{1,0:T(8,128)(2,1)}) %reduce-scatter.5.cloned.1.call-update) | async-done | bytes 368656 | tf_op jit(solution)/shard_map/reduce_scatter | solution.py:1431
  486.0 124.8 %scatter_grads.1 = (f32[48,2304]{1,0:T(8,128)S(1)}, f32[48,6144]{1,0:T(8,128)}, f32[192,768]{1,0:T(8,128)S(1)}, bf16[48,2304]{1,0:T(8,128)(2,1)S(1)}, bf16[48,61...) custom-call(bf16[16,48,2304]{2,1,0:T(8,128)(2,1)} %bitcast.191, ...), custom_call_target="tpu_custom_call" | custom-call | tf_op jit(solution)/shard_map/scatter_grads/pallas_call | solution.py:1076
  617.6 1.9 fusion.40
  623.9 2.1 fusion.33
  627.8 1.9 dynamic_slice.58
  636.8 10.5 %share_over_all.1 = f32[32,8,128]{2,1,0:T(8,128)} custom-call(f32[8,128]{1,0:T(8,128)} %broadcast_in_dim.196.x_ref), custom_call_target="tpu_custom_call" | custom-call | tf_op jit(solution)/shard_map/share_over_all/pallas_call | solution.py:514
  651.7 22.0 %step_layers.1 = (f32[6912,128]{1,0:T(8,128)}, f32[6912,128]{1,0:T(8,128)}, f32[6912,128]{1,0:T(8,128)}, f32[6912,128]{1,0:T(8,128)}, f32[6912,128]{1,0:T(8,128)}) custom-call(f32[2]{0:T(128)S(1)} %pad_maximum_fusion.10.factors, f32[48,6144]{1,0:T(8,128)} %get-tuple-element.95.refs_0_, f32[192,768]{1,0:T(8,128)S(1)} %get-tuple-element.96.refs_1_, ...), custom_call_target="tpu_custom_call" | custom-call | tf_op jit(solution)/shard_map/step_layers/pallas_call | solution.py:1267
  673.8 3.8 multiply_subtract_fusion
  (515 shorter events, 110.4 us)
Async XLA Ops:
  7.2 465.8 %reduce-scatter.3.cloned.1.call-start = ((), (), s32[]{:S(2)}) async-start(), calls=%async_computation.2 | async-start | bytes 5013504 | tf_op jit(solution)/shard_map/reduce_scatter | solution.py:1431
  8.8 11.3 %copy-start.104 = (f32[256,20]{0,1:T(8,128)S(1)}, f32[256,20]{0,1:T(8,128)}, u32[]{:S(2)}) copy-start(f32[256,20]{0,1:T(8,128)} %param.23) | copy-start | bytes 61444
  8.8 11.3 %copy-start.105 = (f32[256,20]{0,1:T(8,128)S(1)}, f32[256,20]{0,1:T(8,128)}, u32[]{:S(2)}) copy-start(f32[256,20]{0,1:T(8,128)} %param.22) | copy-start | bytes 61444
  15.3 153.7 %copy-start.83 = (s32[1280]{0:T(1024)}, s32[1280]{0:T(1024)S(1)}, u32[]{:S(2)}) copy-start(s32[1280]{0:T(1024)S(1)} %and_select_fusion) | copy-start | bytes 15364
  20.7 142.2 %copy-start.142 = (s32[1,12]{1,0:T(1,128)S(1)}, s32[1,12]{1,0:T(1,128)}, u32[]{:S(2)}) copy-start(s32[1,12]{1,0:T(1,128)} %param.26) | copy-start | bytes 148
  162.9 40.7 %copy-start.89 = (f32[768]{0:T(1024)}, f32[768]{0:T(1024)S(1)}, u32[]{:S(2)}) copy-start(f32[768]{0:T(1024)S(1)} %get-tuple-element.164) | copy-start | bytes 9220
  171.0 23.3 %copy-start.22 = (f32[1280,768]{0,1:T(8,128)}, f32[1280,768]{0,1:T(8,128)S(1)}, u32[]{:S(2)}) copy-start(f32[1280,768]{0,1:T(8,128)S(1)} %get-tuple-element.175) | copy-start | bytes 11796484
  181.8 12.5 %copy-start.20 = (bf16[256,768]{1,0:T(8,128)(2,1)}, bf16[256,768]{1,0:T(8,128)(2,1)S(1)}, u32[]{:S(2)}) copy-start(bf16[256,768]{1,0:T(8,128)(2,1)S(1)} %convolution_convert_fusion.14.q_ref) | copy-start | bytes 1179652
  182.1 12.3 %copy-start.6 = (s32[1280,1]{1,0:T(8,128)}, s32[1280,1]{1,0:T(8,128)S(1)}, u32[]{:S(2)}) copy-start(s32[1280,1]{1,0:T(8,128)S(1)} %reshape_select_fusion.key_item_ref) | copy-start | bytes 15364
  203.4 17.9 %copy-start.33 = (f32[256,768]{0,1:T(8,128)}, f32[256,768]{0,1:T(8,128)S(1)}, u32[]{:S(2)}) copy-start(f32[256,768]{0,1:T(8,128)S(1)} %get-tuple-element.179) | copy-start | bytes 2359300
  203.8 15.0 %copy-start.40 = (bf16[256,768]{0,1:T(8,128)(2,1)}, bf16[256,768]{0,1:T(8,128)(2,1)S(1)}, u32[]{:S(2)}) copy-start(bf16[256,768]{0,1:T(8,128)(2,1)S(1)} %multiply_convert_fusion.4) | copy-start | bytes 1179652
  203.8 17.5 %copy-start.144 = (s32[1,12]{1,0:T(1,128)S(1)}, s32[1,12]{1,0:T(1,128)}, u32[]{:S(2)}) copy-start(s32[1,12]{1,0:T(1,128)} %param.24) | copy-start | bytes 148
  203.8 18.1 %copy-start.92 = (f32[768]{0:T(1024)S(1)}, f32[768]{0:T(1024)}, u32[]{:S(2)}) copy-start(f32[768]{0:T(1024)} %copy-done.91) | copy-start | bytes 9220
  203.9 18.1 %copy-start.122 = (pred[12]{0:T(512)(128)(4,1)S(1)}, pred[12]{0:T(512)(128)(4,1)}, u32[]{:S(2)}) copy-start(pred[12]{0:T(512)(128)(4,1)} %copy-done.121) | copy-start | bytes 40
  203.9 18.2 %copy-start.69 = (f32[12,384]{1,0:T(8,128)S(1)}, f32[12,384]{1,0:T(8,128)}, u32[]{:S(2)}) copy-start(f32[12,384]{1,0:T(8,128)} %copy-done.68) | copy-start | bytes 55300
  203.9 18.2 %copy-start.71 = (f32[12,384]{1,0:T(8,128)S(1)}, f32[12,384]{1,0:T(8,128)}, u32[]{:S(2)}) copy-start(f32[12,384]{1,0:T(8,128)} %copy-done.70) | copy-start | bytes 55300
  204.2 19.5 %copy-start.5 = (bf16[768,512]{1,0:T(8,128)(2,1)S(1)}, bf16[768,512]{1,0:T(8,128)(2,1)}, u32[]{:S(2)}) copy-start(bf16[768,512]{1,0:T(8,128)(2,1)} %copy-done.4) | copy-start | bytes 2359300
  204.2 22.5 %copy-start.84 = (s32[1280]{0:T(1024)S(1)}, s32[1280]{0:T(1024)}, u32[]{:S(2)}) copy-start(s32[1280]{0:T(1024)} %copy-done.83) | copy-start | bytes 15364
  204.2 24.0 %copy-start.78 = (bf16[120,128]{1,0:T(8,128)(2,1)S(1)}, bf16[120,128]{1,0:T(8,128)(2,1)}, u32[]{:S(2)}) copy-start(bf16[120,128]{1,0:T(8,128)(2,1)} %get-tuple-element.152) | copy-start | bytes 92164
  207.7 22.5 %collective-permute-start = (bf16[256,1536]{1,0:T(8,128)(2,1)}, bf16[256,1536]{1,0:T(8,128)(2,1)}, u32[]{:S(2)}, u32[]{:S(2)}) collective-permute-start(bf16[256,1536]{1,0:T(8,128)(2,1)} %convolution_convert_fusion.7), channel_id=1, source_target_pairs={{0,2},{1,3},{2,6},{3,7},{6,4},{7,5},{4,8},{5,9},{8,10},{9,11},{10,... | collective-permute-start | bytes 2359304 | tf_op jit(solution)/shard_map/ppermute | solution.py:45
  211.3 20.0 %collective-permute-start.1 = (bf16[256,1536]{1,0:T(8,128)(2,1)}, bf16[256,1536]{1,0:T(8,128)(2,1)}, u32[]{:S(2)}, u32[]{:S(2)}) collective-permute-start(bf16[256,1536]{1,0:T(8,128)(2,1)} %convolution_convert_fusion.7), channel_id=1, source_target_pairs={{0,1},{1,2},{2,3},{3,6},{6,7},{7,4},{4,5},{5,8},{8,9},{9,10},{10,1... | collective-permute-start | bytes 2359304 | tf_op jit(solution)/shard_map/ppermute | solution.py:45
  214.2 19.7 %collective-permute-start.2 = (bf16[256,1536]{1,0:T(8,128)(2,1)}, bf16[256,1536]{1,0:T(8,128)(2,1)}, u32[]{:S(2)}, u32[]{:S(2)}) collective-permute-start(bf16[256,1536]{1,0:T(8,128)(2,1)} %convolution_convert_fusion.7), channel_id=1, source_target_pairs={{1,0},{2,1},{3,2},{6,3},{7,6},{4,7},{5,4},{8,5},{9,8},{10,9},{11,1... | collective-permute-start | bytes 2359304 | tf_op jit(solution)/shard_map/ppermute | solution.py:45
  215.4 28.5 %collective-permute-start.3 = (bf16[256,1536]{1,0:T(8,128)(2,1)}, bf16[256,1536]{1,0:T(8,128)(2,1)}, u32[]{:S(2)}, u32[]{:S(2)}) collective-permute-start(bf16[256,1536]{1,0:T(8,128)(2,1)} %convolution_convert_fusion.7), channel_id=1, source_target_pairs={{2,0},{3,1},{6,2},{7,3},{4,6},{5,7},{8,4},{9,5},{10,8},{11,9},{14,... | collective-permute-start | bytes 2359304 | tf_op jit(solution)/shard_map/ppermute | solution.py:45
  216.7 457.0 %collective-permute-start.10 = (f32[125088]{0:T(1024)}, f32[125088]{0:T(1024)}, u32[]{:S(2)}, u32[]{:S(2)}) collective-permute-start(f32[125088]{0:T(1024)} %reduce.2), channel_id=1, source_target_pairs={{0,16},{16,0},{1,17},{17,1},{2,18},{18,2},{3,19},{19,3},{4,20},{20... | collective-permute-start | bytes 1501064 | tf_op jit(solution)/shard_map/ppermute | solution.py:1287
  231.3 15.7 %copy-start.7 = (s32[1280,1]{1,0:T(8,128)S(1)}, s32[1280,1]{1,0:T(8,128)}, u32[]{:S(2)}) copy-start(s32[1280,1]{1,0:T(8,128)} %copy-done.6) | copy-start | bytes 15364
  231.3 15.7 %copy-start.18 = (bf16[256,768]{1,0:T(8,128)(2,1)S(1)}, bf16[256,768]{1,0:T(8,128)(2,1)}, u32[]{:S(2)}) copy-start(bf16[256,768]{1,0:T(8,128)(2,1)} %convolution_convert_fusion.13.q_ref) | copy-start | bytes 1179652
  247.0 12.1 %copy-start.34 = (f32[256,768]{0,1:T(8,128)S(1)}, f32[256,768]{0,1:T(8,128)}, u32[]{:S(2)}) copy-start(f32[256,768]{0,1:T(8,128)} %copy-done.33) | copy-start | bytes 2359300
  268.3 26.0 %copy-start.76 = (f32[12,512]{1,0:T(8,128)S(1)}, f32[12,512]{1,0:T(8,128)}, u32[]{:S(2)}) copy-start(f32[12,512]{1,0:T(8,128)} %get-tuple-element.187) | copy-start | bytes 73732
  310.8 173.2 %reduce-scatter.5.cloned.1.call-start = ((), (), s32[]{:S(2)}) async-start(), calls=%async_computation.3 | async-start | bytes 6266880 | tf_op jit(solution)/shard_map/reduce_scatter | solution.py:1431
  351.8 14.9 %copy-start.139 = (f32[12]{0:T(128)S(1)}, f32[12]{0:T(128)}, u32[]{:S(2)}) copy-start(f32[12]{0:T(128)} %copy-done.138) | copy-start | bytes 148
  351.8 14.9 %copy-start.145 = (f32[12]{0:T(128)S(1)}, f32[12]{0:T(128)}, u32[]{:S(2)}) copy-start(f32[12]{0:T(128)} %get-tuple-element.123) | copy-start | bytes 148
  351.8 14.9 %copy-start.77 = (f32[12,512]{1,0:T(8,128)S(1)}, f32[12,512]{1,0:T(8,128)}, u32[]{:S(2)}) copy-start(f32[12,512]{1,0:T(8,128)} %get-tuple-element.187) | copy-start | bytes 73732
  351.8 14.9 %copy-start.97 = (f32[12,512]{1,0:T(8,128)S(1)}, f32[12,512]{1,0:T(8,128)}, u32[]{:S(2)}) copy-start(f32[12,512]{1,0:T(8,128)} %get-tuple-element.191) | copy-start | bytes 73732
  351.8 14.9 %copy-start.140 = (f32[12]{0:T(128)S(1)}, f32[12]{0:T(128)}, u32[]{:S(2)}) copy-start(f32[12]{0:T(128)} %add_rsqrt_fusion.1) | copy-start | bytes 148
  351.9 15.7 %copy-start.42 = (bf16[256,768]{0,1:T(8,128)(2,1)S(1)}, bf16[256,768]{0,1:T(8,128)(2,1)}, u32[]{:S(2)}) copy-start(bf16[256,768]{0,1:T(8,128)(2,1)} %multiply_convert_fusion.6) | copy-start | bytes 1179652
  351.9 15.7 %copy-start.67 = (f32[256,20]{0,1:T(8,128)S(1)}, f32[256,20]{0,1:T(8,128)}, u32[]{:S(2)}) copy-start(f32[256,20]{0,1:T(8,128)} %get-tuple-element.185) | copy-start | bytes 61444
  351.9 15.9 %copy-start.127 = (f32[12]{0:T(128)S(1)}, f32[12]{0:T(128)}, u32[]{:S(2)}) copy-start(f32[12]{0:T(128)} %copy-done.126) | copy-start | bytes 148
  351.9 15.9 %copy-start.129 = (f32[12]{0:T(128)S(1)}, f32[12]{0:T(128)}, u32[]{:S(2)}) copy-start(f32[12]{0:T(128)} %copy-done.128) | copy-start | bytes 148
  351.9 15.9 %copy-start.133 = (f32[12]{0:T(128)S(1)}, f32[12]{0:T(128)}, u32[]{:S(2)}) copy-start(f32[12]{0:T(128)} %copy-done.132) | copy-start | bytes 148
  351.9 15.9 %copy-start.135 = (f32[12]{0:T(128)S(1)}, f32[12]{0:T(128)}, u32[]{:S(2)}) copy-start(f32[12]{0:T(128)} %copy-done.134) | copy-start | bytes 148
  351.9 15.9 %copy-start.141 = (f32[12]{0:T(128)S(1)}, f32[12]{0:T(128)}, u32[]{:S(2)}) copy-start(f32[12]{0:T(128)} %get-tuple-element.122) | copy-start | bytes 148
  351.9 18.4 %copy-start.109 = (f32[768]{0:T(1024)S(1)}, f32[768]{0:T(1024)}, u32[]{:S(2)}) copy-start(f32[768]{0:T(1024)} %get-tuple-element.114) | copy-start | bytes 9220
  351.9 18.4 %copy-start.108 = (f32[768]{0:T(1024)S(1)}, f32[768]{0:T(1024)}, u32[]{:S(2)}) copy-start(f32[768]{0:T(1024)} %get-tuple-element.118) | copy-start | bytes 9220
  355.6 21.7 %collective-permute-start.4 = (bf16[256,1536]{1,0:T(8,128)(2,1)}, bf16[256,1536]{1,0:T(8,128)(2,1)}, u32[]{:S(2)}, u32[]{:S(2)}) collective-permute-start(bf16[256,1536]{1,0:T(8,128)(2,1)} %get-tuple-element.144), channel_id=1, source_target_pairs={{2,0},{3,1},{6,2},{7,3},{4,6},{5,7},{8,4},{9,5},{10,8},{11,9},{14,... | collective-permute-start | bytes 2359304 | tf_op jit(solution)/shard_map/ppermute | solution.py:45
  356.9 22.5 %collective-permute-start.5 = (bf16[256,1536]{1,0:T(8,128)(2,1)}, bf16[256,1536]{1,0:T(8,128)(2,1)}, u32[]{:S(2)}, u32[]{:S(2)}) collective-permute-start(bf16[256,1536]{1,0:T(8,128)(2,1)} %get-tuple-element.147), channel_id=1, source_target_pairs={{1,0},{2,1},{3,2},{6,3},{7,6},{4,7},{5,4},{8,5},{9,8},{10,9},{11,1... | collective-permute-start | bytes 2359304 | tf_op jit(solution)/shard_map/ppermute | solution.py:45
  358.2 21.2 %collective-permute-start.6 = (bf16[256,1536]{1,0:T(8,128)(2,1)}, bf16[256,1536]{1,0:T(8,128)(2,1)}, u32[]{:S(2)}, u32[]{:S(2)}) collective-permute-start(bf16[256,1536]{1,0:T(8,128)(2,1)} %get-tuple-element.146), channel_id=1, source_target_pairs={{0,1},{1,2},{2,3},{3,6},{6,7},{7,4},{4,5},{5,8},{8,9},{9,10},{10,1... | collective-permute-start | bytes 2359304 | tf_op jit(solution)/shard_map/ppermute | solution.py:45
  362.2 25.1 %collective-permute-start.7 = (bf16[256,1536]{1,0:T(8,128)(2,1)}, bf16[256,1536]{1,0:T(8,128)(2,1)}, u32[]{:S(2)}, u32[]{:S(2)}) collective-permute-start(bf16[256,1536]{1,0:T(8,128)(2,1)} %get-tuple-element.145), channel_id=1, source_target_pairs={{0,2},{1,3},{2,6},{3,7},{6,4},{7,5},{4,8},{5,9},{8,10},{9,11},{10,... | collective-permute-start | bytes 2359304 | tf_op jit(solution)/shard_map/ppermute | solution.py:45
  375.5 14.4 %copy-start.35 = (f32[256,768]{0,1:T(8,128)S(1)}, f32[256,768]{0,1:T(8,128)}, u32[]{:S(2)}) copy-start(f32[256,768]{0,1:T(8,128)} %copy-done.33) | copy-start | bytes 2359300
  375.5 14.4 %copy-start.90 = (f32[768]{0:T(1024)S(1)}, f32[768]{0:T(1024)}, u32[]{:S(2)}) copy-start(f32[768]{0:T(1024)} %copy-done.89) | copy-start | bytes 9220
  375.6 14.4 %copy-start.107 = (f32[256]{0:T(256)S(1)}, f32[256]{0:T(256)}, u32[]{:S(2)}) copy-start(f32[256]{0:T(256)} %copy-done.106) | copy-start | bytes 3076
  375.6 14.4 %copy-start.112 = (f32[256]{0:T(256)S(1)}, f32[256]{0:T(256)}, u32[]{:S(2)}) copy-start(f32[256]{0:T(256)} %copy-done.111) | copy-start | bytes 3076
  377.4 296.4 %collective-permute-start.12 = (f32[125088]{0:T(1024)}, f32[125088]{0:T(1024)}, u32[]{:S(2)}, u32[]{:S(2)}) collective-permute-start(f32[125088]{0:T(1024)} %reduce.3), channel_id=1, source_target_pairs={{0,16},{16,0},{1,17},{17,1},{2,18},{18,2},{3,19},{19,3},{4,20},{20... | collective-permute-start | bytes 1501064 | tf_op jit(solution)/shard_map/ppermute | solution.py:1287
  379.4 271.4 %collective-permute-start.8 = (f32[6912,128]{1,0:T(8,128)}, f32[6912,128]{1,0:T(8,128)}, u32[]{:S(2)}, u32[]{:S(2)}) collective-permute-start(f32[6912,128]{1,0:T(8,128)} %bitcast.16.refs_11_), channel_id=1, source_target_pairs={{0,16},{16,0},{1,17},{17,1},{2,18},{18,2},{3,19},{19,3},{4,20},{20... | collective-permute-start | bytes 10616840 | tf_op jit(solution)/shard_map/ppermute | solution.py:1287
  379.4 271.3 %collective-permute-start.9 = (f32[6912,128]{1,0:T(8,128)}, f32[6912,128]{1,0:T(8,128)}, u32[]{:S(2)}, u32[]{:S(2)}) collective-permute-start(f32[6912,128]{1,0:T(8,128)} %bitcast.19.refs_12_), channel_id=1, source_target_pairs={{0,16},{16,0},{1,17},{17,1},{2,18},{18,2},{3,19},{19,3},{4,20},{20... | collective-permute-start | bytes 10616840 | tf_op jit(solution)/shard_map/ppermute | solution.py:1287
  401.5 31.9 %copy-start.36 = (f32[256,768]{0,1:T(8,128)}, f32[256,768]{0,1:T(8,128)S(1)}, u32[]{:S(2)}) copy-start(f32[256,768]{0,1:T(8,128)S(1)} %add_add_fusion.5) | copy-start | bytes 2359300
  486.0 131.6 %copy-start.123 = (pred[12]{0:T(512)(128)(4,1)S(1)}, pred[12]{0:T(512)(128)(4,1)}, u32[]{:S(2)}) copy-start(pred[12]{0:T(512)(128)(4,1)} %copy-done.121) | copy-start | bytes 40
  619.5 10.8 %copy-start.1 = (bf16[48,3840]{1,0:T(8,128)(2,1)S(1)}, bf16[48,3840]{1,0:T(8,128)(2,1)}, u32[]{:S(2)}) copy-start(bf16[48,3840]{1,0:T(8,128)(2,1)} %reduce-scatter.5.cloned.1.call-done.refs_4_.refs_3_) | copy-start | bytes 1105924
  621.3 29.4 %copy-start.3 = (bf16[192,768]{1,0:T(8,128)(2,1)S(1)}, bf16[192,768]{1,0:T(8,128)(2,1)}, u32[]{:S(2)}) copy-start(bf16[192,768]{1,0:T(8,128)(2,1)} %reduce-scatter.3.cloned.1.call-done.refs_3_.refs_4_) | copy-start | bytes 884740
  621.3 29.4 %copy-start.11 = (bf16[48,3840]{1,0:T(8,128)(2,1)S(1)}, bf16[48,3840]{1,0:T(8,128)(2,1)}, u32[]{:S(2)}) copy-start(bf16[48,3840]{1,0:T(8,128)(2,1)} %copy-done.10) | copy-start | bytes 1105924
  621.4 29.4 %copy-start.17 = (bf16[48,2304]{1,0:T(8,128)(2,1)S(1)}, bf16[48,2304]{1,0:T(8,128)(2,1)}, u32[]{:S(2)}) copy-start(bf16[48,2304]{1,0:T(8,128)(2,1)} %copy-done.16) | copy-start | bytes 663556
  629.8 44.0 %collective-permute-start.11 = (bf16[125088]{0:T(1024)(128)(2,1)}, bf16[125088]{0:T(1024)(128)(2,1)}, u32[]{:S(2)}, u32[]{:S(2)}) collective-permute-start(bf16[125088]{0:T(1024)(128)(2,1)} %dynamic_slice.58), channel_id=1, source_target_pairs={{0,16},{16,0},{1,17},{17,1},{2,18},{18,2},{3,19},{19,3},{4,20},{20... | collective-permute-start | bytes 750536 | tf_op jit(solution)/shard_map/ppermute | solution.py:1287
  651.7 22.0 %copy-start.37 = (f32[125952]{0:T(1024)S(1)}, f32[125952]{0:T(1024)}, u32[]{:S(2)}) copy-start(f32[125952]{0:T(1024)} %reshape.752) | copy-start | bytes 1511428
  651.7 22.1 %copy-start.48 = (f32[125088]{0:T(1024)S(1)}, f32[125088]{0:T(1024)}, u32[]{:S(2)}) copy-start(f32[125088]{0:T(1024)} %param.15) | copy-start | bytes 1501060
  651.7 22.1 %copy-start.56 = (f32[125088]{0:T(1024)S(1)}, f32[125088]{0:T(1024)}, u32[]{:S(2)}) copy-start(f32[125088]{0:T(1024)} %param.21) | copy-start | bytes 1501060
  (111 other events, 433.3 us)
Sparse Core Ops, SparseCore 0:
  311.0 85.6 reduce-scatter.2
  401.1 82.9 reduce-scatter.4

commit v6 on v5

--- a/solution.py
+++ b/solution.py
@@ -526,8 +526,8 @@
 
 GRID = (4, 2, 2)
 GATHER_Y_LAG = 2
-GATHER_X_LAG = 5
-GATHER_AHEAD = 1
+GATHER_X_LAG = 7
+GATHER_AHEAD = 0
 
 
 def place_of(me):
@@ -1213,7 +1213,7 @@
     return total / count
 
 
-STEP_BLOCKS = 8
+STEP_BLOCKS = 6
 
 
 def delta_of(grad, first, second, anchor):
@@ -1331,11 +1331,11 @@
     )
     if close:
         first_view, second_view = flat_view(first_layers[0]), flat_view(second_layers[0])
-        sources, other_rows = lax.optimization_barrier(
-            ((first_view, second_view, first_other[0], second_other[0]), other_rows)
-        )
-        twin_views = [swapped(value) for value in sources[:2]]
-        twin_moments = [swapped(value) for value in sources[2:]]
+        (*sources, first_other, second_other), other_rows = lax.optimization_barrier(
+            ((first_view, second_view, first_other, second_other), other_rows)
+        )
+        twin_views = [swapped(value) for value in sources]
+        twin_moments = [swapped(value)[0] for value in (first_other, second_other)]
     late_rows = [lax.all_gather(part, "seq", axis=0) for pair in own_rows[early:] for part in pair]
     layer_parts = [part.reshape(-1, part.shape[-1]) for part in early_rows + late_rows]
     gathered = [split_upper(*layer_parts[2 * depth : 2 * depth + 2]) for depth in range(L)]
@@ -1410,7 +1410,7 @@
     loss = squared_sum / (frames_group * channels) + contrast_weight * clash
     grad_audio_side, grad_text_side = pull_clash(jnp.float32(contrast_weight))
     grad_pred = (2.0 / (frames_group * channels) * error).astype(jnp.bfloat16)
-    grad_w_out = contract_rows(grad_pred, final_low)
+    grad_w_out = contract_rows(final_low, grad_pred).reshape(channels, D)
     grad_pooled = against_rows(grad_audio_side, w_audio_f, HIGH) / lengths_f
     grad_final = against_rows(grad_pred, w_out) + exact(onehot, grad_pooled)
     unused, pull_final = jax.vjp(norm_rows, hidden, gains_f[2 * L])
@@ -1481,10 +1481,21 @@
     left_condition = own_part(features, features_at) + own_part(text, text_at)
     early_view = thirds(pooled, grad_audio_side, own_at - audio_at)
     early_view = early_view + thirds(captions, grad_text_side, own_at - caption_at)
-    early_view, left_condition, layer_grads[0] = lax.optimization_barrier(
-        (early_view, left_condition, layer_grads[0])
-    )
-    small_grads = (grad_w_in, grad_w_out, grad_condition, jnp.stack(gain_grads))
+    left_small = jnp.concatenate(
+        [
+            own_rows_at(0, lead),
+            left_condition,
+            own_rows_at(gains_at, 2 * L + 1),
+        ],
+        axis=0,
+    )
+    silu_slope = pull_silu(jnp.ones_like(condition))[0]
+    slopes = jnp.pad(silu_slope, ((lead, 2 * L + 1), (0, 0)), constant_values=1.0)
+    left_null = own_rows_at(gains_at + 2 * L + 1, 1)
+    early_view, left_small, slopes, left_null, layer_grads[0] = lax.optimization_barrier(
+        (early_view, left_small, slopes, left_null, layer_grads[0])
+    )
+    small_grads = (jnp.concatenate([grad_w_in, grad_w_out, grad_condition, jnp.stack(gain_grads)]),)
     if close:
         sent = sent_early[1:]
         late = [layer_grads[depth][0] for depth in range(1, L)] + list(layer_grads[0])
@@ -1503,19 +1514,11 @@
             twin_parts += [twin_late[depth - 1], passed[2 * depth - 1], passed[2 * depth - 2]]
     else:
         small_grads = lax.psum(small_grads, "seq")
-    grad_w_in, grad_w_out, grad_condition, gain_rows = small_grads
-    grad_before = pull_silu(grad_condition)[0]
-    grad_null = jnp.sum(
-        jnp.where(null_flags[:, None] == 1, against_rows(grad_before, w_text_f, HIGH), 0.0), axis=0
-    )
-    own_view = early_view + contract_rows(left_condition, grad_before, HIGH)
-    for value, start in (
-        (grad_w_in, 0),
-        (grad_w_out.T.reshape(channels, D), channels),
-        (gain_rows, gains_at),
-        (grad_null[None], gains_at + gain_rows.shape[0]),
-    ):
-        own_view = own_view + contract_rows(own_rows_at(start, value.shape[0]), value, HIGH)
+    weighted = small_grads[0] * slopes
+    grad_before = weighted[lead : lead + item_count]
+    flagged = jnp.sum(jnp.where(null_flags[:, None] == 1, grad_before, 0.0), axis=0, keepdims=True)
+    grad_null = against_rows(flagged, w_text_f, HIGH)
+    own_view = early_view + contract_rows(left_small, weighted, HIGH) + left_null.T * grad_null
     other_grad = lax.dynamic_slice_in_dim(own_view.reshape(-1), own_start % D, other_size)
     other_grad_square = jnp.sum(other_grad * other_grad)
     if close:

time: 697 us -> 676 us (0.970)
  matrix products: 131 us -> 118 us
    mul x0 -> x4, other arithmetic: none -> 12.7 us  [the longest x2 8.43 us: adam(): second = beta_two * second + (1.0 - beta_two) * grad * grad]
    dot_general x17 -> x14, matrix products: 40 us -> 33.2 us  [contract_rows(): lax.dot_general(left, right, (((0,), (0,)), ((), ())), precision=precisio...]
    unnamed x328 -> x332, local copies, waits for them, and re-layouts: 26.1 us -> 27.7 us
  transfers between devices with their start and end apart: 15 -> 15, of which waited for: 4 -> 4; matrix products, arithmetic and copies ran while one was open for 26% -> 25% of each run, Pallas kernels for 31% -> 32%
where the time goes in v6:
time: 676 us; the launch traced here: 670 us
  Pallas kernels  365 us (54%)
  matrix products  118 us (17%)
  local copies, waits for them, and re-layouts  60.2 us (9%)
  other arithmetic  55.5 us (8%)
  starting transfers between devices  26.5 us (4%)
  between operations  24.2 us (4%)
  waiting for transfers between devices  20.2 us (3%)
    pallas_call x1, Pallas kernels, gather_pieces(): pl.pallas_call(functools.partial(gather_kernel, tuple(shared)), out_shape...  133 us
    pallas_call x1, Pallas kernels, scatter_grads(): pl.pallas_call(functools.partial(scatter_kernel, tuple(pieces), kinds, ca...  121 us
    dot_general x12, matrix products, dense(): return jnp.dot(left, right, preferred_element_type=jnp.float32)  35.5 us
    pallas_call x2, Pallas kernels, attend_backward(): pl.pallas_call(attend_backward_kernel, out_shape=(jax.ShapeDtypeStruct((r...  33.3 us
    dot_general x14, matrix products, contract_rows(): lax.dot_general(left, right, (((0,), (0,)), ((), ())), precision=precisio...  33.2 us
    dot_general x12, matrix products, against_rows(): lax.dot_general(left, right, (((1,), (1,)), ((), ())), precision=precisio...  30.5 us
    unnamed x332, local copies, waits for them, and re-layouts  27.7 us
    pallas_call x2, Pallas kernels, attend_forward(): pl.pallas_call(attend_forward_kernel, out_shape=(jax.ShapeDtypeStruct((ro...  24.4 us
  transfers between devices with their start and end apart: 15, of which 4 were waited for; matrix products, arithmetic and copies ran while one was open for 25% of the time, Pallas kernels for 32%

profile of v6, /device:TPU:0, one launch (start us, length us, event | category | flops | bytes accessed | tf_op | source)
XLA Modules:
  0.0 669.8 jit_solution(16321395890453899817)
XLA Ops:
  9.8 3.5 lay_out.1
  19.5 132.9 %gather_pieces.1 = (f32[16,40,256]{2,1,0:T(8,128)}, bf16[16,992,128]{2,1,0:T(8,128)(2,1)}, bf16[16,48,6144]{2,1,0:T(8,128)(2,1)}, bf16[16,192,768]{2,1,0:T(8,128...) custom-call(f32[40,256]{1,0:T(8,128)} %maximum_bitcast_fusion.refs_0_, ...), custom_call_target="tpu_custom_call" | custom-call | tf_op jit(solution)/shard_map/gather_pieces/pallas_call | solution.py:746
  152.4 4.0 unpack_others.1
  165.7 2.0 fusion.180
  169.0 7.6 %convolution_convert_fusion.kv_ref = bf16[1280,1536]{1,0:T(8,128)(2,1)} fusion(bf16[1280,768]{0,1:T(8,128)(2,1)S(1)} %multiply_convert_fusion, bf16[768,6144]{1,0:T(8,128)(2,1)} %bitcast.207), kind=kOutput, calls=%fused_computation.1 | convolution fusion | flops 3021864960 | bytes 8257536 | tf_op jit(solution)/shard_map/dot_general | solution.py:51
  176.7 1.8 convolution_convert_fusion.14.q_ref
  178.8 12.1 %attend_forward.2 = (bf16[256,768]{1,0:T(8,128)(2,1)S(1)}, f32[16,256]{1,0:T(8,128)S(1)}) custom-call(bf16[256,768]{1,0:T(8,128)(2,1)S(1)} %convolution_convert_fusion.14.q_ref, bf16[1280,1536]{1,0:T(8,128)(2,1)} %convolution_convert_fusion.kv_ref, s32[1,256]{1,0:T(1,128)S(1)} %bitcast.186, s32[1280,1]{1,0:T(8,128)S(1)} %reshape_select_fusion.key_item_ref), custom_call_target="tpu_custom_call" | custom-call | flops 1006632960 | bytes 4718592 | tf_op jit(solution)/shard_map/attend_forward/pallas_call | solution.py:198
  191.0 1.8 fusion.181
  193.1 4.3 fusion.6
  197.4 2.7 fusion.182
  200.6 3.5 convolution_convert_fusion.7
  204.1 4.3 collective-permute-start
  208.4 3.0 collective-permute-start.1
  215.4 2.5 convolution_convert_fusion.13.q_ref
  219.9 1.7 fusion.36
  223.2 5.0 multiply_reduce_fusion.20
  239.2 1.9 collective-permute-done.3
  242.2 1.9 copy-done.76
  244.2 12.3 %attend_forward.3 = (bf16[256,768]{1,0:T(8,128)(2,1)S(1)}, f32[16,256]{1,0:T(8,128)S(1)}) custom-call(bf16[256,768]{1,0:T(8,128)(2,1)S(1)} %copy-done.21, bf16[1280,1536]{1,0:T(8,128)(2,1)} %copy-done.76, s32[1,256]{1,0:T(1,128)S(1)} %bitcast.187, s32[1280,1]{1,0:T(8,128)S(1)} %copy-done.7), custom_call_target="tpu_custom_call" | custom-call | flops 1006632960 | bytes 4718592 | tf_op jit(solution)/shard_map/attend_forward/pallas_call | solution.py:198
  256.5 2.0 fusion.183
  258.7 4.0 fusion.2
  262.8 2.5 fusion.184
  267.6 2.1 multiply_reduce_fusion.27
  271.1 13.8 %sum_over_seq.1 = f32[16,8,128]{2,1,0:T(8,128)} custom-call(f32[16,8,128]{2,1,0:T(8,128)} %fusion.103.x_ref), custom_call_target="tpu_custom_call" | custom-call | flops 16384 | bytes 262144 | tf_op jit(solution)/shard_map/sum_over_seq/pallas_call | solution.py:449
  290.8 2.3 multiply_reduce_fusion.22
  295.9 2.1 multiply_reduce_fusion.3
  299.8 4.4 convolution_convert_fusion.1
  304.9 3.4 multiply_reduce_fusion.18
  308.3 3.3 multiply_reduce_fusion.19
  311.6 7.4 %fusion.23 = bf16[256,3072]{1,0:T(8,128)(2,1)S(1)} fusion(f32[256,3072]{1,0:T(8,128)} %copy-done.147, bf16[3072,768]{1,0:T(8,128)(2,1)} %bitcast.228, f32[256,768]{0,1:T(8,128)S(1)} %copy-done.49, f32[256]{0:T(256)S(1)} %negate_multiply_fusion.4), kind=kOutput, calls=%fused_computation.44 | convolution fusion | flops 1224081408 | bytes 10224640 | tf_op jit(solution)/shard_map/dot_general | solution.py:69
  324.4 2.9 pad_maximum_fusion.1
  327.4 16.6 %attend_backward.2 = (bf16[256,768]{1,0:T(8,128)(2,1)S(1)}, bf16[1280,1536]{1,0:T(8,128)(2,1)}) custom-call(bf16[256,768]{1,0:T(8,128)(2,1)S(1)} %copy-done.22, bf16[1280,1536]{1,0:T(8,128)(2,1)} %copy-done.76, bf16[256,768]{1,0:T(8,128)(2,1)S(1)} %convolution_convert_fusion.12.do_ref, f32[16,256]{1,0:T(8,128)S(1)} %get-tuple-element.84.lse_ref, ...), custom_call_target="tpu_custom_call" | custom-call | flops 2516582400 | bytes 9437184 | tf_op jit(solution)/shard_map/attend_backward/pallas_call | solution.py:255
  344.1 3.6 fusion.175
  350.3 3.9 collective-permute-start.6
  354.2 4.6 collective-permute-start.7
  365.5 2.0 fusion.37
  371.0 8.4 %collective-permute-done.7 = bf16[256,1536]{1,0:T(8,128)(2,1)} collective-permute-done((bf16[256,1536]{1,0:T(8,128)(2,1)}, bf16[256,1536]{1,0:T(8,128)(2,1)}, u32[]{:S(2)}, u32[]{:S(2)}) %collective-permute-start.7) | collective-permute-done | bytes 786464 | tf_op jit(solution)/shard_map/ppermute | solution.py:45
  379.4 2.6 add_convert_fusion
  382.1 3.6 multiply_reduce_fusion.5
  387.7 3.5 fusion.16
  394.2 16.7 %attend_backward.3 = (bf16[256,768]{1,0:T(8,128)(2,1)S(1)}, bf16[1280,1536]{1,0:T(8,128)(2,1)}) custom-call(bf16[256,768]{1,0:T(8,128)(2,1)S(1)} %copy-done.24, bf16[1280,1536]{1,0:T(8,128)(2,1)} %convolution_convert_fusion.kv_ref, bf16[256,768]{1,0:T(8,128)(2,1)S(1)} %convolution_convert_fusion.11.do_ref, f32[16,256]{1,0:T(8,128)S(1)} %get-tuple-element.87.lse_ref, ...), custom_call_target="tpu_custom_call" | custom-call | flops 2516582400 | bytes 9437184 | tf_op jit(solution)/shard_map/attend_backward/pallas_call | solution.py:255
  410.9 6.5 fusion.27
  417.5 1.8 convolution_add_fusion.1
  422.4 1.9 multiply_reduce_fusion
  428.3 1.9 fusion.25
  430.2 2.2 fusion.24
  434.0 2.5 convolution_convert_fusion.9
  436.6 2.4 copy.133
  440.4 1.8 copy.134
  442.2 6.8 %convolution_convert_fusion.2 = bf16[3072,768]{1,0:T(8,128)(2,1)} fusion(bf16[256,768]{0,1:T(8,128)(2,1)} %copy-done.65, f32[256,3072]{1,0:T(8,128)} %copy-done.145), kind=kOutput, calls=%fused_computation.5 | convolution fusion | flops 1217396736 | bytes 8257536 | tf_op jit(solution)/shard_map/dot_general | solution.py:59
  451.8 3.4 convolution_convert_fusion.6
  455.3 7.0 %pad_maximum_fusion = bf16[768,6144]{1,0:T(8,128)(2,1)} fusion(bf16[768,3072]{1,0:T(8,128)(2,1)S(1)} %convolution_convert_fusion.3, bf16[768,768]{1,0:T(8,128)(2,1)S(1)} %copy.134, bf16[768,1536]{1,0:T(8,128)(2,1)S(1)} %convolution_convert_fusion.6, bf16[768,768]{1,0:T(8,128)(2,1)S(1)} %copy-done.43), kind=kLoop, calls=%fused_computation | loop fusion | flops 37748736 | bytes 18874368 | tf_op jit(solution)/shard_map/concatenate | solution.py:309
  462.3 2.9 convolution_convert_fusion.4
  465.2 1.7 multiply_reduce_fusion.16
  466.9 9.3 %reduce-scatter.5.cloned.1.call-done.refs_4_.refs_3_ = bf16[48,3840]{1,0:T(8,128)(2,1)} async-done(((bf16[768,3840]{1,0:T(8,128)(2,1)}), bf16[48,3840]{1,0:T(8,128)(2,1)}) %reduce-scatter.5.cloned.1.call-update) | async-done | bytes 368656 | tf_op jit(solution)/shard_map/reduce_scatter | solution.py:1431
  478.1 121.4 %scatter_grads.1 = (f32[48,2304]{1,0:T(8,128)S(1)}, f32[48,6144]{1,0:T(8,128)}, f32[192,768]{1,0:T(8,128)S(1)}, bf16[48,2304]{1,0:T(8,128)(2,1)S(1)}, bf16[48,61...) custom-call(bf16[16,48,2304]{2,1,0:T(8,128)(2,1)} %bitcast.191, ...), custom_call_target="tpu_custom_call" | custom-call | tf_op jit(solution)/shard_map/scatter_grads/pallas_call | solution.py:1076
  603.1 1.7 slice.200
  607.1 2.5 fusion.33
  609.7 1.9 reshape.735
  611.5 1.9 dynamic_slice.58
  615.3 1.8 multiply_reduce_fusion.17
  620.4 11.3 %share_over_all.1 = f32[32,8,128]{2,1,0:T(8,128)} custom-call(f32[8,128]{1,0:T(8,128)} %broadcast_in_dim.195.x_ref), custom_call_target="tpu_custom_call" | custom-call | tf_op jit(solution)/shard_map/share_over_all/pallas_call | solution.py:514
  635.3 20.7 %step_layers.1 = (f32[6912,128]{1,0:T(8,128)}, f32[6912,128]{1,0:T(8,128)}, f32[6912,128]{1,0:T(8,128)}, f32[6912,128]{1,0:T(8,128)}, f32[6912,128]{1,0:T(8,128)}) custom-call(f32[2]{0:T(128)S(1)} %pad_maximum_fusion.11.factors, f32[48,6144]{1,0:T(8,128)} %get-tuple-element.99.refs_0_, f32[192,768]{1,0:T(8,128)S(1)} %get-tuple-element.100.refs_1_, ...), custom_call_target="tpu_custom_call" | custom-call | tf_op jit(solution)/shard_map/step_layers/pallas_call | solution.py:1267
  656.1 3.1 multiply_subtract_fusion
  (514 shorter events, 102.8 us)
Async XLA Ops:
  7.2 457.9 %reduce-scatter.3.cloned.1.call-start = ((), (), s32[]{:S(2)}) async-start(), calls=%async_computation.2 | async-start | bytes 5013504 | tf_op jit(solution)/shard_map/reduce_scatter | solution.py:1431
  17.3 148.4 %copy-start.85 = (s32[1280]{0:T(1024)}, s32[1280]{0:T(1024)S(1)}, u32[]{:S(2)}) copy-start(s32[1280]{0:T(1024)S(1)} %and_select_fusion) | copy-start | bytes 15364
  19.5 138.6 %copy-start.141 = (s32[1,12]{1,0:T(1,128)S(1)}, s32[1,12]{1,0:T(1,128)}, u32[]{:S(2)}) copy-start(s32[1,12]{1,0:T(1,128)} %param.26) | copy-start | bytes 148
  158.1 42.2 %copy-start.91 = (f32[768]{0:T(1024)}, f32[768]{0:T(1024)S(1)}, u32[]{:S(2)}) copy-start(f32[768]{0:T(1024)S(1)} %get-tuple-element.166) | copy-start | bytes 9220
  167.7 23.3 %copy-start.25 = (f32[1280,768]{0,1:T(8,128)}, f32[1280,768]{0,1:T(8,128)S(1)}, u32[]{:S(2)}) copy-start(f32[1280,768]{0,1:T(8,128)S(1)} %get-tuple-element.177) | copy-start | bytes 11796484
  200.1 17.8 %copy-start.37 = (f32[256,768]{0,1:T(8,128)}, f32[256,768]{0,1:T(8,128)S(1)}, u32[]{:S(2)}) copy-start(f32[256,768]{0,1:T(8,128)S(1)} %get-tuple-element.181) | copy-start | bytes 2359300
  200.1 17.8 %copy-start.108 = (f32[256]{0:T(256)}, f32[256]{0:T(256)S(1)}, u32[]{:S(2)}) copy-start(f32[256]{0:T(256)S(1)} %broadcast_multiply_fusion.3) | copy-start | bytes 3076
  200.3 17.6 %copy-start.117 = (f32[256]{0:T(256)}, f32[256]{0:T(256)S(1)}, u32[]{:S(2)}) copy-start(f32[256]{0:T(256)S(1)} %multiply_reduce_fusion.13) | copy-start | bytes 3076
  200.3 17.6 %copy-start.113 = (f32[256]{0:T(256)}, f32[256]{0:T(256)S(1)}, u32[]{:S(2)}) copy-start(f32[256]{0:T(256)S(1)} %fusion.145) | copy-start | bytes 3076
  200.5 14.9 %copy-start.44 = (bf16[256,768]{0,1:T(8,128)(2,1)}, bf16[256,768]{0,1:T(8,128)(2,1)S(1)}, u32[]{:S(2)}) copy-start(bf16[256,768]{0,1:T(8,128)(2,1)S(1)} %multiply_convert_fusion.4) | copy-start | bytes 1179652
  200.5 17.4 %copy-start.143 = (s32[1,12]{1,0:T(1,128)S(1)}, s32[1,12]{1,0:T(1,128)}, u32[]{:S(2)}) copy-start(s32[1,12]{1,0:T(1,128)} %param.24) | copy-start | bytes 148
  200.5 18.1 %copy-start.63 = (f32[1,12,768]{2,0,1:T(1,128)S(1)}, f32[1,12,768]{2,0,1:T(1,128)}, u32[]{:S(2)}) copy-start(f32[1,12,768]{2,0,1:T(1,128)} %param.27) | copy-start | bytes 110596
  200.5 18.1 %copy-start.94 = (f32[768]{0:T(1024)S(1)}, f32[768]{0:T(1024)}, u32[]{:S(2)}) copy-start(f32[768]{0:T(1024)} %copy-done.93) | copy-start | bytes 9220
  200.5 18.1 %copy-start.123 = (pred[12]{0:T(512)(128)(4,1)S(1)}, pred[12]{0:T(512)(128)(4,1)}, u32[]{:S(2)}) copy-start(pred[12]{0:T(512)(128)(4,1)} %copy-done.122) | copy-start | bytes 40
  200.5 18.1 %copy-start.72 = (f32[12,384]{1,0:T(8,128)S(1)}, f32[12,384]{1,0:T(8,128)}, u32[]{:S(2)}) copy-start(f32[12,384]{1,0:T(8,128)} %copy-done.71) | copy-start | bytes 55300
  200.5 18.1 %copy-start.74 = (f32[12,384]{1,0:T(8,128)S(1)}, f32[12,384]{1,0:T(8,128)}, u32[]{:S(2)}) copy-start(f32[12,384]{1,0:T(8,128)} %copy-done.73) | copy-start | bytes 55300
  200.6 18.2 %copy-start.5 = (bf16[768,512]{1,0:T(8,128)(2,1)S(1)}, bf16[768,512]{1,0:T(8,128)(2,1)}, u32[]{:S(2)}) copy-start(bf16[768,512]{1,0:T(8,128)(2,1)} %copy-done.4) | copy-start | bytes 2359300
  204.1 24.8 %copy-start.86 = (s32[1280]{0:T(1024)S(1)}, s32[1280]{0:T(1024)}, u32[]{:S(2)}) copy-start(s32[1280]{0:T(1024)} %copy-done.85) | copy-start | bytes 15364
  204.1 26.4 %copy-start.80 = (bf16[120,128]{1,0:T(8,128)(2,1)S(1)}, bf16[120,128]{1,0:T(8,128)(2,1)}, u32[]{:S(2)}) copy-start(bf16[120,128]{1,0:T(8,128)(2,1)} %get-tuple-element.154) | copy-start | bytes 92164
  204.1 28.2 %collective-permute-start = (bf16[256,1536]{1,0:T(8,128)(2,1)}, bf16[256,1536]{1,0:T(8,128)(2,1)}, u32[]{:S(2)}, u32[]{:S(2)}) collective-permute-start(bf16[256,1536]{1,0:T(8,128)(2,1)} %convolution_convert_fusion.7), channel_id=1, source_target_pairs={{0,2},{1,3},{2,6},{3,7},{6,4},{7,5},{4,8},{5,9},{8,10},{9,11},{10,... | collective-permute-start | bytes 2359304 | tf_op jit(solution)/shard_map/ppermute | solution.py:45
  208.4 25.8 %collective-permute-start.1 = (bf16[256,1536]{1,0:T(8,128)(2,1)}, bf16[256,1536]{1,0:T(8,128)(2,1)}, u32[]{:S(2)}, u32[]{:S(2)}) collective-permute-start(bf16[256,1536]{1,0:T(8,128)(2,1)} %convolution_convert_fusion.7), channel_id=1, source_target_pairs={{0,1},{1,2},{2,3},{3,6},{6,7},{7,4},{4,5},{5,8},{8,9},{9,10},{10,1... | collective-permute-start | bytes 2359304 | tf_op jit(solution)/shard_map/ppermute | solution.py:45
  211.4 26.6 %collective-permute-start.2 = (bf16[256,1536]{1,0:T(8,128)(2,1)}, bf16[256,1536]{1,0:T(8,128)(2,1)}, u32[]{:S(2)}, u32[]{:S(2)}) collective-permute-start(bf16[256,1536]{1,0:T(8,128)(2,1)} %convolution_convert_fusion.7), channel_id=1, source_target_pairs={{1,0},{2,1},{3,2},{6,3},{7,6},{4,7},{5,4},{8,5},{9,8},{10,9},{11,1... | collective-permute-start | bytes 2359304 | tf_op jit(solution)/shard_map/ppermute | solution.py:45
  212.6 28.4 %collective-permute-start.3 = (bf16[256,1536]{1,0:T(8,128)(2,1)}, bf16[256,1536]{1,0:T(8,128)(2,1)}, u32[]{:S(2)}, u32[]{:S(2)}) collective-permute-start(bf16[256,1536]{1,0:T(8,128)(2,1)} %convolution_convert_fusion.7), channel_id=1, source_target_pairs={{2,0},{3,1},{6,2},{7,3},{4,6},{5,7},{8,4},{9,5},{10,8},{11,9},{14,... | collective-permute-start | bytes 2359304 | tf_op jit(solution)/shard_map/ppermute | solution.py:45
  213.9 91.0 %collective-permute-start.12 = (f32[1,125088]{1,0:T(1,128)}, f32[1,125088]{1,0:T(1,128)}, u32[]{:S(2)}, u32[]{:S(2)}) collective-permute-start(f32[1,125088]{1,0:T(1,128)} %param.19), channel_id=1, source_target_pairs={{0,16},{16,0},{1,17},{17,1},{2,18},{18,2},{3,19},{19,3},{4,20},{20... | collective-permute-start | bytes 1501064 | tf_op jit(solution)/shard_map/ppermute | solution.py:1287
  219.9 16.9 %copy-start.137 = (f32[12]{0:T(128)}, f32[12]{0:T(128)S(1)}, u32[]{:S(2)}) copy-start(f32[12]{0:T(128)S(1)} %get-tuple-element.188) | copy-start | bytes 148
  232.3 76.0 %collective-permute-start.10 = (f32[1,125088]{1,0:T(1,128)}, f32[1,125088]{1,0:T(1,128)}, u32[]{:S(2)}, u32[]{:S(2)}) collective-permute-start(f32[1,125088]{1,0:T(1,128)} %param.17), channel_id=1, source_target_pairs={{0,16},{16,0},{1,17},{17,1},{2,18},{18,2},{3,19},{19,3},{4,20},{20... | collective-permute-start | bytes 1501064 | tf_op jit(solution)/shard_map/ppermute | solution.py:1287
  234.2 401.0 %collective-permute-start.8 = (f32[6912,128]{1,0:T(8,128)}, f32[6912,128]{1,0:T(8,128)}, u32[]{:S(2)}, u32[]{:S(2)}) collective-permute-start(f32[6912,128]{1,0:T(8,128)} %bitcast.195), channel_id=1, source_target_pairs={{0,16},{16,0},{1,17},{17,1},{2,18},{18,2},{3,19},{19,3},{4,20},{20... | collective-permute-start | bytes 10616840 | tf_op jit(solution)/shard_map/ppermute | solution.py:1287
  304.3 171.9 %reduce-scatter.5.cloned.1.call-start = ((), (), s32[]{:S(2)}) async-start(), calls=%async_computation.3 | async-start | bytes 6266880 | tf_op jit(solution)/shard_map/reduce_scatter | solution.py:1431
  344.0 14.8 %copy-start.138 = (f32[12]{0:T(128)S(1)}, f32[12]{0:T(128)}, u32[]{:S(2)}) copy-start(f32[12]{0:T(128)} %copy-done.137) | copy-start | bytes 148
  344.0 14.8 %copy-start.144 = (f32[12]{0:T(128)S(1)}, f32[12]{0:T(128)}, u32[]{:S(2)}) copy-start(f32[12]{0:T(128)} %get-tuple-element.127) | copy-start | bytes 148
  344.0 14.8 %copy-start.77 = (f32[12,512]{1,0:T(8,128)S(1)}, f32[12,512]{1,0:T(8,128)}, u32[]{:S(2)}) copy-start(f32[12,512]{1,0:T(8,128)} %get-tuple-element.189) | copy-start | bytes 73732
  344.0 14.8 %copy-start.100 = (f32[12,512]{1,0:T(8,128)S(1)}, f32[12,512]{1,0:T(8,128)}, u32[]{:S(2)}) copy-start(f32[12,512]{1,0:T(8,128)} %get-tuple-element.193) | copy-start | bytes 73732
  344.0 14.8 %copy-start.139 = (f32[12]{0:T(128)S(1)}, f32[12]{0:T(128)}, u32[]{:S(2)}) copy-start(f32[12]{0:T(128)} %add_rsqrt_fusion.1) | copy-start | bytes 148
  344.0 15.0 %copy-start.29 = (f32[256,768]{0,1:T(8,128)S(1)}, f32[256,768]{0,1:T(8,128)}, u32[]{:S(2)}) copy-start(f32[256,768]{0,1:T(8,128)} %copy-done.27) | copy-start | bytes 2359300
  344.0 15.3 %copy-start.126 = (f32[12]{0:T(128)S(1)}, f32[12]{0:T(128)}, u32[]{:S(2)}) copy-start(f32[12]{0:T(128)} %copy-done.125) | copy-start | bytes 148
  344.0 15.3 %copy-start.128 = (f32[12]{0:T(128)S(1)}, f32[12]{0:T(128)}, u32[]{:S(2)}) copy-start(f32[12]{0:T(128)} %copy-done.127) | copy-start | bytes 148
  344.1 15.3 %copy-start.132 = (f32[12]{0:T(128)S(1)}, f32[12]{0:T(128)}, u32[]{:S(2)}) copy-start(f32[12]{0:T(128)} %copy-done.131) | copy-start | bytes 148
  344.1 15.3 %copy-start.134 = (f32[12]{0:T(128)S(1)}, f32[12]{0:T(128)}, u32[]{:S(2)}) copy-start(f32[12]{0:T(128)} %copy-done.133) | copy-start | bytes 148
  344.1 15.3 %copy-start.140 = (f32[12]{0:T(128)S(1)}, f32[12]{0:T(128)}, u32[]{:S(2)}) copy-start(f32[12]{0:T(128)} %get-tuple-element.126) | copy-start | bytes 148
  344.1 17.4 %copy-start.111 = (f32[768]{0:T(1024)S(1)}, f32[768]{0:T(1024)}, u32[]{:S(2)}) copy-start(f32[768]{0:T(1024)} %get-tuple-element.118) | copy-start | bytes 9220
  344.1 18.0 %copy-start.110 = (f32[768]{0:T(1024)S(1)}, f32[768]{0:T(1024)}, u32[]{:S(2)}) copy-start(f32[768]{0:T(1024)} %get-tuple-element.122) | copy-start | bytes 9220
  347.7 21.8 %collective-permute-start.4 = (bf16[256,1536]{1,0:T(8,128)(2,1)}, bf16[256,1536]{1,0:T(8,128)(2,1)}, u32[]{:S(2)}, u32[]{:S(2)}) collective-permute-start(bf16[256,1536]{1,0:T(8,128)(2,1)} %get-tuple-element.148), channel_id=1, source_target_pairs={{2,0},{3,1},{6,2},{7,3},{4,6},{5,7},{8,4},{9,5},{10,8},{11,9},{14,... | collective-permute-start | bytes 2359304 | tf_op jit(solution)/shard_map/ppermute | solution.py:45
  349.0 22.0 %collective-permute-start.5 = (bf16[256,1536]{1,0:T(8,128)(2,1)}, bf16[256,1536]{1,0:T(8,128)(2,1)}, u32[]{:S(2)}, u32[]{:S(2)}) collective-permute-start(bf16[256,1536]{1,0:T(8,128)(2,1)} %get-tuple-element.151), channel_id=1, source_target_pairs={{1,0},{2,1},{3,2},{6,3},{7,6},{4,7},{5,4},{8,5},{9,8},{10,9},{11,1... | collective-permute-start | bytes 2359304 | tf_op jit(solution)/shard_map/ppermute | solution.py:45
  350.3 20.7 %collective-permute-start.6 = (bf16[256,1536]{1,0:T(8,128)(2,1)}, bf16[256,1536]{1,0:T(8,128)(2,1)}, u32[]{:S(2)}, u32[]{:S(2)}) collective-permute-start(bf16[256,1536]{1,0:T(8,128)(2,1)} %get-tuple-element.150), channel_id=1, source_target_pairs={{0,1},{1,2},{2,3},{3,6},{6,7},{7,4},{4,5},{5,8},{8,9},{9,10},{10,1... | collective-permute-start | bytes 2359304 | tf_op jit(solution)/shard_map/ppermute | solution.py:45
  354.2 25.1 %collective-permute-start.7 = (bf16[256,1536]{1,0:T(8,128)(2,1)}, bf16[256,1536]{1,0:T(8,128)(2,1)}, u32[]{:S(2)}, u32[]{:S(2)}) collective-permute-start(bf16[256,1536]{1,0:T(8,128)(2,1)} %get-tuple-element.149), channel_id=1, source_target_pairs={{0,2},{1,3},{2,6},{3,7},{6,4},{7,5},{4,8},{5,9},{8,10},{9,11},{10,... | collective-permute-start | bytes 2359304 | tf_op jit(solution)/shard_map/ppermute | solution.py:45
  367.5 14.6 %copy-start.92 = (f32[768]{0:T(1024)S(1)}, f32[768]{0:T(1024)}, u32[]{:S(2)}) copy-start(f32[768]{0:T(1024)} %copy-done.91) | copy-start | bytes 9220
  369.5 265.7 %collective-permute-start.9 = (f32[6912,128]{1,0:T(8,128)}, f32[6912,128]{1,0:T(8,128)}, u32[]{:S(2)}, u32[]{:S(2)}) collective-permute-start(f32[6912,128]{1,0:T(8,128)} %bitcast.19.refs_12_), channel_id=1, source_target_pairs={{0,16},{16,0},{1,17},{17,1},{2,18},{18,2},{3,19},{19,3},{4,20},{20... | collective-permute-start | bytes 10616840 | tf_op jit(solution)/shard_map/ppermute | solution.py:1287
  393.5 33.8 %copy-start.40 = (f32[256,768]{0,1:T(8,128)}, f32[256,768]{0,1:T(8,128)S(1)}, u32[]{:S(2)}) copy-start(f32[256,768]{0,1:T(8,128)S(1)} %add_add_fusion.5) | copy-start | bytes 2359300
  478.1 127.8 %copy-start.124 = (pred[12]{0:T(512)(128)(4,1)S(1)}, pred[12]{0:T(512)(128)(4,1)}, u32[]{:S(2)}) copy-start(pred[12]{0:T(512)(128)(4,1)} %copy-done.122) | copy-start | bytes 40
  478.1 129.0 %copy-start.68 = (f32[57,164]{1,0:T(8,128)S(1)}, f32[57,164]{1,0:T(8,128)}, u32[]{:S(2)}) copy-start(f32[57,164]{1,0:T(8,128)} %pad_maximum_fusion.9) | copy-start | bytes 112180
  478.1 129.0 %copy-start.136 = (f32[1,164]{1,0:T(1,128)S(1)}, f32[1,164]{1,0:T(1,128)}, u32[]{:S(2)}) copy-start(f32[1,164]{1,0:T(1,128)} %compare_convert_fusion.1) | copy-start | bytes 1972
  603.1 32.1 %copy-start.3 = (bf16[192,768]{1,0:T(8,128)(2,1)S(1)}, bf16[192,768]{1,0:T(8,128)(2,1)}, u32[]{:S(2)}) copy-start(bf16[192,768]{1,0:T(8,128)(2,1)} %reduce-scatter.3.cloned.1.call-done.refs_3_.refs_4_) | copy-start | bytes 884740
  607.0 28.2 %copy-start.11 = (bf16[48,3840]{1,0:T(8,128)(2,1)S(1)}, bf16[48,3840]{1,0:T(8,128)(2,1)}, u32[]{:S(2)}) copy-start(bf16[48,3840]{1,0:T(8,128)(2,1)} %copy-done.10) | copy-start | bytes 1105924
  607.1 28.1 %copy-start.15 = (bf16[192,768]{1,0:T(8,128)(2,1)S(1)}, bf16[192,768]{1,0:T(8,128)(2,1)}, u32[]{:S(2)}) copy-start(bf16[192,768]{1,0:T(8,128)(2,1)} %copy-done.14) | copy-start | bytes 884740
  607.1 28.1 %copy-start.17 = (bf16[192,768]{1,0:T(8,128)(2,1)S(1)}, bf16[192,768]{1,0:T(8,128)(2,1)}, u32[]{:S(2)}) copy-start(bf16[192,768]{1,0:T(8,128)(2,1)} %copy-done.16) | copy-start | bytes 884740
  607.1 28.1 %copy-start.19 = (bf16[48,2304]{1,0:T(8,128)(2,1)S(1)}, bf16[48,2304]{1,0:T(8,128)(2,1)}, u32[]{:S(2)}) copy-start(bf16[48,2304]{1,0:T(8,128)(2,1)} %copy-done.18) | copy-start | bytes 663556
  613.4 42.6 %collective-permute-start.11 = (bf16[125088]{0:T(1024)(128)(2,1)}, bf16[125088]{0:T(1024)(128)(2,1)}, u32[]{:S(2)}, u32[]{:S(2)}) collective-permute-start(bf16[125088]{0:T(1024)(128)(2,1)} %dynamic_slice.58), channel_id=1, source_target_pairs={{0,16},{16,0},{1,17},{17,1},{2,18},{18,2},{3,19},{19,3},{4,20},{20... | collective-permute-start | bytes 750536 | tf_op jit(solution)/shard_map/ppermute | solution.py:1287
  635.2 20.8 %copy-start.42 = (f32[125952]{0:T(1024)S(1)}, f32[125952]{0:T(1024)}, u32[]{:S(2)}) copy-start(f32[125952]{0:T(1024)} %reshape.735) | copy-start | bytes 1511428
  635.3 20.8 %copy-start.54 = (f32[125088]{0:T(1024)S(1)}, f32[125088]{0:T(1024)}, u32[]{:S(2)}) copy-start(f32[125088]{0:T(1024)} %param.15) | copy-start | bytes 1501060
  635.3 20.8 %copy-start.55 = (f32[125088]{0:T(1024)S(1)}, f32[125088]{0:T(1024)}, u32[]{:S(2)}) copy-start(f32[125088]{0:T(1024)} %get-tuple-element.210) | copy-start | bytes 1501060
  635.3 20.8 %copy-start.56 = (f32[125088]{0:T(1024)S(1)}, f32[125088]{0:T(1024)}, u32[]{:S(2)}) copy-start(f32[125088]{0:T(1024)} %get-tuple-element.211) | copy-start | bytes 1501060
  635.3 20.8 %copy-start.57 = (f32[125088]{0:T(1024)S(1)}, f32[125088]{0:T(1024)}, u32[]{:S(2)}) copy-start(f32[125088]{0:T(1024)} %multiply_reduce_fusion.18) | copy-start | bytes 1501060
  635.3 20.8 %copy-start.58 = (f32[125088]{0:T(1024)S(1)}, f32[125088]{0:T(1024)}, u32[]{:S(2)}) copy-start(f32[125088]{0:T(1024)} %multiply_reduce_fusion.19) | copy-start | bytes 1501060
  635.3 20.8 %copy-start.61 = (f32[125088]{0:T(1024)S(1)}, f32[125088]{0:T(1024)}, u32[]{:S(2)}) copy-start(f32[125088]{0:T(1024)} %param.21) | copy-start | bytes 1501060
  (113 other events, 524.2 us)
Sparse Core Ops, SparseCore 0:
  304.4 84.3 reduce-scatter.2
  393.2 82.8 reduce-scatter.4

commit v7 on v6

--- a/solution.py
+++ b/solution.py
@@ -142,15 +142,13 @@
     pieces = {}
     for step in (2, 1, -1, -2):
         pieces[step] = passed_along(local_pairs, "seq", step, close)
-    return jnp.concatenate([pieces[2], pieces[1], local_pairs, pieces[-1], pieces[-2]], axis=0)
-
-
-def return_window(grad_window, rows, close):
-    total = grad_window[2 * rows : 3 * rows].astype(jnp.float32)
+    return [jnp.concatenate([pieces[2], pieces[1], local_pairs, pieces[-1], pieces[-2]], axis=0)]
+
+
+def return_window(grad_window, close):
+    total = grad_window[2].astype(jnp.float32)
     for slot, step in ((0, 2), (1, 1), (3, -1), (4, -2)):
-        total = total + passed_along(
-            grad_window[slot * rows : (slot + 1) * rows], "seq", -step, close
-        ).astype(jnp.float32)
+        total = total + passed_along(grad_window[slot], "seq", -step, close).astype(jnp.float32)
     return total
 
 
@@ -170,7 +168,15 @@
     bias_ref[...] = jnp.where(keep, 0.0, -1e30).astype(jnp.float32)
 
 
-def attend_forward_kernel(q_ref, kv_ref, query_item_ref, key_item_ref, o_ref, lse_ref, bias_ref):
+def joined(refs, cols):
+    if len(refs) == 1:
+        return refs[0][:, cols]
+    return jnp.concatenate([ref[:, cols] for ref in refs], axis=0)
+
+
+def attend_forward_kernel(parts, q_ref, *refs):
+    kv_refs = refs[:parts]
+    query_item_ref, key_item_ref, o_ref, lse_ref, bias_ref = refs[parts:]
     fill_bias(bias_ref, query_item_ref, key_item_ref)
     width = HEADS * HD
     masks = lane_masks(jnp.bfloat16)
@@ -178,8 +184,8 @@
     for pair in range(PAIRS):
         cols = slice(pair * LANES, (pair + 1) * LANES)
         query = q_ref[:, cols] * jnp.bfloat16(HD ** (-0.5))
-        key_rows = kv_ref[:, cols]
-        value_rows = kv_ref[:, width + pair * LANES : width + (pair + 1) * LANES]
+        key_rows = joined(kv_refs, cols)
+        value_rows = joined(kv_refs, slice(width + pair * LANES, width + (pair + 1) * LANES))
         halves = []
         for half in range(2):
             scores = against_rows(key_rows, query * masks[half]) * LOG2E + bias_ref[...]
@@ -194,14 +200,14 @@
 
 def attend_forward(queries, window, query_item, key_item):
     rows, width = queries.shape
-    span = window.shape[0]
+    parts, span = len(window), sum(piece.shape[0] for piece in window)
     return pl.pallas_call(
-        attend_forward_kernel,
+        functools.partial(attend_forward_kernel, parts),
         out_shape=(
             jax.ShapeDtypeStruct((rows, width), jnp.bfloat16),
             jax.ShapeDtypeStruct((16, rows), jnp.float32),
         ),
-        in_specs=[pl.BlockSpec(memory_space=pltpu.VMEM)] * 4,
+        in_specs=[pl.BlockSpec(memory_space=pltpu.VMEM)] * (3 + parts),
         out_specs=(pl.BlockSpec(memory_space=pltpu.VMEM),) * 2,
         scratch_shapes=[pltpu.VMEM((span, rows), jnp.float32)],
         compiler_params=pltpu.CompilerParams(vmem_limit_bytes=VMEM_LIMIT),
@@ -211,12 +217,13 @@
             bytes_accessed=4 * rows * width + 4 * span * width,
         ),
         name="attend_forward",
-    )(queries, window, query_item[None, :], key_item[:, None])
-
-
-def attend_backward_kernel(
-    q_ref, kv_ref, do_ref, lse_ref, query_item_ref, key_item_ref, dq_ref, dkv_ref, bias_ref
-):
+    )(queries, *window, query_item[None, :], key_item[:, None])
+
+
+def attend_backward_kernel(parts, splits, q_ref, *refs):
+    kv_refs = refs[:parts]
+    do_ref, lse_ref, query_item_ref, key_item_ref, dq_ref = refs[parts : parts + 5]
+    dkv_refs, bias_ref = refs[parts + 5 : parts + 5 + splits], refs[parts + 5 + splits]
     fill_bias(bias_ref, query_item_ref, key_item_ref)
     width = HEADS * HD
     masks = lane_masks(jnp.bfloat16)
@@ -224,8 +231,8 @@
         cols = slice(pair * LANES, (pair + 1) * LANES)
         value_cols = slice(width + pair * LANES, width + (pair + 1) * LANES)
         query = q_ref[:, cols] * jnp.bfloat16(HD ** (-0.5))
-        key_rows = kv_ref[:, cols]
-        value_rows = kv_ref[:, value_cols]
+        key_rows = joined(kv_refs, cols)
+        value_rows = joined(kv_refs, value_cols)
         grad_out = do_ref[:, cols]
         halves = []
         grad_key = grad_value = None
@@ -245,21 +252,23 @@
             halves.append(one_query[half * HD : (half + 1) * HD])
         grad_query = jnp.concatenate(halves, axis=0).T * HD ** (-0.5)
         dq_ref[:, cols] = grad_query.astype(dq_ref.dtype)
-        dkv_ref[:, cols] = grad_key.astype(dkv_ref.dtype)
-        dkv_ref[:, value_cols] = grad_value.astype(dkv_ref.dtype)
-
-
-def attend_backward(queries, window, grad_out, lse, query_item, key_item):
+        start = 0
+        for dkv_ref in dkv_refs:
+            there = slice(start, start + dkv_ref.shape[0])
+            dkv_ref[:, cols] = grad_key[there].astype(dkv_ref.dtype)
+            dkv_ref[:, value_cols] = grad_value[there].astype(dkv_ref.dtype)
+            start += dkv_ref.shape[0]
+
+
+def attend_backward(queries, window, grad_out, lse, query_item, key_item, splits):
     rows, width = queries.shape
-    span = window.shape[0]
-    return pl.pallas_call(
-        attend_backward_kernel,
-        out_shape=(
-            jax.ShapeDtypeStruct((rows, width), jnp.bfloat16),
-            jax.ShapeDtypeStruct((span, 2 * width), jnp.bfloat16),
-        ),
-        in_specs=[pl.BlockSpec(memory_space=pltpu.VMEM)] * 6,
-        out_specs=(pl.BlockSpec(memory_space=pltpu.VMEM),) * 2,
+    parts, span = len(window), sum(piece.shape[0] for piece in window)
+    grad_query, *grad_window = pl.pallas_call(
+        functools.partial(attend_backward_kernel, parts, splits),
+        out_shape=[jax.ShapeDtypeStruct((rows, width), jnp.bfloat16)]
+        + [jax.ShapeDtypeStruct((span // splits, 2 * width), jnp.bfloat16)] * splits,
+        in_specs=[pl.BlockSpec(memory_space=pltpu.VMEM)] * (5 + parts),
+        out_specs=[pl.BlockSpec(memory_space=pltpu.VMEM)] * (1 + splits),
         scratch_shapes=[pltpu.VMEM((span, rows), jnp.float32)],
         compiler_params=pltpu.CompilerParams(vmem_limit_bytes=VMEM_LIMIT),
         cost_estimate=pl.CostEstimate(
@@ -268,7 +277,8 @@
             bytes_accessed=8 * rows * width + 8 * span * width,
         ),
         name="attend_backward",
-    )(queries, window, grad_out, lse, query_item[None, :], key_item[:, None])
+    )(queries, *window, grad_out, lse, query_item[None, :], key_item[:, None])
+    return grad_query, grad_window
 
 
 def layer_forward(hidden, normed, queries, window, weights, gain_two, items):
@@ -284,7 +294,7 @@
     )
 
 
-def layer_backward(grad_hidden, weights, gain_two, items, saved, early):
+def layer_backward(grad_hidden, weights, gain_two, items, saved, early, splits):
     normed, queries, window, lse, attended, middle, second, upper, activated = saved
     proj_qkv, proj_out, proj_up, proj_down = weights
     branch_top = grad_hidden.astype(jnp.bfloat16)
@@ -301,7 +311,7 @@
     pairs = [(attended, branch_mid), (second, grad_upper)]
     if early:
         grad_attended, rest_full = lax.optimization_barrier((grad_attended, side_by_side(pairs)))
-    grad_query, grad_window = attend_backward(queries, window, grad_attended, lse, *items)
+    grad_query, grad_window = attend_backward(queries, window, grad_attended, lse, *items, splits)
     return grad_middle, grad_query, grad_window, (rest_full if early else pairs), lower_full, grad_gain_two
 
 
@@ -326,9 +336,7 @@
     return jnp.concatenate(parts, axis=1)
 
 
-def thirds(value, right, at):
-    joint = right.shape[1]
-    half = joint // 2
+def thirds_left(value, joint, at):
     inside = (at >= 0) & (at < value.shape[1] * joint // D)
     matrix_row, odd = at // 2 * 3, at % 2
     wanted = jnp.stack(
@@ -339,7 +347,12 @@
     )
     width = jnp.arange(value.shape[1], dtype=jnp.int32)
     choice = (width[:, None, None] == wanted[None]).astype(jnp.float32)
-    left = jnp.einsum("iw,wkv->kiv", value, choice, precision=HIGH)
+    return jnp.einsum("iw,wkv->kiv", value, choice, precision=HIGH)
+
+
+def thirds(left, right):
+    joint = right.shape[1]
+    half = joint // 2
     rights = jnp.stack(
         [
             jnp.pad(right, ((0, 0), (0, half))),
@@ -1378,6 +1391,27 @@
     before_silu = exact(features, w_time_f) + exact(text, w_text_f)
     condition, pull_silu = jax.vjp(jax.nn.silu, before_silu)
     hidden_window = dense(noisy_low, w_in) + exact(window_hot, condition)
+    lead = 2 * channels
+    features_at, text_at = lead, lead + D
+    audio_at = text_at + text_width
+    caption_at = audio_at + D * E // D
+    gains_at = caption_at + text_width * E // D
+    own_rows_count = -(-other_size // D) + 1
+    own_start = rank * other_size
+    own_row = own_start // D
+    own_at = own_row + jnp.arange(own_rows_count, dtype=jnp.int32)
+
+    def own_part(value, start):
+        reach = gains_at + 2 * own_rows_count
+        value = jnp.pad(value, ((0, 0), (start, reach - start - value.shape[1])))
+        return lax.dynamic_slice_in_dim(value, own_row, own_rows_count, axis=1)
+
+    def own_rows_at(start, amount):
+        there = start + jnp.arange(amount, dtype=jnp.int32)
+        return (there[:, None] == own_at[None, :]).astype(jnp.float32)
+
+    left_condition = own_part(features, features_at) + own_part(text, text_at)
+    caption_left = thirds_left(captions, E, own_at - caption_at)
     saved_all = []
     entering = []
     for depth in range(L):
@@ -1387,11 +1421,15 @@
             normed_window = norm_rows(hidden_window, gains_f[0]).astype(jnp.bfloat16)
             hidden, normed = hidden_window[inner], normed_window[inner]
             queries = dense(normed, proj_qkv[:, :D]).astype(jnp.bfloat16)
-            window = dense(normed_window, proj_qkv[:, D:]).astype(jnp.bfloat16)
+            window = [dense(normed_window, proj_qkv[:, D:]).astype(jnp.bfloat16)]
         else:
             normed = norm_rows(hidden, gains_f[2 * depth]).astype(jnp.bfloat16)
             window = gather_window(dense(normed, proj_qkv[:, D:]).astype(jnp.bfloat16), close)
             queries = dense(normed, proj_qkv[:, :D]).astype(jnp.bfloat16)
+        if depth == 1 and close:
+            queries, caption_left, left_condition = lax.optimization_barrier(
+                (queries, caption_left, left_condition)
+            )
         entering.append(hidden)
         hidden, saved = layer_forward(
             hidden, normed, queries, window, weights, gains_f[2 * depth + 1], items
@@ -1424,7 +1462,7 @@
         proj_qkv = weights[0]
         early = depth > 0 and close
         grad_middle, grad_query, grad_pairs, rest, lower_full, gain_grads[2 * depth + 1] = layer_backward(
-            grad_hidden, weights, gains_f[2 * depth + 1], items, saved_all[depth], early
+            grad_hidden, weights, gains_f[2 * depth + 1], items, saved_all[depth], early, 5 if depth > 0 else 1
         )
         if early:
             sent_early[depth] = [
@@ -1433,6 +1471,7 @@
             ]
         normed = saved_all[depth][0]
         if depth == 0:
+            (grad_pairs,) = grad_pairs
             qkv_parts = [(normed, grad_query), (normed_window, grad_pairs)]
             grad_normed = against_rows(grad_pairs, proj_qkv[:, D:])
             grad_own = grad_normed[inner] + against_rows(grad_query, proj_qkv[:, :D])
@@ -1441,7 +1480,7 @@
             )
             unused, pull_one = jax.vjp(norm_rows, hidden_window, gains_f[0])
         else:
-            grad_pairs = return_window(grad_pairs, rows, close).astype(jnp.bfloat16)
+            grad_pairs = return_window(grad_pairs, close).astype(jnp.bfloat16)
             grad_projected = jnp.concatenate([grad_query, grad_pairs], axis=1)
             qkv_parts = [(normed, grad_projected)]
             grad_normed = against_rows(grad_projected, proj_qkv)
@@ -1459,28 +1498,8 @@
             )
     grad_w_in = contract_rows(noisy_low.astype(jnp.float32), grad_hidden, HIGH)
     grad_condition = contract_rows(window_hot, grad_hidden, HIGH)
-    lead = 2 * channels
-    features_at, text_at = lead, lead + D
-    audio_at = text_at + text_width
-    caption_at = audio_at + D * E // D
-    gains_at = caption_at + text_width * E // D
-    own_rows_count = -(-other_size // D) + 1
-    own_start = rank * other_size
-    own_row = own_start // D
-    own_at = own_row + jnp.arange(own_rows_count, dtype=jnp.int32)
-
-    def own_part(value, start):
-        reach = gains_at + 2 * own_rows_count
-        value = jnp.pad(value, ((0, 0), (start, reach - start - value.shape[1])))
-        return lax.dynamic_slice_in_dim(value, own_row, own_rows_count, axis=1)
-
-    def own_rows_at(start, amount):
-        there = start + jnp.arange(amount, dtype=jnp.int32)
-        return (there[:, None] == own_at[None, :]).astype(jnp.float32)
-
-    left_condition = own_part(features, features_at) + own_part(text, text_at)
-    early_view = thirds(pooled, grad_audio_side, own_at - audio_at)
-    early_view = early_view + thirds(captions, grad_text_side, own_at - caption_at)
+    early_view = thirds(thirds_left(pooled, E, own_at - audio_at), grad_audio_side)
+    early_view = early_view + thirds(caption_left, grad_text_side)
     left_small = jnp.concatenate(
         [
             own_rows_at(0, lead),

time: 676 us -> 680 us (level)
  Pallas kernels: 365 us -> 373 us
    reduce_scatter x2, waiting for transfers between devices: 9.28 us -> 0.55 us  [per_device(): lax.psum_scatter(grad, 'seq', scatter_dimension=0, tiled=True)]
    pallas_call x1, Pallas kernels: 121 us -> 130 us  [scatter_grads(): pl.pallas_call(functools.partial(scatter_kernel, tuple(pieces), kinds, ca...]
    unnamed x332 -> x316, local copies, waits for them, and re-layouts: 27.7 us -> 29.3 us
  transfers between devices with their start and end apart: 15 -> 15, of which waited for: 4 -> 4; matrix products, arithmetic and copies ran while one was open for 25% -> 25% of each run, Pallas kernels for 32% -> 33%
where the time goes in v7:
time: 680 us; the launch traced here: 673 us
  Pallas kernels  373 us (55%)
  matrix products  118 us (17%)
  local copies, waits for them, and re-layouts  59.7 us (9%)
  other arithmetic  55.5 us (8%)
  starting transfers between devices  26.7 us (4%)
  between operations  24.1 us (4%)
  waiting for transfers between devices  16.2 us (2%)
    pallas_call x1, Pallas kernels, gather_pieces(): pl.pallas_call(functools.partial(gather_kernel, tuple(shared)), out_shape...  133 us
    pallas_call x1, Pallas kernels, scatter_grads(): pl.pallas_call(functools.partial(scatter_kernel, tuple(pieces), kinds, ca...  130 us
    dot_general x12, matrix products, dense(): return jnp.dot(left, right, preferred_element_type=jnp.float32)  35.6 us
    pallas_call x2, Pallas kernels, attend_backward(): pl.pallas_call(functools.partial(attend_backward_kernel, parts, splits),...  33.5 us
    dot_general x14, matrix products, contract_rows(): lax.dot_general(left, right, (((0,), (0,)), ((), ())), precision=precisio...  33 us
    dot_general x12, matrix products, against_rows(): lax.dot_general(left, right, (((1,), (1,)), ((), ())), precision=precisio...  29.9 us
    unnamed x316, local copies, waits for them, and re-layouts  29.3 us
    pallas_call x2, Pallas kernels, attend_forward(): pl.pallas_call(functools.partial(attend_forward_kernel, parts), out_shape...  24.2 us
  transfers between devices with their start and end apart: 15, of which 4 were waited for; matrix products, arithmetic and copies ran while one was open for 25% of the time, Pallas kernels for 33%

profile of v7, /device:TPU:0, one launch (start us, length us, event | category | flops | bytes accessed | tf_op | source)
XLA Modules:
  0.0 673.0 jit_solution(4257010546923126795)
XLA Ops:
  8.8 3.5 lay_out.1
  17.5 132.9 %gather_pieces.1 = (f32[16,40,256]{2,1,0:T(8,128)}, bf16[16,992,128]{2,1,0:T(8,128)(2,1)}, bf16[16,48,6144]{2,1,0:T(8,128)(2,1)}, bf16[16,192,768]{2,1,0:T(8,128...) custom-call(f32[40,256]{1,0:T(8,128)} %maximum_bitcast_fusion.refs_0_, ...), custom_call_target="tpu_custom_call" | custom-call | tf_op jit(solution)/shard_map/gather_pieces/pallas_call | solution.py:759
  150.4 4.0 unpack_others.1
  162.9 2.0 fusion.179
  166.8 7.6 %convolution_convert_fusion.refs_0_ = bf16[1280,1536]{1,0:T(8,128)(2,1)} fusion(bf16[1280,768]{0,1:T(8,128)(2,1)S(1)} %multiply_convert_fusion, bf16[768,6144]{1,0:T(8,128)(2,1)} %bitcast.207), kind=kOutput, calls=%fused_computation.1 | convolution fusion | flops 3021864960 | bytes 8257536 | tf_op jit(solution)/shard_map/dot_general | solution.py:51
  174.4 1.8 convolution_convert_fusion.14.q_ref
  176.6 12.1 %attend_forward.2 = (bf16[256,768]{1,0:T(8,128)(2,1)S(1)}, f32[16,256]{1,0:T(8,128)S(1)}) custom-call(bf16[256,768]{1,0:T(8,128)(2,1)S(1)} %convolution_convert_fusion.14.q_ref, bf16[1280,1536]{1,0:T(8,128)(2,1)} %convolution_convert_fusion.refs_0_, s32[1,256]{1,0:T(1,128)S(1)} %bitcast.186, s32[1280,1]{1,0:T(8,128)S(1)} %reshape_select_fusion.refs_2_.refs_4_), custom_call_target="tpu_custom_call" | custom-call | flops 1006632960 | bytes 4718592 | tf_op jit(solution)/shard_map/attend_forward/pallas_call | solution.py:204
  188.7 1.8 fusion.180
  190.8 4.3 fusion.6
  195.2 2.7 fusion.181
  198.7 3.4 convolution_convert_fusion.7
  202.1 4.2 collective-permute-start
  206.3 2.9 collective-permute-start.1
  213.3 2.5 convolution_convert_fusion.13.q_ref
  217.7 1.7 fusion.36
  230.9 8.1 %collective-permute-done.3 = bf16[256,1536]{1,0:T(8,128)(2,1)} collective-permute-done((bf16[256,1536]{1,0:T(8,128)(2,1)}, bf16[256,1536]{1,0:T(8,128)(2,1)}, u32[]{:S(2)}, u32[]{:S(2)}) %collective-permute-start.3) | collective-permute-done | bytes 786464 | tf_op jit(solution)/shard_map/ppermute | solution.py:45
  240.2 1.9 copy-done.73
  242.1 12.1 %attend_forward.3 = (bf16[256,768]{1,0:T(8,128)(2,1)S(1)}, f32[16,256]{1,0:T(8,128)S(1)}) custom-call(bf16[256,768]{1,0:T(8,128)(2,1)S(1)} %copy-done.21, bf16[1280,1536]{1,0:T(8,128)(2,1)} %copy-done.73, s32[1,256]{1,0:T(1,128)S(1)} %bitcast.187, s32[1280,1]{1,0:T(8,128)S(1)} %copy-done.7), custom_call_target="tpu_custom_call" | custom-call | flops 1006632960 | bytes 4718592 | tf_op jit(solution)/shard_map/attend_forward/pallas_call | solution.py:204
  254.2 2.2 fusion.182
  256.7 4.0 fusion.2
  260.7 2.5 fusion.183
  265.5 2.1 multiply_reduce_fusion.27
  269.6 13.2 %sum_over_seq.1 = f32[16,8,128]{2,1,0:T(8,128)} custom-call(f32[16,8,128]{2,1,0:T(8,128)} %fusion.103.x_ref), custom_call_target="tpu_custom_call" | custom-call | flops 16384 | bytes 262144 | tf_op jit(solution)/shard_map/sum_over_seq/pallas_call | solution.py:462
  288.8 2.4 multiply_reduce_fusion.22
  294.0 2.1 multiply_reduce_fusion.3
  297.9 4.4 convolution_convert_fusion.1
  302.9 5.0 multiply_reduce_fusion.20
  310.8 2.3 iota_compare_fusion.2
  313.1 3.4 multiply_reduce_fusion.18
  316.5 3.3 multiply_reduce_fusion.19
  319.8 7.3 %fusion.23 = bf16[256,3072]{1,0:T(8,128)(2,1)S(1)} fusion(f32[256,3072]{1,0:T(8,128)} %copy-done.139, bf16[3072,768]{1,0:T(8,128)(2,1)} %bitcast.228, f32[256,768]{0,1:T(8,128)S(1)} %copy-done.49, f32[256]{0:T(256)S(1)} %negate_multiply_fusion.4), kind=kOutput, calls=%fused_computation.44 | convolution fusion | flops 1224081408 | bytes 10224640 | tf_op jit(solution)/shard_map/dot_general | solution.py:69
  332.5 2.9 pad_maximum_fusion.1
  335.6 16.5 %attend_backward.2 = (bf16[256,768]{1,0:T(8,128)(2,1)S(1)}, bf16[256,1536]{1,0:T(8,128)(2,1)}, bf16[256,1536]{1,0:T(8,128)(2,1)}, bf16[256,1536]{1,0:T(8,128)(2,...) custom-call(bf16[256,768]{1,0:T(8,128)(2,1)S(1)} %copy-done.22, bf16[1280,1536]{1,0:T(8,128)(2,1)} %copy-done.73, ...), custom_call_target="tpu_custom_call" | custom-call | flops 2516582400 | bytes 9437184 | tf_op jit(solution)/shard_map/attend_backward/pallas_call | solution.py:266
  354.7 3.9 collective-permute-start.6
  358.6 4.6 collective-permute-start.7
  371.2 2.0 fusion.37
  374.7 2.4 collective-permute-done.4
  377.6 5.2 collective-permute-done.7
  382.8 2.3 add_convert_fusion
  385.2 3.5 multiply_reduce_fusion.5
  390.8 3.6 fusion.16
  397.4 17.0 %attend_backward.3 = (bf16[256,768]{1,0:T(8,128)(2,1)S(1)}, bf16[1280,1536]{1,0:T(8,128)(2,1)}) custom-call(bf16[256,768]{1,0:T(8,128)(2,1)S(1)} %copy-done.24, bf16[1280,1536]{1,0:T(8,128)(2,1)} %convolution_convert_fusion.refs_0_, bf16[256,768]{1,0:T(8,128)(2,1)S(1)} %convolution_convert_fusion.11.refs_1_, f32[16,256]{1,0:T(8,128)S(1)} %get-tuple-element.101.refs_2_, ...), custom_call_target="tpu_custom_call" | custom-call | flops 2516582400 | bytes 9437184 | tf_op jit(solution)/shard_map/attend_backward/pallas_call | solution.py:266
  414.4 6.1 fusion.27
  420.5 1.8 convolution_add_fusion.1
  425.4 1.9 multiply_reduce_fusion
  431.3 1.9 fusion.25
  433.2 2.2 fusion.24
  437.0 2.5 convolution_convert_fusion.9
  439.6 2.4 copy.133
  443.5 1.8 copy.134
  445.3 6.6 convolution_convert_fusion.2
  454.9 3.4 convolution_convert_fusion.6
  458.3 7.0 %pad_maximum_fusion = bf16[768,6144]{1,0:T(8,128)(2,1)} fusion(bf16[768,3072]{1,0:T(8,128)(2,1)S(1)} %convolution_convert_fusion.3, bf16[768,768]{1,0:T(8,128)(2,1)S(1)} %copy.134, bf16[768,1536]{1,0:T(8,128)(2,1)S(1)} %convolution_convert_fusion.6, bf16[768,768]{1,0:T(8,128)(2,1)S(1)} %copy-done.43), kind=kLoop, calls=%fused_computation | loop fusion | flops 37748736 | bytes 18874368 | tf_op jit(solution)/shard_map/concatenate | solution.py:319
  465.4 2.9 convolution_convert_fusion.4
  468.2 1.7 multiply_reduce_fusion.16
  472.5 130.0 %scatter_grads.1 = (f32[48,2304]{1,0:T(8,128)S(1)}, f32[48,6144]{1,0:T(8,128)}, f32[192,768]{1,0:T(8,128)S(1)}, bf16[48,2304]{1,0:T(8,128)(2,1)S(1)}, bf16[48,61...) custom-call(bf16[16,48,2304]{2,1,0:T(8,128)(2,1)} %bitcast.191, ...), custom_call_target="tpu_custom_call" | custom-call | tf_op jit(solution)/shard_map/scatter_grads/pallas_call | solution.py:1089
  606.0 1.7 slice.180
  610.0 2.5 fusion.33
  612.5 1.9 reshape.735
  614.4 1.9 dynamic_slice.58
  619.0 1.8 multiply_reduce_fusion.17
  624.0 10.9 %share_over_all.1 = f32[32,8,128]{2,1,0:T(8,128)} custom-call(f32[8,128]{1,0:T(8,128)} %broadcast_in_dim.195.x_ref), custom_call_target="tpu_custom_call" | custom-call | tf_op jit(solution)/shard_map/share_over_all/pallas_call | solution.py:527
  638.5 20.7 %step_layers.1 = (f32[6912,128]{1,0:T(8,128)}, f32[6912,128]{1,0:T(8,128)}, f32[6912,128]{1,0:T(8,128)}, f32[6912,128]{1,0:T(8,128)}, f32[6912,128]{1,0:T(8,128)}) custom-call(f32[2]{0:T(128)S(1)} %pad_maximum_fusion.11.factors, f32[48,6144]{1,0:T(8,128)} %get-tuple-element.113.refs_0_, f32[192,768]{1,0:T(8,128)S(1)} %get-tuple-element.114.refs_1_, ...), custom_call_target="tpu_custom_call" | custom-call | tf_op jit(solution)/shard_map/step_layers/pallas_call | solution.py:1280
  659.3 3.1 multiply_subtract_fusion
  (498 shorter events, 104.7 us)
Async XLA Ops:
  7.2 461.0 %reduce-scatter.3.cloned.1.call-start = ((), (), s32[]{:S(2)}) async-start(), calls=%async_computation.2 | async-start | bytes 5013504 | tf_op jit(solution)/shard_map/reduce_scatter | solution.py:1469
  16.3 205.0 %copy-start.81 = (s32[1280]{0:T(1024)}, s32[1280]{0:T(1024)S(1)}, u32[]{:S(2)}) copy-start(s32[1280]{0:T(1024)S(1)} %and_select_fusion) | copy-start | bytes 15364
  17.5 138.0 %copy-start.133 = (s32[1,12]{1,0:T(1,128)S(1)}, s32[1,12]{1,0:T(1,128)}, u32[]{:S(2)}) copy-start(s32[1,12]{1,0:T(1,128)} %param.26) | copy-start | bytes 148
  155.5 42.6 %copy-start.86 = (f32[768]{0:T(1024)}, f32[768]{0:T(1024)S(1)}, u32[]{:S(2)}) copy-start(f32[768]{0:T(1024)S(1)} %get-tuple-element.176) | copy-start | bytes 9220
  155.5 61.6 %copy-start.113 = (pred[12]{0:T(512)(128)(4,1)}, pred[12]{0:T(512)(128)(4,1)S(1)}, u32[]{:S(2)}) copy-start(pred[12]{0:T(512)(128)(4,1)S(1)} %compare_bitcast_fusion) | copy-start | bytes 40
  164.9 23.9 %copy-start.25 = (f32[1280,768]{0,1:T(8,128)}, f32[1280,768]{0,1:T(8,128)S(1)}, u32[]{:S(2)}) copy-start(f32[1280,768]{0,1:T(8,128)S(1)} %get-tuple-element.187) | copy-start | bytes 11796484
  176.2 12.5 %copy-start.23 = (bf16[256,768]{1,0:T(8,128)(2,1)}, bf16[256,768]{1,0:T(8,128)(2,1)S(1)}, u32[]{:S(2)}) copy-start(bf16[256,768]{1,0:T(8,128)(2,1)S(1)} %convolution_convert_fusion.14.q_ref) | copy-start | bytes 1179652
  176.5 12.3 %copy-start.6 = (s32[1280,1]{1,0:T(8,128)}, s32[1280,1]{1,0:T(8,128)S(1)}, u32[]{:S(2)}) copy-start(s32[1280,1]{1,0:T(8,128)S(1)} %reshape_select_fusion.refs_2_.refs_4_) | copy-start | bytes 15364
  197.9 18.0 %copy-start.101 = (f32[256]{0:T(256)}, f32[256]{0:T(256)S(1)}, u32[]{:S(2)}) copy-start(f32[256]{0:T(256)S(1)} %broadcast_multiply_fusion.3) | copy-start | bytes 3076
  198.0 17.8 %copy-start.108 = (f32[256]{0:T(256)}, f32[256]{0:T(256)S(1)}, u32[]{:S(2)}) copy-start(f32[256]{0:T(256)S(1)} %multiply_reduce_fusion.13) | copy-start | bytes 3076
  198.0 17.8 %copy-start.104 = (f32[256]{0:T(256)}, f32[256]{0:T(256)S(1)}, u32[]{:S(2)}) copy-start(f32[256]{0:T(256)S(1)} %fusion.145) | copy-start | bytes 3076
  198.2 15.1 %copy-start.44 = (bf16[256,768]{0,1:T(8,128)(2,1)}, bf16[256,768]{0,1:T(8,128)(2,1)S(1)}, u32[]{:S(2)}) copy-start(bf16[256,768]{0,1:T(8,128)(2,1)S(1)} %multiply_convert_fusion.4) | copy-start | bytes 1179652
  198.7 18.5 %copy-start.135 = (s32[1,12]{1,0:T(1,128)S(1)}, s32[1,12]{1,0:T(1,128)}, u32[]{:S(2)}) copy-start(s32[1,12]{1,0:T(1,128)} %param.24) | copy-start | bytes 148
  198.7 20.8 %copy-start.5 = (bf16[768,512]{1,0:T(8,128)(2,1)S(1)}, bf16[768,512]{1,0:T(8,128)(2,1)}, u32[]{:S(2)}) copy-start(bf16[768,512]{1,0:T(8,128)(2,1)} %copy-done.4) | copy-start | bytes 2359300
  202.1 21.9 %collective-permute-start = (bf16[256,1536]{1,0:T(8,128)(2,1)}, bf16[256,1536]{1,0:T(8,128)(2,1)}, u32[]{:S(2)}, u32[]{:S(2)}) collective-permute-start(bf16[256,1536]{1,0:T(8,128)(2,1)} %convolution_convert_fusion.7), channel_id=1, source_target_pairs={{0,2},{1,3},{2,6},{3,7},{6,4},{7,5},{4,8},{5,9},{8,10},{9,11},{10,... | collective-permute-start | bytes 2359304 | tf_op jit(solution)/shard_map/ppermute | solution.py:45
  206.3 19.9 %collective-permute-start.1 = (bf16[256,1536]{1,0:T(8,128)(2,1)}, bf16[256,1536]{1,0:T(8,128)(2,1)}, u32[]{:S(2)}, u32[]{:S(2)}) collective-permute-start(bf16[256,1536]{1,0:T(8,128)(2,1)} %convolution_convert_fusion.7), channel_id=1, source_target_pairs={{0,1},{1,2},{2,3},{3,6},{6,7},{7,4},{4,5},{5,8},{8,9},{9,10},{10,1... | collective-permute-start | bytes 2359304 | tf_op jit(solution)/shard_map/ppermute | solution.py:45
  209.3 20.4 %collective-permute-start.2 = (bf16[256,1536]{1,0:T(8,128)(2,1)}, bf16[256,1536]{1,0:T(8,128)(2,1)}, u32[]{:S(2)}, u32[]{:S(2)}) collective-permute-start(bf16[256,1536]{1,0:T(8,128)(2,1)} %convolution_convert_fusion.7), channel_id=1, source_target_pairs={{1,0},{2,1},{3,2},{6,3},{7,6},{4,7},{5,4},{8,5},{9,8},{10,9},{11,1... | collective-permute-start | bytes 2359304 | tf_op jit(solution)/shard_map/ppermute | solution.py:45
  210.6 28.4 %collective-permute-start.3 = (bf16[256,1536]{1,0:T(8,128)(2,1)}, bf16[256,1536]{1,0:T(8,128)(2,1)}, u32[]{:S(2)}, u32[]{:S(2)}) collective-permute-start(bf16[256,1536]{1,0:T(8,128)(2,1)} %convolution_convert_fusion.7), channel_id=1, source_target_pairs={{2,0},{3,1},{6,2},{7,3},{4,6},{5,7},{8,4},{9,5},{10,8},{11,9},{14,... | collective-permute-start | bytes 2359304 | tf_op jit(solution)/shard_map/ppermute | solution.py:45
  211.9 101.2 %collective-permute-start.12 = (f32[1,125088]{1,0:T(1,128)}, f32[1,125088]{1,0:T(1,128)}, u32[]{:S(2)}, u32[]{:S(2)}) collective-permute-start(f32[1,125088]{1,0:T(1,128)} %param.19), channel_id=1, source_target_pairs={{0,16},{16,0},{1,17},{17,1},{2,18},{18,2},{3,19},{19,3},{4,20},{20... | collective-permute-start | bytes 1501064 | tf_op jit(solution)/shard_map/ppermute | solution.py:1300
  224.0 92.5 %collective-permute-start.10 = (f32[1,125088]{1,0:T(1,128)}, f32[1,125088]{1,0:T(1,128)}, u32[]{:S(2)}, u32[]{:S(2)}) collective-permute-start(f32[1,125088]{1,0:T(1,128)} %param.17), channel_id=1, source_target_pairs={{0,16},{16,0},{1,17},{17,1},{2,18},{18,2},{3,19},{19,3},{4,20},{20... | collective-permute-start | bytes 1501064 | tf_op jit(solution)/shard_map/ppermute | solution.py:1300
  226.2 16.0 %copy-start.7 = (s32[1280,1]{1,0:T(8,128)S(1)}, s32[1280,1]{1,0:T(8,128)}, u32[]{:S(2)}) copy-start(s32[1280,1]{1,0:T(8,128)} %copy-done.6) | copy-start | bytes 15364
  226.2 16.0 %copy-start.21 = (bf16[256,768]{1,0:T(8,128)(2,1)S(1)}, bf16[256,768]{1,0:T(8,128)(2,1)}, u32[]{:S(2)}) copy-start(bf16[256,768]{1,0:T(8,128)(2,1)} %convolution_convert_fusion.13.q_ref) | copy-start | bytes 1179652
  226.2 412.2 %collective-permute-start.8 = (f32[6912,128]{1,0:T(8,128)}, f32[6912,128]{1,0:T(8,128)}, u32[]{:S(2)}, u32[]{:S(2)}) collective-permute-start(f32[6912,128]{1,0:T(8,128)} %bitcast.195), channel_id=1, source_target_pairs={{0,16},{16,0},{1,17},{17,1},{2,18},{18,2},{3,19},{19,3},{4,20},{20... | collective-permute-start | bytes 10616840 | tf_op jit(solution)/shard_map/ppermute | solution.py:1300
  242.1 12.1 %copy-start.38 = (f32[256,768]{0,1:T(8,128)S(1)}, f32[256,768]{0,1:T(8,128)}, u32[]{:S(2)}) copy-start(f32[256,768]{0,1:T(8,128)} %copy-done.37) | copy-start | bytes 2359300
  302.4 17.4 %copy-start.49 = (f32[256,768]{0,1:T(8,128)S(1)}, f32[256,768]{0,1:T(8,128)}, u32[]{:S(2)}) copy-start(f32[256,768]{0,1:T(8,128)} %copy-done.48) | copy-start | bytes 2359300
  302.4 168.1 %reduce-scatter.5.cloned.1.call-start = ((), (), s32[]{:S(2)}) async-start(), calls=%async_computation.3 | async-start | bytes 6266880 | tf_op jit(solution)/shard_map/reduce_scatter | solution.py:1469
  313.1 14.0 %slice-start = ((s8[9437184]{0:T(1024)(128)(4,1)}), s8[4194304]{0:T(1024)(128)(4,1)S(1)}, s32[]{:S(2)}) async-start(s8[9437184]{0:T(1024)(128)(4,1)} %bitcast.203), calls=%async_computation.4 | async-start | bytes 8388608
  335.5 27.7 %copy-start.126 = (f32[12]{0:T(128)S(1)}, f32[12]{0:T(128)}, u32[]{:S(2)}) copy-start(f32[12]{0:T(128)} %copy-done.125) | copy-start | bytes 148
  335.5 27.7 %copy-start.136 = (f32[12]{0:T(128)S(1)}, f32[12]{0:T(128)}, u32[]{:S(2)}) copy-start(f32[12]{0:T(128)} %get-tuple-element.141) | copy-start | bytes 148
  335.5 27.7 %copy-start.74 = (f32[12,512]{1,0:T(8,128)S(1)}, f32[12,512]{1,0:T(8,128)}, u32[]{:S(2)}) copy-start(f32[12,512]{1,0:T(8,128)} %get-tuple-element.199) | copy-start | bytes 73732
  335.5 27.7 %copy-start.93 = (f32[12,512]{1,0:T(8,128)S(1)}, f32[12,512]{1,0:T(8,128)}, u32[]{:S(2)}) copy-start(f32[12,512]{1,0:T(8,128)} %get-tuple-element.203) | copy-start | bytes 73732
  335.5 27.7 %copy-start.127 = (f32[12]{0:T(128)S(1)}, f32[12]{0:T(128)}, u32[]{:S(2)}) copy-start(f32[12]{0:T(128)} %add_rsqrt_fusion.1) | copy-start | bytes 148
  335.5 27.9 %copy-start.29 = (f32[256,768]{0,1:T(8,128)S(1)}, f32[256,768]{0,1:T(8,128)}, u32[]{:S(2)}) copy-start(f32[256,768]{0,1:T(8,128)} %copy-done.27) | copy-start | bytes 2359300
  335.5 28.2 %copy-start.120 = (f32[12]{0:T(128)S(1)}, f32[12]{0:T(128)}, u32[]{:S(2)}) copy-start(f32[12]{0:T(128)} %copy-done.119) | copy-start | bytes 148
  335.5 28.2 %copy-start.122 = (f32[12]{0:T(128)S(1)}, f32[12]{0:T(128)}, u32[]{:S(2)}) copy-start(f32[12]{0:T(128)} %copy-done.121) | copy-start | bytes 148
  335.5 28.2 %copy-start.129 = (f32[12]{0:T(128)S(1)}, f32[12]{0:T(128)}, u32[]{:S(2)}) copy-start(f32[12]{0:T(128)} %copy-done.128) | copy-start | bytes 148
  335.5 28.2 %copy-start.131 = (f32[12]{0:T(128)S(1)}, f32[12]{0:T(128)}, u32[]{:S(2)}) copy-start(f32[12]{0:T(128)} %copy-done.130) | copy-start | bytes 148
  335.6 28.2 %copy-start.132 = (f32[12]{0:T(128)S(1)}, f32[12]{0:T(128)}, u32[]{:S(2)}) copy-start(f32[12]{0:T(128)} %get-tuple-element.140) | copy-start | bytes 148
  352.1 24.9 %collective-permute-start.4 = (bf16[256,1536]{1,0:T(8,128)(2,1)}, bf16[256,1536]{1,0:T(8,128)(2,1)}, u32[]{:S(2)}, u32[]{:S(2)}) collective-permute-start(bf16[256,1536]{1,0:T(8,128)(2,1)} %get-tuple-element.95), channel_id=1, source_target_pairs={{2,0},{3,1},{6,2},{7,3},{4,6},{5,7},{8,4},{9,5},{10,8},{11,9},{14,... | collective-permute-start | bytes 2359304 | tf_op jit(solution)/shard_map/ppermute | solution.py:45
  353.4 24.3 %collective-permute-start.5 = (bf16[256,1536]{1,0:T(8,128)(2,1)}, bf16[256,1536]{1,0:T(8,128)(2,1)}, u32[]{:S(2)}, u32[]{:S(2)}) collective-permute-start(bf16[256,1536]{1,0:T(8,128)(2,1)} %get-tuple-element.96), channel_id=1, source_target_pairs={{1,0},{2,1},{3,2},{6,3},{7,6},{4,7},{5,4},{8,5},{9,8},{10,9},{11,1... | collective-permute-start | bytes 2359304 | tf_op jit(solution)/shard_map/ppermute | solution.py:45
  354.7 23.0 %collective-permute-start.6 = (bf16[256,1536]{1,0:T(8,128)(2,1)}, bf16[256,1536]{1,0:T(8,128)(2,1)}, u32[]{:S(2)}, u32[]{:S(2)}) collective-permute-start(bf16[256,1536]{1,0:T(8,128)(2,1)} %get-tuple-element.97), channel_id=1, source_target_pairs={{0,1},{1,2},{2,3},{3,6},{6,7},{7,4},{4,5},{5,8},{8,9},{9,10},{10,1... | collective-permute-start | bytes 2359304 | tf_op jit(solution)/shard_map/ppermute | solution.py:45
  358.6 24.2 %collective-permute-start.7 = (bf16[256,1536]{1,0:T(8,128)(2,1)}, bf16[256,1536]{1,0:T(8,128)(2,1)}, u32[]{:S(2)}, u32[]{:S(2)}) collective-permute-start(bf16[256,1536]{1,0:T(8,128)(2,1)} %get-tuple-element.98), channel_id=1, source_target_pairs={{0,2},{1,3},{2,6},{3,7},{6,4},{7,5},{4,8},{5,9},{8,10},{9,11},{10,... | collective-permute-start | bytes 2359304 | tf_op jit(solution)/shard_map/ppermute | solution.py:45
  370.4 12.4 %copy-start.61 = (bf16[256,1536]{1,0:T(8,128)(2,1)S(1)}, bf16[256,1536]{1,0:T(8,128)(2,1)}, u32[]{:S(2)}) copy-start(bf16[256,1536]{1,0:T(8,128)(2,1)} %get-tuple-element.94) | copy-start | bytes 2359300
  373.2 12.0 %copy-start.87 = (f32[768]{0:T(1024)S(1)}, f32[768]{0:T(1024)}, u32[]{:S(2)}) copy-start(f32[768]{0:T(1024)} %copy-done.86) | copy-start | bytes 9220
  373.2 12.0 %copy-start.102 = (f32[256]{0:T(256)S(1)}, f32[256]{0:T(256)}, u32[]{:S(2)}) copy-start(f32[256]{0:T(256)} %copy-done.101) | copy-start | bytes 3076
  373.2 12.0 %copy-start.105 = (f32[256]{0:T(256)S(1)}, f32[256]{0:T(256)}, u32[]{:S(2)}) copy-start(f32[256]{0:T(256)} %copy-done.104) | copy-start | bytes 3076
  377.0 261.4 %collective-permute-start.9 = (f32[6912,128]{1,0:T(8,128)}, f32[6912,128]{1,0:T(8,128)}, u32[]{:S(2)}, u32[]{:S(2)}) collective-permute-start(f32[6912,128]{1,0:T(8,128)} %bitcast.19.refs_12_), channel_id=1, source_target_pairs={{0,16},{16,0},{1,17},{17,1},{2,18},{18,2},{3,19},{19,3},{4,20},{20... | collective-permute-start | bytes 10616840 | tf_op jit(solution)/shard_map/ppermute | solution.py:1300
  396.7 33.7 %copy-start.40 = (f32[256,768]{0,1:T(8,128)}, f32[256,768]{0,1:T(8,128)S(1)}, u32[]{:S(2)}) copy-start(f32[256,768]{0,1:T(8,128)S(1)} %add_add_fusion.5) | copy-start | bytes 2359300
  472.5 136.3 %copy-start.114 = (pred[12]{0:T(512)(128)(4,1)S(1)}, pred[12]{0:T(512)(128)(4,1)}, u32[]{:S(2)}) copy-start(pred[12]{0:T(512)(128)(4,1)} %copy-done.113) | copy-start | bytes 40
  472.5 137.5 %copy-start.69 = (f32[57,164]{1,0:T(8,128)S(1)}, f32[57,164]{1,0:T(8,128)}, u32[]{:S(2)}) copy-start(f32[57,164]{1,0:T(8,128)} %pad_maximum_fusion.9) | copy-start | bytes 112180
  472.5 137.5 %copy-start.124 = (f32[1,164]{1,0:T(1,128)S(1)}, f32[1,164]{1,0:T(1,128)}, u32[]{:S(2)}) copy-start(f32[1,164]{1,0:T(1,128)} %compare_convert_fusion.1) | copy-start | bytes 1972
  606.0 32.4 %copy-start.3 = (bf16[192,768]{1,0:T(8,128)(2,1)S(1)}, bf16[192,768]{1,0:T(8,128)(2,1)}, u32[]{:S(2)}) copy-start(bf16[192,768]{1,0:T(8,128)(2,1)} %reduce-scatter.3.cloned.1.call-done.refs_3_.refs_4_) | copy-start | bytes 884740
  609.9 28.4 %copy-start.11 = (bf16[48,3840]{1,0:T(8,128)(2,1)S(1)}, bf16[48,3840]{1,0:T(8,128)(2,1)}, u32[]{:S(2)}) copy-start(bf16[48,3840]{1,0:T(8,128)(2,1)} %copy-done.10) | copy-start | bytes 1105924
  610.0 28.4 %copy-start.15 = (bf16[192,768]{1,0:T(8,128)(2,1)S(1)}, bf16[192,768]{1,0:T(8,128)(2,1)}, u32[]{:S(2)}) copy-start(bf16[192,768]{1,0:T(8,128)(2,1)} %copy-done.14) | copy-start | bytes 884740
  610.0 28.4 %copy-start.17 = (bf16[192,768]{1,0:T(8,128)(2,1)S(1)}, bf16[192,768]{1,0:T(8,128)(2,1)}, u32[]{:S(2)}) copy-start(bf16[192,768]{1,0:T(8,128)(2,1)} %copy-done.16) | copy-start | bytes 884740
  610.0 28.4 %copy-start.19 = (bf16[48,2304]{1,0:T(8,128)(2,1)S(1)}, bf16[48,2304]{1,0:T(8,128)(2,1)}, u32[]{:S(2)}) copy-start(bf16[48,2304]{1,0:T(8,128)(2,1)} %copy-done.18) | copy-start | bytes 663556
  616.3 42.9 %collective-permute-start.11 = (bf16[125088]{0:T(1024)(128)(2,1)}, bf16[125088]{0:T(1024)(128)(2,1)}, u32[]{:S(2)}, u32[]{:S(2)}) collective-permute-start(bf16[125088]{0:T(1024)(128)(2,1)} %dynamic_slice.58), channel_id=1, source_target_pairs={{0,16},{16,0},{1,17},{17,1},{2,18},{18,2},{3,19},{19,3},{4,20},{20... | collective-permute-start | bytes 750536 | tf_op jit(solution)/shard_map/ppermute | solution.py:1300
  638.4 20.8 %copy-start.42 = (f32[125952]{0:T(1024)S(1)}, f32[125952]{0:T(1024)}, u32[]{:S(2)}) copy-start(f32[125952]{0:T(1024)} %reshape.735) | copy-start | bytes 1511428
  638.4 20.8 %copy-start.54 = (f32[125088]{0:T(1024)S(1)}, f32[125088]{0:T(1024)}, u32[]{:S(2)}) copy-start(f32[125088]{0:T(1024)} %param.15) | copy-start | bytes 1501060
  638.4 20.8 %copy-start.55 = (f32[125088]{0:T(1024)S(1)}, f32[125088]{0:T(1024)}, u32[]{:S(2)}) copy-start(f32[125088]{0:T(1024)} %get-tuple-element.220) | copy-start | bytes 1501060
  638.5 20.8 %copy-start.56 = (f32[125088]{0:T(1024)S(1)}, f32[125088]{0:T(1024)}, u32[]{:S(2)}) copy-start(f32[125088]{0:T(1024)} %get-tuple-element.221) | copy-start | bytes 1501060
  638.5 20.8 %copy-start.57 = (f32[125088]{0:T(1024)S(1)}, f32[125088]{0:T(1024)}, u32[]{:S(2)}) copy-start(f32[125088]{0:T(1024)} %multiply_reduce_fusion.18) | copy-start | bytes 1501060
  638.5 20.8 %copy-start.58 = (f32[125088]{0:T(1024)S(1)}, f32[125088]{0:T(1024)}, u32[]{:S(2)}) copy-start(f32[125088]{0:T(1024)} %multiply_reduce_fusion.19) | copy-start | bytes 1501060
  638.5 20.8 %copy-start.62 = (f32[125088]{0:T(1024)S(1)}, f32[125088]{0:T(1024)}, u32[]{:S(2)}) copy-start(f32[125088]{0:T(1024)} %param.21) | copy-start | bytes 1501060
  (105 other events, 415.5 us)
Sparse Core Ops, SparseCore 0:
  302.5 79.4 reduce-scatter.2
  386.5 84.0 reduce-scatter.4
